TPU v7x, 32 devices: a whole 2x2x4 slice. The times are simulated.
32 devices in a mesh: grp: 2 (over y), depth: 4 (over z), shot: 2 (over x), lat: 2 (over core).
Axes of the slice: x: 2, y: 2, z: 4, core: 2. Of those that a mesh axis runs over, the one named last changes fastest.
Arguments:
- fwd_prev: float32 [8, 8, 128, 128], P(('grp', 'shot'), 'depth', 'lat'), parts along dimension 0, may hold values from -6 to 6
- fwd_now: float32 [8, 8, 128, 128], P(('grp', 'shot'), 'depth', 'lat'), parts along dimension 0, may hold values from -6 to 6
- adj_late: float32 [8, 8, 128, 128], P(('grp', 'shot'), 'depth', 'lat'), parts along dimension 0, may hold values from -6 to 6
- adj_last: float32 [8, 8, 128, 128], P(('grp', 'shot'), 'depth', 'lat'), parts along dimension 0, may hold values from -6 to 6
- velocity: float32 [16, 128, 128], P(('grp', 'depth'), 'lat', 'shot'), parts along dimension 0, may hold values from 1.5 to 4.5
- density: float32 [16, 128, 128], P(('grp', 'depth'), 'lat'), parts along dimension 0, may hold values from 1.5 to 2.5
- wavelet: float32 [8, 2], P(('grp', 'shot')), parts along dimension 0, may hold values from -48 to 48
- source_cell: int32 [8], P(('grp', 'shot')), parts along dimension 0, may hold values from 0 to 131071
- receiver_cell: int32 [8, 2048], P(('grp', 'shot')), parts along dimension 0, may hold values from 0 to 131071
- observed: float32 [8, 2, 2048], P(('grp', 'shot')), parts along dimension 0, may hold values from -18 to 18
Outputs:
- updated_velocity: float32 [16, 128, 128], P(('grp', 'depth'), 'lat', 'shot'), parts along dimension 0
- update_direction: float32 [16, 128, 128], P(('grp', 'depth'), 'lat', 'shot'), parts along dimension 0
There are 2 independent parts, one for each index of `grp`. A program takes and returns all parts, laid end to end along the dimension named above; each array names one. Nothing has to cross between parts.
Inputs may be any that keep to these rules, and one draw needn't show every extreme that they name: `source_cell`: a flattened cell index depth * 128 * 128 + x * 128 + y. `receiver_cell`: flattened cell indices depth * 128 * 128 + x * 128 + y; a cell may repeat.
All inputs are finite; a program needn't handle non-finite values. Where the computation divides by a largest or mean magnitude, that divisor is 1e-20 or more.
Results may differ from a plain program's by a relative error of at most 0.00002.
Values sent between devices are 32-bit elements; how exact they have to be, the bound alone decides.
No kernel may reach another device: no remote copies, remote signals or barrier semaphores. Data moves between devices by JAX's collectives and lax.ppermute only.
A program may use at most 64 MiB of HBM per device.

v0:
```python
import jax
import jax.numpy as jnp
from jax import lax
from jax.sharding import PartitionSpec as P

ITERS = 2


COURANT = 0.1
STEP_SIZE = 0.1
EPSILON = 1e-06
NEIGHBOURS = ((1, 0, 0), (-1, 0, 0), (0, 1, 0), (0, -1, 0), (0, 0, 1), (0, 0, -1))


def with_halo(block, sides, width):
    for axis, dim in sides:
        count = lax.axis_size(axis)
        forward = [(i, i + 1) for i in range(count - 1)]
        backward = [(target, source) for source, target in forward]
        low = lax.ppermute(
            lax.slice_in_dim(block, block.shape[dim] - width, None, axis=dim), axis, forward
        )
        high = lax.ppermute(lax.slice_in_dim(block, 0, width, axis=dim), axis, backward)
        block = jnp.concatenate([low, block, high], axis=dim)
    return block


def laplace(padded, buoy_pad):
    depth_cells = padded.shape[-3] - 2
    row_cells = padded.shape[-2] - 2
    col_cells = padded.shape[-1] - 2
    center_field = padded[..., 1:-1, 1:-1, 1:-1]
    center_buoy = buoy_pad[1:-1, 1:-1, 1:-1]
    summed = jnp.zeros(center_field.shape, jnp.float32)
    for shift_depth, shift_row, shift_col in NEIGHBOURS:
        near_buoy = buoy_pad[
            1 + shift_depth : 1 + shift_depth + depth_cells,
            1 + shift_row : 1 + shift_row + row_cells,
            1 + shift_col : 1 + shift_col + col_cells,
        ]
        near_field = padded[
            ...,
            1 + shift_depth : 1 + shift_depth + depth_cells,
            1 + shift_row : 1 + shift_row + row_cells,
            1 + shift_col : 1 + shift_col + col_cells,
        ]
        summed = summed + 0.5 * (center_buoy + near_buoy) * (near_field - center_field)
    return summed


def shrink(cells_array, cut_cells):
    if cut_cells == 0:
        return cells_array
    return cells_array[..., cut_cells:-cut_cells, cut_cells:-cut_cells, cut_cells:-cut_cells]


def pad_lines(cells_array, cut_cells):
    widths = [(0, 0)] * (cells_array.ndim - 1) + [(cut_cells, cut_cells)]
    return jnp.pad(cells_array, widths)


def local_cells(cells, depth_start, row_start, extents, full_rows, margin):
    depth_cells, row_cells, col_cells = extents
    plane_cells = full_rows * col_cells
    depth_pos = cells // plane_cells - depth_start + margin
    row_pos = cells // col_cells % full_rows - row_start + margin
    col_pos = cells % col_cells + margin
    inside = (
        (depth_pos >= 0)
        & (depth_pos < depth_cells + 2 * margin)
        & (row_pos >= 0)
        & (row_pos < row_cells + 2 * margin)
    )
    local_index = (depth_pos * (row_cells + 2 * margin) + row_pos) * (
        col_cells + 2 * margin
    ) + col_pos
    return (jnp.where(inside, local_index, 0), inside)


def shards(
    fwd_prev,
    fwd_now,
    adj_late,
    adj_last,
    velocity,
    density,
    wavelet,
    source_cell,
    receiver_cell,
    observed,
):
    shot_local, depth_cells, row_cells, col_cells = fwd_now.shape
    extents = (depth_cells, row_cells, col_cells)
    full_rows = row_cells * lax.axis_size("lat")
    depth_start = lax.axis_index("depth") * depth_cells
    row_start = lax.axis_index("lat") * row_cells
    steps_count = wavelet.shape[1]
    shot_rows = jnp.arange(shot_local)[:, None]
    shot_ids = jnp.arange(shot_local)
    buoy_width = 1
    buoy_edge = with_halo(1.0 / density, (("depth", 0), ("lat", 1)), buoy_width)
    buoy_pad = pad_lines(buoy_edge, buoy_width)
    receiver_local, receiver_inside = local_cells(
        receiver_cell, depth_start, row_start, extents, full_rows, 0
    )

    def advance(wave_prev, padded_now, stiff_cut, margin, step_index):
        laplacian = laplace(padded_now, shrink(buoy_pad, buoy_width - margin - 1))
        wave_next = 2.0 * shrink(padded_now, 1) - wave_prev + stiff_cut * laplacian
        source_local, source_inside = local_cells(
            source_cell, depth_start, row_start, extents, full_rows, margin
        )
        amount = jnp.where(source_inside, wavelet[:, step_index], 0.0)
        flattened = wave_next.reshape(shot_local, -1).at[shot_ids, source_local].add(amount)
        return (laplacian, flattened.reshape(wave_next.shape))

    def sample(interior, step_index):
        predicted = jnp.take_along_axis(interior.reshape(shot_local, -1), receiver_local, axis=1)
        return predicted - observed[:, step_index, :]

    def forward(stiffness, scaled_first):
        laplacians = []
        misfits = []
        wave_prev = fwd_prev
        wave_now = fwd_now
        for step_index in range(steps_count):
            if step_index == 0:
                padded = with_halo(wave_now, (("depth", 1), ("lat", 2)), 1)
                padded = pad_lines(padded, 1)
            else:
                padded = with_halo(wave_now, (("depth", 1), ("lat", 2)), 1)
                padded = pad_lines(padded, 1)
            laplacian, wave_next = advance(wave_prev, padded, stiffness, 0, step_index)
            laplacians.append(laplacian)
            misfits.append(sample(wave_next, step_index))
            wave_prev, wave_now = (wave_now, wave_next)
        return (laplacians, misfits, scaled_first)

    own_width = velocity.shape[2]
    own_start = lax.axis_index("shot") * own_width
    own_velocity = velocity
    direction = jnp.zeros(velocity.shape, jnp.float32)
    full_velocity = lax.all_gather(velocity, "shot", axis=2, tiled=True)
    for update_index in range(ITERS):
        stiffness = (full_velocity * COURANT) ** 2 * density
        scaled_first = stiffness * adj_last
        laplacians, misfits, adjoint_pad = forward(stiffness, scaled_first)
        gradient = jnp.zeros(extents, jnp.float32)
        late_adj = adj_late
        last_adj = adj_last
        for adjoint_step_index in reversed(range(steps_count)):
            if adjoint_step_index == steps_count - 1:
                adjoint_padded = with_halo(stiffness * last_adj, (("depth", 1), ("lat", 2)), 1)
                adjoint_padded = pad_lines(adjoint_padded, 1)
            else:
                adjoint_padded = with_halo(stiffness * last_adj, (("depth", 1), ("lat", 2)), 1)
                adjoint_padded = pad_lines(adjoint_padded, 1)
            adj_next = (
                2.0 * last_adj
                - late_adj
                + laplace(adjoint_padded, shrink(buoy_pad, buoy_width - 1))
            )
            adjoint_amount = jnp.where(receiver_inside, misfits[adjoint_step_index], 0.0)
            adj_next = (
                adj_next.reshape(shot_local, -1)
                .at[shot_rows, receiver_local]
                .add(adjoint_amount)
                .reshape(last_adj.shape)
            )
            gradient = gradient + jnp.sum(
                adj_next * stiffness * laplacians[adjoint_step_index], axis=0
            )
            late_adj, last_adj = (last_adj, adj_next)
        summed = lax.psum(gradient, "shot")
        largest = lax.pmax(jnp.max(jnp.abs(summed)), ("depth", "lat"))
        whole_direction = summed / (largest + EPSILON)
        full_velocity = full_velocity * jnp.exp(-STEP_SIZE * whole_direction)
        direction = lax.dynamic_slice_in_dim(whole_direction, own_start, own_width, 2)
        own_velocity = lax.dynamic_slice_in_dim(full_velocity, own_start, own_width, 2)
    return (own_velocity, direction)


def solution(mesh):
    placed = (
        P(("grp", "shot"), "depth", "lat", None),
        P(("grp", "shot"), "depth", "lat", None),
        P(("grp", "shot"), "depth", "lat", None),
        P(("grp", "shot"), "depth", "lat", None),
        P(("grp", "depth"), "lat", "shot"),
        P(("grp", "depth"), "lat", None),
        P(("grp", "shot"), None),
        P(("grp", "shot")),
        P(("grp", "shot"), None),
        P(("grp", "shot"), None, None),
    )
    return jax.shard_map(
        shards,
        mesh=mesh,
        in_specs=placed,
        out_specs=(P(("grp", "depth"), "lat", "shot"), P(("grp", "depth"), "lat", "shot")),
        check_vma=False,
    )
```

profile of v0, /device:TPU:0, one launch (start us, length us, event | category | flops | bytes accessed | tf_op | source)
XLA Modules:
  0.0 448.1 jit_solution(14772146906799206289)
XLA Ops:
  7.3 0.9 broadcast_divide_fusion.1
  8.1 1.3 collective-permute-start
  9.4 5.6 %collective-permute-start.2 = (f32[1,64,128]{2,1,0:T(8,128)S(1)}, f32[1,64,128]{2,1,0:T(8,128)S(1)}, u32[]{:S(2)}, u32[]{:S(2)}) collective-permute-start(f32[1,64,128]{2,1,0:T(8,128)S(1)} %get-tuple-element.69), channel_id=1, source_target_pairs={{0,4},{4,8},{8,12},{1,5},{5,9},{9,13},{2,6},{6,10},{10,14},{3,7},{... | collective-permute-start | bytes 98312 | tf_op jit(solution)/shard_map/ppermute | solution.py:20
  15.0 0.9 fusion.158
  15.9 3.9 collective-permute-start.9
  19.9 1.3 collective-permute-start.8
  21.2 1.0 slice_reduce_fusion
  22.1 0.9 fusion.129
  23.5 1.3 collective-permute-start.4
  24.8 3.0 collective-permute-start.6
  27.9 4.9 %all_gather.3 = f32[2,64,128]{1,0,2:T(2,128)S(1)} all-gather(f32[2,64,64]{1,0,2:T(2,128)S(1)} %copy.22), channel_id=1, replica_groups=mesh['grp'=2,'depth'=4,'shot'=2,'lat'=2] {'shot'}, dimensions={2}, use_global_device_ids=true | all-gather | bytes 98304 | tf_op jit(solution)/shard_map/all_gather | solution.py:143
  33.8 1.3 collective-permute-start.1
  35.1 5.2 %collective-permute-start.3 = (f32[2,1,64,128]{3,2,1,0:T(8,128)S(1)}, f32[2,1,64,128]{3,2,1,0:T(8,128)S(1)}, u32[]{:S(2)}, u32[]{:S(2)}) collective-permute-start(f32[2,1,64,128]{3,2,1,0:T(8,128)S(1)} %get-tuple-element.54), channel_id=1, source_target_pairs={{0,4},{4,8},{8,12},{1,5},{5,9},{9,13},{2,6},{6,10},{10,14},{3,7},{... | collective-permute-start | bytes 196616 | tf_op jit(solution)/shard_map/ppermute | solution.py:20
  40.3 1.3 collective-permute-start.10
  41.7 3.2 collective-permute-start.11
  44.9 0.8 collective-permute-done.11
  46.2 0.6 scatter_fusion
  46.8 3.9 collective-permute-start.13
  50.8 1.3 collective-permute-start.12
  52.1 34.9 %gather_fusion.1 = f32[4096]{0:T(1024)S(1)} fusion(f32[2,16384]{1,0:T(2,128)S(1)} %scatter_fusion, s32[4096]{0:T(1024)S(1)} %bitcast.81), kind=kCustom, calls=%fused_computation.1.clone | custom fusion | bytes 65536 | tf_op jit(solution)/shard_map/jit(take_along_axis)/gather | solution.py:118
  87.0 1.3 collective-permute-start.5
  88.3 3.0 collective-permute-start.7
  91.4 0.7 collective-permute-done.7
  92.5 1.3 collective-permute-start.14
  93.8 3.0 collective-permute-start.15
  98.2 0.6 scatter_fusion.1
  98.8 34.9 %gather_fusion = f32[4096]{0:T(1024)S(1)} fusion(f32[2,16384]{1,0:T(2,128)S(1)} %scatter_fusion.1, s32[4096]{0:T(1024)S(1)} %bitcast.82), kind=kCustom, calls=%fused_computation.clone | custom fusion | bytes 65536 | tf_op jit(solution)/shard_map/jit(take_along_axis)/gather | solution.py:118
  133.7 25.7 %scatter_fusion.4 = f32[32768]{0:T(1024)S(1)} fusion(f32[32768]{0:T(1024)S(1)} %bitcast.91, s32[4096]{0:T(1024)S(1)} %bitcast.111, f32[4096]{0:T(1024)S(1)} %bitcast.120), kind=kCustom, calls=%fused_computation.8 | custom fusion | flops 4096 | bytes 65536
  159.5 1.3 collective-permute-start.16
  160.8 5.3 %collective-permute-start.17 = (f32[2,1,64,128]{3,2,1,0:T(8,128)S(1)}, f32[2,1,64,128]{3,2,1,0:T(8,128)S(1)}, u32[]{:S(2)}, u32[]{:S(2)}) collective-permute-start(f32[2,1,64,128]{3,2,1,0:T(8,128)S(1)} %get-tuple-element.52), channel_id=1, source_target_pairs={{0,4},{4,8},{8,12},{1,5},{5,9},{9,13},{2,6},{6,10},{10,14},{3,7},{... | collective-permute-start | bytes 196616 | tf_op jit(solution)/shard_map/ppermute | solution.py:20
  166.1 0.7 collective-permute-done.16
  166.8 1.2 collective-permute-done.17
  168.0 1.3 collective-permute-start.18
  169.3 3.0 collective-permute-start.19
  172.3 0.8 collective-permute-done.19
  173.5 25.7 %scatter_fusion.5 = f32[32768]{0:T(1024)S(1)} fusion(f32[32768]{0:T(1024)S(1)} %bitcast.99, s32[4096]{0:T(1024)S(1)} %bitcast.112, f32[4096]{0:T(1024)S(1)} %bitcast.118), kind=kCustom, calls=%fused_computation.9 | custom fusion | flops 4096 | bytes 65536
  200.0 23.7 %all-reduce.11.cloned.1.call-done = f32[2,64,128]{2,1,0:T(8,128)} async-done(((f32[2,64,128]{2,1,0:T(8,128)}), f32[2,64,128]{2,1,0:T(8,128)}) %all-reduce.11.cloned.1.call-update) | async-done | bytes 65552 | tf_op jit(solution)/shard_map/psum | solution.py:174
  223.6 1.4 abs_reduce_fusion.1
  225.1 16.5 %pmax.14 = f32[]{:T(128)} all-reduce(f32[]{:T(128)} %abs_reduce_fusion.1), channel_id=1, replica_groups=mesh['grp'=2,'depth'=4,'shot'=2,'lat'=2] {'depth','lat'}, use_global_device_ids=true, to_apply=%region_8.10 | all-reduce | flops 1 | bytes 8 | tf_op jit(solution)/shard_map/pmax | solution.py:175
  242.3 0.9 multiply_multiply_fusion
  243.3 0.6 scatter_fusion.2
  243.9 34.9 %gather_fusion.3 = f32[4096]{0:T(1024)S(1)} fusion(f32[2,16384]{1,0:T(2,128)S(1)} %scatter_fusion.2, s32[4096]{0:T(1024)S(1)} %bitcast.83), kind=kCustom, calls=%fused_computation.3.clone | custom fusion | bytes 65536 | tf_op jit(solution)/shard_map/jit(take_along_axis)/gather | solution.py:118
  278.8 1.3 collective-permute-start.25
  280.1 1.3 collective-permute-start.24
  281.4 1.3 collective-permute-start.20
  282.7 5.2 %collective-permute-start.21 = (f32[2,1,64,128]{3,2,1,0:T(8,128)S(1)}, f32[2,1,64,128]{3,2,1,0:T(8,128)S(1)}, u32[]{:S(2)}, u32[]{:S(2)}) collective-permute-start(f32[2,1,64,128]{3,2,1,0:T(8,128)S(1)} %get-tuple-element.48), channel_id=1, source_target_pairs={{0,4},{4,8},{8,12},{1,5},{5,9},{9,13},{2,6},{6,10},{10,14},{3,7},{... | collective-permute-start | bytes 196616 | tf_op jit(solution)/shard_map/ppermute | solution.py:20
  288.0 1.3 collective-permute-start.26
  289.3 3.0 collective-permute-start.27
  292.4 1.3 collective-permute-start.22
  293.7 3.0 collective-permute-start.23
  297.9 34.9 %gather_fusion.2 = f32[4096]{0:T(1024)S(1)} fusion(f32[2,16384]{1,0:T(2,128)S(1)} %scatter_fusion.3, s32[4096]{0:T(1024)S(1)} %bitcast.84), kind=kCustom, calls=%fused_computation.2.clone | custom fusion | bytes 65536 | tf_op jit(solution)/shard_map/jit(take_along_axis)/gather | solution.py:118
  333.3 25.9 %scatter_fusion.6 = f32[32768]{0:T(1024)S(1)} fusion(f32[32768]{0:T(1024)S(1)} %bitcast.94, s32[4096]{0:T(1024)S(1)} %bitcast.113, f32[4096]{0:T(1024)S(1)} %bitcast.119), kind=kCustom, calls=%fused_computation.10 | custom fusion | flops 4096 | bytes 65536
  359.3 1.3 collective-permute-start.28
  360.6 4.6 %collective-permute-start.29 = (f32[2,1,64,128]{3,2,1,0:T(8,128)S(1)}, f32[2,1,64,128]{3,2,1,0:T(8,128)S(1)}, u32[]{:S(2)}, u32[]{:S(2)}) collective-permute-start(f32[2,1,64,128]{3,2,1,0:T(8,128)S(1)} %get-tuple-element.46), channel_id=1, source_target_pairs={{0,4},{4,8},{8,12},{1,5},{5,9},{9,13},{2,6},{6,10},{10,14},{3,7},{... | collective-permute-start | bytes 196616 | tf_op jit(solution)/shard_map/ppermute | solution.py:20
  365.5 1.6 collective-permute-done.29
  367.1 1.3 collective-permute-start.30
  368.4 3.0 collective-permute-start.31
  371.4 0.8 collective-permute-done.31
  372.6 25.7 %scatter_fusion.7 = f32[32768]{0:T(1024)S(1)} fusion(f32[32768]{0:T(1024)S(1)} %bitcast.97, s32[4096]{0:T(1024)S(1)} %bitcast.114, f32[4096]{0:T(1024)S(1)} %bitcast.117), kind=kCustom, calls=%fused_computation.11 | custom fusion | flops 4096 | bytes 65536
  399.1 22.0 %all-reduce.13.cloned.1.call-done = f32[2,64,128]{2,1,0:T(8,128)} async-done(((f32[2,64,128]{2,1,0:T(8,128)}), f32[2,64,128]{2,1,0:T(8,128)}) %all-reduce.13.cloned.1.call-update) | async-done | bytes 65552 | tf_op jit(solution)/shard_map/psum | solution.py:174
  421.0 1.4 abs_reduce_fusion
  422.5 16.5 %pmax.15 = f32[]{:T(128)} all-reduce(f32[]{:T(128)} %abs_reduce_fusion), channel_id=1, replica_groups=mesh['grp'=2,'depth'=4,'shot'=2,'lat'=2] {'depth','lat'}, use_global_device_ids=true, to_apply=%region_17.19 | all-reduce | flops 1 | bytes 8 | tf_op jit(solution)/shard_map/pmax | solution.py:175
  439.6 0.9 broadcast_divide_fusion
  440.5 0.7 dynamic-slice_multiply_fusion
  (128 shorter events, 8.1 us)
Async XLA Ops:
  7.2 15.9 %copy-start.9 = (s32[2]{0:T(128)S(1)}, s32[2]{0:T(128)}, u32[]{:S(2)}) copy-start(s32[2]{0:T(128)} %constant.190) | copy-start | bytes 28
  7.2 16.0 %copy-start.8 = (s32[2]{0:T(128)S(1)}, s32[2]{0:T(128)}, u32[]{:S(2)}) copy-start(s32[2]{0:T(128)} %constant.187) | copy-start | bytes 28
  7.2 16.1 %copy-start.6 = (f32[2,2,2048]{2,1,0:T(2,128)S(1)}, f32[2,2,2048]{2,1,0:T(2,128)}, u32[]{:S(2)}) copy-start(f32[2,2,2048]{2,1,0:T(2,128)} %param.21) | copy-start | bytes 98308
  7.2 16.1 %copy-start.7 = (s32[2]{0:T(128)S(1)}, s32[2]{0:T(128)}, u32[]{:S(2)}) copy-start(s32[2]{0:T(128)} %param.19) | copy-start | bytes 28
  7.2 16.2 %copy-start.5 = (f32[2,64,64]{2,1,0:T(8,128)S(1)}, f32[2,64,64]{2,1,0:T(8,128)}, u32[]{:S(2)}) copy-start(f32[2,64,64]{2,1,0:T(8,128)} %param.16) | copy-start | bytes 98308
  7.2 216.4 %all-reduce.11.cloned.1.call-start = ((), (), s32[]{:S(2)}) async-start(), calls=%async_computation | async-start | bytes 131072 | tf_op jit(solution)/shard_map/psum | solution.py:174
  8.1 15.4 %collective-permute-start = (f32[1,64,128]{2,1,0:T(8,128)S(1)}, f32[1,64,128]{2,1,0:T(8,128)S(1)}, u32[]{:S(2)}, u32[]{:S(2)}) collective-permute-start(f32[1,64,128]{2,1,0:T(8,128)S(1)} %get-tuple-element.70), channel_id=1, source_target_pairs={{4,0},{8,4},{12,8},{5,1},{9,5},{13,9},{6,2},{10,6},{14,10},{7,3},{... | collective-permute-start | bytes 98312 | tf_op jit(solution)/shard_map/ppermute | solution.py:23
  9.4 14.1 %collective-permute-start.2 = (f32[1,64,128]{2,1,0:T(8,128)S(1)}, f32[1,64,128]{2,1,0:T(8,128)S(1)}, u32[]{:S(2)}, u32[]{:S(2)}) collective-permute-start(f32[1,64,128]{2,1,0:T(8,128)S(1)} %get-tuple-element.69), channel_id=1, source_target_pairs={{0,4},{4,8},{8,12},{1,5},{5,9},{9,13},{2,6},{6,10},{10,14},{3,7},{... | collective-permute-start | bytes 98312 | tf_op jit(solution)/shard_map/ppermute | solution.py:20
  15.9 24.3 %collective-permute-start.9 = (f32[2,1,64,128]{3,2,1,0:T(8,128)S(1)}, f32[2,1,64,128]{3,2,1,0:T(8,128)S(1)}, u32[]{:S(2)}, u32[]{:S(2)}) collective-permute-start(f32[2,1,64,128]{3,2,1,0:T(8,128)S(1)} %get-tuple-element.63), channel_id=1, source_target_pairs={{0,4},{4,8},{8,12},{1,5},{5,9},{9,13},{2,6},{6,10},{10,14},{3,7},{... | collective-permute-start | bytes 196616 | tf_op jit(solution)/shard_map/ppermute | solution.py:20
  19.9 20.4 %collective-permute-start.8 = (f32[2,1,64,128]{3,2,1,0:T(8,128)S(1)}, f32[2,1,64,128]{3,2,1,0:T(8,128)S(1)}, u32[]{:S(2)}, u32[]{:S(2)}) collective-permute-start(f32[2,1,64,128]{3,2,1,0:T(8,128)S(1)} %get-tuple-element.62), channel_id=1, source_target_pairs={{4,0},{8,4},{12,8},{5,1},{9,5},{13,9},{6,2},{10,6},{14,10},{7,3},{... | collective-permute-start | bytes 196616 | tf_op jit(solution)/shard_map/ppermute | solution.py:23
  23.4 9.8 %copy-start.2 = (f32[2,64,128]{2,1,0:T(8,128)S(1)}, f32[2,64,128]{2,1,0:T(8,128)}, u32[]{:S(2)}) copy-start(f32[2,64,128]{2,1,0:T(8,128)} %param.17) | copy-start | bytes 196612
  23.5 9.4 %collective-permute-start.4 = (f32[4,1,128]{2,1,0:T(1,128)S(1)}, f32[4,1,128]{2,1,0:T(1,128)S(1)}, u32[]{:S(2)}, u32[]{:S(2)}) collective-permute-start(f32[4,1,128]{2,1,0:T(1,128)S(1)} %get-tuple-element.61), channel_id=1, source_target_pairs={{1,0},{3,2},{5,4},{7,6},{9,8},{11,10},{13,12},{15,14},{17,16},{19,... | collective-permute-start | bytes 6152 | tf_op jit(solution)/shard_map/ppermute | solution.py:23
  24.8 8.1 %collective-permute-start.6 = (f32[4,1,128]{2,1,0:T(1,128)S(1)}, f32[4,1,128]{2,1,0:T(1,128)S(1)}, u32[]{:S(2)}, u32[]{:S(2)}) collective-permute-start(f32[4,1,128]{2,1,0:T(1,128)S(1)} %get-tuple-element.60), channel_id=1, source_target_pairs={{0,1},{2,3},{4,5},{6,7},{8,9},{10,11},{12,13},{14,15},{16,17},{18,... | collective-permute-start | bytes 6152 | tf_op jit(solution)/shard_map/ppermute | solution.py:20
  32.8 0.9 copy-start.1
  33.1 7.1 %copy-start = (f32[2,2,64,128]{3,2,1,0:T(8,128)S(1)}, f32[2,2,64,128]{3,2,1,0:T(8,128)}, u32[]{:S(2)}) copy-start(f32[2,2,64,128]{3,2,1,0:T(8,128)} %param.13) | copy-start | bytes 393220
  33.8 53.2 %collective-permute-start.1 = (f32[2,1,64,128]{3,2,1,0:T(8,128)S(1)}, f32[2,1,64,128]{3,2,1,0:T(8,128)S(1)}, u32[]{:S(2)}, u32[]{:S(2)}) collective-permute-start(f32[2,1,64,128]{3,2,1,0:T(8,128)S(1)} %get-tuple-element.55), channel_id=1, source_target_pairs={{4,0},{8,4},{12,8},{5,1},{9,5},{13,9},{6,2},{10,6},{14,10},{7,3},{... | collective-permute-start | bytes 196616 | tf_op jit(solution)/shard_map/ppermute | solution.py:23
  35.1 51.9 %collective-permute-start.3 = (f32[2,1,64,128]{3,2,1,0:T(8,128)S(1)}, f32[2,1,64,128]{3,2,1,0:T(8,128)S(1)}, u32[]{:S(2)}, u32[]{:S(2)}) collective-permute-start(f32[2,1,64,128]{3,2,1,0:T(8,128)S(1)} %get-tuple-element.54), channel_id=1, source_target_pairs={{0,4},{4,8},{8,12},{1,5},{5,9},{9,13},{2,6},{6,10},{10,14},{3,7},{... | collective-permute-start | bytes 196616 | tf_op jit(solution)/shard_map/ppermute | solution.py:20
  40.3 4.5 %collective-permute-start.10 = (f32[2,4,1,128]{3,2,1,0:T(1,128)S(1)}, f32[2,4,1,128]{3,2,1,0:T(1,128)S(1)}, u32[]{:S(2)}, u32[]{:S(2)}) collective-permute-start(f32[2,4,1,128]{3,2,1,0:T(1,128)S(1)} %get-tuple-element.45), channel_id=1, source_target_pairs={{1,0},{3,2},{5,4},{7,6},{9,8},{11,10},{13,12},{15,14},{17,16},{19,... | collective-permute-start | bytes 12296 | tf_op jit(solution)/shard_map/ppermute | solution.py:23
  41.6 4.2 copy-start.4
  41.7 4.0 collective-permute-start.11
  46.8 45.6 %collective-permute-start.13 = (f32[2,1,64,128]{3,2,1,0:T(8,128)S(1)}, f32[2,1,64,128]{3,2,1,0:T(8,128)S(1)}, u32[]{:S(2)}, u32[]{:S(2)}) collective-permute-start(f32[2,1,64,128]{3,2,1,0:T(8,128)S(1)} %get-tuple-element.57), channel_id=1, source_target_pairs={{0,4},{4,8},{8,12},{1,5},{5,9},{9,13},{2,6},{6,10},{10,14},{3,7},{... | collective-permute-start | bytes 196616 | tf_op jit(solution)/shard_map/ppermute | solution.py:20
  50.8 41.7 %collective-permute-start.12 = (f32[2,1,64,128]{3,2,1,0:T(8,128)S(1)}, f32[2,1,64,128]{3,2,1,0:T(8,128)S(1)}, u32[]{:S(2)}, u32[]{:S(2)}) collective-permute-start(f32[2,1,64,128]{3,2,1,0:T(8,128)S(1)} %get-tuple-element.56), channel_id=1, source_target_pairs={{4,0},{8,4},{12,8},{5,1},{9,5},{13,9},{6,2},{10,6},{14,10},{7,3},{... | collective-permute-start | bytes 196616 | tf_op jit(solution)/shard_map/ppermute | solution.py:23
  87.0 4.4 collective-permute-start.5
  88.3 3.8 collective-permute-start.7
  91.4 5.4 %copy-start.3 = (f32[2,2,64,128]{3,2,1,0:T(8,128)S(1)}, f32[2,2,64,128]{3,2,1,0:T(8,128)}, u32[]{:S(2)}) copy-start(f32[2,2,64,128]{3,2,1,0:T(8,128)} %param.14) | copy-start | bytes 393220
  92.5 4.5 %collective-permute-start.14 = (f32[2,4,1,128]{3,2,1,0:T(1,128)S(1)}, f32[2,4,1,128]{3,2,1,0:T(1,128)S(1)}, u32[]{:S(2)}, u32[]{:S(2)}) collective-permute-start(f32[2,4,1,128]{3,2,1,0:T(1,128)S(1)} %get-tuple-element.43), channel_id=1, source_target_pairs={{1,0},{3,2},{5,4},{7,6},{9,8},{11,10},{13,12},{15,14},{17,16},{19,... | collective-permute-start | bytes 12296 | tf_op jit(solution)/shard_map/ppermute | solution.py:23
  93.8 3.8 collective-permute-start.15
  159.5 7.3 %collective-permute-start.16 = (f32[2,1,64,128]{3,2,1,0:T(8,128)S(1)}, f32[2,1,64,128]{3,2,1,0:T(8,128)S(1)}, u32[]{:S(2)}, u32[]{:S(2)}) collective-permute-start(f32[2,1,64,128]{3,2,1,0:T(8,128)S(1)} %get-tuple-element.53), channel_id=1, source_target_pairs={{4,0},{8,4},{12,8},{5,1},{9,5},{13,9},{6,2},{10,6},{14,10},{7,3},{... | collective-permute-start | bytes 196616 | tf_op jit(solution)/shard_map/ppermute | solution.py:23
  160.8 7.2 %collective-permute-start.17 = (f32[2,1,64,128]{3,2,1,0:T(8,128)S(1)}, f32[2,1,64,128]{3,2,1,0:T(8,128)S(1)}, u32[]{:S(2)}, u32[]{:S(2)}) collective-permute-start(f32[2,1,64,128]{3,2,1,0:T(8,128)S(1)} %get-tuple-element.52), channel_id=1, source_target_pairs={{0,4},{4,8},{8,12},{1,5},{5,9},{9,13},{2,6},{6,10},{10,14},{3,7},{... | collective-permute-start | bytes 196616 | tf_op jit(solution)/shard_map/ppermute | solution.py:20
  168.0 4.3 collective-permute-start.18
  169.3 3.8 collective-permute-start.19
  199.9 221.1 %all-reduce.13.cloned.1.call-start = ((), (), s32[]{:S(2)}) async-start(), calls=%async_computation.1 | async-start | bytes 131072 | tf_op jit(solution)/shard_map/psum | solution.py:174
  278.8 9.1 %collective-permute-start.25 = (f32[2,1,64,128]{3,2,1,0:T(8,128)S(1)}, f32[2,1,64,128]{3,2,1,0:T(8,128)S(1)}, u32[]{:S(2)}, u32[]{:S(2)}) collective-permute-start(f32[2,1,64,128]{3,2,1,0:T(8,128)S(1)} %get-tuple-element.51), channel_id=1, source_target_pairs={{0,4},{4,8},{8,12},{1,5},{5,9},{9,13},{2,6},{6,10},{10,14},{3,7},{... | collective-permute-start | bytes 196616 | tf_op jit(solution)/shard_map/ppermute | solution.py:20
  280.1 7.9 %collective-permute-start.24 = (f32[2,1,64,128]{3,2,1,0:T(8,128)S(1)}, f32[2,1,64,128]{3,2,1,0:T(8,128)S(1)}, u32[]{:S(2)}, u32[]{:S(2)}) collective-permute-start(f32[2,1,64,128]{3,2,1,0:T(8,128)S(1)} %get-tuple-element.50), channel_id=1, source_target_pairs={{4,0},{8,4},{12,8},{5,1},{9,5},{13,9},{6,2},{10,6},{14,10},{7,3},{... | collective-permute-start | bytes 196616 | tf_op jit(solution)/shard_map/ppermute | solution.py:23
  281.4 10.9 %collective-permute-start.20 = (f32[2,1,64,128]{3,2,1,0:T(8,128)S(1)}, f32[2,1,64,128]{3,2,1,0:T(8,128)S(1)}, u32[]{:S(2)}, u32[]{:S(2)}) collective-permute-start(f32[2,1,64,128]{3,2,1,0:T(8,128)S(1)} %get-tuple-element.49), channel_id=1, source_target_pairs={{4,0},{8,4},{12,8},{5,1},{9,5},{13,9},{6,2},{10,6},{14,10},{7,3},{... | collective-permute-start | bytes 196616 | tf_op jit(solution)/shard_map/ppermute | solution.py:23
  282.7 9.6 %collective-permute-start.21 = (f32[2,1,64,128]{3,2,1,0:T(8,128)S(1)}, f32[2,1,64,128]{3,2,1,0:T(8,128)S(1)}, u32[]{:S(2)}, u32[]{:S(2)}) collective-permute-start(f32[2,1,64,128]{3,2,1,0:T(8,128)S(1)} %get-tuple-element.48), channel_id=1, source_target_pairs={{0,4},{4,8},{8,12},{1,5},{5,9},{9,13},{2,6},{6,10},{10,14},{3,7},{... | collective-permute-start | bytes 196616 | tf_op jit(solution)/shard_map/ppermute | solution.py:20
  288.0 8.7 %collective-permute-start.26 = (f32[2,4,1,128]{3,2,1,0:T(1,128)S(1)}, f32[2,4,1,128]{3,2,1,0:T(1,128)S(1)}, u32[]{:S(2)}, u32[]{:S(2)}) collective-permute-start(f32[2,4,1,128]{3,2,1,0:T(1,128)S(1)} %get-tuple-element.37), channel_id=1, source_target_pairs={{1,0},{3,2},{5,4},{7,6},{9,8},{11,10},{13,12},{15,14},{17,16},{19,... | collective-permute-start | bytes 12296 | tf_op jit(solution)/shard_map/ppermute | solution.py:23
  289.3 7.4 %collective-permute-start.27 = (f32[2,4,1,128]{3,2,1,0:T(1,128)S(1)}, f32[2,4,1,128]{3,2,1,0:T(1,128)S(1)}, u32[]{:S(2)}, u32[]{:S(2)}) collective-permute-start(f32[2,4,1,128]{3,2,1,0:T(1,128)S(1)} %get-tuple-element.36), channel_id=1, source_target_pairs={{0,1},{2,3},{4,5},{6,7},{8,9},{10,11},{12,13},{14,15},{16,17},{18,... | collective-permute-start | bytes 12296 | tf_op jit(solution)/shard_map/ppermute | solution.py:20
  292.4 40.5 %collective-permute-start.22 = (f32[2,4,1,128]{3,2,1,0:T(1,128)S(1)}, f32[2,4,1,128]{3,2,1,0:T(1,128)S(1)}, u32[]{:S(2)}, u32[]{:S(2)}) collective-permute-start(f32[2,4,1,128]{3,2,1,0:T(1,128)S(1)} %get-tuple-element.35), channel_id=1, source_target_pairs={{1,0},{3,2},{5,4},{7,6},{9,8},{11,10},{13,12},{15,14},{17,16},{19,... | collective-permute-start | bytes 12296 | tf_op jit(solution)/shard_map/ppermute | solution.py:23
  293.7 39.2 %collective-permute-start.23 = (f32[2,4,1,128]{3,2,1,0:T(1,128)S(1)}, f32[2,4,1,128]{3,2,1,0:T(1,128)S(1)}, u32[]{:S(2)}, u32[]{:S(2)}) collective-permute-start(f32[2,4,1,128]{3,2,1,0:T(1,128)S(1)} %get-tuple-element.34), channel_id=1, source_target_pairs={{0,1},{2,3},{4,5},{6,7},{8,9},{10,11},{12,13},{14,15},{16,17},{18,... | collective-permute-start | bytes 12296 | tf_op jit(solution)/shard_map/ppermute | solution.py:20
  359.3 6.2 %collective-permute-start.28 = (f32[2,1,64,128]{3,2,1,0:T(8,128)S(1)}, f32[2,1,64,128]{3,2,1,0:T(8,128)S(1)}, u32[]{:S(2)}, u32[]{:S(2)}) collective-permute-start(f32[2,1,64,128]{3,2,1,0:T(8,128)S(1)} %get-tuple-element.47), channel_id=1, source_target_pairs={{4,0},{8,4},{12,8},{5,1},{9,5},{13,9},{6,2},{10,6},{14,10},{7,3},{... | collective-permute-start | bytes 196616 | tf_op jit(solution)/shard_map/ppermute | solution.py:23
  360.6 6.5 %collective-permute-start.29 = (f32[2,1,64,128]{3,2,1,0:T(8,128)S(1)}, f32[2,1,64,128]{3,2,1,0:T(8,128)S(1)}, u32[]{:S(2)}, u32[]{:S(2)}) collective-permute-start(f32[2,1,64,128]{3,2,1,0:T(8,128)S(1)} %get-tuple-element.46), channel_id=1, source_target_pairs={{0,4},{4,8},{8,12},{1,5},{5,9},{9,13},{2,6},{6,10},{10,14},{3,7},{... | collective-permute-start | bytes 196616 | tf_op jit(solution)/shard_map/ppermute | solution.py:20
  367.1 4.3 collective-permute-start.30
  368.4 3.8 collective-permute-start.31
Sparse Core Ops, SparseCore 0:
  200.0 23.5 all-reduce.10
  399.2 21.7 all-reduce.12
where the time goes:
time: 449 us; the launch traced here: 448 us
  local copies, waits for them, and re-layouts  143 us (32%)
  other arithmetic  118 us (26%)
  starting transfers between devices  80 us (18%)
  waiting for transfers between devices  53.2 us (12%)
  blocking collectives  38 us (8%)
  between operations  16.5 us (4%)
    gather x8, local copies, waits for them, and re-layouts, sample(): jnp.take_along_axis(interior.reshape(shot_local, -1), receiver_local, axi...  139 us
    unnamed x11, other arithmetic  104 us
    ppermute x16, starting transfers between devices, with_halo(): lax.ppermute(lax.slice_in_dim(block, block.shape[dim] - width, None, axis...  59.3 us
    psum x2, waiting for transfers between devices, shards(): summed = lax.psum(gradient, 'shot')  45.6 us
    pmax x2, blocking collectives, shards(): largest = lax.pmax(jnp.max(jnp.abs(summed)), ('depth', 'lat'))  33 us
    ppermute x16, starting transfers between devices, with_halo(): lax.ppermute(lax.slice_in_dim(block, 0, width, axis=dim), axis, backward)  20.6 us
  transfers between devices with their start and end apart: 34, of which 11 were waited for; matrix products, arithmetic and copies ran while one was open for 17% of the time, Pallas kernels for 0%

commit v1 on v0

v1 whole, which is shorter than its diff:
```python
import functools

import jax
import jax.numpy as jnp
from jax import lax
from jax.experimental import pallas as pl
from jax.experimental.pallas import tpu as pltpu
from jax.sharding import PartitionSpec as P

ITERS = 2

COURANT = 0.1
STEP_SIZE = 0.1
EPSILON = 1e-06
PAD = 8


def even_pairs(count):
    return [(i, i ^ 1) for i in range(count) if i ^ 1 < count]


def odd_pairs(count):
    ups = [(i, i + 1) for i in range(1, count - 1, 2)]
    return ups + [(b, a) for a, b in ups]


def two_pairs(count, first):
    ups = [(i, i + 2) for i in range(count - 2) if (i % 4 < 2) == first]
    return ups + [(b, a) for a, b in ups]


def send(block, axis, pairs):
    if not pairs:
        return jnp.zeros_like(block)
    return lax.ppermute(block, axis, pairs)


def pack(arrays):
    return jnp.concatenate([a.reshape(-1, a.shape[-1]) for a in arrays], axis=0)


def unpack(packed, shapes):
    out = []
    start = 0
    for shape in shapes:
        rows = 1
        for size in shape[:-1]:
            rows *= size
        out.append(packed[start : start + rows].reshape(shape))
        start += rows
    return out


def split_three(values):
    high = values.astype(jnp.bfloat16)
    rest = values - high.astype(jnp.float32)
    middle = rest.astype(jnp.bfloat16)
    low = (rest - middle.astype(jnp.float32)).astype(jnp.bfloat16)
    return high, middle, low


def spread_kernel(rows, cols, row_ref, col_ref, obs_ref, out_ref):
    nrec = row_ref.shape[-1]
    steps = obs_ref.shape[1]
    row_iota = lax.broadcasted_iota(jnp.int32, (rows, nrec), 0)
    col_iota = lax.broadcasted_iota(jnp.int32, (cols, nrec), 0)
    dims = (((1,), (1,)), ((), ()))
    for shot in range(row_ref.shape[0]):
        at_row = (row_ref[shot] == row_iota).astype(jnp.float32).astype(jnp.bfloat16)
        at_col = col_ref[shot] == col_iota
        ones = at_col.astype(jnp.float32).astype(jnp.bfloat16)
        out_ref[shot, 0] = lax.dot_general(
            at_row, ones, dims, preferred_element_type=jnp.float32
        )
        for step in range(steps):
            obs = obs_ref[shot, step : step + 1, :]
            high = obs.astype(jnp.bfloat16).astype(jnp.float32)
            rest = obs - high
            middle = rest.astype(jnp.bfloat16).astype(jnp.float32)
            low = rest - middle
            total = None
            for part in (high, middle, low):
                term = lax.dot_general(
                    at_row,
                    jnp.where(at_col, part, 0.0).astype(jnp.bfloat16),
                    dims,
                    preferred_element_type=jnp.float32,
                )
                total = term if total is None else total + term
            out_ref[shot, 1 + step] = total


def spread(row_id, col_id, observed, rows, cols):
    shots, nrec = row_id.shape
    steps = observed.shape[1]
    return pl.pallas_call(
        functools.partial(spread_kernel, rows, cols),
        out_shape=jax.ShapeDtypeStruct((shots, 1 + steps, rows, cols), jnp.float32),
        in_specs=[pl.BlockSpec(memory_space=pltpu.VMEM)] * 3,
        out_specs=pl.BlockSpec(memory_space=pltpu.VMEM),
        cost_estimate=pl.CostEstimate(
            flops=2 * shots * (1 + 3 * steps) * rows * cols * nrec,
            bytes_accessed=4 * shots * (1 + steps) * rows * cols,
            transcendentals=0,
        ),
        name="spread",
    )(row_id[:, None, :], col_id[:, None, :], observed)


def laplace(field, buoy):
    planes = field.shape[-3] - 2
    rows, cols = field.shape[-2:]
    wide = [(0, 0)] * (field.ndim - 2) + [(1, 1), (1, 1)]
    field = jnp.pad(field, wide)
    buoy = jnp.pad(buoy, [(0, 0), (1, 1), (1, 1)])
    center_field = field[..., 1:-1, 1:-1, 1:-1]
    center_buoy = buoy[1:-1, 1:-1, 1:-1]
    summed = None
    for dz, dx, dy in ((1, 0, 0), (-1, 0, 0), (0, 1, 0), (0, -1, 0), (0, 0, 1), (0, 0, -1)):
        near_buoy = buoy[1 + dz : 1 + dz + planes, 1 + dx : 1 + dx + rows, 1 + dy : 1 + dy + cols]
        near = field[..., 1 + dz : 1 + dz + planes, 1 + dx : 1 + dx + rows, 1 + dy : 1 + dy + cols]
        term = 0.5 * (center_buoy + near_buoy) * (near - center_field)
        summed = term if summed is None else summed + term
    return summed


def inner(block, cut):
    return block[..., cut : block.shape[-3] - cut, :, :]


def shards(
    fwd_prev,
    fwd_now,
    adj_late,
    adj_last,
    velocity,
    density,
    wavelet,
    source_cell,
    receiver_cell,
    observed,
):
    shots, planes, rows, cols = fwd_now.shape
    depth_count = lax.axis_size("depth")
    shot_count = lax.axis_size("shot")
    lat_count = lax.axis_size("lat")
    if planes != 2 or wavelet.shape[1] != 2 or lat_count != 2:
        raise ValueError("unsupported split")
    depth_at = lax.axis_index("depth")
    lat_at = lax.axis_index("lat")
    shot_at = lax.axis_index("shot")
    even = depth_at % 2 == 0
    front = depth_at % 4 < 2
    own_width = velocity.shape[2]
    evens = even_pairs(depth_count)
    odds = odd_pairs(depth_count)
    swap = [(0, 1), (1, 0)]

    def shot_sum(block):
        if shot_count == 2:
            return block + lax.ppermute(block, "shot", swap)
        return lax.psum(block, "shot")

    def depth_max(value):
        if depth_count & (depth_count - 1):
            return lax.pmax(value, "depth")
        step = 1
        while step < depth_count:
            pairs = [(i, i ^ step) for i in range(depth_count)]
            value = jnp.maximum(value, lax.ppermute(value, "depth", pairs))
            step *= 2
        return value

    if shot_count == 2:
        other = lax.ppermute(velocity, "shot", swap)
        full_velocity = jnp.where(
            shot_at == 0,
            jnp.concatenate([velocity, other], axis=2),
            jnp.concatenate([other, velocity], axis=2),
        )
    else:
        full_velocity = lax.all_gather(velocity, "shot", axis=2, tiled=True)

    near_shapes = [fwd_now.shape, fwd_prev.shape, adj_last.shape, density.shape, (shots, 1, rows, cols)]
    top_late = adj_late[:, planes - 1 :]
    low_late = adj_late[:, :1]
    common = [fwd_now, fwd_prev, adj_last, density]
    by_even = send(pack(common + [jnp.where(even, top_late, low_late)]), "depth", evens)
    by_odd = send(pack(common + [jnp.where(even, low_late, top_late)]), "depth", odds)
    up = unpack(jnp.where(even, by_even, by_odd), near_shapes)
    low = unpack(jnp.where(even, by_odd, by_even), near_shapes)
    far_shapes = [(shots, 1, rows, cols), (1, rows, cols)]
    top_far = pack([fwd_now[:, planes - 1 :], density[planes - 1 :]])
    low_far = pack([fwd_now[:, :1], density[:1]])
    by_first = send(jnp.where(front, top_far, low_far), "depth", two_pairs(depth_count, True))
    by_second = send(jnp.where(front, low_far, top_far), "depth", two_pairs(depth_count, False))
    far_up = unpack(jnp.where(front, by_first, by_second), far_shapes)
    far_low = unpack(jnp.where(front, by_second, by_first), far_shapes)
    vel_even = send(full_velocity, "depth", evens)
    vel_odd = send(full_velocity, "depth", odds)
    vel_up = jnp.where(even, vel_even, vel_odd)
    vel_low = jnp.where(even, vel_odd, vel_even)

    now = jnp.concatenate([far_low[0], low[0], fwd_now, up[0], far_up[0]], axis=1)
    prev = jnp.concatenate([low[1], fwd_prev, up[1]], axis=1)
    last = jnp.concatenate([low[2], adj_last, up[2]], axis=1)
    late = jnp.concatenate([low[4], adj_late, up[4]], axis=1)
    dens = jnp.concatenate([far_low[1], low[3], density, up[3], far_up[1]], axis=0)
    vel = jnp.concatenate([vel_low, full_velocity, vel_up], axis=0)

    def add_rows(blocks, extra=None):
        edges = pack([jnp.where(lat_at == 0, b[..., rows - PAD :, :], b[..., :PAD, :]) for b in blocks])
        if extra is not None:
            edges = jnp.concatenate([edges, extra], axis=0)
        got = lax.ppermute(edges, "lat", swap)
        parts = unpack(got, [b.shape[:-2] + (PAD, cols) for b in blocks])
        wide = [
            jnp.concatenate(
                [jnp.where(lat_at == 1, part, 0.0), block, jnp.where(lat_at == 0, part, 0.0)],
                axis=-2,
            )
            for part, block in zip(parts, blocks)
        ]
        if extra is None:
            return wide
        return wide, got[got.shape[0] - extra.shape[0] :]

    now, prev, last, late, dens, vel = add_rows([now, prev, last, late, dens, vel])
    buoy = jnp.where(dens > 0.0, 1.0 / jnp.where(dens > 0.0, dens, 1.0), 0.0)

    wide_rows = rows + 2 * PAD
    full_rows = rows * lat_count
    depth_start = depth_at * planes
    row_start = lat_at * rows

    def place(cells, margin):
        plane_at = cells // (full_rows * cols) - depth_start + margin
        row_at = cells // cols % full_rows - row_start + PAD
        inside = (
            (plane_at >= 0)
            & (plane_at < planes + 2 * margin)
            & (row_at >= 0)
            & (row_at < wide_rows)
        )
        return jnp.where(inside, plane_at * wide_rows + row_at, -1), cells % cols

    row_id, col_id = place(receiver_cell, 1)
    dense = spread(row_id, col_id, observed, (planes + 2) * wide_rows, cols)
    dense = dense.reshape(shots, 3, planes + 2, wide_rows, cols)
    hits, sums = dense[:, 0], [dense[:, 1], dense[:, 2]]

    def source(step, margin):
        at_row, at_col = place(source_cell, margin)
        shape = (shots, planes + 2 * margin, wide_rows, cols)
        line = lax.broadcasted_iota(jnp.int32, shape, 1) * wide_rows
        line = line + lax.broadcasted_iota(jnp.int32, shape, 2)
        column = lax.broadcasted_iota(jnp.int32, shape, 3)
        here = (line == at_row[:, None, None, None]) & (column == at_col[:, None, None, None])
        return jnp.where(here, wavelet[:, step][:, None, None, None], 0.0)

    lap_first = laplace(now, buoy)
    base = 2.0 * inner(now, 1) - prev + source(0, 2)

    def gradient_of(stiff):
        second = base + stiff * lap_first
        lap_second = laplace(second, inner(buoy, 1))
        third = (
            2.0 * inner(second, 1)
            - inner(now, 2)
            + inner(stiff, 1) * lap_second
            + source(1, 1)
        )
        upper = (
            2.0 * inner(last, 1)
            - late
            + laplace(stiff * last, inner(buoy, 1))
            + (hits * third - sums[1])
        )
        lower = (
            2.0 * inner(upper, 1)
            - inner(last, 2)
            + laplace(inner(stiff, 1) * upper, inner(buoy, 2))
            + (inner(hits, 1) * inner(second, 2) - inner(sums[0], 1))
        )
        shared = upper[:, 1:-1] * lap_second[:, 1:-1] + lower * lap_first[:, 2:-2]
        return (inner(stiff, 2) * jnp.sum(shared, axis=0))[:, PAD:-PAD, :]

    def own_lines(block):
        return lax.dynamic_slice_in_dim(block, shot_at * own_width, own_width, 2)

    stiff = (vel * COURANT) ** 2 * inner(dens, 1)
    own_velocity = velocity
    direction = None
    for update_index in range(ITERS):
        summed = shot_sum(gradient_of(stiff))
        largest = jnp.broadcast_to(jnp.max(jnp.abs(summed)), (1, cols))
        if update_index + 1 == ITERS:
            largest = jnp.maximum(largest, lax.ppermute(largest, "lat", swap))
            largest = depth_max(largest)
            direction = own_lines(summed) / (largest[0, 0] + EPSILON)
            own_velocity = own_velocity * jnp.exp(-STEP_SIZE * direction)
            break
        (summed,), got = add_rows([summed], largest)
        largest = jnp.maximum(largest, got)
        by_even = send(summed, "depth", evens)
        by_odd = send(summed, "depth", odds)
        largest = depth_max(largest)
        up_sum = jnp.where(even, by_even, by_odd)
        low_sum = jnp.where(even, by_odd, by_even)
        whole = jnp.concatenate([low_sum, summed, up_sum], axis=0) / (largest[0, 0] + EPSILON)
        stiff = stiff * jnp.exp(-2.0 * STEP_SIZE * whole)
        own_velocity = own_velocity * jnp.exp(
            -STEP_SIZE * own_lines(inner(whole, 2)[:, PAD:-PAD, :])
        )
    return (own_velocity, direction)


def solution(mesh):
    fields = P(("grp", "shot"), "depth", "lat", None)
    model = P(("grp", "depth"), "lat", "shot")
    placed = (
        fields,
        fields,
        fields,
        fields,
        model,
        P(("grp", "depth"), "lat", None),
        P(("grp", "shot"), None),
        P(("grp", "shot")),
        P(("grp", "shot"), None),
        P(("grp", "shot"), None, None),
    )
    return jax.shard_map(
        shards,
        mesh=mesh,
        in_specs=placed,
        out_specs=(model, model),
        check_vma=False,
    )
```

time: 449 us -> 76.9 us (0.17)
  local copies, waits for them, and re-layouts: 143 us -> 12.1 us
  other arithmetic: 118 us -> 10.7 us
  starting transfers between devices: 80 us -> 26.5 us
  blocking collectives: 38 us -> 0 us
  waiting for transfers between devices: 53.2 us -> 19.1 us
  between operations: 16.5 us -> 1.41 us
  Pallas kernels: 0 us -> 6.68 us
    gather x8 -> x0, local copies, waits for them, and re-layouts: 139 us -> none  [sample(): jnp.take_along_axis(interior.reshape(shot_local, -1), receiver_local, axi...]
    unnamed x11 -> x1, other arithmetic: 104 us -> 0.62 us
    ppermute x32 -> x17, starting transfers between devices: 80 us -> 26.5 us  [the longest x7 12.8 us: send(): return lax.ppermute(block, axis, pairs)]
    psum x2 -> x0, waiting for transfers between devices: 45.6 us -> none  [shards(): summed = lax.psum(gradient, 'shot')]
    pmax x2 -> x0, blocking collectives: 33 us -> none  [shards(): largest = lax.pmax(jnp.max(jnp.abs(summed)), ('depth', 'lat'))]
    ppermute x32 -> x17, waiting for transfers between devices: 7.54 us -> 19.1 us  [the longest x2 7.46 us: shot_sum(): return block + lax.ppermute(block, 'shot', swap)]
    unnamed x39 -> x47, local copies, waits for them, and re-layouts: 1.15 us -> 7.86 us
    pallas_call x0 -> x1, Pallas kernels: none -> 6.68 us  [spread(): pl.pallas_call(functools.partial(spread_kernel, rows, cols), out_shape=ja...]
  transfers between devices with their start and end apart: 34 -> 17, of which waited for: 11 -> 10; matrix products, arithmetic and copies ran while one was open for 17% -> 5% of each run, Pallas kernels for 0% -> 9%
where the time goes in v1:
time: 76.9 us; the launch traced here: 76.5 us
  starting transfers between devices  26.5 us (34%)
  waiting for transfers between devices  19.1 us (25%)
  local copies, waits for them, and re-layouts  12.1 us (16%)
  other arithmetic  10.7 us (14%)
  Pallas kernels  6.68 us (9%)
  between operations  1.41 us (2%)
    ppermute x7, starting transfers between devices, send(): return lax.ppermute(block, axis, pairs)  12.8 us
    ppermute x4, starting transfers between devices, depth_max(): value = jnp.maximum(value, lax.ppermute(value, 'depth', pairs))  10.8 us
    unnamed x47, local copies, waits for them, and re-layouts  7.86 us
    ppermute x2, waiting for transfers between devices, shot_sum(): return block + lax.ppermute(block, 'shot', swap)  7.46 us
    pallas_call x1, Pallas kernels, spread(): pl.pallas_call(functools.partial(spread_kernel, rows, cols), out_shape=ja...  6.68 us
    ppermute x4, waiting for transfers between devices, depth_max(): value = jnp.maximum(value, lax.ppermute(value, 'depth', pairs))  5.89 us
    ppermute x2, waiting for transfers between devices, add_rows(): got = lax.ppermute(edges, 'lat', swap)  2.84 us
    ppermute x7, waiting for transfers between devices, send(): return lax.ppermute(block, axis, pairs)  1.75 us
  transfers between devices with their start and end apart: 17, of which 10 were waited for; matrix products, arithmetic and copies ran while one was open for 5% of the time, Pallas kernels for 9%

profile of v1, /device:TPU:0, one launch (start us, length us, event | category | flops | bytes accessed | tf_op | source)
XLA Modules:
  0.0 76.5 jit_solution(9874302019194668900)
XLA Ops:
  0.7 1.0 %constant_dynamic-update-slice_fusion.4 = f32[1024,128]{1,0:T(8,128)S(1)} fusion(f32[256,128]{1,0:T(8,128)} %bitcast.118), kind=kLoop, calls=%fused_computation.271 | loop fusion | bytes 262144
  1.6 0.9 %constant_dynamic-update-slice_fusion.3 = f32[1024,128]{1,0:T(8,128)S(1)} fusion(f32[1024,128]{1,0:T(8,128)S(1)} %constant_dynamic-update-slice_fusion.4, f32[256,128]{1,0:T(8,128)} %bitcast.110), kind=kLoop, calls=%fused_computation.270 | loop fusion | bytes 262144
  2.5 1.0 %constant_dynamic-update-slice_fusion.2 = f32[1024,128]{1,0:T(8,128)S(1)} fusion(f32[1024,128]{1,0:T(8,128)S(1)} %constant_dynamic-update-slice_fusion.3, f32[256,128]{1,0:T(8,128)} %bitcast.117), kind=kLoop, calls=%fused_computation.269 | loop fusion | bytes 262144
  3.5 0.9 %constant_dynamic-update-slice_fusion.1 = f32[1024,128]{1,0:T(8,128)S(1)} fusion(f32[1024,128]{1,0:T(8,128)S(1)} %constant_dynamic-update-slice_fusion.2, f32[128,128]{1,0:T(8,128)} %bitcast.125), kind=kLoop, calls=%fused_computation.268 | loop fusion | bytes 131072
  4.4 0.8 %copy.25 = f32[1024,128]{1,0:T(8,128)} copy(f32[1024,128]{1,0:T(8,128)S(1)} %constant_dynamic-update-slice_fusion.1) | data formatting | bytes 1048576
  5.3 0.6 constant_dynamic-update-slice_fusion
  5.9 0.7 collective-permute-start.1
  6.6 5.9 %collective-permute-start.2 = (f32[1024,128]{1,0:T(8,128)S(1)}, f32[1024,128]{1,0:T(8,128)S(1)}, u32[]{:S(2)}, u32[]{:S(2)}) collective-permute-start(f32[1024,128]{1,0:T(8,128)S(1)} %constant_dynamic-update-slice_fusion.5), channel_id=1, source_target_pairs={{0,4},{4,0},{8,12},{12,8},{1,5},{5,1},{9,13},{13,9},{2,6},{6,2},{1... | collective-permute-start | bytes 1572872 | tf_op jit(solution)/shard_map/ppermute | solution.py:35
  12.7 1.6 %collective-permute-start.3 = (f32[2,64,64]{2,1,0:T(8,128)S(1)}, f32[2,64,64]{2,1,0:T(8,128)S(1)}, u32[]{:S(2)}, u32[]{:S(2)}) collective-permute-start(f32[2,64,64]{2,1,0:T(8,128)S(1)} %copy-done.8), channel_id=1, source_target_pairs={{0,2},{2,0},{1,3},{3,1},{4,6},{6,4},{5,7},{7,5},{8,10},{10,8},{9,1... | collective-permute-start | bytes 98312 | tf_op jit(solution)/shard_map/ppermute | solution.py:175
  14.3 0.1 and_select_fusion
  14.4 0.6 broadcast_in_dim.86.col_ref
  15.0 0.6 copy.14.row_ref
  15.6 0.6 and_select_fusion.7
  16.2 6.7 %spread.1 = f32[2,3,320,128]{3,2,1,0:T(8,128)} custom-call(s32[2,1,2048]{2,1,0:T(1,128)} %copy.14.row_ref, s32[2,1,2048]{2,1,0:T(1,128)} %broadcast_in_dim.86.col_ref, f32[2,2,2048]{2,1,0:T(2,128)} %obs_ref.1), custom_call_target="tpu_custom_call" | custom-call | flops 2348810240 | bytes 983040 | tf_op jit(solution)/shard_map/spread/pallas_call | solution.py:96
  22.9 0.2 slice_reduce_fusion
  23.1 0.1 maximum_select_fusion.1
  23.2 0.7 collective-permute-start.4
  23.9 4.7 %collective-permute-start.5 = (f32[2,64,128]{2,1,0:T(8,128)S(1)}, f32[2,64,128]{2,1,0:T(8,128)S(1)}, u32[]{:S(2)}, u32[]{:S(2)}) collective-permute-start(f32[2,64,128]{2,1,0:T(8,128)S(1)} %maximum_select_fusion.1), channel_id=1, source_target_pairs={{0,4},{4,0},{8,12},{12,8},{1,5},{5,1},{9,13},{13,9},{2,6},{6,2},{1... | collective-permute-start | bytes 196616 | tf_op jit(solution)/shard_map/ppermute | solution.py:35
  28.6 0.5 iota_multiply_fusion.1
  29.1 1.7 %collective-permute-done.5 = f32[2,64,128]{2,1,0:T(8,128)S(1)} collective-permute-done((f32[2,64,128]{2,1,0:T(8,128)S(1)}, f32[2,64,128]{2,1,0:T(8,128)S(1)}, u32[]{:S(2)}, u32[]{:S(2)}) %collective-permute-start.5) | collective-permute-done | bytes 65568 | tf_op jit(solution)/shard_map/ppermute | solution.py:35
  31.3 0.6 constant_dynamic-update-slice_fusion.25
  32.0 0.1 copy-done.5
  32.1 0.6 constant_dynamic-update-slice_fusion.24
  32.8 0.6 constant_dynamic-update-slice_fusion.23
  33.4 0.6 constant_dynamic-update-slice_fusion.22
  34.0 0.6 constant_dynamic-update-slice_fusion.21
  34.6 0.6 constant_dynamic-update-slice_fusion.20
  35.3 1.7 %collective-permute-done.6 = f32[496,128]{1,0:T(8,128)S(1)} collective-permute-done((f32[496,128]{1,0:T(8,128)}, f32[496,128]{1,0:T(8,128)S(1)}, u32[]{:S(2)}, u32[]{:S(2)}) %collective-permute-start.6) | collective-permute-done | bytes 253984 | tf_op jit(solution)/shard_map/ppermute | solution.py:215
  37.2 0.2 fusion.187
  37.4 0.2 fusion.100
  37.5 0.1 fusion.160
  37.8 0.6 copy-done.12
  38.4 0.5 multiply_add_fusion.1
  38.9 0.7 broadcast_multiply_fusion.3
  39.7 0.2 fusion.150
  39.9 0.7 slice-done
  40.5 0.6 collective-permute-start.7
  41.1 3.7 %collective-permute-done.7 = f32[2,64,128]{2,1,0:T(8,128)S(1)} collective-permute-done((f32[2,64,128]{2,1,0:T(8,128)S(1)}, f32[2,64,128]{2,1,0:T(8,128)S(1)}, u32[]{:S(2)}, u32[]{:S(2)}) %collective-permute-start.7) | collective-permute-done | bytes 65568 | tf_op jit(solution)/shard_map/ppermute | solution.py:161
  44.9 0.6 abs_reduce_fusion.1
  45.5 0.6 concatenate.85
  46.2 1.2 %collective-permute-done.8 = f32[17,128]{1,0:T(8,128)S(1)} collective-permute-done((f32[17,128]{1,0:T(8,128)S(1)}, f32[17,128]{1,0:T(8,128)S(1)}, u32[]{:S(2)}, u32[]{:S(2)}) %collective-permute-start.8) | collective-permute-done | bytes 8736 | tf_op jit(solution)/shard_map/ppermute | solution.py:215
  47.4 0.6 slice_maximum_fusion
  48.0 2.1 %collective-permute-start.11 = (f32[1,128]{1,0:T(1,128)S(1)}, f32[1,128]{1,0:T(1,128)S(1)}, u32[]{:S(2)}, u32[]{:S(2)}) collective-permute-start(f32[1,128]{1,0:T(1,128)S(1)} %slice_maximum_fusion), channel_id=1, source_target_pairs={{0,4},{4,0},{8,12},{12,8},{1,5},{5,1},{9,13},{13,9},{2,6},{6,2},{1... | collective-permute-start | bytes 1544 | tf_op jit(solution)/shard_map/ppermute | solution.py:170
  50.1 0.1 collective-permute-start.10
  50.2 0.7 collective-permute-start.9
  50.9 0.8 %collective-permute-done.11 = f32[1,128]{1,0:T(1,128)S(1)} collective-permute-done((f32[1,128]{1,0:T(1,128)S(1)}, f32[1,128]{1,0:T(1,128)S(1)}, u32[]{:S(2)}, u32[]{:S(2)}) %collective-permute-start.11) | collective-permute-done | bytes 544 | tf_op jit(solution)/shard_map/ppermute | solution.py:170
  51.7 0.6 fusion.190
  52.3 4.0 %collective-permute-start.12 = (f32[1,128]{1,0:T(1,128)S(1)}, f32[1,128]{1,0:T(1,128)S(1)}, u32[]{:S(2)}, u32[]{:S(2)}) collective-permute-start(f32[1,128]{1,0:T(1,128)S(1)} %fusion.190), channel_id=1, source_target_pairs={{0,8},{4,12},{8,0},{12,4},{1,9},{5,13},{9,1},{13,5},{2,10},{6,14},... | collective-permute-start | bytes 1544 | tf_op jit(solution)/shard_map/ppermute | solution.py:170
  56.3 1.7 %collective-permute-done.12 = f32[1,128]{1,0:T(1,128)S(1)} collective-permute-done((f32[1,128]{1,0:T(1,128)S(1)}, f32[1,128]{1,0:T(1,128)S(1)}, u32[]{:S(2)}, u32[]{:S(2)}) %collective-permute-start.12) | collective-permute-done | bytes 544 | tf_op jit(solution)/shard_map/ppermute | solution.py:170
  58.2 0.2 broadcast_multiply_fusion
  58.4 0.7 broadcast_multiply_fusion.2
  59.1 0.2 fusion.149
  59.4 0.6 collective-permute-start.13
  60.0 3.7 %collective-permute-done.13 = f32[2,64,128]{2,1,0:T(8,128)S(1)} collective-permute-done((f32[2,64,128]{2,1,0:T(8,128)S(1)}, f32[2,64,128]{2,1,0:T(8,128)S(1)}, u32[]{:S(2)}, u32[]{:S(2)}) %collective-permute-start.13) | collective-permute-done | bytes 65568 | tf_op jit(solution)/shard_map/ppermute | solution.py:161
  63.7 0.6 abs_reduce_fusion
  64.3 0.6 broadcast_in_dim.157
  65.0 1.1 %collective-permute-done.14 = f32[1,128]{1,0:T(1,128)S(1)} collective-permute-done((f32[1,128]{1,0:T(1,128)S(1)}, f32[1,128]{1,0:T(1,128)S(1)}, u32[]{:S(2)}, u32[]{:S(2)}) %collective-permute-start.14) | collective-permute-done | bytes 544 | tf_op jit(solution)/shard_map/ppermute | solution.py:298
  66.2 0.6 broadcast_maximum_fusion
  66.8 1.9 %collective-permute-start.15 = (f32[1,128]{1,0:T(1,128)S(1)}, f32[1,128]{1,0:T(1,128)S(1)}, u32[]{:S(2)}, u32[]{:S(2)}) collective-permute-start(f32[1,128]{1,0:T(1,128)S(1)} %broadcast_maximum_fusion), channel_id=1, source_target_pairs={{0,4},{4,0},{8,12},{12,8},{1,5},{5,1},{9,13},{13,9},{2,6},{6,2},{1... | collective-permute-start | bytes 1544 | tf_op jit(solution)/shard_map/ppermute | solution.py:170
  68.7 1.8 %collective-permute-done.15 = f32[1,128]{1,0:T(1,128)S(1)} collective-permute-done((f32[1,128]{1,0:T(1,128)S(1)}, f32[1,128]{1,0:T(1,128)S(1)}, u32[]{:S(2)}, u32[]{:S(2)}) %collective-permute-start.15) | collective-permute-done | bytes 544 | tf_op jit(solution)/shard_map/ppermute | solution.py:170
  70.5 0.6 fusion.189
  71.1 2.9 %collective-permute-start.16 = (f32[1,128]{1,0:T(1,128)S(1)}, f32[1,128]{1,0:T(1,128)S(1)}, u32[]{:S(2)}, u32[]{:S(2)}) collective-permute-start(f32[1,128]{1,0:T(1,128)S(1)} %fusion.189), channel_id=1, source_target_pairs={{0,8},{4,12},{8,0},{12,4},{1,9},{5,13},{9,1},{13,5},{2,10},{6,14},... | collective-permute-start | bytes 1544 | tf_op jit(solution)/shard_map/ppermute | solution.py:170
  74.0 1.7 %collective-permute-done.16 = f32[1,128]{1,0:T(1,128)S(1)} collective-permute-done((f32[1,128]{1,0:T(1,128)S(1)}, f32[1,128]{1,0:T(1,128)S(1)}, u32[]{:S(2)}, u32[]{:S(2)}) %collective-permute-start.16) | collective-permute-done | bytes 544 | tf_op jit(solution)/shard_map/ppermute | solution.py:170
  75.7 0.8 %exponential_multiply_fusion.1 = (f32[2,64,64]{2,1,0:T(8,128)}, f32[2,64,64]{2,1,0:T(8,128)}) fusion(f32[2,64,64]{2,1,0:T(8,128)S(1)} %copy-done.9, f32[2,64,128]{2,1,0:T(8,128)S(1)} %slice.708, s32[]{:T(128)S(6)} %select_n.429, f32[]{:T(128)} %bitcast.53, f32[2,64,128]{2,1,0:T(8,128)S(1)} %get-tuple-element.7), kind=kLoop, calls=%fused_computation.259 | loop fusion | flops 40960 | bytes 163848 | tf_op jit(solution)/shard_map/mul | solution.py:301
  (90 shorter events, 1.2 us)
Async XLA Ops:
  0.6 4.6 %copy-start.3 = (f32[2,2,64,128]{3,2,1,0:T(8,128)S(1)}, f32[2,2,64,128]{3,2,1,0:T(8,128)}, u32[]{:S(2)}) copy-start(f32[2,2,64,128]{3,2,1,0:T(8,128)} %param.12) | copy-start | bytes 393220
  2.5 10.0 %copy-start.6 = (f32[2,2,64,128]{3,2,1,0:T(8,128)S(1)}, f32[2,2,64,128]{3,2,1,0:T(8,128)}, u32[]{:S(2)}) copy-start(f32[2,2,64,128]{3,2,1,0:T(8,128)} %param.11) | copy-start | bytes 393220
  3.5 9.0 %copy-start.7 = (f32[2,64,128]{2,1,0:T(8,128)S(1)}, f32[2,64,128]{2,1,0:T(8,128)}, u32[]{:S(2)}) copy-start(f32[2,64,128]{2,1,0:T(8,128)} %param.15) | copy-start | bytes 196612
  4.4 8.2 %copy-start.8 = (f32[2,64,64]{2,1,0:T(8,128)S(1)}, f32[2,64,64]{2,1,0:T(8,128)}, u32[]{:S(2)}) copy-start(f32[2,64,64]{2,1,0:T(8,128)} %param.14) | copy-start | bytes 98308
  4.4 9.8 %copy-start.14 = (s32[2]{0:T(128)S(1)}, s32[2]{0:T(128)}, u32[]{:S(2)}) copy-start(s32[2]{0:T(128)} %param.17) | copy-start | bytes 28
  4.4 9.8 %copy-start.10 = (s32[2,2048]{1,0:T(2,128)S(1)}, s32[2,2048]{1,0:T(2,128)}, u32[]{:S(2)}) copy-start(s32[2,2048]{1,0:T(2,128)} %param.18) | copy-start | bytes 49156
  5.9 25.1 %collective-permute-start.1 = (f32[1024,128]{1,0:T(8,128)}, f32[1024,128]{1,0:T(8,128)S(1)}, u32[]{:S(2)}, u32[]{:S(2)}) collective-permute-start(f32[1024,128]{1,0:T(8,128)} %constant_dynamic-update-slice_fusion), channel_id=1, source_target_pairs={{4,8},{8,4},{5,9},{9,5},{6,10},{10,6},{7,11},{11,7},{20,24},{24,20... | collective-permute-start | bytes 1572872 | tf_op jit(solution)/shard_map/ppermute | solution.py:35
  6.6 24.4 %collective-permute-start.2 = (f32[1024,128]{1,0:T(8,128)S(1)}, f32[1024,128]{1,0:T(8,128)S(1)}, u32[]{:S(2)}, u32[]{:S(2)}) collective-permute-start(f32[1024,128]{1,0:T(8,128)S(1)} %constant_dynamic-update-slice_fusion.5), channel_id=1, source_target_pairs={{0,4},{4,0},{8,12},{12,8},{1,5},{5,1},{9,13},{13,9},{2,6},{6,2},{1... | collective-permute-start | bytes 1572872 | tf_op jit(solution)/shard_map/ppermute | solution.py:35
  12.6 18.3 %collective-permute-start = (f32[192,128]{1,0:T(8,128)S(1)}, f32[192,128]{1,0:T(8,128)S(1)}, u32[]{:S(2)}, u32[]{:S(2)}) collective-permute-start(f32[192,128]{1,0:T(8,128)S(1)} %maximum_select_fusion), channel_id=1, source_target_pairs={{0,8},{4,12},{8,0},{12,4},{1,9},{5,13},{9,1},{13,5},{2,10},{6,14},... | collective-permute-start | bytes 294920 | tf_op jit(solution)/shard_map/ppermute | solution.py:35
  12.7 10.4 %collective-permute-start.3 = (f32[2,64,64]{2,1,0:T(8,128)S(1)}, f32[2,64,64]{2,1,0:T(8,128)S(1)}, u32[]{:S(2)}, u32[]{:S(2)}) collective-permute-start(f32[2,64,64]{2,1,0:T(8,128)S(1)} %copy-done.8), channel_id=1, source_target_pairs={{0,2},{2,0},{1,3},{3,1},{4,6},{6,4},{5,7},{7,5},{8,10},{10,8},{9,1... | collective-permute-start | bytes 98312 | tf_op jit(solution)/shard_map/ppermute | solution.py:175
  16.2 6.7 %copy-start.11 = (f32[2,2]{1,0:T(2,128)S(1)}, f32[2,2]{1,0:T(2,128)}, u32[]{:S(2)}) copy-start(f32[2,2]{1,0:T(2,128)} %param.16) | copy-start | bytes 52
  23.2 5.9 %collective-permute-start.4 = (f32[2,64,128]{2,1,0:T(8,128)S(1)}, f32[2,64,128]{2,1,0:T(8,128)S(1)}, u32[]{:S(2)}, u32[]{:S(2)}) collective-permute-start(f32[2,64,128]{2,1,0:T(8,128)S(1)} %maximum_select_fusion.1), channel_id=1, source_target_pairs={{4,8},{8,4},{5,9},{9,5},{6,10},{10,6},{7,11},{11,7},{20,24},{24,20... | collective-permute-start | bytes 196616 | tf_op jit(solution)/shard_map/ppermute | solution.py:35
  23.9 7.0 %collective-permute-start.5 = (f32[2,64,128]{2,1,0:T(8,128)S(1)}, f32[2,64,128]{2,1,0:T(8,128)S(1)}, u32[]{:S(2)}, u32[]{:S(2)}) collective-permute-start(f32[2,64,128]{2,1,0:T(8,128)S(1)} %maximum_select_fusion.1), channel_id=1, source_target_pairs={{0,4},{4,0},{8,12},{12,8},{1,5},{5,1},{9,13},{13,9},{2,6},{6,2},{1... | collective-permute-start | bytes 196616 | tf_op jit(solution)/shard_map/ppermute | solution.py:35
  31.1 0.9 %copy-start.5 = (f32[2,2,64,128]{3,2,1,0:T(8,128)S(1)}, f32[2,2,64,128]{3,2,1,0:T(8,128)}, u32[]{:S(2)}) copy-start(f32[2,2,64,128]{3,2,1,0:T(8,128)} %param.13) | copy-start | bytes 393220
  31.2 0.9 %copy-start.4 = (f32[2,2,64,128]{3,2,1,0:T(8,128)S(1)}, f32[2,2,64,128]{3,2,1,0:T(8,128)}, u32[]{:S(2)}) copy-start(f32[2,2,64,128]{3,2,1,0:T(8,128)} %param.10) | copy-start | bytes 393220
  31.3 3.9 %copy-start.2 = (f32[2,3,320,128]{3,2,1,0:T(8,128)S(1)}, f32[2,3,320,128]{3,2,1,0:T(8,128)}, u32[]{:S(2)}) copy-start(f32[2,3,320,128]{3,2,1,0:T(8,128)} %spread.1) | copy-start | bytes 2949124
  35.2 1.7 %collective-permute-start.6 = (f32[496,128]{1,0:T(8,128)}, f32[496,128]{1,0:T(8,128)S(1)}, u32[]{:S(2)}, u32[]{:S(2)}) collective-permute-start(f32[496,128]{1,0:T(8,128)} %constant_dynamic-update-slice_fusion.20), channel_id=1, source_target_pairs={{0,1},{1,0},{2,3},{3,2},{4,5},{5,4},{6,7},{7,6},{8,9},{9,8},{10,11... | collective-permute-start | bytes 761864 | tf_op jit(solution)/shard_map/ppermute | solution.py:215
  37.1 0.7 copy-start
  37.7 0.7 copy-start.12
  37.8 0.7 copy-start.13
  39.6 0.9 %slice-start = ((f32[6,80,128]{2,1,0:T(8,128)}), f32[2,80,128]{2,1,0:T(8,128)S(1)}, s32[]{:S(2)}) async-start(f32[6,80,128]{2,1,0:T(8,128)} %copy-done), calls=%async_computation | async-start | bytes 163840 | tf_op jit(solution)/shard_map/slice | solution.py:128
  40.5 17.6 %copy-start.1 = (f32[6,80,128]{2,1,0:T(8,128)S(1)}, f32[6,80,128]{2,1,0:T(8,128)}, u32[]{:S(2)}) copy-start(f32[6,80,128]{2,1,0:T(8,128)} %copy-done) | copy-start | bytes 737284
  40.5 4.3 %collective-permute-start.7 = (f32[2,64,128]{2,1,0:T(8,128)S(1)}, f32[2,64,128]{2,1,0:T(8,128)S(1)}, u32[]{:S(2)}, u32[]{:S(2)}) collective-permute-start(f32[2,64,128]{2,1,0:T(8,128)S(1)} %slice_multiply_fusion.7), channel_id=1, source_target_pairs={{0,2},{2,0},{1,3},{3,1},{4,6},{6,4},{5,7},{7,5},{8,10},{10,8},{9,1... | collective-permute-start | bytes 196616 | tf_op jit(solution)/shard_map/ppermute | solution.py:161
  46.1 1.2 %collective-permute-start.8 = (f32[17,128]{1,0:T(8,128)S(1)}, f32[17,128]{1,0:T(8,128)S(1)}, u32[]{:S(2)}, u32[]{:S(2)}) collective-permute-start(f32[17,128]{1,0:T(8,128)S(1)} %concatenate.85), channel_id=1, source_target_pairs={{0,1},{1,0},{2,3},{3,2},{4,5},{5,4},{6,7},{7,6},{8,9},{9,8},{10,11... | collective-permute-start | bytes 26120 | tf_op jit(solution)/shard_map/ppermute | solution.py:215
  48.0 3.6 %collective-permute-start.11 = (f32[1,128]{1,0:T(1,128)S(1)}, f32[1,128]{1,0:T(1,128)S(1)}, u32[]{:S(2)}, u32[]{:S(2)}) collective-permute-start(f32[1,128]{1,0:T(1,128)S(1)} %slice_maximum_fusion), channel_id=1, source_target_pairs={{0,4},{4,0},{8,12},{12,8},{1,5},{5,1},{9,13},{13,9},{2,6},{6,2},{1... | collective-permute-start | bytes 1544 | tf_op jit(solution)/shard_map/ppermute | solution.py:170
  50.1 7.9 %collective-permute-start.10 = (f32[2,80,128]{2,1,0:T(8,128)S(1)}, f32[2,80,128]{2,1,0:T(8,128)S(1)}, u32[]{:S(2)}, u32[]{:S(2)}) collective-permute-start(f32[2,80,128]{2,1,0:T(8,128)S(1)} %pad_maximum_fusion.3), channel_id=1, source_target_pairs={{0,4},{4,0},{8,12},{12,8},{1,5},{5,1},{9,13},{13,9},{2,6},{6,2},{1... | collective-permute-start | bytes 245768 | tf_op jit(solution)/shard_map/ppermute | solution.py:35
  50.2 7.8 %collective-permute-start.9 = (f32[2,80,128]{2,1,0:T(8,128)S(1)}, f32[2,80,128]{2,1,0:T(8,128)S(1)}, u32[]{:S(2)}, u32[]{:S(2)}) collective-permute-start(f32[2,80,128]{2,1,0:T(8,128)S(1)} %pad_maximum_fusion.3), channel_id=1, source_target_pairs={{4,8},{8,4},{5,9},{9,5},{6,10},{10,6},{7,11},{11,7},{20,24},{24,20... | collective-permute-start | bytes 245768 | tf_op jit(solution)/shard_map/ppermute | solution.py:35
  52.3 5.7 %collective-permute-start.12 = (f32[1,128]{1,0:T(1,128)S(1)}, f32[1,128]{1,0:T(1,128)S(1)}, u32[]{:S(2)}, u32[]{:S(2)}) collective-permute-start(f32[1,128]{1,0:T(1,128)S(1)} %fusion.190), channel_id=1, source_target_pairs={{0,8},{4,12},{8,0},{12,4},{1,9},{5,13},{9,1},{13,5},{2,10},{6,14},... | collective-permute-start | bytes 1544 | tf_op jit(solution)/shard_map/ppermute | solution.py:170
  59.1 16.6 %copy-start.9 = (f32[2,64,64]{2,1,0:T(8,128)S(1)}, f32[2,64,64]{2,1,0:T(8,128)}, u32[]{:S(2)}) copy-start(f32[2,64,64]{2,1,0:T(8,128)} %param.14) | copy-start | bytes 98308
  59.4 4.3 %collective-permute-start.13 = (f32[2,64,128]{2,1,0:T(8,128)S(1)}, f32[2,64,128]{2,1,0:T(8,128)S(1)}, u32[]{:S(2)}, u32[]{:S(2)}) collective-permute-start(f32[2,64,128]{2,1,0:T(8,128)S(1)} %slice_multiply_fusion.6), channel_id=1, source_target_pairs={{0,2},{2,0},{1,3},{3,1},{4,6},{6,4},{5,7},{7,5},{8,10},{10,8},{9,1... | collective-permute-start | bytes 196616 | tf_op jit(solution)/shard_map/ppermute | solution.py:161
  65.0 1.2 %collective-permute-start.14 = (f32[1,128]{1,0:T(1,128)S(1)}, f32[1,128]{1,0:T(1,128)S(1)}, u32[]{:S(2)}, u32[]{:S(2)}) collective-permute-start(f32[1,128]{1,0:T(1,128)S(1)} %broadcast_in_dim.157), channel_id=1, source_target_pairs={{0,1},{1,0},{2,3},{3,2},{4,5},{5,4},{6,7},{7,6},{8,9},{9,8},{10,11... | collective-permute-start | bytes 1544 | tf_op jit(solution)/shard_map/ppermute | solution.py:298
  66.8 3.6 %collective-permute-start.15 = (f32[1,128]{1,0:T(1,128)S(1)}, f32[1,128]{1,0:T(1,128)S(1)}, u32[]{:S(2)}, u32[]{:S(2)}) collective-permute-start(f32[1,128]{1,0:T(1,128)S(1)} %broadcast_maximum_fusion), channel_id=1, source_target_pairs={{0,4},{4,0},{8,12},{12,8},{1,5},{5,1},{9,13},{13,9},{2,6},{6,2},{1... | collective-permute-start | bytes 1544 | tf_op jit(solution)/shard_map/ppermute | solution.py:170
  71.1 4.5 %collective-permute-start.16 = (f32[1,128]{1,0:T(1,128)S(1)}, f32[1,128]{1,0:T(1,128)S(1)}, u32[]{:S(2)}, u32[]{:S(2)}) collective-permute-start(f32[1,128]{1,0:T(1,128)S(1)} %fusion.189), channel_id=1, source_target_pairs={{0,8},{4,12},{8,0},{12,4},{1,9},{5,13},{9,1},{13,5},{2,10},{6,14},... | collective-permute-start | bytes 1544 | tf_op jit(solution)/shard_map/ppermute | solution.py:170

commit v2 on v1

v2 whole, which is shorter than its diff:
```python
import functools

import jax
import jax.numpy as jnp
from jax import lax
from jax.experimental import pallas as pl
from jax.experimental.pallas import tpu as pltpu
from jax.sharding import PartitionSpec as P

ITERS = 2

COURANT = 0.1
STEP_SIZE = 0.1
EPSILON = 1e-06
PAD = 8
WIDE = 3


def even_pairs(count):
    return [(i, i ^ 1) for i in range(count) if i ^ 1 < count]


def odd_pairs(count):
    ups = [(i, i + 1) for i in range(1, count - 1, 2)]
    return ups + [(b, a) for a, b in ups]


def two_pairs(count, first):
    ups = [(i, i + 2) for i in range(count - 2) if (i % 4 < 2) == first]
    return ups + [(b, a) for a, b in ups]


def send(block, axis, pairs):
    if not pairs:
        return jnp.zeros_like(block)
    return lax.ppermute(block, axis, pairs)


def on_chip(kernel, out_shapes, args, scratch=(), flops=0, limit=8, name=None):
    spec = pl.BlockSpec(memory_space=pltpu.VMEM)
    outs = tuple(pltpu.VMEM(shape, jnp.float32) for shape in out_shapes)
    moved = sum(a.size * 4 for a in args)
    return pl.pallas_call(
        kernel,
        out_shape=outs,
        in_specs=[spec] * len(args),
        out_specs=tuple(spec for _ in outs),
        scratch_shapes=[pltpu.VMEM(shape, jnp.float32) for shape in scratch],
        compiler_params=pltpu.CompilerParams(vmem_limit_bytes=limit << 20),
        cost_estimate=pl.CostEstimate(flops=flops, bytes_accessed=moved, transcendentals=0),
        name=name,
    )(*[pltpu.with_memory_space_constraint(a, pltpu.VMEM) for a in args])


def pack_kernel(now, prev, last, dens, late, to_even, to_odd, to_far):
    depth_at = lax.axis_index("depth")
    even = depth_at % 2 == 0
    front = depth_at % 4 < 2
    shots, planes, rows, cols = now.shape
    block = planes * rows
    start = 0
    for field in (now, prev, last):
        for shot in range(shots):
            value = field[shot].reshape(block, cols)
            to_even[start : start + block] = value
            to_odd[start : start + block] = value
            start += block
    value = dens[...].reshape(block, cols)
    to_even[start : start + block] = value
    to_odd[start : start + block] = value
    start += block
    for shot in range(shots):
        low, top = late[shot, 0], late[shot, planes - 1]
        to_even[start : start + rows] = jnp.where(even, top, low)
        to_odd[start : start + rows] = jnp.where(even, low, top)
        start += rows
        to_far[0, shot * rows : (shot + 1) * rows] = jnp.where(
            front, now[shot, planes - 1], now[shot, 0]
        )
        to_far[1, shot * rows : (shot + 1) * rows] = jnp.where(
            front, now[shot, 0], now[shot, planes - 1]
        )
    end = shots * rows
    to_far[0, end:] = jnp.where(front, dens[planes - 1], dens[0])
    to_far[1, end:] = jnp.where(front, dens[0], dens[planes - 1])


def spread_kernel(row_ref, col_ref, obs_ref, out_ref):
    shots, nrec = row_ref.shape
    rows, cols = out_ref.shape[2:]
    steps = obs_ref.shape[1]
    row_iota = lax.broadcasted_iota(jnp.int32, (rows, nrec), 0)
    col_iota = lax.broadcasted_iota(jnp.int32, (cols, nrec), 0)
    dims = (((1,), (1,)), ((), ()))
    for shot in range(shots):
        at_row = (row_ref[shot : shot + 1, :] == row_iota).astype(jnp.float32)
        at_row = at_row.astype(jnp.bfloat16)
        at_col = col_ref[shot : shot + 1, :] == col_iota
        ones = at_col.astype(jnp.float32).astype(jnp.bfloat16)
        out_ref[shot, 0] = lax.dot_general(
            at_row, ones, dims, preferred_element_type=jnp.float32
        )
        for step in range(steps):
            obs = obs_ref[shot, step : step + 1, :]
            high = obs.astype(jnp.bfloat16).astype(jnp.float32)
            rest = obs - high
            middle = rest.astype(jnp.bfloat16).astype(jnp.float32)
            low = rest - middle
            total = None
            for part in (high, middle, low):
                term = lax.dot_general(
                    at_row,
                    jnp.where(at_col, part, 0.0).astype(jnp.bfloat16),
                    dims,
                    preferred_element_type=jnp.float32,
                )
                total = term if total is None else total + term
            out_ref[shot, 1 + step] = total


class Halo:
    def __init__(self, own, near_even, near_odd, far_first, far_second, vel_own, vel_even, vel_odd):
        depth_at = lax.axis_index("depth")
        self.even = depth_at % 2 == 0
        self.front = depth_at % 4 < 2
        self.own = own
        self.near = (near_even, near_odd)
        self.far = (far_first, far_second)
        self.vel = (vel_own, vel_even, vel_odd)
        self.shots, self.planes, self.rows, self.cols = own[0].shape

    def near_rows(self, start, upper, rows):
        first, second = self.near if upper else self.near[::-1]
        return jnp.where(self.even, first[start : start + rows], second[start : start + rows])

    def far_rows(self, start, upper, rows):
        first, second = self.far if upper else self.far[::-1]
        return jnp.where(self.front, first[start : start + rows], second[start : start + rows])

    def field(self, which, shot, at):
        rows, planes = self.rows, self.planes
        if 0 <= at < planes:
            return self.own[which][shot, at]
        upper = at >= planes
        step = at - planes if upper else planes + at
        if which == 4:
            start = (3 * self.shots * planes + planes + shot) * rows
            return self.near_rows(start, upper, rows)
        if 0 <= step < planes:
            start = ((which * self.shots + shot) * planes + step) * rows
            return self.near_rows(start, upper, rows)
        return self.far_rows(shot * rows, upper, rows)

    def dens(self, at):
        rows, planes = self.rows, self.planes
        if 0 <= at < planes:
            return self.own[3][at]
        upper = at >= planes
        step = at - planes if upper else planes + at
        if 0 <= step < planes:
            return self.near_rows((3 * self.shots * planes + step) * rows, upper, rows)
        return self.far_rows(self.shots * rows, upper, rows)

    def velocity(self, at):
        planes = self.planes
        if 0 <= at < planes:
            return self.vel[0][at]
        upper = at >= planes
        step = at - planes if upper else planes + at
        first, second = self.vel[1:] if upper else self.vel[:0:-1]
        return jnp.where(self.even, first[step], second[step])

    def plane_list(self):
        out = []
        planes = self.planes
        for which, margin in ((0, 3), (1, 2), (2, 2), (4, 1)):
            for shot in range(self.shots):
                for at in range(-margin, planes + margin):
                    out.append((which, shot, at))
        for at in range(-3, planes + 3):
            out.append((3, 0, at))
        for at in range(-2, planes + 2):
            out.append((5, 0, at))
        return out

    def plane(self, item):
        which, shot, at = item
        if which == 3:
            return self.dens(at)
        if which == 5:
            return self.velocity(at)
        return self.field(which, shot, at)


def edge_kernel(now, prev, last, dens, late, near_even, near_odd, far_first, far_second, vel, vel_even, vel_odd, out):
    halo = Halo((now, prev, last, dens, late), near_even, near_odd, far_first, far_second, vel, vel_even, vel_odd)
    first = lax.axis_index("lat") == 0
    rows = halo.rows
    for index, item in enumerate(halo.plane_list()):
        value = halo.plane(item)
        out[index * PAD : (index + 1) * PAD] = jnp.where(first, value[rows - PAD :], value[:PAD])


def near_cols(value):
    lane = lax.broadcasted_iota(jnp.int32, value.shape, 1)
    cols = value.shape[1]
    above = jnp.where(lane == cols - 1, 0.0, pltpu.roll(value, cols - 1, 1))
    below = jnp.where(lane == 0, 0.0, pltpu.roll(value, 1, 1))
    return above, below


def laplace(field, at, cz, cx, cp, cm):
    middle = field(at)
    rows = middle.shape[0]
    flux = cx(at) * (pltpu.roll(middle, rows - 1, 0) - middle)
    total = flux - pltpu.roll(flux, 1, 0)
    above, below = near_cols(middle)
    total = total + (cp(at) * (above - middle) + cm(at) * (below - middle))
    return total + (cz(at) * (field(at + 1) - middle) + cz(at - 1) * (field(at - 1) - middle))


def prepare_kernel(
    now,
    prev,
    last,
    dens,
    late,
    near_even,
    near_odd,
    far_first,
    far_second,
    vel,
    vel_even,
    vel_odd,
    edges,
    dense,
    source_at,
    wavelet,
    lap_out,
    base_out,
    turn_out,
    late_out,
    last_out,
    low_out,
    stiff_out,
    cz_out,
    cx_out,
    cp_out,
    cm_out,
    now_buf,
    buoy_buf,
):
    halo = Halo((now, prev, last, dens, late), near_even, near_odd, far_first, far_second, vel, vel_even, vel_odd)
    lat_at = lax.axis_index("lat")
    rows, cols, shots, planes = halo.rows, halo.cols, halo.shots, halo.planes
    wide = rows + 2 * PAD
    where_is = {item: index for index, item in enumerate(halo.plane_list())}

    def whole(item):
        index = where_is[item]
        part = edges[index * PAD : (index + 1) * PAD]
        low = jnp.where(lat_at == 1, part, 0.0)
        high = jnp.where(lat_at == 0, part, 0.0)
        return jnp.concatenate([low, halo.plane(item), high], axis=0)

    for at in range(-3, planes + 3):
        density = whole((3, 0, at))
        inside = density > 0.0
        buoy_buf[at + 3] = jnp.where(inside, 1.0 / jnp.where(inside, density, 1.0), 0.0)
        if -2 <= at < planes + 2:
            speed = whole((5, 0, at)) * COURANT
            stiff_out[at + 2] = speed * speed * density
        for shot in range(shots):
            now_buf[shot, at + 3] = whole((0, shot, at))
    for at in range(-3, planes + 2):
        cz_out[at + 3] = 0.5 * (buoy_buf[at + 3] + buoy_buf[at + 4])
    for at in range(-2, planes + 2):
        buoy = buoy_buf[at + 3]
        cx_out[at + 2] = 0.5 * (buoy + pltpu.roll(buoy, wide - 1, 0))
        above, below = near_cols(buoy)
        cp_out[at + 2] = 0.5 * (buoy + above)
        cm_out[at + 2] = 0.5 * (buoy + below)
    line = lax.broadcasted_iota(jnp.int32, (wide, cols), 0)
    column = lax.broadcasted_iota(jnp.int32, (wide, cols), 1)
    for shot in range(shots):
        for at in range(-2, planes + 2):
            here = (line + (at + 2) * wide == source_at[shot, 0]) & (column == source_at[shot, 1])
            middle = now_buf[shot, at + 3]
            lap_out[shot, at + 2] = laplace(
                lambda k: now_buf[shot, k + 3],
                at,
                lambda k: cz_out[k + 3],
                lambda k: cx_out[k + 2],
                lambda k: cp_out[k + 2],
                lambda k: cm_out[k + 2],
            )
            base_out[shot, at + 2] = (
                2.0 * middle - whole((1, shot, at)) + jnp.where(here, wavelet[shot, 0], 0.0)
            )
            newest = whole((2, shot, at))
            last_out[shot, at + 2] = newest
            if -1 <= at < planes + 1:
                turn_out[shot, at + 1] = jnp.where(here, wavelet[shot, 1], 0.0) - middle
                late_out[shot, at + 1] = (
                    2.0 * newest
                    - whole((4, shot, at))
                    - dense[shot, 2, (at + 1) * wide : (at + 2) * wide]
                )
            if 0 <= at < planes:
                low_out[shot, at] = newest + dense[shot, 1, (at + 1) * wide : (at + 2) * wide]


def update_kernel(
    stiff,
    lap,
    base,
    turn,
    late,
    last,
    low,
    dense,
    cz_ref,
    cx_ref,
    cp_ref,
    cm_ref,
    out,
    second,
    scaled,
    upper,
    lap_second,
):
    shots, planes = low.shape[:2]
    wide, cols = low.shape[2:]
    cz = lambda k: cz_ref[k + 1]
    cx = lambda k: cx_ref[k]
    cp = lambda k: cp_ref[k]
    cm = lambda k: cm_ref[k]
    for at in range(planes + 4):
        rigid = stiff[at]
        for shot in range(shots):
            second[shot, at] = base[shot, at] + rigid * lap[shot, at]
            scaled[shot, at] = rigid * last[shot, at]
    for at in range(1, planes + 3):
        rigid = stiff[at]
        for shot in range(shots):
            hits = dense[shot, 0, (at - 1) * wide : at * wide]
            lap_now = laplace(lambda k: second[shot, k], at, cz, cx, cp, cm)
            third = 2.0 * second[shot, at] + turn[shot, at - 1] + rigid * lap_now
            adj = late[shot, at - 1] + hits * third
            adj = adj + laplace(lambda k: scaled[shot, k], at, cz, cx, cp, cm)
            upper[shot, at - 1] = adj
            if 2 <= at < planes + 2:
                lap_second[shot, at - 2] = lap_now
    for at in range(1, planes + 3):
        for shot in range(shots):
            scaled[shot, at] = stiff[at] * upper[shot, at - 1]
    for at in range(2, planes + 2):
        total = None
        for shot in range(shots):
            hits = dense[shot, 0, (at - 1) * wide : at * wide]
            lower = 2.0 * upper[shot, at - 1] - low[shot, at - 2] + hits * second[shot, at]
            lower = lower + laplace(lambda k: scaled[shot, k], at, cz, cx, cp, cm)
            term = upper[shot, at - 1] * lap_second[shot, at - 2] + lower * lap[shot, at]
            total = term if total is None else total + term
        out[at - 2] = (stiff[at] * total)[PAD : wide - PAD]


def tile_max(value):
    planes, rows, cols = value.shape
    return jnp.max(jnp.abs(value).reshape(planes * rows // 8, 8, cols), axis=0)


def sum_kernel(mine, other, total, edges):
    value = mine[...] + other[...]
    total[...] = value
    first = lax.axis_index("lat") == 0
    planes, rows, cols = value.shape
    for at in range(planes):
        edges[at * PAD : (at + 1) * PAD] = jnp.where(
            first, value[at, rows - PAD :], value[at, :PAD]
        )
    edges[planes * PAD :] = tile_max(value)


def last_sum_kernel(mine, other, total, largest):
    value = mine[...] + other[...]
    total[...] = value
    largest[...] = tile_max(value)


def widen_kernel(total, mine, got, out):
    planes, rows, cols = total.shape
    wide = rows + 2 * PAD
    lat_at = lax.axis_index("lat")
    for at in range(planes):
        part = got[at * PAD : (at + 1) * PAD]
        start = at * wide
        out[start : start + PAD] = jnp.where(lat_at == 1, part, 0.0)
        out[start + PAD : start + PAD + rows] = total[at]
        out[start + PAD + rows : start + wide] = jnp.where(lat_at == 0, part, 0.0)
    out[planes * wide :] = jnp.maximum(mine[planes * PAD :], got[planes * PAD :])


def restiff_kernel(stiff, mine, by_even, by_odd, largest, velocity, stiff_out, vel_out):
    planes, rows, own = velocity.shape
    wide = rows + 2 * PAD
    even = lax.axis_index("depth") % 2 == 0
    shot_at = lax.axis_index("shot")
    cols = mine.shape[1]
    scale = jnp.max(jnp.max(largest[...], axis=1, keepdims=True), axis=0, keepdims=True) + EPSILON
    for at in range(-2, planes + 2):
        if 0 <= at < planes:
            value = mine[at * wide : (at + 1) * wide]
        else:
            upper = at >= planes
            step = at - planes if upper else planes + at
            first, second = (by_even, by_odd) if upper else (by_odd, by_even)
            value = jnp.where(
                even, first[step * wide : (step + 1) * wide], second[step * wide : (step + 1) * wide]
            )
        value = value / scale
        stiff_out[at + 2] = stiff[at + 2] * jnp.exp(-2.0 * STEP_SIZE * value)
        if 0 <= at < planes:
            shifted = pltpu.roll(value[PAD : PAD + rows], (cols - shot_at * own) % cols, 1)
            vel_out[at] = velocity[at] * jnp.exp(-STEP_SIZE * shifted[:, :own])


def finish_kernel(total, largest, velocity, vel_out, dir_out):
    planes, rows, own = velocity.shape
    shot_at = lax.axis_index("shot")
    cols = total.shape[2]
    scale = jnp.max(jnp.max(largest[...], axis=1, keepdims=True), axis=0, keepdims=True) + EPSILON
    for at in range(planes):
        value = total[at] / scale
        shifted = pltpu.roll(value, (cols - shot_at * own) % cols, 1)[:, :own]
        dir_out[at] = shifted
        vel_out[at] = velocity[at] * jnp.exp(-STEP_SIZE * shifted)


def shards(
    fwd_prev,
    fwd_now,
    adj_late,
    adj_last,
    velocity,
    density,
    wavelet,
    source_cell,
    receiver_cell,
    observed,
):
    shots, planes, rows, cols = fwd_now.shape
    depth_count = lax.axis_size("depth")
    shot_count = lax.axis_size("shot")
    lat_count = lax.axis_size("lat")
    if planes != 2 or wavelet.shape[1] != 2 or lat_count != 2:
        raise ValueError("unsupported split")
    depth_at = lax.axis_index("depth")
    lat_at = lax.axis_index("lat")
    shot_at = lax.axis_index("shot")
    evens = even_pairs(depth_count)
    odds = odd_pairs(depth_count)
    swap = [(0, 1), (1, 0)]
    wide = rows + 2 * PAD

    def shot_terms(block):
        if shot_count == 2:
            return block, lax.ppermute(block, "shot", swap)
        return lax.psum(block, "shot"), jnp.zeros_like(block)

    def depth_max(value, from_pair=None):
        if depth_count & (depth_count - 1):
            return lax.pmax(value, "depth")
        first = 1 if from_pair is None else 2
        if depth_count <= 4:
            parts = [
                lax.ppermute(value, "depth", [(i, i ^ k) for i in range(depth_count)])
                for k in range(first, depth_count)
            ]
            if from_pair is not None:
                parts.append(from_pair)
            for part in parts:
                value = jnp.maximum(value, part)
            return value
        if from_pair is not None:
            value = jnp.maximum(value, from_pair)
        step = first
        while step < depth_count:
            pairs = [(i, i ^ step) for i in range(depth_count)]
            value = jnp.maximum(value, lax.ppermute(value, "depth", pairs))
            step *= 2
        return value

    if shot_count == 2:
        other = lax.ppermute(velocity, "shot", swap)
        full_velocity = jnp.where(
            shot_at == 0,
            jnp.concatenate([velocity, other], axis=2),
            jnp.concatenate([other, velocity], axis=2),
        )
    else:
        full_velocity = lax.all_gather(velocity, "shot", axis=2, tiled=True)

    own = (fwd_now, fwd_prev, adj_last, density, adj_late)
    near_rows = (3 * shots * planes + planes + shots) * rows
    far_rows = (shots + 1) * rows
    to_even, to_odd, to_far = on_chip(
        pack_kernel,
        [(near_rows, cols), (near_rows, cols), (2, far_rows, cols)],
        own,
        name="pack",
    )
    near_even = send(to_even, "depth", evens)
    near_odd = send(to_odd, "depth", odds)
    far_first = send(to_far[0], "depth", two_pairs(depth_count, True))
    far_second = send(to_far[1], "depth", two_pairs(depth_count, False))

    full_rows = rows * lat_count
    depth_start = depth_at * planes
    row_start = lat_at * rows

    def place(cells, margin):
        plane_at = cells // (full_rows * cols) - depth_start + margin
        row_at = cells // cols % full_rows - row_start + PAD
        inside = (
            (plane_at >= 0)
            & (plane_at < planes + 2 * margin)
            & (row_at >= 0)
            & (row_at < wide)
        )
        return jnp.where(inside, plane_at * wide + row_at, -1), cells % cols

    row_id, col_id = place(receiver_cell, 1)
    row_id, full_velocity = lax.optimization_barrier((row_id, full_velocity))
    vel_even = send(full_velocity, "depth", evens)
    vel_odd = send(full_velocity, "depth", odds)
    spread_shape = (shots, 3, (planes + 2) * wide, cols)
    (dense,) = on_chip(
        spread_kernel,
        [spread_shape],
        (row_id, col_id, observed),
        flops=14 * shots * spread_shape[2] * cols * row_id.shape[1],
        limit=24,
        name="spread",
    )
    source_at = jnp.stack(place(source_cell, 2), axis=1)

    halos = own + (near_even, near_odd, far_first, far_second, full_velocity, vel_even, vel_odd)
    strips = shots * (4 * planes + 16) + 2 * planes + 10
    (edges,) = on_chip(edge_kernel, [(strips * PAD, cols)], halos, name="edge")
    edges = lax.ppermute(edges, "lat", swap)

    deep, deeper = planes + 4, planes + 6
    model = (wide, cols)
    spec = pl.BlockSpec(memory_space=pltpu.VMEM)
    scalars = pl.BlockSpec(memory_space=pltpu.SMEM)
    prepared_shapes = [
        (shots, deep) + model,
        (shots, deep) + model,
        (shots, planes + 2) + model,
        (shots, planes + 2) + model,
        (shots, deep) + model,
        (shots, planes) + model,
        (deep,) + model,
        (planes + 5,) + model,
        (deep,) + model,
        (deep,) + model,
        (deep,) + model,
    ]
    vectors = halos + (edges, dense)
    prepared = pl.pallas_call(
        prepare_kernel,
        out_shape=tuple(pltpu.VMEM(shape, jnp.float32) for shape in prepared_shapes),
        in_specs=[spec] * len(vectors) + [scalars, scalars],
        out_specs=tuple(spec for _ in prepared_shapes),
        scratch_shapes=[
            pltpu.VMEM((shots, deeper) + model, jnp.float32),
            pltpu.VMEM((deeper,) + model, jnp.float32),
        ],
        compiler_params=pltpu.CompilerParams(vmem_limit_bytes=8 << 20),
        name="prepare",
    )(
        *[pltpu.with_memory_space_constraint(a, pltpu.VMEM) for a in vectors],
        source_at,
        wavelet,
    )
    lap, base, turn, late, last, low, stiff, cz, cx, cp, cm = prepared

    def gradient_of(stiff):
        (out,) = on_chip(
            update_kernel,
            [(planes, rows, cols)],
            (stiff, lap, base, turn, late, last, low, dense, cz, cx, cp, cm),
            scratch=[
                (shots, deep) + model,
                (shots, deep) + model,
                (shots, planes + 2) + model,
                (shots, planes) + model,
            ],
            name="update",
        )
        return out

    own_velocity = velocity
    for update_index in range(ITERS):
        mine, other = shot_terms(gradient_of(stiff))
        if update_index + 1 == ITERS:
            summed, largest = on_chip(
                last_sum_kernel, [(planes, rows, cols), (8, cols)], (mine, other), name="last_sum"
            )
            largest = jnp.maximum(largest, lax.ppermute(largest, "lat", swap))
            largest = depth_max(largest)
            return tuple(
                on_chip(
                    finish_kernel,
                    [velocity.shape, velocity.shape],
                    (summed, largest, own_velocity),
                    name="finish",
                )
            )
        edge_rows = planes * PAD + 8
        summed, tail = on_chip(
            sum_kernel, [(planes, rows, cols), (edge_rows, cols)], (mine, other), name="sum"
        )
        got = lax.ppermute(tail, "lat", swap)
        (widened,) = on_chip(
            widen_kernel, [(planes * wide + 8, cols)], (summed, tail, got), name="widen"
        )
        by_even = send(widened, "depth", evens)
        by_odd = send(widened, "depth", odds)
        largest = depth_max(widened[planes * wide :], by_even[planes * wide :])
        stiff, own_velocity = on_chip(
            restiff_kernel,
            [stiff.shape, velocity.shape],
            (stiff, widened, by_even, by_odd, largest, own_velocity),
            name="restiff",
        )


def solution(mesh):
    fields = P(("grp", "shot"), "depth", "lat", None)
    model = P(("grp", "depth"), "lat", "shot")
    placed = (
        fields,
        fields,
        fields,
        fields,
        model,
        P(("grp", "depth"), "lat", None),
        P(("grp", "shot"), None),
        P(("grp", "shot")),
        P(("grp", "shot"), None),
        P(("grp", "shot"), None, None),
    )
    return jax.shard_map(
        shards,
        mesh=mesh,
        in_specs=placed,
        out_specs=(model, model),
        check_vma=False,
    )
```

time: 76.9 us -> 67.2 us (0.87)
  other arithmetic: 10.7 us -> 0.36 us
  local copies, waits for them, and re-layouts: 12.1 us -> 6.52 us
  waiting for transfers between devices: 19.1 us -> 23.8 us
  Pallas kernels: 6.68 us -> 8.43 us
    ppermute x7, waiting for transfers between devices: 1.75 us -> 7.08 us  [send(): return lax.ppermute(block, axis, pairs)]
    mul x12 -> x0, other arithmetic: 3.3 us -> none  [the longest x2 1.41 us: gradient_of(): inner(stiff, 1) * upper]
    ppermute x8 -> x9, starting transfers between devices: 12.1 us -> 9.84 us  [the longest x5 8.53 us: depth_max(): lax.ppermute(value, 'depth', [(i, i ^ k) for i in range(depth_count)])]
    max x5 -> x2, other arithmetic: 1.95 us -> 0.01 us  [depth_max(): value = jnp.maximum(value, part)]
    broadcast_in_dim x3 -> x1, local copies, waits for them, and re-layouts: 1.89 us -> 0.01 us  [send(): return jnp.zeros_like(block)]
    pallas_call x1 -> x11, Pallas kernels: 6.68 us -> 8.43 us  [the longest x10 7.05 us: on_chip(): pl.pallas_call(kernel, out_shape=outs, in_specs=[spec] * len(args), out_s...]
    unnamed x47 -> x32, local copies, waits for them, and re-layouts: 7.86 us -> 6.31 us
    ppermute x1, starting transfers between devices: 1.56 us -> 3.03 us  [shards(): other = lax.ppermute(velocity, 'shot', swap)]
  transfers between devices with their start and end apart: 17 -> 18, of which waited for: 10 -> 10; matrix products, arithmetic and copies ran while one was open for 5% -> 1% of each run, Pallas kernels for 9% -> 7%
where the time goes in v2:
time: 67.2 us; the launch traced here: 66.9 us
  starting transfers between devices  26.9 us (40%)
  waiting for transfers between devices  23.8 us (35%)
  Pallas kernels  8.43 us (13%)
  local copies, waits for them, and re-layouts  6.52 us (10%)
  between operations  0.94 us (1%)
    ppermute x7, starting transfers between devices, send(): return lax.ppermute(block, axis, pairs)  13.9 us
    ppermute x5, starting transfers between devices, depth_max(): lax.ppermute(value, 'depth', [(i, i ^ k) for i in range(depth_count)])  8.53 us
    ppermute x2, waiting for transfers between devices, shot_terms(): return (block, lax.ppermute(block, 'shot', swap))  7.49 us
    ppermute x7, waiting for transfers between devices, send(): return lax.ppermute(block, axis, pairs)  7.08 us
    pallas_call x10, Pallas kernels, on_chip(): pl.pallas_call(kernel, out_shape=outs, in_specs=[spec] * len(args), out_s...  7.05 us
    ppermute x5, waiting for transfers between devices, depth_max(): lax.ppermute(value, 'depth', [(i, i ^ k) for i in range(depth_count)])  6.89 us
    unnamed x32, local copies, waits for them, and re-layouts  6.31 us
    ppermute x1, starting transfers between devices, shards(): other = lax.ppermute(velocity, 'shot', swap)  3.03 us
  transfers between devices with their start and end apart: 18, of which 10 were waited for; matrix products, arithmetic and copies ran while one was open for 1% of the time, Pallas kernels for 7%

profile of v2, /device:TPU:0, one launch (start us, length us, event | category | flops | bytes accessed | tf_op | source)
XLA Modules:
  0.0 66.9 jit_solution(1282560735722276931)
XLA Ops:
  0.6 3.0 %collective-permute-start.3 = (f32[2,64,64]{2,1,0:T(8,128)}, f32[2,64,64]{2,1,0:T(8,128)S(1)}, u32[]{:S(2)}, u32[]{:S(2)}) collective-permute-start(f32[2,64,64]{2,1,0:T(8,128)} %velocity.1), channel_id=1, source_target_pairs={{0,2},{2,0},{1,3},{3,1},{4,6},{6,4},{5,7},{7,5},{8,10},{10,8},{9,1... | collective-permute-start | bytes 98312 | tf_op jit(solution)/shard_map/ppermute | solution.py:495
  3.7 0.9 %copy-done = f32[2,2,64,128]{3,2,1,0:T(8,128)S(1)} copy-done((f32[2,2,64,128]{3,2,1,0:T(8,128)S(1)}, f32[2,2,64,128]{3,2,1,0:T(8,128)}, u32[]{:S(2)}) %copy-start) | copy-done | bytes 131096
  4.6 0.9 %copy-done.2 = f32[2,2,64,128]{3,2,1,0:T(8,128)S(1)} copy-done((f32[2,2,64,128]{3,2,1,0:T(8,128)S(1)}, f32[2,2,64,128]{3,2,1,0:T(8,128)}, u32[]{:S(2)}) %copy-start.2) | copy-done | bytes 131096
  5.5 0.9 %copy-done.4 = f32[2,2,64,128]{3,2,1,0:T(8,128)S(1)} copy-done((f32[2,2,64,128]{3,2,1,0:T(8,128)S(1)}, f32[2,2,64,128]{3,2,1,0:T(8,128)}, u32[]{:S(2)}) %copy-start.4) | copy-done | bytes 131096
  6.4 0.9 %copy-done.6 = f32[2,2,64,128]{3,2,1,0:T(8,128)S(1)} copy-done((f32[2,2,64,128]{3,2,1,0:T(8,128)S(1)}, f32[2,2,64,128]{3,2,1,0:T(8,128)}, u32[]{:S(2)}) %copy-start.6) | copy-done | bytes 131096
  7.3 0.8 %copy-done.8 = f32[2,64,128]{2,1,0:T(8,128)S(1)} copy-done((f32[2,64,128]{2,1,0:T(8,128)S(1)}, f32[2,64,128]{2,1,0:T(8,128)}, u32[]{:S(2)}) %copy-start.8) | copy-done | bytes 65560
  8.1 0.1 pack.1
  8.2 0.0 copy-start.13
  8.2 0.0 copy-start.5
  8.2 0.0 copy-start.7
  8.3 2.7 %collective-permute-start.2 = (f32[192,128]{1,0:T(8,128)S(1)}, f32[192,128]{1,0:T(8,128)S(1)}, u32[]{:S(2)}, u32[]{:S(2)}) collective-permute-start(f32[192,128]{1,0:T(8,128)S(1)} %slice_bitcast_fusion), channel_id=1, source_target_pairs={{0,8},{4,12},{8,0},{12,4},{1,9},{5,13},{9,1},{13,5},{2,10},{6,14},... | collective-permute-start | bytes 294920 | tf_op jit(solution)/shard_map/ppermute | solution.py:36
  10.9 1.6 %collective-permute-start = (f32[1024,128]{1,0:T(8,128)S(1)}, f32[1024,128]{1,0:T(8,128)S(1)}, u32[]{:S(2)}, u32[]{:S(2)}) collective-permute-start(f32[1024,128]{1,0:T(8,128)S(1)} %get-tuple-element.24), channel_id=1, source_target_pairs={{0,4},{4,0},{8,12},{12,8},{1,5},{5,1},{9,13},{13,9},{2,6},{6,2},{1... | collective-permute-start | bytes 1572872 | tf_op jit(solution)/shard_map/ppermute | solution.py:36
  12.5 0.7 %collective-permute-start.1 = (f32[1024,128]{1,0:T(8,128)S(1)}, f32[1024,128]{1,0:T(8,128)S(1)}, u32[]{:S(2)}, u32[]{:S(2)}) collective-permute-start(f32[1024,128]{1,0:T(8,128)S(1)} %get-tuple-element.25), channel_id=1, source_target_pairs={{4,8},{8,4},{5,9},{9,5},{6,10},{10,6},{7,11},{11,7},{20,24},{24,20... | collective-permute-start | bytes 1572872 | tf_op jit(solution)/shard_map/ppermute | solution.py:36
  13.2 0.0 copy-start.14
  13.2 0.1 and_select_fusion
  13.4 0.0 copy-start.1
  13.4 0.0 copy-start.3
  13.4 0.0 collective-permute-done.3
  13.4 0.1 maximum_select_fusion.vel
  13.5 0.7 collective-permute-start.5
  14.2 5.0 %collective-permute-start.4 = (f32[2,64,128]{2,1,0:T(8,128)S(1)}, f32[2,64,128]{2,1,0:T(8,128)S(1)}, u32[]{:S(2)}, u32[]{:S(2)}) collective-permute-start(f32[2,64,128]{2,1,0:T(8,128)S(1)} %maximum_select_fusion.vel), channel_id=1, source_target_pairs={{0,4},{4,0},{8,12},{12,8},{1,5},{5,1},{9,13},{13,9},{2,6},{6,2},{1... | collective-permute-start | bytes 196616 | tf_op jit(solution)/shard_map/ppermute | solution.py:36
  19.2 0.0 copy-done.14
  19.2 0.1 copy.12
  19.3 0.1 copy.13
  19.4 0.0 collective-permute-done.5.vel_odd
  19.4 7.1 %collective-permute-done.4.vel_even = f32[2,64,128]{2,1,0:T(8,128)S(1)} collective-permute-done((f32[2,64,128]{2,1,0:T(8,128)S(1)}, f32[2,64,128]{2,1,0:T(8,128)S(1)}, u32[]{:S(2)}, u32[]{:S(2)}) %collective-permute-start.4) | collective-permute-done | bytes 65568 | tf_op jit(solution)/shard_map/ppermute | solution.py:36
  26.5 0.0 collective-permute-done.2.far_first
  26.5 0.0 collective-permute-done.near_even
  26.5 0.0 collective-permute-done.1.near_odd
  26.6 0.0 copy-start.12
  26.6 0.1 collective-permute-start.6
  26.7 0.1 pad_add_fusion.source_at
  26.8 0.5 copy-done.12
  27.3 4.9 %spread.1.dense = f32[2,3,320,128]{3,2,1,0:T(8,128)S(1)} custom-call(s32[2,2048]{1,0:T(2,128)S(1)} %get-tuple-element.28.row_ref, s32[2,2048]{1,0:T(2,128)S(1)} %get-tuple-element.46.col_ref, f32[2,2,2048]{2,1,0:T(2,128)S(1)} %copy-done.12), custom_call_target="tpu_custom_call" | custom-call | flops 2348810240 | bytes 65536 | tf_op jit(solution)/shard_map/spread/pallas_call | solution.py:43
  32.2 0.0 collective-permute-done.6.edges
  32.2 1.4 %prepare.1 = (f32[2,6,80,128]{3,2,1,0:T(8,128)S(1)}, f32[2,6,80,128]{3,2,1,0:T(8,128)S(1)}, f32[2,4,80,128]{3,2,1,0:T(8,128)S(1)}, f32[2,4,80,128]{3,2,1,0:T(8,1...) custom-call(f32[2,2,64,128]{3,2,1,0:T(8,128)S(1)} %copy-done.1, ...), custom_call_target="tpu_custom_call" | custom-call | tf_op jit(solution)/shard_map/prepare/pallas_call | solution.py:571
  33.6 0.8 %update.2.mine = f32[2,64,128]{2,1,0:T(8,128)S(1)} custom-call(f32[6,80,128]{2,1,0:T(8,128)S(1)} %get-tuple-element.29.stiff, f32[2,6,80,128]{3,2,1,0:T(8,128)S(1)} %get-tuple-element.30.lap, f32[2,6,80,128]{3,2,1,0:T(8,128)S(1)} %get-tuple-element.31.base, f32[2,4,80,128]{3,2,1,0:T(8,128)S(1)} %get-tuple-element.32.turn, ...), custom_call_target="tpu_custom_call" | custom-call | bytes 4546560 | tf_op jit(solution)/shard_map/update/pallas_call | solution.py:43
  34.4 0.6 collective-permute-start.7
  35.0 3.8 %collective-permute-done.7.other = f32[2,64,128]{2,1,0:T(8,128)S(1)} collective-permute-done((f32[2,64,128]{2,1,0:T(8,128)S(1)}, f32[2,64,128]{2,1,0:T(8,128)S(1)}, u32[]{:S(2)}, u32[]{:S(2)}) %collective-permute-start.7) | collective-permute-done | bytes 65568 | tf_op jit(solution)/shard_map/ppermute | solution.py:468
  38.8 0.1 collective-permute-start.8
  38.8 1.2 %collective-permute-done.8.got = f32[24,128]{1,0:T(8,128)S(1)} collective-permute-done((f32[24,128]{1,0:T(8,128)S(1)}, f32[24,128]{1,0:T(8,128)S(1)}, u32[]{:S(2)}, u32[]{:S(2)}) %collective-permute-start.8) | collective-permute-done | bytes 12320 | tf_op jit(solution)/shard_map/ppermute | solution.py:625
  40.0 2.7 %collective-permute-start.9 = (f32[168,128]{1,0:T(8,128)S(1)}, f32[168,128]{1,0:T(8,128)S(1)}, u32[]{:S(2)}, u32[]{:S(2)}) collective-permute-start(f32[168,128]{1,0:T(8,128)S(1)} %widen.1.mine), channel_id=1, source_target_pairs={{0,4},{4,0},{8,12},{12,8},{1,5},{5,1},{9,13},{13,9},{2,6},{6,2},{1... | collective-permute-start | bytes 258056 | tf_op jit(solution)/shard_map/ppermute | solution.py:36
  42.7 3.2 %collective-permute-start.12 = (f32[8,128]{1,0:T(8,128)S(1)}, f32[8,128]{1,0:T(8,128)S(1)}, u32[]{:S(2)}, u32[]{:S(2)}) collective-permute-start(f32[8,128]{1,0:T(8,128)S(1)} %slice.12), channel_id=1, source_target_pairs={{0,12},{4,8},{8,4},{12,0},{1,13},{5,9},{9,5},{13,1},{2,14},{6,10},... | collective-permute-start | bytes 12296 | tf_op jit(solution)/shard_map/ppermute | solution.py:477
  45.9 0.0 collective-permute-start.11
  45.9 0.7 collective-permute-start.10
  46.6 2.0 %collective-permute-done.12 = f32[8,128]{1,0:T(8,128)S(1)} collective-permute-done((f32[8,128]{1,0:T(8,128)S(1)}, f32[8,128]{1,0:T(8,128)S(1)}, u32[]{:S(2)}, u32[]{:S(2)}) %collective-permute-start.12) | collective-permute-done | bytes 4128 | tf_op jit(solution)/shard_map/ppermute | solution.py:477
  48.6 1.8 %collective-permute-done.11 = f32[8,128]{1,0:T(8,128)S(1)} collective-permute-done((f32[8,128]{1,0:T(8,128)S(1)}, f32[8,128]{1,0:T(8,128)S(1)}, u32[]{:S(2)}, u32[]{:S(2)}) %collective-permute-start.11) | collective-permute-done | bytes 4128 | tf_op jit(solution)/shard_map/ppermute | solution.py:477
  50.4 0.0 collective-permute-done.9.by_even
  50.4 0.0 collective-permute-done.10.by_odd
  50.4 0.2 restiff.1
  50.7 0.8 %update.3.mine = f32[2,64,128]{2,1,0:T(8,128)S(1)} custom-call(f32[6,80,128]{2,1,0:T(8,128)S(1)} %get-tuple-element.42.stiff, f32[2,6,80,128]{3,2,1,0:T(8,128)S(1)} %get-tuple-element.30.lap, f32[2,6,80,128]{3,2,1,0:T(8,128)S(1)} %get-tuple-element.31.base, f32[2,4,80,128]{3,2,1,0:T(8,128)S(1)} %get-tuple-element.32.turn, ...), custom_call_target="tpu_custom_call" | custom-call | bytes 4546560 | tf_op jit(solution)/shard_map/update/pallas_call | solution.py:43
  51.5 0.6 collective-permute-start.13
  52.1 3.7 %collective-permute-done.13.other = f32[2,64,128]{2,1,0:T(8,128)S(1)} collective-permute-done((f32[2,64,128]{2,1,0:T(8,128)S(1)}, f32[2,64,128]{2,1,0:T(8,128)S(1)}, u32[]{:S(2)}, u32[]{:S(2)}) %collective-permute-start.13) | collective-permute-done | bytes 65568 | tf_op jit(solution)/shard_map/ppermute | solution.py:468
  55.8 0.1 collective-permute-start.14
  55.9 1.2 %collective-permute-done.14 = f32[8,128]{1,0:T(8,128)S(1)} collective-permute-done((f32[8,128]{1,0:T(8,128)S(1)}, f32[8,128]{1,0:T(8,128)S(1)}, u32[]{:S(2)}, u32[]{:S(2)}) %collective-permute-start.14) | collective-permute-done | bytes 4128 | tf_op jit(solution)/shard_map/ppermute | solution.py:611
  57.0 0.9 %collective-permute-start.17 = (f32[8,128]{1,0:T(8,128)S(1)}, f32[8,128]{1,0:T(8,128)S(1)}, u32[]{:S(2)}, u32[]{:S(2)}) collective-permute-start(f32[8,128]{1,0:T(8,128)S(1)} %max.24), channel_id=1, source_target_pairs={{0,12},{4,8},{8,4},{12,0},{1,13},{5,9},{9,5},{13,1},{2,14},{6,10},... | collective-permute-start | bytes 12296 | tf_op jit(solution)/shard_map/ppermute | solution.py:477
  57.9 3.9 %collective-permute-start.16 = (f32[8,128]{1,0:T(8,128)S(1)}, f32[8,128]{1,0:T(8,128)S(1)}, u32[]{:S(2)}, u32[]{:S(2)}) collective-permute-start(f32[8,128]{1,0:T(8,128)S(1)} %max.24), channel_id=1, source_target_pairs={{0,8},{4,12},{8,0},{12,4},{1,9},{5,13},{9,1},{13,5},{2,10},{6,14},... | collective-permute-start | bytes 12296 | tf_op jit(solution)/shard_map/ppermute | solution.py:477
  61.8 0.6 collective-permute-start.15
  62.4 0.1 collective-permute-done.17
  62.4 1.0 %collective-permute-done.16 = f32[8,128]{1,0:T(8,128)S(1)} collective-permute-done((f32[8,128]{1,0:T(8,128)S(1)}, f32[8,128]{1,0:T(8,128)S(1)}, u32[]{:S(2)}, u32[]{:S(2)}) %collective-permute-start.16) | collective-permute-done | bytes 4128 | tf_op jit(solution)/shard_map/ppermute | solution.py:477
  63.4 2.0 %collective-permute-done.15 = f32[8,128]{1,0:T(8,128)S(1)} collective-permute-done((f32[8,128]{1,0:T(8,128)S(1)}, f32[8,128]{1,0:T(8,128)S(1)}, u32[]{:S(2)}, u32[]{:S(2)}) %collective-permute-start.15) | collective-permute-done | bytes 4128 | tf_op jit(solution)/shard_map/ppermute | solution.py:477
  65.4 0.2 finish.1
  65.6 0.6 copy.14
  66.3 0.6 copy.15
  (27 shorter events, 0.2 us)
Async XLA Ops:
  0.6 12.8 %collective-permute-start.3 = (f32[2,64,64]{2,1,0:T(8,128)}, f32[2,64,64]{2,1,0:T(8,128)S(1)}, u32[]{:S(2)}, u32[]{:S(2)}) collective-permute-start(f32[2,64,64]{2,1,0:T(8,128)} %velocity.1), channel_id=1, source_target_pairs={{0,2},{2,0},{1,3},{3,1},{4,6},{6,4},{5,7},{7,5},{8,10},{10,8},{9,1... | collective-permute-start | bytes 98312 | tf_op jit(solution)/shard_map/ppermute | solution.py:495
  3.7 0.9 %copy-start = (f32[2,2,64,128]{3,2,1,0:T(8,128)S(1)}, f32[2,2,64,128]{3,2,1,0:T(8,128)}, u32[]{:S(2)}) copy-start(f32[2,2,64,128]{3,2,1,0:T(8,128)} %now.5) | copy-start | bytes 393220
  4.6 0.9 %copy-start.2 = (f32[2,2,64,128]{3,2,1,0:T(8,128)S(1)}, f32[2,2,64,128]{3,2,1,0:T(8,128)}, u32[]{:S(2)}) copy-start(f32[2,2,64,128]{3,2,1,0:T(8,128)} %prev.5) | copy-start | bytes 393220
  5.5 0.9 %copy-start.4 = (f32[2,2,64,128]{3,2,1,0:T(8,128)S(1)}, f32[2,2,64,128]{3,2,1,0:T(8,128)}, u32[]{:S(2)}) copy-start(f32[2,2,64,128]{3,2,1,0:T(8,128)} %last.5) | copy-start | bytes 393220
  6.4 0.9 %copy-start.6 = (f32[2,2,64,128]{3,2,1,0:T(8,128)S(1)}, f32[2,2,64,128]{3,2,1,0:T(8,128)}, u32[]{:S(2)}) copy-start(f32[2,2,64,128]{3,2,1,0:T(8,128)} %late.5) | copy-start | bytes 393220
  7.3 0.8 %copy-start.8 = (f32[2,64,128]{2,1,0:T(8,128)S(1)}, f32[2,64,128]{2,1,0:T(8,128)}, u32[]{:S(2)}) copy-start(f32[2,64,128]{2,1,0:T(8,128)} %dens.5) | copy-start | bytes 196612
  8.1 5.3 %copy-start.10 = (f32[2,64,64]{2,1,0:T(8,128)S(1)}, f32[2,64,64]{2,1,0:T(8,128)}, u32[]{:S(2)}) copy-start(f32[2,64,64]{2,1,0:T(8,128)} %velocity.1) | copy-start | bytes 98308
  8.1 18.4 %copy-start.9 = (f32[2,64,128]{2,1,0:T(8,128)S(1)}, f32[2,64,128]{2,1,0:T(8,128)}, u32[]{:S(2)}) copy-start(f32[2,64,128]{2,1,0:T(8,128)} %dens.5) | copy-start | bytes 196612
  8.2 5.0 %copy-start.13 = (s32[2,2048]{1,0:T(2,128)S(1)}, s32[2,2048]{1,0:T(2,128)}, u32[]{:S(2)}) copy-start(s32[2,2048]{1,0:T(2,128)} %param.18) | copy-start | bytes 49156
  8.2 18.3 %copy-start.5 = (f32[2,2,64,128]{3,2,1,0:T(8,128)S(1)}, f32[2,2,64,128]{3,2,1,0:T(8,128)}, u32[]{:S(2)}) copy-start(f32[2,2,64,128]{3,2,1,0:T(8,128)} %last.5) | copy-start | bytes 393220
  8.2 18.3 %copy-start.7 = (f32[2,2,64,128]{3,2,1,0:T(8,128)S(1)}, f32[2,2,64,128]{3,2,1,0:T(8,128)}, u32[]{:S(2)}) copy-start(f32[2,2,64,128]{3,2,1,0:T(8,128)} %late.5) | copy-start | bytes 393220
  8.3 18.2 %collective-permute-start.2 = (f32[192,128]{1,0:T(8,128)S(1)}, f32[192,128]{1,0:T(8,128)S(1)}, u32[]{:S(2)}, u32[]{:S(2)}) collective-permute-start(f32[192,128]{1,0:T(8,128)S(1)} %slice_bitcast_fusion), channel_id=1, source_target_pairs={{0,8},{4,12},{8,0},{12,4},{1,9},{5,13},{9,1},{13,5},{2,10},{6,14},... | collective-permute-start | bytes 294920 | tf_op jit(solution)/shard_map/ppermute | solution.py:36
  10.9 15.6 %collective-permute-start = (f32[1024,128]{1,0:T(8,128)S(1)}, f32[1024,128]{1,0:T(8,128)S(1)}, u32[]{:S(2)}, u32[]{:S(2)}) collective-permute-start(f32[1024,128]{1,0:T(8,128)S(1)} %get-tuple-element.24), channel_id=1, source_target_pairs={{0,4},{4,0},{8,12},{12,8},{1,5},{5,1},{9,13},{13,9},{2,6},{6,2},{1... | collective-permute-start | bytes 1572872 | tf_op jit(solution)/shard_map/ppermute | solution.py:36
  12.5 14.0 %collective-permute-start.1 = (f32[1024,128]{1,0:T(8,128)S(1)}, f32[1024,128]{1,0:T(8,128)S(1)}, u32[]{:S(2)}, u32[]{:S(2)}) collective-permute-start(f32[1024,128]{1,0:T(8,128)S(1)} %get-tuple-element.25), channel_id=1, source_target_pairs={{4,8},{8,4},{5,9},{9,5},{6,10},{10,6},{7,11},{11,7},{20,24},{24,20... | collective-permute-start | bytes 1572872 | tf_op jit(solution)/shard_map/ppermute | solution.py:36
  13.2 6.0 %copy-start.14 = (s32[2]{0:T(128)S(1)}, s32[2]{0:T(128)}, u32[]{:S(2)}) copy-start(s32[2]{0:T(128)} %param.17) | copy-start | bytes 28
  13.4 13.2 %copy-start.1 = (f32[2,2,64,128]{3,2,1,0:T(8,128)S(1)}, f32[2,2,64,128]{3,2,1,0:T(8,128)}, u32[]{:S(2)}) copy-start(f32[2,2,64,128]{3,2,1,0:T(8,128)} %now.5) | copy-start | bytes 393220
  13.4 13.2 %copy-start.3 = (f32[2,2,64,128]{3,2,1,0:T(8,128)S(1)}, f32[2,2,64,128]{3,2,1,0:T(8,128)}, u32[]{:S(2)}) copy-start(f32[2,2,64,128]{3,2,1,0:T(8,128)} %prev.5) | copy-start | bytes 393220
  13.5 5.9 %collective-permute-start.5 = (f32[2,64,128]{2,1,0:T(8,128)S(1)}, f32[2,64,128]{2,1,0:T(8,128)S(1)}, u32[]{:S(2)}, u32[]{:S(2)}) collective-permute-start(f32[2,64,128]{2,1,0:T(8,128)S(1)} %maximum_select_fusion.vel), channel_id=1, source_target_pairs={{4,8},{8,4},{5,9},{9,5},{6,10},{10,6},{7,11},{11,7},{20,24},{24,20... | collective-permute-start | bytes 196616 | tf_op jit(solution)/shard_map/ppermute | solution.py:36
  14.2 12.3 %collective-permute-start.4 = (f32[2,64,128]{2,1,0:T(8,128)S(1)}, f32[2,64,128]{2,1,0:T(8,128)S(1)}, u32[]{:S(2)}, u32[]{:S(2)}) collective-permute-start(f32[2,64,128]{2,1,0:T(8,128)S(1)} %maximum_select_fusion.vel), channel_id=1, source_target_pairs={{0,4},{4,0},{8,12},{12,8},{1,5},{5,1},{9,13},{13,9},{2,6},{6,2},{1... | collective-permute-start | bytes 196616 | tf_op jit(solution)/shard_map/ppermute | solution.py:36
  26.6 0.8 %copy-start.12 = (f32[2,2,2048]{2,1,0:T(2,128)S(1)}, f32[2,2,2048]{2,1,0:T(2,128)}, u32[]{:S(2)}) copy-start(f32[2,2,2048]{2,1,0:T(2,128)} %obs_ref.1) | copy-start | bytes 98308
  26.6 5.6 %collective-permute-start.6 = (f32[496,128]{1,0:T(8,128)S(1)}, f32[496,128]{1,0:T(8,128)S(1)}, u32[]{:S(2)}, u32[]{:S(2)}) collective-permute-start(f32[496,128]{1,0:T(8,128)S(1)} %edge.1), channel_id=1, source_target_pairs={{0,1},{1,0},{2,3},{3,2},{4,5},{5,4},{6,7},{7,6},{8,9},{9,8},{10,11... | collective-permute-start | bytes 761864 | tf_op jit(solution)/shard_map/ppermute | solution.py:551
  27.3 4.9 %copy-start.11 = (f32[2,2]{1,0:T(2,128)S(1)}, f32[2,2]{1,0:T(2,128)}, u32[]{:S(2)}) copy-start(f32[2,2]{1,0:T(2,128)} %wavelet.1) | copy-start | bytes 52
  34.4 4.3 %collective-permute-start.7 = (f32[2,64,128]{2,1,0:T(8,128)S(1)}, f32[2,64,128]{2,1,0:T(8,128)S(1)}, u32[]{:S(2)}, u32[]{:S(2)}) collective-permute-start(f32[2,64,128]{2,1,0:T(8,128)S(1)} %update.2.mine), channel_id=1, source_target_pairs={{0,2},{2,0},{1,3},{3,1},{4,6},{6,4},{5,7},{7,5},{8,10},{10,8},{9,1... | collective-permute-start | bytes 196616 | tf_op jit(solution)/shard_map/ppermute | solution.py:468
  38.8 1.2 %collective-permute-start.8 = (f32[24,128]{1,0:T(8,128)S(1)}, f32[24,128]{1,0:T(8,128)S(1)}, u32[]{:S(2)}, u32[]{:S(2)}) collective-permute-start(f32[24,128]{1,0:T(8,128)S(1)} %get-tuple-element.41.mine), channel_id=1, source_target_pairs={{0,1},{1,0},{2,3},{3,2},{4,5},{5,4},{6,7},{7,6},{8,9},{9,8},{10,11... | collective-permute-start | bytes 36872 | tf_op jit(solution)/shard_map/ppermute | solution.py:625
  40.0 10.4 %collective-permute-start.9 = (f32[168,128]{1,0:T(8,128)S(1)}, f32[168,128]{1,0:T(8,128)S(1)}, u32[]{:S(2)}, u32[]{:S(2)}) collective-permute-start(f32[168,128]{1,0:T(8,128)S(1)} %widen.1.mine), channel_id=1, source_target_pairs={{0,4},{4,0},{8,12},{12,8},{1,5},{5,1},{9,13},{13,9},{2,6},{6,2},{1... | collective-permute-start | bytes 258056 | tf_op jit(solution)/shard_map/ppermute | solution.py:36
  42.7 5.9 %collective-permute-start.12 = (f32[8,128]{1,0:T(8,128)S(1)}, f32[8,128]{1,0:T(8,128)S(1)}, u32[]{:S(2)}, u32[]{:S(2)}) collective-permute-start(f32[8,128]{1,0:T(8,128)S(1)} %slice.12), channel_id=1, source_target_pairs={{0,12},{4,8},{8,4},{12,0},{1,13},{5,9},{9,5},{13,1},{2,14},{6,10},... | collective-permute-start | bytes 12296 | tf_op jit(solution)/shard_map/ppermute | solution.py:477
  45.9 4.5 %collective-permute-start.11 = (f32[8,128]{1,0:T(8,128)S(1)}, f32[8,128]{1,0:T(8,128)S(1)}, u32[]{:S(2)}, u32[]{:S(2)}) collective-permute-start(f32[8,128]{1,0:T(8,128)S(1)} %slice.12), channel_id=1, source_target_pairs={{0,8},{4,12},{8,0},{12,4},{1,9},{5,13},{9,1},{13,5},{2,10},{6,14},... | collective-permute-start | bytes 12296 | tf_op jit(solution)/shard_map/ppermute | solution.py:477
  45.9 4.5 %collective-permute-start.10 = (f32[168,128]{1,0:T(8,128)S(1)}, f32[168,128]{1,0:T(8,128)S(1)}, u32[]{:S(2)}, u32[]{:S(2)}) collective-permute-start(f32[168,128]{1,0:T(8,128)S(1)} %widen.1.mine), channel_id=1, source_target_pairs={{4,8},{8,4},{5,9},{9,5},{6,10},{10,6},{7,11},{11,7},{20,24},{24,20... | collective-permute-start | bytes 258056 | tf_op jit(solution)/shard_map/ppermute | solution.py:36
  51.5 4.3 %collective-permute-start.13 = (f32[2,64,128]{2,1,0:T(8,128)S(1)}, f32[2,64,128]{2,1,0:T(8,128)S(1)}, u32[]{:S(2)}, u32[]{:S(2)}) collective-permute-start(f32[2,64,128]{2,1,0:T(8,128)S(1)} %update.3.mine), channel_id=1, source_target_pairs={{0,2},{2,0},{1,3},{3,1},{4,6},{6,4},{5,7},{7,5},{8,10},{10,8},{9,1... | collective-permute-start | bytes 196616 | tf_op jit(solution)/shard_map/ppermute | solution.py:468
  55.8 1.2 %collective-permute-start.14 = (f32[8,128]{1,0:T(8,128)S(1)}, f32[8,128]{1,0:T(8,128)S(1)}, u32[]{:S(2)}, u32[]{:S(2)}) collective-permute-start(f32[8,128]{1,0:T(8,128)S(1)} %get-tuple-element.44), channel_id=1, source_target_pairs={{0,1},{1,0},{2,3},{3,2},{4,5},{5,4},{6,7},{7,6},{8,9},{9,8},{10,11... | collective-permute-start | bytes 12296 | tf_op jit(solution)/shard_map/ppermute | solution.py:611
  57.0 5.4 %collective-permute-start.17 = (f32[8,128]{1,0:T(8,128)S(1)}, f32[8,128]{1,0:T(8,128)S(1)}, u32[]{:S(2)}, u32[]{:S(2)}) collective-permute-start(f32[8,128]{1,0:T(8,128)S(1)} %max.24), channel_id=1, source_target_pairs={{0,12},{4,8},{8,4},{12,0},{1,13},{5,9},{9,5},{13,1},{2,14},{6,10},... | collective-permute-start | bytes 12296 | tf_op jit(solution)/shard_map/ppermute | solution.py:477
  57.9 5.5 %collective-permute-start.16 = (f32[8,128]{1,0:T(8,128)S(1)}, f32[8,128]{1,0:T(8,128)S(1)}, u32[]{:S(2)}, u32[]{:S(2)}) collective-permute-start(f32[8,128]{1,0:T(8,128)S(1)} %max.24), channel_id=1, source_target_pairs={{0,8},{4,12},{8,0},{12,4},{1,9},{5,13},{9,1},{13,5},{2,10},{6,14},... | collective-permute-start | bytes 12296 | tf_op jit(solution)/shard_map/ppermute | solution.py:477
  61.8 3.6 %collective-permute-start.15 = (f32[8,128]{1,0:T(8,128)S(1)}, f32[8,128]{1,0:T(8,128)S(1)}, u32[]{:S(2)}, u32[]{:S(2)}) collective-permute-start(f32[8,128]{1,0:T(8,128)S(1)} %max.24), channel_id=1, source_target_pairs={{0,4},{4,0},{8,12},{12,8},{1,5},{5,1},{9,13},{13,9},{2,6},{6,2},{1... | collective-permute-start | bytes 12296 | tf_op jit(solution)/shard_map/ppermute | solution.py:477

commit v3 on v2

--- a/solution.py
+++ b/solution.py
@@ -1,5 +1,3 @@
-import functools
-
 import jax
 import jax.numpy as jnp
 from jax import lax
@@ -7,13 +5,13 @@
 from jax.experimental.pallas import tpu as pltpu
 from jax.sharding import PartitionSpec as P
 
+
 ITERS = 2
 
 COURANT = 0.1
 STEP_SIZE = 0.1
 EPSILON = 1e-06
 PAD = 8
-WIDE = 3
 
 
 def even_pairs(count):
@@ -36,9 +34,10 @@
     return lax.ppermute(block, axis, pairs)
 
 
-def on_chip(kernel, out_shapes, args, scratch=(), flops=0, limit=8, name=None):
+def on_chip(kernel, out_shapes, args, scratch=(), flops=0, limit=8, keep=True):
     spec = pl.BlockSpec(memory_space=pltpu.VMEM)
-    outs = tuple(pltpu.VMEM(shape, jnp.float32) for shape in out_shapes)
+    place = pltpu.VMEM if keep else jax.ShapeDtypeStruct
+    outs = tuple(place(shape, jnp.float32) for shape in out_shapes)
     moved = sum(a.size * 4 for a in args)
     return pl.pallas_call(
         kernel,
@@ -48,41 +47,42 @@
         scratch_shapes=[pltpu.VMEM(shape, jnp.float32) for shape in scratch],
         compiler_params=pltpu.CompilerParams(vmem_limit_bytes=limit << 20),
         cost_estimate=pl.CostEstimate(flops=flops, bytes_accessed=moved, transcendentals=0),
-        name=name,
     )(*[pltpu.with_memory_space_constraint(a, pltpu.VMEM) for a in args])
 
 
-def pack_kernel(now, prev, last, dens, late, to_even, to_odd, to_far):
+def pack_kernel(now, prev, last, dens, late, to_even, to_odd, to_far, late_out, sems):
     depth_at = lax.axis_index("depth")
     even = depth_at % 2 == 0
     front = depth_at % 4 < 2
-    shots, planes, rows, cols = now.shape
-    block = planes * rows
+    shots, planes, _, _ = now.shape
+    copies = []
     start = 0
     for field in (now, prev, last):
         for shot in range(shots):
-            value = field[shot].reshape(block, cols)
-            to_even[start : start + block] = value
-            to_odd[start : start + block] = value
-            start += block
-    value = dens[...].reshape(block, cols)
-    to_even[start : start + block] = value
-    to_odd[start : start + block] = value
-    start += block
+            copies.append((field.at[shot], to_even.at[start : start + planes]))
+            start += planes
+    copies.append((dens, to_even.at[start : start + planes]))
+    start += planes
+    copies.append((late, late_out))
+    copies = [
+        pltpu.make_async_copy(source, target, sems.at[index])
+        for index, (source, target) in enumerate(copies)
+    ]
+    for copy in copies:
+        copy.start()
+    for copy in copies:
+        copy.wait()
+    to_odd[:start] = to_even[:start]
     for shot in range(shots):
-        low, top = late[shot, 0], late[shot, planes - 1]
-        to_even[start : start + rows] = jnp.where(even, top, low)
-        to_odd[start : start + rows] = jnp.where(even, low, top)
-        start += rows
-        to_far[0, shot * rows : (shot + 1) * rows] = jnp.where(
-            front, now[shot, planes - 1], now[shot, 0]
-        )
-        to_far[1, shot * rows : (shot + 1) * rows] = jnp.where(
-            front, now[shot, 0], now[shot, planes - 1]
-        )
-    end = shots * rows
-    to_far[0, end:] = jnp.where(front, dens[planes - 1], dens[0])
-    to_far[1, end:] = jnp.where(front, dens[0], dens[planes - 1])
+        low, top = late_out[shot, 0], late_out[shot, planes - 1]
+        to_even[start + shot] = jnp.where(even, top, low)
+        to_odd[start + shot] = jnp.where(even, low, top)
+        low, top = to_even[shot * planes], to_even[shot * planes + planes - 1]
+        to_far[0, shot] = jnp.where(front, top, low)
+        to_far[1, shot] = jnp.where(front, low, top)
+    low, top = to_even[start - planes], to_even[start - 1]
+    to_far[0, shots] = jnp.where(front, top, low)
+    to_far[1, shots] = jnp.where(front, low, top)
 
 
 def spread_kernel(row_ref, col_ref, obs_ref, out_ref):
@@ -119,56 +119,38 @@
 
 
 class Halo:
-    def __init__(self, own, near_even, near_odd, far_first, far_second, vel_own, vel_even, vel_odd):
+    def __init__(self, own, late, near_even, near_odd, far_first, far_second, vel_own, vel_even, vel_odd):
         depth_at = lax.axis_index("depth")
         self.even = depth_at % 2 == 0
         self.front = depth_at % 4 < 2
-        self.own = own
+        self.own, self.late = own, late
         self.near = (near_even, near_odd)
         self.far = (far_first, far_second)
         self.vel = (vel_own, vel_even, vel_odd)
-        self.shots, self.planes, self.rows, self.cols = own[0].shape
-
-    def near_rows(self, start, upper, rows):
-        first, second = self.near if upper else self.near[::-1]
-        return jnp.where(self.even, first[start : start + rows], second[start : start + rows])
-
-    def far_rows(self, start, upper, rows):
-        first, second = self.far if upper else self.far[::-1]
-        return jnp.where(self.front, first[start : start + rows], second[start : start + rows])
-
-    def field(self, which, shot, at):
-        rows, planes = self.rows, self.planes
-        if 0 <= at < planes:
-            return self.own[which][shot, at]
+        self.shots, self.planes, self.rows, self.cols = late.shape
+
+    def pick(self, pair, flag, upper, index):
+        first, second = pair if upper else pair[::-1]
+        return jnp.where(flag, first[index], second[index])
+
+    def plane(self, item):
+        which, shot, at = item
+        planes, shots = self.planes, self.shots
+        inside = 0 <= at < planes
         upper = at >= planes
-        step = at - planes if upper else planes + at
+        step = at if inside else (at - planes if upper else planes + at)
+        if which == 5:
+            if inside:
+                return self.vel[0][at]
+            return self.pick(self.vel[1:], self.even, upper, step)
         if which == 4:
-            start = (3 * self.shots * planes + planes + shot) * rows
-            return self.near_rows(start, upper, rows)
+            if inside:
+                return self.late[shot, at]
+            return self.pick(self.near, self.even, upper, (3 * shots + 1) * planes + shot)
         if 0 <= step < planes:
-            start = ((which * self.shots + shot) * planes + step) * rows
-            return self.near_rows(start, upper, rows)
-        return self.far_rows(shot * rows, upper, rows)
-
-    def dens(self, at):
-        rows, planes = self.rows, self.planes
-        if 0 <= at < planes:
-            return self.own[3][at]
-        upper = at >= planes
-        step = at - planes if upper else planes + at
-        if 0 <= step < planes:
-            return self.near_rows((3 * self.shots * planes + step) * rows, upper, rows)
-        return self.far_rows(self.shots * rows, upper, rows)
-
-    def velocity(self, at):
-        planes = self.planes
-        if 0 <= at < planes:
-            return self.vel[0][at]
-        upper = at >= planes
-        step = at - planes if upper else planes + at
-        first, second = self.vel[1:] if upper else self.vel[:0:-1]
-        return jnp.where(self.even, first[step], second[step])
+            index = (which * shots + shot) * planes + step
+            return self.own[index] if inside else self.pick(self.near, self.even, upper, index)
+        return self.pick(self.far, self.front, upper, shots if which == 3 else shot)
 
     def plane_list(self):
         out = []
@@ -183,17 +165,10 @@
             out.append((5, 0, at))
         return out
 
-    def plane(self, item):
-        which, shot, at = item
-        if which == 3:
-            return self.dens(at)
-        if which == 5:
-            return self.velocity(at)
-        return self.field(which, shot, at)
-
-
-def edge_kernel(now, prev, last, dens, late, near_even, near_odd, far_first, far_second, vel, vel_even, vel_odd, out):
-    halo = Halo((now, prev, last, dens, late), near_even, near_odd, far_first, far_second, vel, vel_even, vel_odd)
+
+def edge_kernel(*refs):
+    halo = Halo(*refs[:-1])
+    out = refs[-1]
     first = lax.axis_index("lat") == 0
     rows = halo.rows
     for index, item in enumerate(halo.plane_list()):
@@ -220,10 +195,7 @@
 
 
 def prepare_kernel(
-    now,
-    prev,
-    last,
-    dens,
+    own,
     late,
     near_even,
     near_odd,
@@ -250,7 +222,7 @@
     now_buf,
     buoy_buf,
 ):
-    halo = Halo((now, prev, last, dens, late), near_even, near_odd, far_first, far_second, vel, vel_even, vel_odd)
+    halo = Halo(own, late, near_even, near_odd, far_first, far_second, vel, vel_even, vel_odd)
     lat_at = lax.axis_index("lat")
     rows, cols, shots, planes = halo.rows, halo.cols, halo.shots, halo.planes
     wide = rows + 2 * PAD
@@ -330,7 +302,7 @@
     lap_second,
 ):
     shots, planes = low.shape[:2]
-    wide, cols = low.shape[2:]
+    wide, _ = low.shape[2:]
     cz = lambda k: cz_ref[k + 1]
     cx = lambda k: cx_ref[k]
     cp = lambda k: cp_ref[k]
@@ -374,7 +346,7 @@
     value = mine[...] + other[...]
     total[...] = value
     first = lax.axis_index("lat") == 0
-    planes, rows, cols = value.shape
+    planes, rows, _ = value.shape
     for at in range(planes):
         edges[at * PAD : (at + 1) * PAD] = jnp.where(
             first, value[at, rows - PAD :], value[at, :PAD]
@@ -389,7 +361,7 @@
 
 
 def widen_kernel(total, mine, got, out):
-    planes, rows, cols = total.shape
+    planes, rows, _ = total.shape
     wide = rows + 2 * PAD
     lat_at = lax.axis_index("lat")
     for at in range(planes):
@@ -426,7 +398,7 @@
 
 
 def finish_kernel(total, largest, velocity, vel_out, dir_out):
-    planes, rows, own = velocity.shape
+    planes, _, own = velocity.shape
     shot_at = lax.axis_index("shot")
     cols = total.shape[2]
     scale = jnp.max(jnp.max(largest[...], axis=1, keepdims=True), axis=0, keepdims=True) + EPSILON
@@ -472,13 +444,11 @@
         if depth_count & (depth_count - 1):
             return lax.pmax(value, "depth")
         first = 1 if from_pair is None else 2
-        if depth_count <= 4:
+        if depth_count <= 4 and from_pair is None:
             parts = [
                 lax.ppermute(value, "depth", [(i, i ^ k) for i in range(depth_count)])
-                for k in range(first, depth_count)
+                for k in range(1, depth_count)
             ]
-            if from_pair is not None:
-                parts.append(from_pair)
             for part in parts:
                 value = jnp.maximum(value, part)
             return value
@@ -492,7 +462,7 @@
         return value
 
     if shot_count == 2:
-        other = lax.ppermute(velocity, "shot", swap)
+        other = send(velocity, "shot", swap)
         full_velocity = jnp.where(
             shot_at == 0,
             jnp.concatenate([velocity, other], axis=2),
@@ -501,19 +471,27 @@
     else:
         full_velocity = lax.all_gather(velocity, "shot", axis=2, tiled=True)
 
-    own = (fwd_now, fwd_prev, adj_last, density, adj_late)
-    near_rows = (3 * shots * planes + planes + shots) * rows
-    far_rows = (shots + 1) * rows
-    to_even, to_odd, to_far = on_chip(
+    near_planes = (3 * shots + 1) * planes + shots
+    hbm = pl.BlockSpec(memory_space=pl.ANY)
+    spec = pl.BlockSpec(memory_space=pltpu.VMEM)
+    to_even, to_odd, to_far, own_late = pl.pallas_call(
         pack_kernel,
-        [(near_rows, cols), (near_rows, cols), (2, far_rows, cols)],
-        own,
+        out_shape=(
+            pltpu.VMEM((near_planes, rows, cols), jnp.float32),
+            pltpu.VMEM((near_planes, rows, cols), jnp.float32),
+            pltpu.VMEM((2, shots + 1, rows, cols), jnp.float32),
+            pltpu.VMEM(adj_late.shape, jnp.float32),
+        ),
+        in_specs=[hbm] * 5,
+        out_specs=(spec, spec, spec, spec),
+        scratch_shapes=[pltpu.SemaphoreType.DMA((3 * shots + 2,))],
+        compiler_params=pltpu.CompilerParams(vmem_limit_bytes=8 << 20),
         name="pack",
-    )
-    near_even = send(to_even, "depth", evens)
+    )(fwd_now, fwd_prev, adj_last, density, adj_late)
     near_odd = send(to_odd, "depth", odds)
     far_first = send(to_far[0], "depth", two_pairs(depth_count, True))
     far_second = send(to_far[1], "depth", two_pairs(depth_count, False))
+    near_even = send(to_even, "depth", evens)
 
     full_rows = rows * lat_count
     depth_start = depth_at * planes
@@ -532,8 +510,8 @@
 
     row_id, col_id = place(receiver_cell, 1)
     row_id, full_velocity = lax.optimization_barrier((row_id, full_velocity))
+    vel_odd = send(full_velocity, "depth", odds)
     vel_even = send(full_velocity, "depth", evens)
-    vel_odd = send(full_velocity, "depth", odds)
     spread_shape = (shots, 3, (planes + 2) * wide, cols)
     (dense,) = on_chip(
         spread_kernel,
@@ -541,18 +519,16 @@
         (row_id, col_id, observed),
         flops=14 * shots * spread_shape[2] * cols * row_id.shape[1],
         limit=24,
-        name="spread",
     )
     source_at = jnp.stack(place(source_cell, 2), axis=1)
 
-    halos = own + (near_even, near_odd, far_first, far_second, full_velocity, vel_even, vel_odd)
+    halos = (to_even, own_late) + (near_even, near_odd, far_first, far_second, full_velocity, vel_even, vel_odd)
     strips = shots * (4 * planes + 16) + 2 * planes + 10
-    (edges,) = on_chip(edge_kernel, [(strips * PAD, cols)], halos, name="edge")
-    edges = lax.ppermute(edges, "lat", swap)
+    (edges,) = on_chip(edge_kernel, [(strips * PAD, cols)], halos)
+    edges = send(edges, "lat", swap)
 
     deep, deeper = planes + 4, planes + 6
     model = (wide, cols)
-    spec = pl.BlockSpec(memory_space=pltpu.VMEM)
     scalars = pl.BlockSpec(memory_space=pltpu.SMEM)
     prepared_shapes = [
         (shots, deep) + model,
@@ -597,7 +573,6 @@
                 (shots, planes + 2) + model,
                 (shots, planes) + model,
             ],
-            name="update",
         )
         return out
 
@@ -606,7 +581,7 @@
         mine, other = shot_terms(gradient_of(stiff))
         if update_index + 1 == ITERS:
             summed, largest = on_chip(
-                last_sum_kernel, [(planes, rows, cols), (8, cols)], (mine, other), name="last_sum"
+                last_sum_kernel, [(planes, rows, cols), (8, cols)], (mine, other)
             )
             largest = jnp.maximum(largest, lax.ppermute(largest, "lat", swap))
             largest = depth_max(largest)
@@ -615,25 +590,20 @@
                     finish_kernel,
                     [velocity.shape, velocity.shape],
                     (summed, largest, own_velocity),
-                    name="finish",
+                    keep=False,
                 )
             )
         edge_rows = planes * PAD + 8
-        summed, tail = on_chip(
-            sum_kernel, [(planes, rows, cols), (edge_rows, cols)], (mine, other), name="sum"
-        )
+        summed, tail = on_chip(sum_kernel, [(planes, rows, cols), (edge_rows, cols)], (mine, other))
         got = lax.ppermute(tail, "lat", swap)
-        (widened,) = on_chip(
-            widen_kernel, [(planes * wide + 8, cols)], (summed, tail, got), name="widen"
-        )
+        (widened,) = on_chip(widen_kernel, [(planes * wide + 8, cols)], (summed, tail, got))
         by_even = send(widened, "depth", evens)
-        by_odd = send(widened, "depth", odds)
+        by_odd = send(widened[: planes * wide], "depth", odds)
         largest = depth_max(widened[planes * wide :], by_even[planes * wide :])
         stiff, own_velocity = on_chip(
             restiff_kernel,
             [stiff.shape, velocity.shape],
             (stiff, widened, by_even, by_odd, largest, own_velocity),
-            name="restiff",
         )
 
 
@@ -652,6 +622,7 @@
         P(("grp", "shot"), None),
         P(("grp", "shot"), None, None),
     )
+
     return jax.shard_map(
         shards,
         mesh=mesh,

time: 67.2 us -> 67.4 us (level)
  waiting for transfers between devices: 23.8 us -> 27.1 us
  starting transfers between devices: 26.9 us -> 23.6 us
  Pallas kernels: 8.43 us -> 9.88 us
  local copies, waits for them, and re-layouts: 6.52 us -> 5.24 us
    ppermute x7 -> x9, waiting for transfers between devices: 7.08 us -> 11.9 us  [send(): return lax.ppermute(block, axis, pairs)]
    ppermute x5 -> x3, starting transfers between devices: 8.53 us -> 4.39 us  [depth_max(): lax.ppermute(value, 'depth', [(i, i ^ k) for i in range(depth_count)])]
    ppermute x5 -> x3, waiting for transfers between devices: 6.89 us -> 3.77 us  [depth_max(): lax.ppermute(value, 'depth', [(i, i ^ k) for i in range(depth_count)])]
    ppermute x2 -> x1, waiting for transfers between devices: 0.01 us -> 1.6 us  [depth_max(): value = jnp.maximum(value, lax.ppermute(value, 'depth', pairs))]
    unnamed x32 -> x20, local copies, waits for them, and re-layouts: 6.31 us -> 5.03 us
    ppermute x7 -> x9, starting transfers between devices: 13.9 us -> 15.1 us  [send(): return lax.ppermute(block, axis, pairs)]
    pallas_call x0 -> x1, Pallas kernels: none -> 0.86 us  [shards(): pl.pallas_call(pack_kernel, out_shape=(pltpu.VMEM((near_planes, rows, col...]
    pallas_call x10 -> x9, Pallas kernels: 7.05 us -> 7.64 us  [on_chip(): pl.pallas_call(kernel, out_shape=outs, in_specs=[spec] * len(args), out_s...]
  transfers between devices with their start and end apart: 18 -> 17, of which waited for: 10 -> 9; matrix products, arithmetic and copies ran while one was open for 1% -> 1% of each run, Pallas kernels for 7% -> 9%
where the time goes in v3:
time: 67.4 us; the launch traced here: 67.1 us
  waiting for transfers between devices  27.1 us (40%)
  starting transfers between devices  23.6 us (35%)
  Pallas kernels  9.88 us (15%)
  local copies, waits for them, and re-layouts  5.24 us (8%)
  between operations  0.85 us (1%)
    ppermute x9, starting transfers between devices, send(): return lax.ppermute(block, axis, pairs)  15.1 us
    ppermute x9, waiting for transfers between devices, send(): return lax.ppermute(block, axis, pairs)  11.9 us
    pallas_call x9, Pallas kernels, on_chip(): pl.pallas_call(kernel, out_shape=outs, in_specs=[spec] * len(args), out_s...  7.64 us
    ppermute x2, waiting for transfers between devices, shot_terms(): return (block, lax.ppermute(block, 'shot', swap))  7.52 us
    unnamed x20, local copies, waits for them, and re-layouts  5.03 us
    ppermute x3, starting transfers between devices, depth_max(): lax.ppermute(value, 'depth', [(i, i ^ k) for i in range(depth_count)])  4.39 us
    ppermute x3, waiting for transfers between devices, depth_max(): lax.ppermute(value, 'depth', [(i, i ^ k) for i in range(depth_count)])  3.77 us
    ppermute x1, starting transfers between devices, depth_max(): value = jnp.maximum(value, lax.ppermute(value, 'depth', pairs))  2.9 us
  transfers between devices with their start and end apart: 17, of which 9 were waited for; matrix products, arithmetic and copies ran while one was open for 1% of the time, Pallas kernels for 9%

profile of v3, /device:TPU:0, one launch (start us, length us, event | category | flops | bytes accessed | tf_op | source)
XLA Modules:
  0.0 67.1 jit_solution(12289260624198257682)
XLA Ops:
  0.6 3.0 %collective-permute-start.3 = (f32[2,64,64]{2,1,0:T(8,128)}, f32[2,64,64]{2,1,0:T(8,128)S(1)}, u32[]{:S(2)}, u32[]{:S(2)}) collective-permute-start(f32[2,64,64]{2,1,0:T(8,128)} %velocity.1), channel_id=1, source_target_pairs={{0,2},{2,0},{1,3},{3,1},{4,6},{6,4},{5,7},{7,5},{8,10},{10,8},{9,1... | collective-permute-start | bytes 98312 | tf_op jit(solution)/shard_map/ppermute | solution.py:34
  3.7 0.0 copy-start.1
  3.7 0.9 %copy-done.1 = f32[2,2,64,128]{3,2,1,0:T(8,128)S(1)} copy-done((f32[2,2,64,128]{3,2,1,0:T(8,128)S(1)}, f32[2,2,64,128]{3,2,1,0:T(8,128)}, u32[]{:S(2)}) %copy-start.1) | copy-done | bytes 131096
  4.6 0.0 copy-start.2
  4.6 0.9 %copy-done.2 = f32[2,2,64,128]{3,2,1,0:T(8,128)S(1)} copy-done((f32[2,2,64,128]{3,2,1,0:T(8,128)S(1)}, f32[2,2,64,128]{3,2,1,0:T(8,128)}, u32[]{:S(2)}) %copy-start.2) | copy-done | bytes 131096
  5.5 0.0 copy-start.3
  5.5 0.9 %copy-done.3 = f32[2,2,64,128]{3,2,1,0:T(8,128)S(1)} copy-done((f32[2,2,64,128]{3,2,1,0:T(8,128)S(1)}, f32[2,2,64,128]{3,2,1,0:T(8,128)}, u32[]{:S(2)}) %copy-start.3) | copy-done | bytes 131096
  6.4 0.0 copy-start.4
  6.4 0.9 %copy-done.4 = f32[2,2,64,128]{3,2,1,0:T(8,128)S(1)} copy-done((f32[2,2,64,128]{3,2,1,0:T(8,128)S(1)}, f32[2,2,64,128]{3,2,1,0:T(8,128)}, u32[]{:S(2)}) %copy-start.4) | copy-done | bytes 131096
  7.3 0.8 %copy-done.5 = f32[2,64,128]{2,1,0:T(8,128)S(1)} copy-done((f32[2,64,128]{2,1,0:T(8,128)S(1)}, f32[2,64,128]{2,1,0:T(8,128)}, u32[]{:S(2)}) %copy-start.5) | copy-done | bytes 65560
  8.1 0.9 %pack.1 = (f32[16,64,128]{2,1,0:T(8,128)S(1)}, f32[16,64,128]{2,1,0:T(8,128)S(1)}, f32[2,3,64,128]{3,2,1,0:T(8,128)S(1)}, f32[2,2,64,128]{3,2,1,0:T(8,128)S(1)}) custom-call(f32[2,2,64,128]{3,2,1,0:T(8,128)S(1)} %copy-done.1, f32[2,2,64,128]{3,2,1,0:T(8,128)S(1)} %copy-done.2, f32[2,2,64,128]{3,2,1,0:T(8,128)S(1)} %copy-done.3, f32[2,64,128]{2,1,0:T(8,128)S(1)} %copy-done.5, ...), custom_call_target="tpu_custom_call" | custom-call | tf_op jit(solution)/shard_map/pack/pallas_call | solution.py:477
  9.0 0.0 copy-start.8
  9.0 0.0 copy-start
  9.0 2.7 %collective-permute-start.2 = (f32[3,64,128]{2,1,0:T(8,128)S(1)}, f32[3,64,128]{2,1,0:T(8,128)S(1)}, u32[]{:S(2)}, u32[]{:S(2)}) collective-permute-start(f32[3,64,128]{2,1,0:T(8,128)S(1)} %slice_bitcast_fusion), channel_id=1, source_target_pairs={{0,8},{4,12},{8,0},{12,4},{1,9},{5,13},{9,1},{13,5},{2,10},{6,14},... | collective-permute-start | bytes 294920 | tf_op jit(solution)/shard_map/ppermute | solution.py:34
  11.7 0.7 %collective-permute-start.1 = (f32[16,64,128]{2,1,0:T(8,128)S(1)}, f32[16,64,128]{2,1,0:T(8,128)S(1)}, u32[]{:S(2)}, u32[]{:S(2)}) collective-permute-start(f32[16,64,128]{2,1,0:T(8,128)S(1)} %get-tuple-element.27), channel_id=1, source_target_pairs={{4,8},{8,4},{5,9},{9,5},{6,10},{10,6},{7,11},{11,7},{20,24},{24,20... | collective-permute-start | bytes 1572872 | tf_op jit(solution)/shard_map/ppermute | solution.py:34
  12.4 2.9 %collective-permute-start = (f32[16,64,128]{2,1,0:T(8,128)S(1)}, f32[16,64,128]{2,1,0:T(8,128)S(1)}, u32[]{:S(2)}, u32[]{:S(2)}) collective-permute-start(f32[16,64,128]{2,1,0:T(8,128)S(1)} %get-tuple-element.25.refs_0_.own), channel_id=1, source_target_pairs={{0,4},{4,0},{8,12},{12,8},{1,5},{5,1},{9,13},{13,9},{2,6},{6,2},{1... | collective-permute-start | bytes 1572872 | tf_op jit(solution)/shard_map/ppermute | solution.py:34
  15.2 0.0 copy-done.8
  15.2 0.1 and_select_fusion
  15.4 0.0 collective-permute-done.3
  15.4 0.0 copy-done
  15.4 0.1 maximum_select_fusion.refs_6_.vel
  15.5 0.0 copy-start.9
  15.5 0.7 collective-permute-start.5
  16.2 3.4 %collective-permute-start.4 = (f32[2,64,128]{2,1,0:T(8,128)S(1)}, f32[2,64,128]{2,1,0:T(8,128)S(1)}, u32[]{:S(2)}, u32[]{:S(2)}) collective-permute-start(f32[2,64,128]{2,1,0:T(8,128)S(1)} %maximum_select_fusion.refs_6_.vel), channel_id=1, source_target_pairs={{0,4},{4,0},{8,12},{12,8},{1,5},{5,1},{9,13},{13,9},{2,6},{6,2},{1... | collective-permute-start | bytes 196616 | tf_op jit(solution)/shard_map/ppermute | solution.py:34
  19.6 0.0 copy-done.9
  19.6 0.1 copy.12
  19.7 0.1 copy.13
  19.8 0.0 collective-permute-done.5.refs_8_.vel_odd
  19.8 9.0 %collective-permute-done.4.refs_7_.vel_even = f32[2,64,128]{2,1,0:T(8,128)S(1)} collective-permute-done((f32[2,64,128]{2,1,0:T(8,128)S(1)}, f32[2,64,128]{2,1,0:T(8,128)S(1)}, u32[]{:S(2)}, u32[]{:S(2)}) %collective-permute-start.4) | collective-permute-done | bytes 65568 | tf_op jit(solution)/shard_map/ppermute | solution.py:34
  28.7 0.0 collective-permute-done.2.refs_4_.far_first
  28.7 0.0 collective-permute-done.1.refs_3_.near_odd
  28.7 0.0 collective-permute-done.refs_2_.near_even
  28.8 0.0 copy-start.7
  28.8 0.1 collective-permute-start.6
  28.9 0.1 pad_add_fusion.source_at
  29.0 0.5 copy-done.7
  29.5 4.9 %shard_map.114.dense = f32[2,3,320,128]{3,2,1,0:T(8,128)S(1)} custom-call(s32[2,2048]{1,0:T(2,128)S(1)} %get-tuple-element.30.row_ref, s32[2,2048]{1,0:T(2,128)S(1)} %get-tuple-element.48.col_ref, f32[2,2,2048]{2,1,0:T(2,128)S(1)} %copy-done.7), custom_call_target="tpu_custom_call" | custom-call | flops 2348810240 | bytes 65536 | tf_op jit(solution)/shard_map/pallas_call | solution.py:42
  34.4 0.0 collective-permute-done.6.edges
  34.4 0.0 copy-done.6
  34.4 1.4 %prepare.1 = (f32[2,6,80,128]{3,2,1,0:T(8,128)S(1)}, f32[2,6,80,128]{3,2,1,0:T(8,128)S(1)}, f32[2,4,80,128]{3,2,1,0:T(8,128)S(1)}, f32[2,4,80,128]{3,2,1,0:T(8,1...) custom-call(f32[16,64,128]{2,1,0:T(8,128)S(1)} %get-tuple-element.25, ...), custom_call_target="tpu_custom_call" | custom-call | tf_op jit(solution)/shard_map/prepare/pallas_call | solution.py:547
  35.8 0.8 %shard_map.115.mine = f32[2,64,128]{2,1,0:T(8,128)S(1)} custom-call(f32[6,80,128]{2,1,0:T(8,128)S(1)} %get-tuple-element.31.stiff, f32[2,6,80,128]{3,2,1,0:T(8,128)S(1)} %get-tuple-element.32.lap, f32[2,6,80,128]{3,2,1,0:T(8,128)S(1)} %get-tuple-element.33.base, f32[2,4,80,128]{3,2,1,0:T(8,128)S(1)} %get-tuple-element.34.turn, ...), custom_call_target="tpu_custom_call" | custom-call | bytes 4546560 | tf_op jit(solution)/shard_map/pallas_call | solution.py:42
  36.6 0.6 collective-permute-start.7
  37.2 3.8 %collective-permute-done.7.other = f32[2,64,128]{2,1,0:T(8,128)S(1)} collective-permute-done((f32[2,64,128]{2,1,0:T(8,128)S(1)}, f32[2,64,128]{2,1,0:T(8,128)S(1)}, u32[]{:S(2)}, u32[]{:S(2)}) %collective-permute-start.7) | collective-permute-done | bytes 65568 | tf_op jit(solution)/shard_map/ppermute | solution.py:440
  41.0 0.1 collective-permute-start.8
  41.1 1.2 %collective-permute-done.8.got = f32[24,128]{1,0:T(8,128)S(1)} collective-permute-done((f32[24,128]{1,0:T(8,128)S(1)}, f32[24,128]{1,0:T(8,128)S(1)}, u32[]{:S(2)}, u32[]{:S(2)}) %collective-permute-start.8) | collective-permute-done | bytes 12320 | tf_op jit(solution)/shard_map/ppermute | solution.py:598
  42.2 1.1 %collective-permute-start.9 = (f32[168,128]{1,0:T(8,128)S(1)}, f32[168,128]{1,0:T(8,128)S(1)}, u32[]{:S(2)}, u32[]{:S(2)}) collective-permute-start(f32[168,128]{1,0:T(8,128)S(1)} %shard_map.117.mine), channel_id=1, source_target_pairs={{0,4},{4,0},{8,12},{12,8},{1,5},{5,1},{9,13},{13,9},{2,6},{6,2},{1... | collective-permute-start | bytes 258056 | tf_op jit(solution)/shard_map/ppermute | solution.py:34
  43.3 0.7 collective-permute-start.10
  44.0 2.9 %collective-permute-done.9.by_even = f32[168,128]{1,0:T(8,128)S(1)} collective-permute-done((f32[168,128]{1,0:T(8,128)S(1)}, f32[168,128]{1,0:T(8,128)S(1)}, u32[]{:S(2)}, u32[]{:S(2)}) %collective-permute-start.9) | collective-permute-done | bytes 86048 | tf_op jit(solution)/shard_map/ppermute | solution.py:34
  46.9 2.9 %collective-permute-start.11 = (f32[8,128]{1,0:T(8,128)S(1)}, f32[8,128]{1,0:T(8,128)S(1)}, u32[]{:S(2)}, u32[]{:S(2)}) collective-permute-start(f32[8,128]{1,0:T(8,128)S(1)} %slice_maximum_fusion), channel_id=1, source_target_pairs={{0,8},{4,12},{8,0},{12,4},{1,9},{5,13},{9,1},{13,5},{2,10},{6,14},... | collective-permute-start | bytes 12296 | tf_op jit(solution)/shard_map/ppermute | solution.py:460
  49.8 1.6 %collective-permute-done.11 = f32[8,128]{1,0:T(8,128)S(1)} collective-permute-done((f32[8,128]{1,0:T(8,128)S(1)}, f32[8,128]{1,0:T(8,128)S(1)}, u32[]{:S(2)}, u32[]{:S(2)}) %collective-permute-start.11) | collective-permute-done | bytes 4128 | tf_op jit(solution)/shard_map/ppermute | solution.py:460
  51.4 0.0 collective-permute-done.10.by_odd
  51.4 0.2 shard_map.118
  51.6 0.8 %shard_map.119.mine = f32[2,64,128]{2,1,0:T(8,128)S(1)} custom-call(f32[6,80,128]{2,1,0:T(8,128)S(1)} %get-tuple-element.44.stiff, f32[2,6,80,128]{3,2,1,0:T(8,128)S(1)} %get-tuple-element.32.lap, f32[2,6,80,128]{3,2,1,0:T(8,128)S(1)} %get-tuple-element.33.base, f32[2,4,80,128]{3,2,1,0:T(8,128)S(1)} %get-tuple-element.34.turn, ...), custom_call_target="tpu_custom_call" | custom-call | bytes 4546560 | tf_op jit(solution)/shard_map/pallas_call | solution.py:42
  52.5 0.6 collective-permute-start.12
  53.1 3.8 %collective-permute-done.12.other = f32[2,64,128]{2,1,0:T(8,128)S(1)} collective-permute-done((f32[2,64,128]{2,1,0:T(8,128)S(1)}, f32[2,64,128]{2,1,0:T(8,128)S(1)}, u32[]{:S(2)}, u32[]{:S(2)}) %collective-permute-start.12) | collective-permute-done | bytes 65568 | tf_op jit(solution)/shard_map/ppermute | solution.py:440
  56.8 0.1 collective-permute-start.13
  56.9 1.2 %collective-permute-done.13 = f32[8,128]{1,0:T(8,128)S(1)} collective-permute-done((f32[8,128]{1,0:T(8,128)S(1)}, f32[8,128]{1,0:T(8,128)S(1)}, u32[]{:S(2)}, u32[]{:S(2)}) %collective-permute-start.13) | collective-permute-done | bytes 4128 | tf_op jit(solution)/shard_map/ppermute | solution.py:586
  58.1 3.6 %collective-permute-start.16 = (f32[8,128]{1,0:T(8,128)S(1)}, f32[8,128]{1,0:T(8,128)S(1)}, u32[]{:S(2)}, u32[]{:S(2)}) collective-permute-start(f32[8,128]{1,0:T(8,128)S(1)} %max.20), channel_id=1, source_target_pairs={{0,12},{4,8},{8,4},{12,0},{1,13},{5,9},{9,5},{13,1},{2,14},{6,10},... | collective-permute-start | bytes 12296 | tf_op jit(solution)/shard_map/ppermute | solution.py:449
  61.7 0.0 collective-permute-start.15
  61.7 0.7 %collective-permute-start.14 = (f32[8,128]{1,0:T(8,128)S(1)}, f32[8,128]{1,0:T(8,128)S(1)}, u32[]{:S(2)}, u32[]{:S(2)}) collective-permute-start(f32[8,128]{1,0:T(8,128)S(1)} %max.20), channel_id=1, source_target_pairs={{0,4},{4,0},{8,12},{12,8},{1,5},{5,1},{9,13},{13,9},{2,6},{6,2},{1... | collective-permute-start | bytes 12296 | tf_op jit(solution)/shard_map/ppermute | solution.py:449
  62.4 1.0 %collective-permute-done.16 = f32[8,128]{1,0:T(8,128)S(1)} collective-permute-done((f32[8,128]{1,0:T(8,128)S(1)}, f32[8,128]{1,0:T(8,128)S(1)}, u32[]{:S(2)}, u32[]{:S(2)}) %collective-permute-start.16) | collective-permute-done | bytes 4128 | tf_op jit(solution)/shard_map/ppermute | solution.py:449
  63.5 2.7 %collective-permute-done.15 = f32[8,128]{1,0:T(8,128)S(1)} collective-permute-done((f32[8,128]{1,0:T(8,128)S(1)}, f32[8,128]{1,0:T(8,128)S(1)}, u32[]{:S(2)}, u32[]{:S(2)}) %collective-permute-start.15) | collective-permute-done | bytes 4128 | tf_op jit(solution)/shard_map/ppermute | solution.py:449
  66.2 0.0 collective-permute-done.14
  66.2 0.8 %shard_map.121 = (f32[2,64,64]{2,1,0:T(8,128)}, f32[2,64,64]{2,1,0:T(8,128)}) custom-call(f32[2,64,128]{2,1,0:T(8,128)S(1)} %get-tuple-element.45.total, f32[8,128]{1,0:T(8,128)S(1)} %maximum_maximum_fusion.largest, f32[2,64,64]{2,1,0:T(8,128)S(1)} %get-tuple-element.47.velocity), custom_call_target="tpu_custom_call" | custom-call | bytes 102400 | tf_op jit(solution)/shard_map/pallas_call | solution.py:42
  (14 shorter events, 0.1 us)
Async XLA Ops:
  0.6 14.8 %collective-permute-start.3 = (f32[2,64,64]{2,1,0:T(8,128)}, f32[2,64,64]{2,1,0:T(8,128)S(1)}, u32[]{:S(2)}, u32[]{:S(2)}) collective-permute-start(f32[2,64,64]{2,1,0:T(8,128)} %velocity.1), channel_id=1, source_target_pairs={{0,2},{2,0},{1,3},{3,1},{4,6},{6,4},{5,7},{7,5},{8,10},{10,8},{9,1... | collective-permute-start | bytes 98312 | tf_op jit(solution)/shard_map/ppermute | solution.py:34
  3.7 0.9 %copy-start.1 = (f32[2,2,64,128]{3,2,1,0:T(8,128)S(1)}, f32[2,2,64,128]{3,2,1,0:T(8,128)}, u32[]{:S(2)}) copy-start(f32[2,2,64,128]{3,2,1,0:T(8,128)} %now.1) | copy-start | bytes 393220
  4.6 0.9 %copy-start.2 = (f32[2,2,64,128]{3,2,1,0:T(8,128)S(1)}, f32[2,2,64,128]{3,2,1,0:T(8,128)}, u32[]{:S(2)}) copy-start(f32[2,2,64,128]{3,2,1,0:T(8,128)} %prev.1) | copy-start | bytes 393220
  5.5 0.9 %copy-start.3 = (f32[2,2,64,128]{3,2,1,0:T(8,128)S(1)}, f32[2,2,64,128]{3,2,1,0:T(8,128)}, u32[]{:S(2)}) copy-start(f32[2,2,64,128]{3,2,1,0:T(8,128)} %last.1) | copy-start | bytes 393220
  6.4 0.9 %copy-start.4 = (f32[2,2,64,128]{3,2,1,0:T(8,128)S(1)}, f32[2,2,64,128]{3,2,1,0:T(8,128)}, u32[]{:S(2)}) copy-start(f32[2,2,64,128]{3,2,1,0:T(8,128)} %late.1) | copy-start | bytes 393220
  7.3 0.8 %copy-start.5 = (f32[2,64,128]{2,1,0:T(8,128)S(1)}, f32[2,64,128]{2,1,0:T(8,128)}, u32[]{:S(2)}) copy-start(f32[2,64,128]{2,1,0:T(8,128)} %dens.1) | copy-start | bytes 196612
  9.0 6.3 %copy-start.8 = (s32[2,2048]{1,0:T(2,128)S(1)}, s32[2,2048]{1,0:T(2,128)}, u32[]{:S(2)}) copy-start(s32[2,2048]{1,0:T(2,128)} %param.18) | copy-start | bytes 49156
  9.0 6.4 %copy-start = (f32[2,64,64]{2,1,0:T(8,128)S(1)}, f32[2,64,64]{2,1,0:T(8,128)}, u32[]{:S(2)}) copy-start(f32[2,64,64]{2,1,0:T(8,128)} %velocity.1) | copy-start | bytes 98308
  9.0 19.7 %collective-permute-start.2 = (f32[3,64,128]{2,1,0:T(8,128)S(1)}, f32[3,64,128]{2,1,0:T(8,128)S(1)}, u32[]{:S(2)}, u32[]{:S(2)}) collective-permute-start(f32[3,64,128]{2,1,0:T(8,128)S(1)} %slice_bitcast_fusion), channel_id=1, source_target_pairs={{0,8},{4,12},{8,0},{12,4},{1,9},{5,13},{9,1},{13,5},{2,10},{6,14},... | collective-permute-start | bytes 294920 | tf_op jit(solution)/shard_map/ppermute | solution.py:34
  11.7 17.1 %collective-permute-start.1 = (f32[16,64,128]{2,1,0:T(8,128)S(1)}, f32[16,64,128]{2,1,0:T(8,128)S(1)}, u32[]{:S(2)}, u32[]{:S(2)}) collective-permute-start(f32[16,64,128]{2,1,0:T(8,128)S(1)} %get-tuple-element.27), channel_id=1, source_target_pairs={{4,8},{8,4},{5,9},{9,5},{6,10},{10,6},{7,11},{11,7},{20,24},{24,20... | collective-permute-start | bytes 1572872 | tf_op jit(solution)/shard_map/ppermute | solution.py:34
  12.4 16.4 %collective-permute-start = (f32[16,64,128]{2,1,0:T(8,128)S(1)}, f32[16,64,128]{2,1,0:T(8,128)S(1)}, u32[]{:S(2)}, u32[]{:S(2)}) collective-permute-start(f32[16,64,128]{2,1,0:T(8,128)S(1)} %get-tuple-element.25.refs_0_.own), channel_id=1, source_target_pairs={{0,4},{4,0},{8,12},{12,8},{1,5},{5,1},{9,13},{13,9},{2,6},{6,2},{1... | collective-permute-start | bytes 1572872 | tf_op jit(solution)/shard_map/ppermute | solution.py:34
  15.5 4.0 %copy-start.9 = (s32[2]{0:T(128)S(1)}, s32[2]{0:T(128)}, u32[]{:S(2)}) copy-start(s32[2]{0:T(128)} %param.17) | copy-start | bytes 28
  15.5 4.2 %collective-permute-start.5 = (f32[2,64,128]{2,1,0:T(8,128)S(1)}, f32[2,64,128]{2,1,0:T(8,128)S(1)}, u32[]{:S(2)}, u32[]{:S(2)}) collective-permute-start(f32[2,64,128]{2,1,0:T(8,128)S(1)} %maximum_select_fusion.refs_6_.vel), channel_id=1, source_target_pairs={{4,8},{8,4},{5,9},{9,5},{6,10},{10,6},{7,11},{11,7},{20,24},{24,20... | collective-permute-start | bytes 196616 | tf_op jit(solution)/shard_map/ppermute | solution.py:34
  16.2 12.5 %collective-permute-start.4 = (f32[2,64,128]{2,1,0:T(8,128)S(1)}, f32[2,64,128]{2,1,0:T(8,128)S(1)}, u32[]{:S(2)}, u32[]{:S(2)}) collective-permute-start(f32[2,64,128]{2,1,0:T(8,128)S(1)} %maximum_select_fusion.refs_6_.vel), channel_id=1, source_target_pairs={{0,4},{4,0},{8,12},{12,8},{1,5},{5,1},{9,13},{13,9},{2,6},{6,2},{1... | collective-permute-start | bytes 196616 | tf_op jit(solution)/shard_map/ppermute | solution.py:34
  28.8 0.8 %copy-start.7 = (f32[2,2,2048]{2,1,0:T(2,128)S(1)}, f32[2,2,2048]{2,1,0:T(2,128)}, u32[]{:S(2)}) copy-start(f32[2,2,2048]{2,1,0:T(2,128)} %obs_ref.1) | copy-start | bytes 98308
  28.8 5.6 %collective-permute-start.6 = (f32[496,128]{1,0:T(8,128)S(1)}, f32[496,128]{1,0:T(8,128)S(1)}, u32[]{:S(2)}, u32[]{:S(2)}) collective-permute-start(f32[496,128]{1,0:T(8,128)S(1)} %shard_map.113), channel_id=1, source_target_pairs={{0,1},{1,0},{2,3},{3,2},{4,5},{5,4},{6,7},{7,6},{8,9},{9,8},{10,11... | collective-permute-start | bytes 761864 | tf_op jit(solution)/shard_map/ppermute | solution.py:34
  29.5 4.9 %copy-start.6 = (f32[2,2]{1,0:T(2,128)S(1)}, f32[2,2]{1,0:T(2,128)}, u32[]{:S(2)}) copy-start(f32[2,2]{1,0:T(2,128)} %wavelet.1) | copy-start | bytes 52
  36.6 4.3 %collective-permute-start.7 = (f32[2,64,128]{2,1,0:T(8,128)S(1)}, f32[2,64,128]{2,1,0:T(8,128)S(1)}, u32[]{:S(2)}, u32[]{:S(2)}) collective-permute-start(f32[2,64,128]{2,1,0:T(8,128)S(1)} %shard_map.115.mine), channel_id=1, source_target_pairs={{0,2},{2,0},{1,3},{3,1},{4,6},{6,4},{5,7},{7,5},{8,10},{10,8},{9,1... | collective-permute-start | bytes 196616 | tf_op jit(solution)/shard_map/ppermute | solution.py:440
  41.0 1.2 %collective-permute-start.8 = (f32[24,128]{1,0:T(8,128)S(1)}, f32[24,128]{1,0:T(8,128)S(1)}, u32[]{:S(2)}, u32[]{:S(2)}) collective-permute-start(f32[24,128]{1,0:T(8,128)S(1)} %get-tuple-element.43.mine), channel_id=1, source_target_pairs={{0,1},{1,0},{2,3},{3,2},{4,5},{5,4},{6,7},{7,6},{8,9},{9,8},{10,11... | collective-permute-start | bytes 36872 | tf_op jit(solution)/shard_map/ppermute | solution.py:598
  42.2 4.7 %collective-permute-start.9 = (f32[168,128]{1,0:T(8,128)S(1)}, f32[168,128]{1,0:T(8,128)S(1)}, u32[]{:S(2)}, u32[]{:S(2)}) collective-permute-start(f32[168,128]{1,0:T(8,128)S(1)} %shard_map.117.mine), channel_id=1, source_target_pairs={{0,4},{4,0},{8,12},{12,8},{1,5},{5,1},{9,13},{13,9},{2,6},{6,2},{1... | collective-permute-start | bytes 258056 | tf_op jit(solution)/shard_map/ppermute | solution.py:34
  43.3 8.1 %collective-permute-start.10 = (f32[160,128]{1,0:T(8,128)S(1)}, f32[160,128]{1,0:T(8,128)S(1)}, u32[]{:S(2)}, u32[]{:S(2)}) collective-permute-start(f32[160,128]{1,0:T(8,128)S(1)} %slice.16), channel_id=1, source_target_pairs={{4,8},{8,4},{5,9},{9,5},{6,10},{10,6},{7,11},{11,7},{20,24},{24,20... | collective-permute-start | bytes 245768 | tf_op jit(solution)/shard_map/ppermute | solution.py:34
  46.9 4.5 %collective-permute-start.11 = (f32[8,128]{1,0:T(8,128)S(1)}, f32[8,128]{1,0:T(8,128)S(1)}, u32[]{:S(2)}, u32[]{:S(2)}) collective-permute-start(f32[8,128]{1,0:T(8,128)S(1)} %slice_maximum_fusion), channel_id=1, source_target_pairs={{0,8},{4,12},{8,0},{12,4},{1,9},{5,13},{9,1},{13,5},{2,10},{6,14},... | collective-permute-start | bytes 12296 | tf_op jit(solution)/shard_map/ppermute | solution.py:460
  52.5 4.3 %collective-permute-start.12 = (f32[2,64,128]{2,1,0:T(8,128)S(1)}, f32[2,64,128]{2,1,0:T(8,128)S(1)}, u32[]{:S(2)}, u32[]{:S(2)}) collective-permute-start(f32[2,64,128]{2,1,0:T(8,128)S(1)} %shard_map.119.mine), channel_id=1, source_target_pairs={{0,2},{2,0},{1,3},{3,1},{4,6},{6,4},{5,7},{7,5},{8,10},{10,8},{9,1... | collective-permute-start | bytes 196616 | tf_op jit(solution)/shard_map/ppermute | solution.py:440
  56.8 1.2 %collective-permute-start.13 = (f32[8,128]{1,0:T(8,128)S(1)}, f32[8,128]{1,0:T(8,128)S(1)}, u32[]{:S(2)}, u32[]{:S(2)}) collective-permute-start(f32[8,128]{1,0:T(8,128)S(1)} %get-tuple-element.46), channel_id=1, source_target_pairs={{0,1},{1,0},{2,3},{3,2},{4,5},{5,4},{6,7},{7,6},{8,9},{9,8},{10,11... | collective-permute-start | bytes 12296 | tf_op jit(solution)/shard_map/ppermute | solution.py:586
  58.1 5.4 %collective-permute-start.16 = (f32[8,128]{1,0:T(8,128)S(1)}, f32[8,128]{1,0:T(8,128)S(1)}, u32[]{:S(2)}, u32[]{:S(2)}) collective-permute-start(f32[8,128]{1,0:T(8,128)S(1)} %max.20), channel_id=1, source_target_pairs={{0,12},{4,8},{8,4},{12,0},{1,13},{5,9},{9,5},{13,1},{2,14},{6,10},... | collective-permute-start | bytes 12296 | tf_op jit(solution)/shard_map/ppermute | solution.py:449
  61.7 4.5 %collective-permute-start.15 = (f32[8,128]{1,0:T(8,128)S(1)}, f32[8,128]{1,0:T(8,128)S(1)}, u32[]{:S(2)}, u32[]{:S(2)}) collective-permute-start(f32[8,128]{1,0:T(8,128)S(1)} %max.20), channel_id=1, source_target_pairs={{0,8},{4,12},{8,0},{12,4},{1,9},{5,13},{9,1},{13,5},{2,10},{6,14},... | collective-permute-start | bytes 12296 | tf_op jit(solution)/shard_map/ppermute | solution.py:449
  61.7 4.5 %collective-permute-start.14 = (f32[8,128]{1,0:T(8,128)S(1)}, f32[8,128]{1,0:T(8,128)S(1)}, u32[]{:S(2)}, u32[]{:S(2)}) collective-permute-start(f32[8,128]{1,0:T(8,128)S(1)} %max.20), channel_id=1, source_target_pairs={{0,4},{4,0},{8,12},{12,8},{1,5},{5,1},{9,13},{13,9},{2,6},{6,2},{1... | collective-permute-start | bytes 12296 | tf_op jit(solution)/shard_map/ppermute | solution.py:449

commit v4 on v3

--- a/solution.py
+++ b/solution.py
@@ -12,6 +12,7 @@
 STEP_SIZE = 0.1
 EPSILON = 1e-06
 PAD = 8
+NOW, PREV, LAST, LATE, DENS, VEL, LAP = range(7)
 
 
 def even_pairs(count):
@@ -20,11 +21,6 @@
 
 def odd_pairs(count):
     ups = [(i, i + 1) for i in range(1, count - 1, 2)]
-    return ups + [(b, a) for a, b in ups]
-
-
-def two_pairs(count, first):
-    ups = [(i, i + 2) for i in range(count - 2) if (i % 4 < 2) == first]
     return ups + [(b, a) for a, b in ups]
 
 
@@ -50,20 +46,7 @@
     )(*[pltpu.with_memory_space_constraint(a, pltpu.VMEM) for a in args])
 
 
-def pack_kernel(now, prev, last, dens, late, to_even, to_odd, to_far, late_out, sems):
-    depth_at = lax.axis_index("depth")
-    even = depth_at % 2 == 0
-    front = depth_at % 4 < 2
-    shots, planes, _, _ = now.shape
-    copies = []
-    start = 0
-    for field in (now, prev, last):
-        for shot in range(shots):
-            copies.append((field.at[shot], to_even.at[start : start + planes]))
-            start += planes
-    copies.append((dens, to_even.at[start : start + planes]))
-    start += planes
-    copies.append((late, late_out))
+def copy_all(copies, sems):
     copies = [
         pltpu.make_async_copy(source, target, sems.at[index])
         for index, (source, target) in enumerate(copies)
@@ -72,17 +55,37 @@
         copy.start()
     for copy in copies:
         copy.wait()
-    to_odd[:start] = to_even[:start]
-    for shot in range(shots):
-        low, top = late_out[shot, 0], late_out[shot, planes - 1]
-        to_even[start + shot] = jnp.where(even, top, low)
-        to_odd[start + shot] = jnp.where(even, low, top)
-        low, top = to_even[shot * planes], to_even[shot * planes + planes - 1]
-        to_far[0, shot] = jnp.where(front, top, low)
-        to_far[1, shot] = jnp.where(front, low, top)
-    low, top = to_even[start - planes], to_even[start - 1]
-    to_far[0, shots] = jnp.where(front, top, low)
-    to_far[1, shots] = jnp.where(front, low, top)
+
+
+def first_kernel(now, dens, vel, out, edges, vel_buf, sems):
+    shots, planes, rows, cols = now.shape
+    count = shots * planes
+    copies = [
+        (now.at[shot], out.at[shot * planes : (shot + 1) * planes]) for shot in range(shots)
+    ]
+    copies += [(dens, out.at[count : count + planes]), (vel, vel_buf)]
+    copy_all(copies, sems)
+    lines = [vel_buf[at] for at in range(planes)]
+    spare = cols - planes * vel.shape[2]
+    if spare:
+        lines.append(jnp.zeros((rows, spare), jnp.float32))
+    out[count + planes] = jnp.concatenate(lines, axis=1)
+    first = lax.axis_index("lat") == 0
+    for at in range(count + planes):
+        edges[at * PAD : (at + 1) * PAD] = jnp.where(
+            first, out[at, rows - PAD :], out[at, :PAD]
+        )
+
+
+def second_kernel(prev, last, late, out, late_out, sems):
+    shots, planes, _, _ = prev.shape
+    copies = []
+    start = 0
+    for field in (prev, last):
+        for shot in range(shots):
+            copies.append((field.at[shot], out.at[start : start + planes]))
+            start += planes
+    copy_all(copies + [(late, late_out)], sems)
 
 
 def spread_kernel(row_ref, col_ref, obs_ref, out_ref):
@@ -119,19 +122,15 @@
 
 
 class Halo:
-    def __init__(self, own, late, near_even, near_odd, far_first, far_second, vel_own, vel_even, vel_odd):
-        depth_at = lax.axis_index("depth")
-        self.even = depth_at % 2 == 0
-        self.front = depth_at % 4 < 2
-        self.own, self.late = own, late
-        self.near = (near_even, near_odd)
-        self.far = (far_first, far_second)
-        self.vel = (vel_own, vel_even, vel_odd)
+    def __init__(self, first, second, late, first_by, second_by, third_by, vel):
+        self.even = lax.axis_index("depth") % 2 == 0
+        self.first, self.second, self.late, self.vel = first, second, late, vel
+        self.first_by, self.second_by, self.third_by = first_by, second_by, third_by
         self.shots, self.planes, self.rows, self.cols = late.shape
 
-    def pick(self, pair, flag, upper, index):
-        first, second = pair if upper else pair[::-1]
-        return jnp.where(flag, first[index], second[index])
+    def pick(self, pair, upper, index):
+        a, b = pair if upper else pair[::-1]
+        return jnp.where(self.even, a[index], b[index])
 
     def plane(self, item):
         which, shot, at = item
@@ -139,35 +138,40 @@
         inside = 0 <= at < planes
         upper = at >= planes
         step = at if inside else (at - planes if upper else planes + at)
-        if which == 5:
-            if inside:
-                return self.vel[0][at]
-            return self.pick(self.vel[1:], self.even, upper, step)
-        if which == 4:
-            if inside:
-                return self.late[shot, at]
-            return self.pick(self.near, self.even, upper, (3 * shots + 1) * planes + shot)
-        if 0 <= step < planes:
-            index = (which * shots + shot) * planes + step
-            return self.own[index] if inside else self.pick(self.near, self.even, upper, index)
-        return self.pick(self.far, self.front, upper, shots if which == 3 else shot)
+        if which == VEL:
+            return self.vel[at + 2]
+        if which == LAP:
+            return self.pick(self.third_by, upper, shots + shot)
+        if which == LATE:
+            return self.late[shot, at] if inside else self.pick(self.third_by, upper, shot)
+        if which in (NOW, DENS):
+            index = (shot if which == NOW else shots) * planes + step
+            return self.first[index] if inside else self.pick(self.first_by, upper, index)
+        index = ((0 if which == PREV else shots) + shot) * planes + step
+        return self.second[index] if inside else self.pick(self.second_by, upper, index)
 
     def plane_list(self):
+        planes = self.planes
         out = []
-        planes = self.planes
-        for which, margin in ((0, 3), (1, 2), (2, 2), (4, 1)):
+        for which, margin in ((NOW, 2), (PREV, 2), (LAST, 2), (LATE, 1)):
             for shot in range(self.shots):
                 for at in range(-margin, planes + margin):
                     out.append((which, shot, at))
-        for at in range(-3, planes + 3):
-            out.append((3, 0, at))
-        for at in range(-2, planes + 2):
-            out.append((5, 0, at))
+        for shot in range(self.shots):
+            out += [(LAP, shot, -2), (LAP, shot, planes + 1)]
+        for which in (DENS, VEL):
+            for at in range(-2, planes + 2):
+                out.append((which, 0, at))
         return out
 
 
+def halo_of(refs):
+    first, second, late, fe, fo, se, so, te, to, vel = refs
+    return Halo(first, second, late, (fe, fo), (se, so), (te, to), vel)
+
+
 def edge_kernel(*refs):
-    halo = Halo(*refs[:-1])
+    halo = halo_of(refs[:-1])
     out = refs[-1]
     first = lax.axis_index("lat") == 0
     rows = halo.rows
@@ -194,16 +198,84 @@
     return total + (cz(at) * (field(at + 1) - middle) + cz(at - 1) * (field(at - 1) - middle))
 
 
+def inverse(density):
+    inside = density > 0.0
+    return jnp.where(inside, 1.0 / jnp.where(inside, density, 1.0), 0.0)
+
+
+def with_rows(part, value, lat_at):
+    low = jnp.where(lat_at == 1, part, 0.0)
+    high = jnp.where(lat_at == 0, part, 0.0)
+    return jnp.concatenate([low, value, high], axis=0)
+
+
+def couple(buoy, at, cz, cx, cp, cm):
+    plane = buoy(at)
+    cz(at, 0.5 * (plane + buoy(at + 1)))
+    cx(at, 0.5 * (plane + pltpu.roll(plane, plane.shape[0] - 1, 0)))
+    above, below = near_cols(plane)
+    cp(at, 0.5 * (plane + above))
+    cm(at, 0.5 * (plane + below))
+
+
+def third_kernel(first, by_even, by_odd, edges, late, to_even, to_odd, now_buf, buoy_buf, cz, cx, cp, cm):
+    even = lax.axis_index("depth") % 2 == 0
+    lat_at = lax.axis_index("lat")
+    shots, planes, rows, cols = late.shape
+
+    def whole(index, at):
+        if 0 <= at < planes:
+            place = index * planes + at
+            return with_rows(edges[place * PAD : (place + 1) * PAD], first[place], lat_at)
+        upper = at >= planes
+        a, b = (by_even, by_odd) if upper else (by_odd, by_even)
+        place = index * planes + (0 if upper else planes - 1)
+        empty = jnp.zeros((PAD, cols), jnp.float32)
+        return jnp.concatenate([empty, jnp.where(even, a[place], b[place]), empty], axis=0)
+
+    for at in range(-1, planes + 1):
+        buoy_buf[at + 1] = inverse(whole(shots, at))
+        for shot in range(shots):
+            now_buf[shot, at + 1] = whole(shot, at)
+
+    def put(ref):
+        def store(at, value):
+            ref[at + 1] = value
+
+        return store
+
+    for at in range(-1, planes):
+        couple(lambda k: buoy_buf[k + 1], at, put(cz), put(cx), put(cp), put(cm))
+    for shot in range(shots):
+        ends = [
+            laplace(
+                lambda k: now_buf[shot, k + 1],
+                at,
+                lambda k: cz[k + 1],
+                lambda k: cx[k + 1],
+                lambda k: cp[k + 1],
+                lambda k: cm[k + 1],
+            )[PAD : PAD + rows]
+            for at in (planes - 2, 1)
+        ]
+        low, top = late[shot, 0], late[shot, planes - 1]
+        to_even[shot] = jnp.where(even, top, low)
+        to_odd[shot] = jnp.where(even, low, top)
+        to_even[shots + shot] = jnp.where(even, ends[0], ends[1])
+        to_odd[shots + shot] = jnp.where(even, ends[1], ends[0])
+
+
 def prepare_kernel(
-    own,
+    first,
+    second,
     late,
-    near_even,
-    near_odd,
-    far_first,
-    far_second,
+    first_even,
+    first_odd,
+    second_even,
+    second_odd,
+    third_even,
+    third_odd,
     vel,
-    vel_even,
-    vel_odd,
     edges,
     dense,
     source_at,
@@ -215,67 +287,75 @@
     last_out,
     low_out,
     stiff_out,
-    cz_out,
-    cx_out,
-    cp_out,
-    cm_out,
+    cz,
+    cx,
+    cp,
+    cm,
     now_buf,
     buoy_buf,
 ):
-    halo = Halo(own, late, near_even, near_odd, far_first, far_second, vel, vel_even, vel_odd)
+    halo = Halo(
+        first,
+        second,
+        late,
+        (first_even, first_odd),
+        (second_even, second_odd),
+        (third_even, third_odd),
+        vel,
+    )
     lat_at = lax.axis_index("lat")
     rows, cols, shots, planes = halo.rows, halo.cols, halo.shots, halo.planes
     wide = rows + 2 * PAD
     where_is = {item: index for index, item in enumerate(halo.plane_list())}
 
-    def whole(item):
+    def whole(which, shot, at):
+        item = (which, shot, at)
         index = where_is[item]
-        part = edges[index * PAD : (index + 1) * PAD]
-        low = jnp.where(lat_at == 1, part, 0.0)
-        high = jnp.where(lat_at == 0, part, 0.0)
-        return jnp.concatenate([low, halo.plane(item), high], axis=0)
-
-    for at in range(-3, planes + 3):
-        density = whole((3, 0, at))
-        inside = density > 0.0
-        buoy_buf[at + 3] = jnp.where(inside, 1.0 / jnp.where(inside, density, 1.0), 0.0)
-        if -2 <= at < planes + 2:
-            speed = whole((5, 0, at)) * COURANT
-            stiff_out[at + 2] = speed * speed * density
+        return with_rows(edges[index * PAD : (index + 1) * PAD], halo.plane(item), lat_at)
+
+    for at in range(-2, planes + 2):
+        density = whole(DENS, 0, at)
+        buoy_buf[at + 2] = inverse(density)
+        speed = whole(VEL, 0, at) * COURANT
+        stiff_out[at + 2] = speed * speed * density
         for shot in range(shots):
-            now_buf[shot, at + 3] = whole((0, shot, at))
-    for at in range(-3, planes + 2):
-        cz_out[at + 3] = 0.5 * (buoy_buf[at + 3] + buoy_buf[at + 4])
-    for at in range(-2, planes + 2):
-        buoy = buoy_buf[at + 3]
-        cx_out[at + 2] = 0.5 * (buoy + pltpu.roll(buoy, wide - 1, 0))
-        above, below = near_cols(buoy)
-        cp_out[at + 2] = 0.5 * (buoy + above)
-        cm_out[at + 2] = 0.5 * (buoy + below)
+            now_buf[shot, at + 2] = whole(NOW, shot, at)
+
+    def put(ref):
+        def store(at, value):
+            ref[at + 2] = value
+
+        return store
+
+    for at in range(-2, planes + 1):
+        couple(lambda k: buoy_buf[k + 2], at, put(cz), put(cx), put(cp), put(cm))
     line = lax.broadcasted_iota(jnp.int32, (wide, cols), 0)
     column = lax.broadcasted_iota(jnp.int32, (wide, cols), 1)
     for shot in range(shots):
         for at in range(-2, planes + 2):
             here = (line + (at + 2) * wide == source_at[shot, 0]) & (column == source_at[shot, 1])
-            middle = now_buf[shot, at + 3]
-            lap_out[shot, at + 2] = laplace(
-                lambda k: now_buf[shot, k + 3],
-                at,
-                lambda k: cz_out[k + 3],
-                lambda k: cx_out[k + 2],
-                lambda k: cp_out[k + 2],
-                lambda k: cm_out[k + 2],
+            middle = now_buf[shot, at + 2]
+            if -1 <= at < planes + 1:
+                lap_out[shot, at + 2] = laplace(
+                    lambda k: now_buf[shot, k + 2],
+                    at,
+                    lambda k: cz[k + 2],
+                    lambda k: cx[k + 2],
+                    lambda k: cp[k + 2],
+                    lambda k: cm[k + 2],
+                )
+            else:
+                lap_out[shot, at + 2] = whole(LAP, shot, at)
+            base_out[shot, at + 2] = (
+                2.0 * middle - whole(PREV, shot, at) + jnp.where(here, wavelet[shot, 0], 0.0)
             )
-            base_out[shot, at + 2] = (
-                2.0 * middle - whole((1, shot, at)) + jnp.where(here, wavelet[shot, 0], 0.0)
-            )
-            newest = whole((2, shot, at))
+            newest = whole(LAST, shot, at)
             last_out[shot, at + 2] = newest
             if -1 <= at < planes + 1:
                 turn_out[shot, at + 1] = jnp.where(here, wavelet[shot, 1], 0.0) - middle
                 late_out[shot, at + 1] = (
                     2.0 * newest
-                    - whole((4, shot, at))
+                    - whole(LATE, shot, at)
                     - dense[shot, 2, (at + 1) * wide : (at + 2) * wide]
                 )
             if 0 <= at < planes:
@@ -303,7 +383,7 @@
 ):
     shots, planes = low.shape[:2]
     wide, _ = low.shape[2:]
-    cz = lambda k: cz_ref[k + 1]
+    cz = lambda k: cz_ref[k]
     cx = lambda k: cx_ref[k]
     cp = lambda k: cp_ref[k]
     cm = lambda k: cm_ref[k]
@@ -433,6 +513,7 @@
     evens = even_pairs(depth_count)
     odds = odd_pairs(depth_count)
     swap = [(0, 1), (1, 0)]
+    own_width = velocity.shape[2]
     wide = rows + 2 * PAD
 
     def shot_terms(block):
@@ -461,37 +542,70 @@
             step *= 2
         return value
 
+    hbm = pl.BlockSpec(memory_space=pltpu.HBM)
+    spec = pl.BlockSpec(memory_space=pltpu.VMEM)
+
+    def load(kernel, shapes, args, scratch, count):
+        return pl.pallas_call(
+            kernel,
+            out_shape=tuple(pltpu.VMEM(shape, jnp.float32) for shape in shapes),
+            in_specs=[hbm] * len(args),
+            out_specs=tuple(spec for _ in shapes),
+            scratch_shapes=scratch + [pltpu.SemaphoreType.DMA((count,))],
+            compiler_params=pltpu.CompilerParams(vmem_limit_bytes=4 << 20),
+        )(*[pltpu.with_memory_space_constraint(a, pltpu.HBM) for a in args])
+
+    own_planes = (shots + 1) * planes
+    first, first_edges = load(
+        first_kernel,
+        [(own_planes + 1, rows, cols), (own_planes * PAD, cols)],
+        (fwd_now, density, velocity),
+        [pltpu.VMEM(velocity.shape, jnp.float32)],
+        shots + 2,
+    )
+    first_odd = send(first, "depth", odds)
+    first_even = send(first, "depth", evens)
+    first_edges = send(first_edges, "lat", swap)
+    second, late = load(
+        second_kernel,
+        [(2 * shots * planes, rows, cols), adj_late.shape],
+        (fwd_prev, adj_last, adj_late),
+        [],
+        2 * shots + 1,
+    )
+    second_odd = send(second, "depth", odds)
+    second_even = send(second, "depth", evens)
+
+    even = depth_at % 2 == 0
+    lines = jnp.stack(
+        [
+            jnp.where(even, first_odd[own_planes], first_even[own_planes]),
+            first[own_planes],
+            jnp.where(even, first_even[own_planes], first_odd[own_planes]),
+        ]
+    )
     if shot_count == 2:
-        other = send(velocity, "shot", swap)
-        full_velocity = jnp.where(
-            shot_at == 0,
-            jnp.concatenate([velocity, other], axis=2),
-            jnp.concatenate([other, velocity], axis=2),
-        )
+        other = send(lines, "shot", swap)
+        parts = [jnp.where(shot_at == 0, lines, other), jnp.where(shot_at == 0, other, lines)]
     else:
-        full_velocity = lax.all_gather(velocity, "shot", axis=2, tiled=True)
-
-    near_planes = (3 * shots + 1) * planes + shots
-    hbm = pl.BlockSpec(memory_space=pl.ANY)
-    spec = pl.BlockSpec(memory_space=pltpu.VMEM)
-    to_even, to_odd, to_far, own_late = pl.pallas_call(
-        pack_kernel,
-        out_shape=(
-            pltpu.VMEM((near_planes, rows, cols), jnp.float32),
-            pltpu.VMEM((near_planes, rows, cols), jnp.float32),
-            pltpu.VMEM((2, shots + 1, rows, cols), jnp.float32),
-            pltpu.VMEM(adj_late.shape, jnp.float32),
-        ),
-        in_specs=[hbm] * 5,
-        out_specs=(spec, spec, spec, spec),
-        scratch_shapes=[pltpu.SemaphoreType.DMA((3 * shots + 2,))],
-        compiler_params=pltpu.CompilerParams(vmem_limit_bytes=8 << 20),
-        name="pack",
-    )(fwd_now, fwd_prev, adj_last, density, adj_late)
-    near_odd = send(to_odd, "depth", odds)
-    far_first = send(to_far[0], "depth", two_pairs(depth_count, True))
-    far_second = send(to_far[1], "depth", two_pairs(depth_count, False))
-    near_even = send(to_even, "depth", evens)
+        gathered = lax.all_gather(lines, "shot")
+        parts = [gathered[k] for k in range(shot_count)]
+    full_velocity = jnp.stack(
+        [
+            jnp.concatenate([p[block, :, k * own_width : (k + 1) * own_width] for p in parts], axis=1)
+            for block in range(3)
+            for k in range(planes)
+        ]
+    )
+    small = (planes + 1, wide, cols)
+    to_even, to_odd = on_chip(
+        third_kernel,
+        [(2 * shots, rows, cols)] * 2,
+        (first, first_even, first_odd, first_edges, late),
+        scratch=[(shots, planes + 2, wide, cols), (planes + 2, wide, cols)] + [small] * 4,
+    )
+    third_odd = send(to_odd, "depth", odds)
+    third_even = send(to_even, "depth", evens)
 
     full_rows = rows * lat_count
     depth_start = depth_at * planes
@@ -509,9 +623,6 @@
         return jnp.where(inside, plane_at * wide + row_at, -1), cells % cols
 
     row_id, col_id = place(receiver_cell, 1)
-    row_id, full_velocity = lax.optimization_barrier((row_id, full_velocity))
-    vel_odd = send(full_velocity, "depth", odds)
-    vel_even = send(full_velocity, "depth", evens)
     spread_shape = (shots, 3, (planes + 2) * wide, cols)
     (dense,) = on_chip(
         spread_kernel,
@@ -522,12 +633,13 @@
     )
     source_at = jnp.stack(place(source_cell, 2), axis=1)
 
-    halos = (to_even, own_late) + (near_even, near_odd, far_first, far_second, full_velocity, vel_even, vel_odd)
-    strips = shots * (4 * planes + 16) + 2 * planes + 10
+    halos = (first, second, late, first_even, first_odd, second_even, second_odd)
+    halos += (third_even, third_odd, full_velocity)
+    strips = shots * (4 * planes + 16) + 2 * (planes + 4)
     (edges,) = on_chip(edge_kernel, [(strips * PAD, cols)], halos)
     edges = send(edges, "lat", swap)
 
-    deep, deeper = planes + 4, planes + 6
+    deep = planes + 4
     model = (wide, cols)
     scalars = pl.BlockSpec(memory_space=pltpu.SMEM)
     prepared_shapes = [
@@ -538,10 +650,10 @@
         (shots, deep) + model,
         (shots, planes) + model,
         (deep,) + model,
-        (planes + 5,) + model,
-        (deep,) + model,
-        (deep,) + model,
-        (deep,) + model,
+        (planes + 3,) + model,
+        (planes + 3,) + model,
+        (planes + 3,) + model,
+        (planes + 3,) + model,
     ]
     vectors = halos + (edges, dense)
     prepared = pl.pallas_call(
@@ -550,8 +662,8 @@
         in_specs=[spec] * len(vectors) + [scalars, scalars],
         out_specs=tuple(spec for _ in prepared_shapes),
         scratch_shapes=[
-            pltpu.VMEM((shots, deeper) + model, jnp.float32),
-            pltpu.VMEM((deeper,) + model, jnp.float32),
+            pltpu.VMEM((shots, deep) + model, jnp.float32),
+            pltpu.VMEM((deep,) + model, jnp.float32),
         ],
         compiler_params=pltpu.CompilerParams(vmem_limit_bytes=8 << 20),
         name="prepare",

time: 67.4 us -> 60.8 us (0.902)
  waiting for transfers between devices: 27.1 us -> 20.9 us
  local copies, waits for them, and re-layouts: 5.24 us -> 1.02 us
  starting transfers between devices: 23.6 us -> 25.7 us
  Pallas kernels: 9.88 us -> 11.2 us
    ppermute x9 -> x11, waiting for transfers between devices: 11.9 us -> 6.1 us  [send(): return lax.ppermute(block, axis, pairs)]
    unnamed x20 -> x10, local copies, waits for them, and re-layouts: 5.03 us -> 0.72 us
    ppermute x9 -> x11, starting transfers between devices: 15.1 us -> 17.8 us  [send(): return lax.ppermute(block, axis, pairs)]
    ppermute x1, starting transfers between devices: 2.9 us -> 1.19 us  [depth_max(): value = jnp.maximum(value, lax.ppermute(value, 'depth', pairs))]
    ppermute x1, waiting for transfers between devices: 1.6 us -> 3.32 us  [depth_max(): value = jnp.maximum(value, lax.ppermute(value, 'depth', pairs))]
    ppermute x3, waiting for transfers between devices: 3.77 us -> 2.42 us  [depth_max(): lax.ppermute(value, 'depth', [(i, i ^ k) for i in range(depth_count)])]
    pallas_call x1 -> x2, Pallas kernels: 0.86 us -> 2.13 us  [load(): pl.pallas_call(kernel, out_shape=tuple((pltpu.VMEM(shape, jnp.float32) fo...]
    ppermute x2, starting transfers between devices: 1.14 us -> 2.18 us  [shot_terms(): return (block, lax.ppermute(block, 'shot', swap))]
  transfers between devices with their start and end apart: 17 -> 19, of which waited for: 9 -> 12; matrix products, arithmetic and copies ran while one was open for 1% -> 2% of each run, Pallas kernels for 9% -> 10%
where the time goes in v4:
time: 60.8 us; the launch traced here: 60.5 us
  starting transfers between devices  25.7 us (42%)
  waiting for transfers between devices  20.9 us (34%)
  Pallas kernels  11.2 us (18%)
  local copies, waits for them, and re-layouts  1.02 us (2%)
  between operations  0.87 us (1%)
  other arithmetic  0.77 us (1%)
    ppermute x11, starting transfers between devices, send(): return lax.ppermute(block, axis, pairs)  17.8 us
    pallas_call x10, Pallas kernels, on_chip(): pl.pallas_call(kernel, out_shape=outs, in_specs=[spec] * len(args), out_s...  7.84 us
    ppermute x2, waiting for transfers between devices, shot_terms(): return (block, lax.ppermute(block, 'shot', swap))  6.71 us
    ppermute x11, waiting for transfers between devices, send(): return lax.ppermute(block, axis, pairs)  6.1 us
    ppermute x3, starting transfers between devices, depth_max(): lax.ppermute(value, 'depth', [(i, i ^ k) for i in range(depth_count)])  4.39 us
    ppermute x1, waiting for transfers between devices, depth_max(): value = jnp.maximum(value, lax.ppermute(value, 'depth', pairs))  3.32 us
    ppermute x3, waiting for transfers between devices, depth_max(): lax.ppermute(value, 'depth', [(i, i ^ k) for i in range(depth_count)])  2.42 us
    ppermute x2, starting transfers between devices, shot_terms(): return (block, lax.ppermute(block, 'shot', swap))  2.18 us
  transfers between devices with their start and end apart: 19, of which 12 were waited for; matrix products, arithmetic and copies ran while one was open for 2% of the time, Pallas kernels for 10%

profile of v4, /device:TPU:0, one launch (start us, length us, event | category | flops | bytes accessed | tf_op | source)
XLA Modules:
  0.0 60.5 jit_solution(281341097790002293)
XLA Ops:
  0.6 1.0 %shard_map.113 = (f32[7,64,128]{2,1,0:T(8,128)S(1)}, f32[48,128]{1,0:T(8,128)S(1)}) custom-call(f32[2,2,64,128]{3,2,1,0:T(8,128)} %now.1, f32[2,64,128]{2,1,0:T(8,128)} %dens.1, f32[2,64,64]{2,1,0:T(8,128)} %velocity.1), custom_call_target="tpu_custom_call" | custom-call | tf_op jit(solution)/shard_map/pallas_call | solution.py:549
  1.7 0.7 %collective-permute-start.1 = (f32[7,64,128]{2,1,0:T(8,128)S(1)}, f32[7,64,128]{2,1,0:T(8,128)S(1)}, u32[]{:S(2)}, u32[]{:S(2)}) collective-permute-start(f32[7,64,128]{2,1,0:T(8,128)S(1)} %get-tuple-element.25.first.refs_0_), channel_id=1, source_target_pairs={{4,8},{8,4},{5,9},{9,5},{6,10},{10,6},{7,11},{11,7},{20,24},{24,20... | collective-permute-start | bytes 688136 | tf_op jit(solution)/shard_map/ppermute | solution.py:30
  2.4 5.9 %collective-permute-start = (f32[7,64,128]{2,1,0:T(8,128)S(1)}, f32[7,64,128]{2,1,0:T(8,128)S(1)}, u32[]{:S(2)}, u32[]{:S(2)}) collective-permute-start(f32[7,64,128]{2,1,0:T(8,128)S(1)} %get-tuple-element.25.first.refs_0_), channel_id=1, source_target_pairs={{0,4},{4,0},{8,12},{12,8},{1,5},{5,1},{9,13},{13,9},{2,6},{6,2},{1... | collective-permute-start | bytes 688136 | tf_op jit(solution)/shard_map/ppermute | solution.py:30
  8.3 1.1 %shard_map.114 = (f32[8,64,128]{2,1,0:T(8,128)S(1)}, f32[2,2,64,128]{3,2,1,0:T(8,128)S(1)}) custom-call(f32[2,2,64,128]{3,2,1,0:T(8,128)} %prev.1, f32[2,2,64,128]{3,2,1,0:T(8,128)} %last.1, f32[2,2,64,128]{3,2,1,0:T(8,128)} %late.1), custom_call_target="tpu_custom_call" | custom-call | tf_op jit(solution)/shard_map/pallas_call | solution.py:549
  9.4 0.7 %collective-permute-start.3 = (f32[8,64,128]{2,1,0:T(8,128)S(1)}, f32[8,64,128]{2,1,0:T(8,128)S(1)}, u32[]{:S(2)}, u32[]{:S(2)}) collective-permute-start(f32[8,64,128]{2,1,0:T(8,128)S(1)} %get-tuple-element.26.refs_1_.second), channel_id=1, source_target_pairs={{4,8},{8,4},{5,9},{9,5},{6,10},{10,6},{7,11},{11,7},{20,24},{24,20... | collective-permute-start | bytes 786440 | tf_op jit(solution)/shard_map/ppermute | solution.py:30
  10.1 1.8 %collective-permute-start.2 = (f32[8,64,128]{2,1,0:T(8,128)S(1)}, f32[8,64,128]{2,1,0:T(8,128)S(1)}, u32[]{:S(2)}, u32[]{:S(2)}) collective-permute-start(f32[8,64,128]{2,1,0:T(8,128)S(1)} %get-tuple-element.26.refs_1_.second), channel_id=1, source_target_pairs={{0,4},{4,0},{8,12},{12,8},{1,5},{5,1},{9,13},{13,9},{2,6},{6,2},{1... | collective-permute-start | bytes 786440 | tf_op jit(solution)/shard_map/ppermute | solution.py:30
  11.8 0.0 collective-permute-start.4
  11.9 0.7 %copy-done.3 = s32[2,2048]{1,0:T(2,128)S(1)} copy-done((s32[2,2048]{1,0:T(2,128)S(1)}, s32[2,2048]{1,0:T(2,128)}, u32[]{:S(2)}) %copy-start.3) | copy-done | bytes 16408
  12.6 0.1 and_select_fusion
  12.7 0.0 collective-permute-done.1.by_odd.refs_4_.first_odd
  12.7 2.0 %collective-permute-done.by_even.refs_3_.first_even = f32[7,64,128]{2,1,0:T(8,128)S(1)} collective-permute-done((f32[7,64,128]{2,1,0:T(8,128)S(1)}, f32[7,64,128]{2,1,0:T(8,128)S(1)}, u32[]{:S(2)}, u32[]{:S(2)}) %collective-permute-start) | collective-permute-done | bytes 229408 | tf_op jit(solution)/shard_map/ppermute | solution.py:30
  14.8 0.0 copy-start.4
  14.8 1.6 %collective-permute-start.7 = (f32[3,64,128]{2,1,0:T(8,128)S(1)}, f32[3,64,128]{2,1,0:T(8,128)S(1)}, u32[]{:S(2)}, u32[]{:S(2)}) collective-permute-start(f32[3,64,128]{2,1,0:T(8,128)S(1)} %pad_maximum_fusion), channel_id=1, source_target_pairs={{0,2},{2,0},{1,3},{3,1},{4,6},{6,4},{5,7},{7,5},{8,10},{10,8},{9,1... | collective-permute-start | bytes 294920 | tf_op jit(solution)/shard_map/ppermute | solution.py:30
  16.3 0.0 copy-done.4
  16.4 0.1 copy.12
  16.5 0.1 copy.13
  16.6 0.0 collective-permute-done.4.edges
  16.6 0.2 shard_map.115
  16.8 2.1 %collective-permute-start.5 = (f32[4,64,128]{2,1,0:T(8,128)S(1)}, f32[4,64,128]{2,1,0:T(8,128)S(1)}, u32[]{:S(2)}, u32[]{:S(2)}) collective-permute-start(f32[4,64,128]{2,1,0:T(8,128)S(1)} %get-tuple-element.29), channel_id=1, source_target_pairs={{0,4},{4,0},{8,12},{12,8},{1,5},{5,1},{9,13},{13,9},{2,6},{6,2},{1... | collective-permute-start | bytes 393224 | tf_op jit(solution)/shard_map/ppermute | solution.py:30
  18.9 0.7 %collective-permute-start.6 = (f32[4,64,128]{2,1,0:T(8,128)S(1)}, f32[4,64,128]{2,1,0:T(8,128)S(1)}, u32[]{:S(2)}, u32[]{:S(2)}) collective-permute-start(f32[4,64,128]{2,1,0:T(8,128)S(1)} %get-tuple-element.30), channel_id=1, source_target_pairs={{4,8},{8,4},{5,9},{9,5},{6,10},{10,6},{7,11},{11,7},{20,24},{24,20... | collective-permute-start | bytes 393224 | tf_op jit(solution)/shard_map/ppermute | solution.py:30
  19.5 0.0 collective-permute-done.7
  19.6 0.1 slice_bitcast_fusion
  19.7 0.1 fusion
  19.8 0.1 fusion.1
  19.9 0.1 fusion.2
  19.9 0.1 fusion.3
  20.0 0.1 fusion.4
  20.1 0.1 fusion.5.refs_9_.vel
  20.2 0.0 collective-permute-done.3.refs_6_.second_odd
  20.2 0.2 collective-permute-done.2.refs_5_.second_even
  20.4 1.7 %collective-permute-done.5.refs_7_.third_even = f32[4,64,128]{2,1,0:T(8,128)S(1)} collective-permute-done((f32[4,64,128]{2,1,0:T(8,128)S(1)}, f32[4,64,128]{2,1,0:T(8,128)S(1)}, u32[]{:S(2)}, u32[]{:S(2)}) %collective-permute-start.5) | collective-permute-done | bytes 131104 | tf_op jit(solution)/shard_map/ppermute | solution.py:30
  22.0 0.0 collective-permute-done.6.refs_8_.third_odd
  22.1 0.1 collective-permute-start.8
  22.2 0.1 pad_add_fusion.source_at
  22.2 0.0 copy-done.2
  22.2 4.9 %shard_map.117.dense = f32[2,3,320,128]{3,2,1,0:T(8,128)S(1)} custom-call(s32[2,2048]{1,0:T(2,128)S(1)} %get-tuple-element.65.row_ref, s32[2,2048]{1,0:T(2,128)S(1)} %get-tuple-element.64.col_ref, f32[2,2,2048]{2,1,0:T(2,128)S(1)} %copy-done.2), custom_call_target="tpu_custom_call" | custom-call | flops 2348810240 | bytes 65536 | tf_op jit(solution)/shard_map/pallas_call | solution.py:38
  27.1 0.0 collective-permute-done.8.edges
  27.2 0.0 copy-done.1
  27.2 1.2 %prepare.1 = (f32[2,6,80,128]{3,2,1,0:T(8,128)S(1)}, f32[2,6,80,128]{3,2,1,0:T(8,128)S(1)}, f32[2,4,80,128]{3,2,1,0:T(8,128)S(1)}, f32[2,4,80,128]{3,2,1,0:T(8,1...) custom-call(f32[7,64,128]{2,1,0:T(8,128)S(1)} %get-tuple-element.25., ...), custom_call_target="tpu_custom_call" | custom-call | tf_op jit(solution)/shard_map/prepare/pallas_call | solution.py:659
  28.4 0.8 %shard_map.118.mine = f32[2,64,128]{2,1,0:T(8,128)S(1)} custom-call(f32[6,80,128]{2,1,0:T(8,128)S(1)} %get-tuple-element.31.stiff, f32[2,6,80,128]{3,2,1,0:T(8,128)S(1)} %get-tuple-element.32.lap, f32[2,6,80,128]{3,2,1,0:T(8,128)S(1)} %get-tuple-element.33.base, f32[2,4,80,128]{3,2,1,0:T(8,128)S(1)} %get-tuple-element.34.turn, ...), custom_call_target="tpu_custom_call" | custom-call | bytes 4341760 | tf_op jit(solution)/shard_map/pallas_call | solution.py:38
  29.2 1.6 %collective-permute-start.9 = (f32[2,64,128]{2,1,0:T(8,128)S(1)}, f32[2,64,128]{2,1,0:T(8,128)S(1)}, u32[]{:S(2)}, u32[]{:S(2)}) collective-permute-start(f32[2,64,128]{2,1,0:T(8,128)S(1)} %shard_map.118.mine), channel_id=1, source_target_pairs={{0,2},{2,0},{1,3},{3,1},{4,6},{6,4},{5,7},{7,5},{8,10},{10,8},{9,1... | collective-permute-start | bytes 196616 | tf_op jit(solution)/shard_map/ppermute | solution.py:521
  30.7 3.0 %collective-permute-done.9.other = f32[2,64,128]{2,1,0:T(8,128)S(1)} collective-permute-done((f32[2,64,128]{2,1,0:T(8,128)S(1)}, f32[2,64,128]{2,1,0:T(8,128)S(1)}, u32[]{:S(2)}, u32[]{:S(2)}) %collective-permute-start.9) | collective-permute-done | bytes 65568 | tf_op jit(solution)/shard_map/ppermute | solution.py:521
  33.8 0.1 collective-permute-start.10
  33.8 1.2 %collective-permute-done.10.got = f32[24,128]{1,0:T(8,128)S(1)} collective-permute-done((f32[24,128]{1,0:T(8,128)S(1)}, f32[24,128]{1,0:T(8,128)S(1)}, u32[]{:S(2)}, u32[]{:S(2)}) %collective-permute-start.10) | collective-permute-done | bytes 12320 | tf_op jit(solution)/shard_map/ppermute | solution.py:710
  35.0 0.0 copy-start
  35.0 3.8 %collective-permute-start.11 = (f32[168,128]{1,0:T(8,128)S(1)}, f32[168,128]{1,0:T(8,128)S(1)}, u32[]{:S(2)}, u32[]{:S(2)}) collective-permute-start(f32[168,128]{1,0:T(8,128)S(1)} %shard_map.120.mine), channel_id=1, source_target_pairs={{0,4},{4,0},{8,12},{12,8},{1,5},{5,1},{9,13},{13,9},{2,6},{6,2},{1... | collective-permute-start | bytes 258056 | tf_op jit(solution)/shard_map/ppermute | solution.py:30
  38.8 0.7 %collective-permute-start.12 = (f32[160,128]{1,0:T(8,128)S(1)}, f32[160,128]{1,0:T(8,128)S(1)}, u32[]{:S(2)}, u32[]{:S(2)}) collective-permute-start(f32[160,128]{1,0:T(8,128)S(1)} %slice.88), channel_id=1, source_target_pairs={{4,8},{8,4},{5,9},{9,5},{6,10},{10,6},{7,11},{11,7},{20,24},{24,20... | collective-permute-start | bytes 245768 | tf_op jit(solution)/shard_map/ppermute | solution.py:30
  39.5 2.2 %collective-permute-done.11.by_even = f32[168,128]{1,0:T(8,128)S(1)} collective-permute-done((f32[168,128]{1,0:T(8,128)S(1)}, f32[168,128]{1,0:T(8,128)S(1)}, u32[]{:S(2)}, u32[]{:S(2)}) %collective-permute-start.11) | collective-permute-done | bytes 86048 | tf_op jit(solution)/shard_map/ppermute | solution.py:30
  41.7 1.2 %collective-permute-start.13 = (f32[8,128]{1,0:T(8,128)S(1)}, f32[8,128]{1,0:T(8,128)S(1)}, u32[]{:S(2)}, u32[]{:S(2)}) collective-permute-start(f32[8,128]{1,0:T(8,128)S(1)} %slice_maximum_fusion), channel_id=1, source_target_pairs={{0,8},{4,12},{8,0},{12,4},{1,9},{5,13},{9,1},{13,5},{2,10},{6,14},... | collective-permute-start | bytes 12296 | tf_op jit(solution)/shard_map/ppermute | solution.py:541
  42.9 3.3 %collective-permute-done.13 = f32[8,128]{1,0:T(8,128)S(1)} collective-permute-done((f32[8,128]{1,0:T(8,128)S(1)}, f32[8,128]{1,0:T(8,128)S(1)}, u32[]{:S(2)}, u32[]{:S(2)}) %collective-permute-start.13) | collective-permute-done | bytes 4128 | tf_op jit(solution)/shard_map/ppermute | solution.py:541
  46.2 0.0 collective-permute-done.12.by_odd
  46.2 0.2 shard_map.121
  46.4 0.8 %shard_map.122.mine = f32[2,64,128]{2,1,0:T(8,128)S(1)} custom-call(f32[6,80,128]{2,1,0:T(8,128)S(1)} %get-tuple-element.44.stiff, f32[2,6,80,128]{3,2,1,0:T(8,128)S(1)} %get-tuple-element.32.lap, f32[2,6,80,128]{3,2,1,0:T(8,128)S(1)} %get-tuple-element.33.base, f32[2,4,80,128]{3,2,1,0:T(8,128)S(1)} %get-tuple-element.34.turn, ...), custom_call_target="tpu_custom_call" | custom-call | bytes 4341760 | tf_op jit(solution)/shard_map/pallas_call | solution.py:38
  47.2 0.6 %collective-permute-start.14 = (f32[2,64,128]{2,1,0:T(8,128)S(1)}, f32[2,64,128]{2,1,0:T(8,128)S(1)}, u32[]{:S(2)}, u32[]{:S(2)}) collective-permute-start(f32[2,64,128]{2,1,0:T(8,128)S(1)} %shard_map.122.mine), channel_id=1, source_target_pairs={{0,2},{2,0},{1,3},{3,1},{4,6},{6,4},{5,7},{7,5},{8,10},{10,8},{9,1... | collective-permute-start | bytes 196616 | tf_op jit(solution)/shard_map/ppermute | solution.py:521
  47.8 3.7 %collective-permute-done.14.other = f32[2,64,128]{2,1,0:T(8,128)S(1)} collective-permute-done((f32[2,64,128]{2,1,0:T(8,128)S(1)}, f32[2,64,128]{2,1,0:T(8,128)S(1)}, u32[]{:S(2)}, u32[]{:S(2)}) %collective-permute-start.14) | collective-permute-done | bytes 65568 | tf_op jit(solution)/shard_map/ppermute | solution.py:521
  51.6 0.1 collective-permute-start.15
  51.6 1.2 %collective-permute-done.15 = f32[8,128]{1,0:T(8,128)S(1)} collective-permute-done((f32[8,128]{1,0:T(8,128)S(1)}, f32[8,128]{1,0:T(8,128)S(1)}, u32[]{:S(2)}, u32[]{:S(2)}) %collective-permute-start.15) | collective-permute-done | bytes 4128 | tf_op jit(solution)/shard_map/ppermute | solution.py:698
  52.8 1.2 %collective-permute-start.18 = (f32[8,128]{1,0:T(8,128)S(1)}, f32[8,128]{1,0:T(8,128)S(1)}, u32[]{:S(2)}, u32[]{:S(2)}) collective-permute-start(f32[8,128]{1,0:T(8,128)S(1)} %max.20), channel_id=1, source_target_pairs={{0,12},{4,8},{8,4},{12,0},{1,13},{5,9},{9,5},{13,1},{2,14},{6,10},... | collective-permute-start | bytes 12296 | tf_op jit(solution)/shard_map/ppermute | solution.py:530
  54.0 2.0 %collective-permute-start.17 = (f32[8,128]{1,0:T(8,128)S(1)}, f32[8,128]{1,0:T(8,128)S(1)}, u32[]{:S(2)}, u32[]{:S(2)}) collective-permute-start(f32[8,128]{1,0:T(8,128)S(1)} %max.20), channel_id=1, source_target_pairs={{0,8},{4,12},{8,0},{12,4},{1,9},{5,13},{9,1},{13,5},{2,10},{6,14},... | collective-permute-start | bytes 12296 | tf_op jit(solution)/shard_map/ppermute | solution.py:530
  56.0 1.2 %collective-permute-start.16 = (f32[8,128]{1,0:T(8,128)S(1)}, f32[8,128]{1,0:T(8,128)S(1)}, u32[]{:S(2)}, u32[]{:S(2)}) collective-permute-start(f32[8,128]{1,0:T(8,128)S(1)} %max.20), channel_id=1, source_target_pairs={{0,4},{4,0},{8,12},{12,8},{1,5},{5,1},{9,13},{13,9},{2,6},{6,2},{1... | collective-permute-start | bytes 12296 | tf_op jit(solution)/shard_map/ppermute | solution.py:530
  57.2 1.0 %collective-permute-done.18 = f32[8,128]{1,0:T(8,128)S(1)} collective-permute-done((f32[8,128]{1,0:T(8,128)S(1)}, f32[8,128]{1,0:T(8,128)S(1)}, u32[]{:S(2)}, u32[]{:S(2)}) %collective-permute-start.18) | collective-permute-done | bytes 4128 | tf_op jit(solution)/shard_map/ppermute | solution.py:530
  58.2 0.3 collective-permute-done.17
  58.5 1.1 %collective-permute-done.16 = f32[8,128]{1,0:T(8,128)S(1)} collective-permute-done((f32[8,128]{1,0:T(8,128)S(1)}, f32[8,128]{1,0:T(8,128)S(1)}, u32[]{:S(2)}, u32[]{:S(2)}) %collective-permute-start.16) | collective-permute-done | bytes 4128 | tf_op jit(solution)/shard_map/ppermute | solution.py:530
  59.6 0.8 %shard_map.124 = (f32[2,64,64]{2,1,0:T(8,128)}, f32[2,64,64]{2,1,0:T(8,128)}) custom-call(f32[2,64,128]{2,1,0:T(8,128)S(1)} %get-tuple-element.45.total, f32[8,128]{1,0:T(8,128)S(1)} %maximum_maximum_fusion.largest, f32[2,64,64]{2,1,0:T(8,128)S(1)} %get-tuple-element.47.velocity), custom_call_target="tpu_custom_call" | custom-call | bytes 102400 | tf_op jit(solution)/shard_map/pallas_call | solution.py:38
  (18 shorter events, 0.2 us)
Async XLA Ops:
  1.7 11.0 %collective-permute-start.1 = (f32[7,64,128]{2,1,0:T(8,128)S(1)}, f32[7,64,128]{2,1,0:T(8,128)S(1)}, u32[]{:S(2)}, u32[]{:S(2)}) collective-permute-start(f32[7,64,128]{2,1,0:T(8,128)S(1)} %get-tuple-element.25.first.refs_0_), channel_id=1, source_target_pairs={{4,8},{8,4},{5,9},{9,5},{6,10},{10,6},{7,11},{11,7},{20,24},{24,20... | collective-permute-start | bytes 688136 | tf_op jit(solution)/shard_map/ppermute | solution.py:30
  2.4 12.4 %collective-permute-start = (f32[7,64,128]{2,1,0:T(8,128)S(1)}, f32[7,64,128]{2,1,0:T(8,128)S(1)}, u32[]{:S(2)}, u32[]{:S(2)}) collective-permute-start(f32[7,64,128]{2,1,0:T(8,128)S(1)} %get-tuple-element.25.first.refs_0_), channel_id=1, source_target_pairs={{0,4},{4,0},{8,12},{12,8},{1,5},{5,1},{9,13},{13,9},{2,6},{6,2},{1... | collective-permute-start | bytes 688136 | tf_op jit(solution)/shard_map/ppermute | solution.py:30
  9.4 10.8 %collective-permute-start.3 = (f32[8,64,128]{2,1,0:T(8,128)S(1)}, f32[8,64,128]{2,1,0:T(8,128)S(1)}, u32[]{:S(2)}, u32[]{:S(2)}) collective-permute-start(f32[8,64,128]{2,1,0:T(8,128)S(1)} %get-tuple-element.26.refs_1_.second), channel_id=1, source_target_pairs={{4,8},{8,4},{5,9},{9,5},{6,10},{10,6},{7,11},{11,7},{20,24},{24,20... | collective-permute-start | bytes 786440 | tf_op jit(solution)/shard_map/ppermute | solution.py:30
  10.1 10.3 %collective-permute-start.2 = (f32[8,64,128]{2,1,0:T(8,128)S(1)}, f32[8,64,128]{2,1,0:T(8,128)S(1)}, u32[]{:S(2)}, u32[]{:S(2)}) collective-permute-start(f32[8,64,128]{2,1,0:T(8,128)S(1)} %get-tuple-element.26.refs_1_.second), channel_id=1, source_target_pairs={{0,4},{4,0},{8,12},{12,8},{1,5},{5,1},{9,13},{13,9},{2,6},{6,2},{1... | collective-permute-start | bytes 786440 | tf_op jit(solution)/shard_map/ppermute | solution.py:30
  11.8 4.7 %collective-permute-start.4 = (f32[48,128]{1,0:T(8,128)S(1)}, f32[48,128]{1,0:T(8,128)S(1)}, u32[]{:S(2)}, u32[]{:S(2)}) collective-permute-start(f32[48,128]{1,0:T(8,128)S(1)} %get-tuple-element.28), channel_id=1, source_target_pairs={{0,1},{1,0},{2,3},{3,2},{4,5},{5,4},{6,7},{7,6},{8,9},{9,8},{10,11... | collective-permute-start | bytes 73736 | tf_op jit(solution)/shard_map/ppermute | solution.py:30
  11.8 0.7 %copy-start.3 = (s32[2,2048]{1,0:T(2,128)S(1)}, s32[2,2048]{1,0:T(2,128)}, u32[]{:S(2)}) copy-start(s32[2,2048]{1,0:T(2,128)} %param.18) | copy-start | bytes 49156
  14.8 1.6 %copy-start.4 = (s32[2]{0:T(128)S(1)}, s32[2]{0:T(128)}, u32[]{:S(2)}) copy-start(s32[2]{0:T(128)} %param.17) | copy-start | bytes 28
  14.8 4.8 %collective-permute-start.7 = (f32[3,64,128]{2,1,0:T(8,128)S(1)}, f32[3,64,128]{2,1,0:T(8,128)S(1)}, u32[]{:S(2)}, u32[]{:S(2)}) collective-permute-start(f32[3,64,128]{2,1,0:T(8,128)S(1)} %pad_maximum_fusion), channel_id=1, source_target_pairs={{0,2},{2,0},{1,3},{3,1},{4,6},{6,4},{5,7},{7,5},{8,10},{10,8},{9,1... | collective-permute-start | bytes 294920 | tf_op jit(solution)/shard_map/ppermute | solution.py:30
  16.8 5.3 %collective-permute-start.5 = (f32[4,64,128]{2,1,0:T(8,128)S(1)}, f32[4,64,128]{2,1,0:T(8,128)S(1)}, u32[]{:S(2)}, u32[]{:S(2)}) collective-permute-start(f32[4,64,128]{2,1,0:T(8,128)S(1)} %get-tuple-element.29), channel_id=1, source_target_pairs={{0,4},{4,0},{8,12},{12,8},{1,5},{5,1},{9,13},{13,9},{2,6},{6,2},{1... | collective-permute-start | bytes 393224 | tf_op jit(solution)/shard_map/ppermute | solution.py:30
  18.9 3.2 %collective-permute-start.6 = (f32[4,64,128]{2,1,0:T(8,128)S(1)}, f32[4,64,128]{2,1,0:T(8,128)S(1)}, u32[]{:S(2)}, u32[]{:S(2)}) collective-permute-start(f32[4,64,128]{2,1,0:T(8,128)S(1)} %get-tuple-element.30), channel_id=1, source_target_pairs={{4,8},{8,4},{5,9},{9,5},{6,10},{10,6},{7,11},{11,7},{20,24},{24,20... | collective-permute-start | bytes 393224 | tf_op jit(solution)/shard_map/ppermute | solution.py:30
  20.2 2.1 %copy-start.2 = (f32[2,2,2048]{2,1,0:T(2,128)S(1)}, f32[2,2,2048]{2,1,0:T(2,128)}, u32[]{:S(2)}) copy-start(f32[2,2,2048]{2,1,0:T(2,128)} %obs_ref.1) | copy-start | bytes 98308
  22.1 5.1 %collective-permute-start.8 = (f32[480,128]{1,0:T(8,128)S(1)}, f32[480,128]{1,0:T(8,128)S(1)}, u32[]{:S(2)}, u32[]{:S(2)}) collective-permute-start(f32[480,128]{1,0:T(8,128)S(1)} %shard_map.116), channel_id=1, source_target_pairs={{0,1},{1,0},{2,3},{3,2},{4,5},{5,4},{6,7},{7,6},{8,9},{9,8},{10,11... | collective-permute-start | bytes 737288 | tf_op jit(solution)/shard_map/ppermute | solution.py:30
  22.2 4.9 %copy-start.1 = (f32[2,2]{1,0:T(2,128)S(1)}, f32[2,2]{1,0:T(2,128)}, u32[]{:S(2)}) copy-start(f32[2,2]{1,0:T(2,128)} %wavelet.1) | copy-start | bytes 52
  29.2 4.6 %collective-permute-start.9 = (f32[2,64,128]{2,1,0:T(8,128)S(1)}, f32[2,64,128]{2,1,0:T(8,128)S(1)}, u32[]{:S(2)}, u32[]{:S(2)}) collective-permute-start(f32[2,64,128]{2,1,0:T(8,128)S(1)} %shard_map.118.mine), channel_id=1, source_target_pairs={{0,2},{2,0},{1,3},{3,1},{4,6},{6,4},{5,7},{7,5},{8,10},{10,8},{9,1... | collective-permute-start | bytes 196616 | tf_op jit(solution)/shard_map/ppermute | solution.py:521
  33.8 1.2 %collective-permute-start.10 = (f32[24,128]{1,0:T(8,128)S(1)}, f32[24,128]{1,0:T(8,128)S(1)}, u32[]{:S(2)}, u32[]{:S(2)}) collective-permute-start(f32[24,128]{1,0:T(8,128)S(1)} %get-tuple-element.43.mine), channel_id=1, source_target_pairs={{0,1},{1,0},{2,3},{3,2},{4,5},{5,4},{6,7},{7,6},{8,9},{9,8},{10,11... | collective-permute-start | bytes 36872 | tf_op jit(solution)/shard_map/ppermute | solution.py:710
  35.0 11.2 %copy-start = (f32[2,64,64]{2,1,0:T(8,128)S(1)}, f32[2,64,64]{2,1,0:T(8,128)}, u32[]{:S(2)}) copy-start(f32[2,64,64]{2,1,0:T(8,128)} %velocity.1) | copy-start | bytes 98308
  35.0 6.6 %collective-permute-start.11 = (f32[168,128]{1,0:T(8,128)S(1)}, f32[168,128]{1,0:T(8,128)S(1)}, u32[]{:S(2)}, u32[]{:S(2)}) collective-permute-start(f32[168,128]{1,0:T(8,128)S(1)} %shard_map.120.mine), channel_id=1, source_target_pairs={{0,4},{4,0},{8,12},{12,8},{1,5},{5,1},{9,13},{13,9},{2,6},{6,2},{1... | collective-permute-start | bytes 258056 | tf_op jit(solution)/shard_map/ppermute | solution.py:30
  38.8 7.4 %collective-permute-start.12 = (f32[160,128]{1,0:T(8,128)S(1)}, f32[160,128]{1,0:T(8,128)S(1)}, u32[]{:S(2)}, u32[]{:S(2)}) collective-permute-start(f32[160,128]{1,0:T(8,128)S(1)} %slice.88), channel_id=1, source_target_pairs={{4,8},{8,4},{5,9},{9,5},{6,10},{10,6},{7,11},{11,7},{20,24},{24,20... | collective-permute-start | bytes 245768 | tf_op jit(solution)/shard_map/ppermute | solution.py:30
  41.7 4.5 %collective-permute-start.13 = (f32[8,128]{1,0:T(8,128)S(1)}, f32[8,128]{1,0:T(8,128)S(1)}, u32[]{:S(2)}, u32[]{:S(2)}) collective-permute-start(f32[8,128]{1,0:T(8,128)S(1)} %slice_maximum_fusion), channel_id=1, source_target_pairs={{0,8},{4,12},{8,0},{12,4},{1,9},{5,13},{9,1},{13,5},{2,10},{6,14},... | collective-permute-start | bytes 12296 | tf_op jit(solution)/shard_map/ppermute | solution.py:541
  47.2 4.3 %collective-permute-start.14 = (f32[2,64,128]{2,1,0:T(8,128)S(1)}, f32[2,64,128]{2,1,0:T(8,128)S(1)}, u32[]{:S(2)}, u32[]{:S(2)}) collective-permute-start(f32[2,64,128]{2,1,0:T(8,128)S(1)} %shard_map.122.mine), channel_id=1, source_target_pairs={{0,2},{2,0},{1,3},{3,1},{4,6},{6,4},{5,7},{7,5},{8,10},{10,8},{9,1... | collective-permute-start | bytes 196616 | tf_op jit(solution)/shard_map/ppermute | solution.py:521
  51.6 1.2 %collective-permute-start.15 = (f32[8,128]{1,0:T(8,128)S(1)}, f32[8,128]{1,0:T(8,128)S(1)}, u32[]{:S(2)}, u32[]{:S(2)}) collective-permute-start(f32[8,128]{1,0:T(8,128)S(1)} %get-tuple-element.46), channel_id=1, source_target_pairs={{0,1},{1,0},{2,3},{3,2},{4,5},{5,4},{6,7},{7,6},{8,9},{9,8},{10,11... | collective-permute-start | bytes 12296 | tf_op jit(solution)/shard_map/ppermute | solution.py:698
  52.8 5.4 %collective-permute-start.18 = (f32[8,128]{1,0:T(8,128)S(1)}, f32[8,128]{1,0:T(8,128)S(1)}, u32[]{:S(2)}, u32[]{:S(2)}) collective-permute-start(f32[8,128]{1,0:T(8,128)S(1)} %max.20), channel_id=1, source_target_pairs={{0,12},{4,8},{8,4},{12,0},{1,13},{5,9},{9,5},{13,1},{2,14},{6,10},... | collective-permute-start | bytes 12296 | tf_op jit(solution)/shard_map/ppermute | solution.py:530
  54.0 4.5 %collective-permute-start.17 = (f32[8,128]{1,0:T(8,128)S(1)}, f32[8,128]{1,0:T(8,128)S(1)}, u32[]{:S(2)}, u32[]{:S(2)}) collective-permute-start(f32[8,128]{1,0:T(8,128)S(1)} %max.20), channel_id=1, source_target_pairs={{0,8},{4,12},{8,0},{12,4},{1,9},{5,13},{9,1},{13,5},{2,10},{6,14},... | collective-permute-start | bytes 12296 | tf_op jit(solution)/shard_map/ppermute | solution.py:530
  56.0 3.6 %collective-permute-start.16 = (f32[8,128]{1,0:T(8,128)S(1)}, f32[8,128]{1,0:T(8,128)S(1)}, u32[]{:S(2)}, u32[]{:S(2)}) collective-permute-start(f32[8,128]{1,0:T(8,128)S(1)} %max.20), channel_id=1, source_target_pairs={{0,4},{4,0},{8,12},{12,8},{1,5},{5,1},{9,13},{13,9},{2,6},{6,2},{1... | collective-permute-start | bytes 12296 | tf_op jit(solution)/shard_map/ppermute | solution.py:530

commit v5 on v4

--- a/solution.py
+++ b/solution.py
@@ -1,3 +1,5 @@
+import functools
+
 import jax
 import jax.numpy as jnp
 from jax import lax
@@ -89,36 +91,35 @@
 
 
 def spread_kernel(row_ref, col_ref, obs_ref, out_ref):
-    shots, nrec = row_ref.shape
-    rows, cols = out_ref.shape[2:]
-    steps = obs_ref.shape[1]
+    nrec = row_ref.shape[1]
+    rows, cols = out_ref.shape[1:]
+    steps = obs_ref.shape[0]
     row_iota = lax.broadcasted_iota(jnp.int32, (rows, nrec), 0)
     col_iota = lax.broadcasted_iota(jnp.int32, (cols, nrec), 0)
-    dims = (((1,), (1,)), ((), ()))
-    for shot in range(shots):
-        at_row = (row_ref[shot : shot + 1, :] == row_iota).astype(jnp.float32)
-        at_row = at_row.astype(jnp.bfloat16)
-        at_col = col_ref[shot : shot + 1, :] == col_iota
-        ones = at_col.astype(jnp.float32).astype(jnp.bfloat16)
-        out_ref[shot, 0] = lax.dot_general(
-            at_row, ones, dims, preferred_element_type=jnp.float32
+    at_row = (row_ref[...] == row_iota).astype(jnp.float32).astype(jnp.bfloat16)
+    at_col = col_ref[...] == col_iota
+    parts = [(0, at_col.astype(jnp.float32).astype(jnp.bfloat16))]
+    for step in range(steps):
+        obs = obs_ref[step : step + 1, :]
+        high = obs.astype(jnp.bfloat16).astype(jnp.float32)
+        rest = obs - high
+        middle = rest.astype(jnp.bfloat16).astype(jnp.float32)
+        for piece in (high, middle, rest - middle):
+            parts.append((1 + step, jnp.where(at_col, piece, 0.0).astype(jnp.bfloat16)))
+    sums = [None] * (1 + steps)
+    for start in range(0, len(parts), 2):
+        pair = parts[start : start + 2]
+        both = lax.dot_general(
+            at_row,
+            jnp.concatenate([p for _, p in pair], axis=0),
+            (((1,), (1,)), ((), ())),
+            preferred_element_type=jnp.float32,
         )
-        for step in range(steps):
-            obs = obs_ref[shot, step : step + 1, :]
-            high = obs.astype(jnp.bfloat16).astype(jnp.float32)
-            rest = obs - high
-            middle = rest.astype(jnp.bfloat16).astype(jnp.float32)
-            low = rest - middle
-            total = None
-            for part in (high, middle, low):
-                term = lax.dot_general(
-                    at_row,
-                    jnp.where(at_col, part, 0.0).astype(jnp.bfloat16),
-                    dims,
-                    preferred_element_type=jnp.float32,
-                )
-                total = term if total is None else total + term
-            out_ref[shot, 1 + step] = total
+        for place, (which, _) in enumerate(pair):
+            term = both[:, place * cols : (place + 1) * cols]
+            sums[which] = term if sums[which] is None else sums[which] + term
+    for which, value in enumerate(sums):
+        out_ref[which] = value
 
 
 class Halo:
@@ -139,7 +140,14 @@
         upper = at >= planes
         step = at if inside else (at - planes if upper else planes + at)
         if which == VEL:
-            return self.vel[at + 2]
+            block, lane = (0, 1, 2)[(at + planes) // planes], (at + planes) % planes
+            own = self.cols // len(self.vel)
+            column = lax.broadcasted_iota(jnp.int32, (self.rows, self.cols), 1)
+            value = None
+            for index, part in enumerate(self.vel):
+                shifted = pltpu.roll(part[block], (index - lane) * own % self.cols, 1)
+                value = shifted if value is None else jnp.where(column >= index * own, shifted, value)
+            return value
         if which == LAP:
             return self.pick(self.third_by, upper, shots + shot)
         if which == LATE:
@@ -166,7 +174,7 @@
 
 
 def halo_of(refs):
-    first, second, late, fe, fo, se, so, te, to, vel = refs
+    first, second, late, fe, fo, se, so, te, to, *vel = refs
     return Halo(first, second, late, (fe, fo), (se, so), (te, to), vel)
 
 
@@ -265,46 +273,15 @@
         to_odd[shots + shot] = jnp.where(even, ends[1], ends[0])
 
 
-def prepare_kernel(
-    first,
-    second,
-    late,
-    first_even,
-    first_odd,
-    second_even,
-    second_odd,
-    third_even,
-    third_odd,
-    vel,
-    edges,
-    dense,
-    source_at,
-    wavelet,
-    lap_out,
-    base_out,
-    turn_out,
-    late_out,
-    last_out,
-    low_out,
-    stiff_out,
-    cz,
-    cx,
-    cp,
-    cm,
-    now_buf,
-    buoy_buf,
-):
-    halo = Halo(
-        first,
-        second,
-        late,
-        (first_even, first_odd),
-        (second_even, second_odd),
-        (third_even, third_odd),
-        vel,
-    )
+def prepare_kernel(halos, shots, *refs):
+    halo = halo_of(refs[:halos])
+    edges, *dense = refs[halos : halos + 1 + shots]
+    source_at, wavelet = refs[halos + 1 + shots : halos + 3 + shots]
+    outs = refs[halos + 3 + shots :]
+    lap_out, base_out, turn_out, late_out, last_out, low_out, stiff_out = outs[:7]
+    cz, cx, cp, cm, now_buf, buoy_buf = outs[7:]
     lat_at = lax.axis_index("lat")
-    rows, cols, shots, planes = halo.rows, halo.cols, halo.shots, halo.planes
+    rows, cols, planes = halo.rows, halo.cols, halo.planes
     wide = rows + 2 * PAD
     where_is = {item: index for index, item in enumerate(halo.plane_list())}
 
@@ -356,32 +333,17 @@
                 late_out[shot, at + 1] = (
                     2.0 * newest
                     - whole(LATE, shot, at)
-                    - dense[shot, 2, (at + 1) * wide : (at + 2) * wide]
+                    - dense[shot][2, (at + 1) * wide : (at + 2) * wide]
                 )
             if 0 <= at < planes:
-                low_out[shot, at] = newest + dense[shot, 1, (at + 1) * wide : (at + 2) * wide]
-
-
-def update_kernel(
-    stiff,
-    lap,
-    base,
-    turn,
-    late,
-    last,
-    low,
-    dense,
-    cz_ref,
-    cx_ref,
-    cp_ref,
-    cm_ref,
-    out,
-    second,
-    scaled,
-    upper,
-    lap_second,
-):
-    shots, planes = low.shape[:2]
+                low_out[shot, at] = newest + dense[shot][1, (at + 1) * wide : (at + 2) * wide]
+
+
+def update_kernel(shots, *refs):
+    stiff, lap, base, turn, late, last, low, cz_ref, cx_ref, cp_ref, cm_ref = refs[:11]
+    dense = refs[11 : 11 + shots]
+    out, second, scaled, upper, lap_second = refs[11 + shots :]
+    planes = low.shape[1]
     wide, _ = low.shape[2:]
     cz = lambda k: cz_ref[k]
     cx = lambda k: cx_ref[k]
@@ -395,7 +357,7 @@
     for at in range(1, planes + 3):
         rigid = stiff[at]
         for shot in range(shots):
-            hits = dense[shot, 0, (at - 1) * wide : at * wide]
+            hits = dense[shot][0, (at - 1) * wide : at * wide]
             lap_now = laplace(lambda k: second[shot, k], at, cz, cx, cp, cm)
             third = 2.0 * second[shot, at] + turn[shot, at - 1] + rigid * lap_now
             adj = late[shot, at - 1] + hits * third
@@ -409,7 +371,7 @@
     for at in range(2, planes + 2):
         total = None
         for shot in range(shots):
-            hits = dense[shot, 0, (at - 1) * wide : at * wide]
+            hits = dense[shot][0, (at - 1) * wide : at * wide]
             lower = 2.0 * upper[shot, at - 1] - low[shot, at - 2] + hits * second[shot, at]
             lower = lower + laplace(lambda k: scaled[shot, k], at, cz, cx, cp, cm)
             term = upper[shot, at - 1] * lap_second[shot, at - 2] + lower * lap[shot, at]
@@ -440,7 +402,7 @@
     largest[...] = tile_max(value)
 
 
-def widen_kernel(total, mine, got, out):
+def widen_kernel(total, mine, got, out, largest):
     planes, rows, _ = total.shape
     wide = rows + 2 * PAD
     lat_at = lax.axis_index("lat")
@@ -450,7 +412,7 @@
         out[start : start + PAD] = jnp.where(lat_at == 1, part, 0.0)
         out[start + PAD : start + PAD + rows] = total[at]
         out[start + PAD + rows : start + wide] = jnp.where(lat_at == 0, part, 0.0)
-    out[planes * wide :] = jnp.maximum(mine[planes * PAD :], got[planes * PAD :])
+    largest[...] = jnp.maximum(mine[planes * PAD :], got[planes * PAD :])
 
 
 def restiff_kernel(stiff, mine, by_even, by_odd, largest, velocity, stiff_out, vel_out):
@@ -513,7 +475,6 @@
     evens = even_pairs(depth_count)
     odds = odd_pairs(depth_count)
     swap = [(0, 1), (1, 0)]
-    own_width = velocity.shape[2]
     wide = rows + 2 * PAD
 
     def shot_terms(block):
@@ -538,7 +499,7 @@
         step = first
         while step < depth_count:
             pairs = [(i, i ^ step) for i in range(depth_count)]
-            value = jnp.maximum(value, lax.ppermute(value, "depth", pairs))
+            value = jnp.maximum(value, send(value, "depth", pairs))
             step *= 2
         return value
 
@@ -590,13 +551,6 @@
     else:
         gathered = lax.all_gather(lines, "shot")
         parts = [gathered[k] for k in range(shot_count)]
-    full_velocity = jnp.stack(
-        [
-            jnp.concatenate([p[block, :, k * own_width : (k + 1) * own_width] for p in parts], axis=1)
-            for block in range(3)
-            for k in range(planes)
-        ]
-    )
     small = (planes + 1, wide, cols)
     to_even, to_odd = on_chip(
         third_kernel,
@@ -623,18 +577,26 @@
         return jnp.where(inside, plane_at * wide + row_at, -1), cells % cols
 
     row_id, col_id = place(receiver_cell, 1)
-    spread_shape = (shots, 3, (planes + 2) * wide, cols)
-    (dense,) = on_chip(
-        spread_kernel,
-        [spread_shape],
-        (row_id, col_id, observed),
-        flops=14 * shots * spread_shape[2] * cols * row_id.shape[1],
-        limit=24,
-    )
+    spread_shape = (3, (planes + 2) * wide, cols)
+
+    def receivers(shot):
+        (out,) = on_chip(
+            spread_kernel,
+            [spread_shape],
+            (row_id[shot : shot + 1], col_id[shot : shot + 1], observed[shot]),
+            flops=14 * spread_shape[1] * cols * row_id.shape[1],
+            limit=24,
+        )
+        return out
+
+    dense = []
+    for shot in range(shots):
+        dense.append(receivers(shot))
+    dense = tuple(dense)
     source_at = jnp.stack(place(source_cell, 2), axis=1)
 
     halos = (first, second, late, first_even, first_odd, second_even, second_odd)
-    halos += (third_even, third_odd, full_velocity)
+    halos += (third_even, third_odd) + tuple(parts)
     strips = shots * (4 * planes + 16) + 2 * (planes + 4)
     (edges,) = on_chip(edge_kernel, [(strips * PAD, cols)], halos)
     edges = send(edges, "lat", swap)
@@ -655,9 +617,9 @@
         (planes + 3,) + model,
         (planes + 3,) + model,
     ]
-    vectors = halos + (edges, dense)
+    vectors = halos + (edges,) + dense
     prepared = pl.pallas_call(
-        prepare_kernel,
+        functools.partial(prepare_kernel, len(halos), shots),
         out_shape=tuple(pltpu.VMEM(shape, jnp.float32) for shape in prepared_shapes),
         in_specs=[spec] * len(vectors) + [scalars, scalars],
         out_specs=tuple(spec for _ in prepared_shapes),
@@ -676,9 +638,9 @@
 
     def gradient_of(stiff):
         (out,) = on_chip(
-            update_kernel,
+            functools.partial(update_kernel, shots),
             [(planes, rows, cols)],
-            (stiff, lap, base, turn, late, last, low, dense, cz, cx, cp, cm),
+            (stiff, lap, base, turn, late, last, low, cz, cx, cp, cm) + dense,
             scratch=[
                 (shots, deep) + model,
                 (shots, deep) + model,
@@ -708,10 +670,17 @@
         edge_rows = planes * PAD + 8
         summed, tail = on_chip(sum_kernel, [(planes, rows, cols), (edge_rows, cols)], (mine, other))
         got = lax.ppermute(tail, "lat", swap)
-        (widened,) = on_chip(widen_kernel, [(planes * wide + 8, cols)], (summed, tail, got))
+        widened, largest = on_chip(
+            widen_kernel, [(planes * wide, cols), (8, cols)], (summed, tail, got)
+        )
+        if depth_count & (depth_count - 1):
+            largest = lax.pmax(largest, "depth")
+        else:
+            from_pair = send(largest, "depth", evens)
         by_even = send(widened, "depth", evens)
-        by_odd = send(widened[: planes * wide], "depth", odds)
-        largest = depth_max(widened[planes * wide :], by_even[planes * wide :])
+        by_odd = send(widened, "depth", odds)
+        if not depth_count & (depth_count - 1):
+            largest = depth_max(largest, from_pair)
         stiff, own_velocity = on_chip(
             restiff_kernel,
             [stiff.shape, velocity.shape],

time: 60.8 us -> 63 us (1.036)
  starting transfers between devices: 25.7 us -> 28.3 us
  Pallas kernels: 11.2 us -> 9.49 us
  local copies, waits for them, and re-layouts: 1.02 us -> 2.24 us
    ppermute x11 -> x13, waiting for transfers between devices: 6.1 us -> 10.3 us  [send(): return lax.ppermute(block, axis, pairs)]
    ppermute x11 -> x13, starting transfers between devices: 17.8 us -> 21.3 us  [send(): return lax.ppermute(block, axis, pairs)]
    ppermute x1 -> x0, waiting for transfers between devices: 3.32 us -> none  [depth_max(): value = jnp.maximum(value, lax.ppermute(value, 'depth', pairs))]
    pallas_call x10 -> x11, Pallas kernels: 7.84 us -> 6.14 us  [on_chip(): pl.pallas_call(kernel, out_shape=outs, in_specs=[spec] * len(args), out_s...]
    unnamed x10, local copies, waits for them, and re-layouts: 0.72 us -> 2.02 us
    ppermute x1 -> x0, starting transfers between devices: 1.19 us -> none  [depth_max(): value = jnp.maximum(value, lax.ppermute(value, 'depth', pairs))]
  transfers between devices with their start and end apart: 19 -> 20, of which waited for: 12 -> 12; matrix products, arithmetic and copies ran while one was open for 2% -> 1% of each run, Pallas kernels for 10% -> 7%
where the time goes in v5:
time: 63 us; the launch traced here: 62.6 us
  starting transfers between devices  28.3 us (45%)
  waiting for transfers between devices  21.4 us (34%)
  Pallas kernels  9.49 us (15%)
  local copies, waits for them, and re-layouts  2.24 us (4%)
  between operations  0.87 us (1%)
    ppermute x13, starting transfers between devices, send(): return lax.ppermute(block, axis, pairs)  21.3 us
    ppermute x13, waiting for transfers between devices, send(): return lax.ppermute(block, axis, pairs)  10.3 us
    ppermute x2, waiting for transfers between devices, shot_terms(): return (block, lax.ppermute(block, 'shot', swap))  6.43 us
    pallas_call x11, Pallas kernels, on_chip(): pl.pallas_call(kernel, out_shape=outs, in_specs=[spec] * len(args), out_s...  6.14 us
    ppermute x3, starting transfers between devices, depth_max(): lax.ppermute(value, 'depth', [(i, i ^ k) for i in range(depth_count)])  4.39 us
    ppermute x2, starting transfers between devices, shot_terms(): return (block, lax.ppermute(block, 'shot', swap))  2.46 us
    ppermute x3, waiting for transfers between devices, depth_max(): lax.ppermute(value, 'depth', [(i, i ^ k) for i in range(depth_count)])  2.37 us
    pallas_call x2, Pallas kernels, load(): pl.pallas_call(kernel, out_shape=tuple((pltpu.VMEM(shape, jnp.float32) fo...  2.13 us
  transfers between devices with their start and end apart: 20, of which 12 were waited for; matrix products, arithmetic and copies ran while one was open for 1% of the time, Pallas kernels for 7%

profile of v5, /device:TPU:0, one launch (start us, length us, event | category | flops | bytes accessed | tf_op | source)
XLA Modules:
  0.0 62.6 jit_solution(1207542918090040494)
XLA Ops:
  0.6 1.0 %shard_map.113 = (f32[7,64,128]{2,1,0:T(8,128)S(1)}, f32[48,128]{1,0:T(8,128)S(1)}) custom-call(f32[2,2,64,128]{3,2,1,0:T(8,128)} %now.1, f32[2,64,128]{2,1,0:T(8,128)} %dens.1, f32[2,64,64]{2,1,0:T(8,128)} %velocity.1), custom_call_target="tpu_custom_call" | custom-call | tf_op jit(solution)/shard_map/pallas_call | solution.py:510
  1.7 0.7 %collective-permute-start.1 = (f32[7,64,128]{2,1,0:T(8,128)S(1)}, f32[7,64,128]{2,1,0:T(8,128)S(1)}, u32[]{:S(2)}, u32[]{:S(2)}) collective-permute-start(f32[7,64,128]{2,1,0:T(8,128)S(1)} %get-tuple-element.27.first.refs_0_), channel_id=1, source_target_pairs={{4,8},{8,4},{5,9},{9,5},{6,10},{10,6},{7,11},{11,7},{20,24},{24,20... | collective-permute-start | bytes 688136 | tf_op jit(solution)/shard_map/ppermute | solution.py:32
  2.4 5.9 %collective-permute-start = (f32[7,64,128]{2,1,0:T(8,128)S(1)}, f32[7,64,128]{2,1,0:T(8,128)S(1)}, u32[]{:S(2)}, u32[]{:S(2)}) collective-permute-start(f32[7,64,128]{2,1,0:T(8,128)S(1)} %get-tuple-element.27.first.refs_0_), channel_id=1, source_target_pairs={{0,4},{4,0},{8,12},{12,8},{1,5},{5,1},{9,13},{13,9},{2,6},{6,2},{1... | collective-permute-start | bytes 688136 | tf_op jit(solution)/shard_map/ppermute | solution.py:32
  8.3 1.1 %shard_map.114 = (f32[8,64,128]{2,1,0:T(8,128)S(1)}, f32[2,2,64,128]{3,2,1,0:T(8,128)S(1)}) custom-call(f32[2,2,64,128]{3,2,1,0:T(8,128)} %prev.1, f32[2,2,64,128]{3,2,1,0:T(8,128)} %last.1, f32[2,2,64,128]{3,2,1,0:T(8,128)} %late.1), custom_call_target="tpu_custom_call" | custom-call | tf_op jit(solution)/shard_map/pallas_call | solution.py:510
  9.4 0.7 %collective-permute-start.3 = (f32[8,64,128]{2,1,0:T(8,128)S(1)}, f32[8,64,128]{2,1,0:T(8,128)S(1)}, u32[]{:S(2)}, u32[]{:S(2)}) collective-permute-start(f32[8,64,128]{2,1,0:T(8,128)S(1)} %get-tuple-element.28.refs_1_), channel_id=1, source_target_pairs={{4,8},{8,4},{5,9},{9,5},{6,10},{10,6},{7,11},{11,7},{20,24},{24,20... | collective-permute-start | bytes 786440 | tf_op jit(solution)/shard_map/ppermute | solution.py:32
  10.1 1.8 %collective-permute-start.2 = (f32[8,64,128]{2,1,0:T(8,128)S(1)}, f32[8,64,128]{2,1,0:T(8,128)S(1)}, u32[]{:S(2)}, u32[]{:S(2)}) collective-permute-start(f32[8,64,128]{2,1,0:T(8,128)S(1)} %get-tuple-element.28.refs_1_), channel_id=1, source_target_pairs={{0,4},{4,0},{8,12},{12,8},{1,5},{5,1},{9,13},{13,9},{2,6},{6,2},{1... | collective-permute-start | bytes 786440 | tf_op jit(solution)/shard_map/ppermute | solution.py:32
  11.8 0.0 collective-permute-start.4
  11.9 0.7 %copy-done.3 = s32[2,2048]{1,0:T(2,128)S(1)} copy-done((s32[2,2048]{1,0:T(2,128)S(1)}, s32[2,2048]{1,0:T(2,128)}, u32[]{:S(2)}) %copy-start.3) | copy-done | bytes 16408
  12.6 0.1 and_select_fusion
  12.7 0.0 copy-start.2
  12.7 0.7 %copy-done.2 = f32[2,2,2048]{2,1,0:T(2,128)S(1)} copy-done((f32[2,2,2048]{2,1,0:T(2,128)S(1)}, f32[2,2,2048]{2,1,0:T(2,128)}, u32[]{:S(2)}) %copy-start.2) | copy-done | bytes 32792
  13.5 0.0 collective-permute-done.1.by_odd.refs_4_
  13.5 1.3 %collective-permute-done.by_even.refs_3_ = f32[7,64,128]{2,1,0:T(8,128)S(1)} collective-permute-done((f32[7,64,128]{2,1,0:T(8,128)S(1)}, f32[7,64,128]{2,1,0:T(8,128)S(1)}, u32[]{:S(2)}, u32[]{:S(2)}) %collective-permute-start) | collective-permute-done | bytes 229408 | tf_op jit(solution)/shard_map/ppermute | solution.py:32
  14.8 0.0 copy-start.4
  14.8 1.6 %collective-permute-start.7 = (f32[3,64,128]{2,1,0:T(8,128)S(1)}, f32[3,64,128]{2,1,0:T(8,128)S(1)}, u32[]{:S(2)}, u32[]{:S(2)}) collective-permute-start(f32[3,64,128]{2,1,0:T(8,128)S(1)} %pad_maximum_fusion), channel_id=1, source_target_pairs={{0,2},{2,0},{1,3},{3,1},{4,6},{6,4},{5,7},{7,5},{8,10},{10,8},{9,1... | collective-permute-start | bytes 294920 | tf_op jit(solution)/shard_map/ppermute | solution.py:32
  16.3 0.0 copy-done.4
  16.4 0.0 collective-permute-done.4.edges
  16.4 0.2 shard_map.115
  16.6 2.1 %collective-permute-start.5 = (f32[4,64,128]{2,1,0:T(8,128)S(1)}, f32[4,64,128]{2,1,0:T(8,128)S(1)}, u32[]{:S(2)}, u32[]{:S(2)}) collective-permute-start(f32[4,64,128]{2,1,0:T(8,128)S(1)} %get-tuple-element.31), channel_id=1, source_target_pairs={{0,4},{4,0},{8,12},{12,8},{1,5},{5,1},{9,13},{13,9},{2,6},{6,2},{1... | collective-permute-start | bytes 393224 | tf_op jit(solution)/shard_map/ppermute | solution.py:32
  18.7 0.7 %collective-permute-start.6 = (f32[4,64,128]{2,1,0:T(8,128)S(1)}, f32[4,64,128]{2,1,0:T(8,128)S(1)}, u32[]{:S(2)}, u32[]{:S(2)}) collective-permute-start(f32[4,64,128]{2,1,0:T(8,128)S(1)} %get-tuple-element.32), channel_id=1, source_target_pairs={{4,8},{8,4},{5,9},{9,5},{6,10},{10,6},{7,11},{11,7},{20,24},{24,20... | collective-permute-start | bytes 393224 | tf_op jit(solution)/shard_map/ppermute | solution.py:32
  19.4 0.1 collective-permute-done.7
  19.5 0.0 collective-permute-done.3.refs_6_
  19.5 0.7 %collective-permute-done.2.refs_5_ = f32[8,64,128]{2,1,0:T(8,128)S(1)} collective-permute-done((f32[8,64,128]{2,1,0:T(8,128)S(1)}, f32[8,64,128]{2,1,0:T(8,128)S(1)}, u32[]{:S(2)}, u32[]{:S(2)}) %collective-permute-start.2) | collective-permute-done | bytes 262176 | tf_op jit(solution)/shard_map/ppermute | solution.py:32
  20.2 1.8 %collective-permute-done.5.refs_7_ = f32[4,64,128]{2,1,0:T(8,128)S(1)} collective-permute-done((f32[4,64,128]{2,1,0:T(8,128)S(1)}, f32[4,64,128]{2,1,0:T(8,128)S(1)}, u32[]{:S(2)}, u32[]{:S(2)}) %collective-permute-start.5) | collective-permute-done | bytes 131104 | tf_op jit(solution)/shard_map/ppermute | solution.py:32
  22.0 0.0 collective-permute-done.6.refs_8_
  22.0 0.1 shard_map.116
  22.1 0.1 collective-permute-start.8
  22.2 1.6 %shard_map.118.refs_13_.refs_12_ = f32[3,320,128]{2,1,0:T(8,128)S(1)} custom-call(s32[1,2048]{1,0:T(1,128)S(1)} %get-tuple-element.67.row_ref, s32[1,2048]{1,0:T(1,128)S(1)} %get-tuple-element.58.col_ref, f32[2,2048]{1,0:T(2,128)S(1)} %get-tuple-element.56.obs_ref), custom_call_target="tpu_custom_call" | custom-call | flops 1174405120 | bytes 32768 | tf_op jit(solution)/shard_map/pallas_call | solution.py:40
  23.8 0.1 copy.12
  23.9 0.1 copy.13
  24.0 1.6 %shard_map.117.refs_12_.refs_11_ = f32[3,320,128]{2,1,0:T(8,128)S(1)} custom-call(s32[1,2048]{1,0:T(1,128)S(1)} %get-tuple-element.66.row_ref, s32[1,2048]{1,0:T(1,128)S(1)} %get-tuple-element.59.col_ref, f32[2,2048]{1,0:T(2,128)S(1)} %get-tuple-element.57.obs_ref), custom_call_target="tpu_custom_call" | custom-call | flops 1174405120 | bytes 32768 | tf_op jit(solution)/shard_map/pallas_call | solution.py:40
  25.5 0.0 copy-start.1
  25.6 0.1 pad_add_fusion.refs_14_
  25.6 0.0 collective-permute-done.8.refs_11_
  25.6 0.6 copy-done.1
  26.2 1.2 %prepare.1 = (f32[2,6,80,128]{3,2,1,0:T(8,128)S(1)}, f32[2,6,80,128]{3,2,1,0:T(8,128)S(1)}, f32[2,4,80,128]{3,2,1,0:T(8,128)S(1)}, f32[2,4,80,128]{3,2,1,0:T(8,1...) custom-call(f32[7,64,128]{2,1,0:T(8,128)S(1)} %get-tuple-element.27., ...), custom_call_target="tpu_custom_call" | custom-call | tf_op jit(solution)/shard_map/prepare/pallas_call | solution.py:621
  27.4 0.8 %shard_map.119.mine = f32[2,64,128]{2,1,0:T(8,128)S(1)} custom-call(f32[6,80,128]{2,1,0:T(8,128)S(1)} %get-tuple-element.33.refs_0_.stiff, f32[2,6,80,128]{3,2,1,0:T(8,128)S(1)} %get-tuple-element.34.refs_1_, f32[2,6,80,128]{3,2,1,0:T(8,128)S(1)} %get-tuple-element.35.refs_2_, f32[2,4,80,128]{3,2,1,0:T(8,128)S(1)} %get-tuple-element.36.refs_3_, ...), custom_call_target="tpu_custom_call" | custom-call | bytes 4341760 | tf_op jit(solution)/shard_map/pallas_call | solution.py:40
  28.3 1.6 %collective-permute-start.9 = (f32[2,64,128]{2,1,0:T(8,128)S(1)}, f32[2,64,128]{2,1,0:T(8,128)S(1)}, u32[]{:S(2)}, u32[]{:S(2)}) collective-permute-start(f32[2,64,128]{2,1,0:T(8,128)S(1)} %shard_map.119.mine), channel_id=1, source_target_pairs={{0,2},{2,0},{1,3},{3,1},{4,6},{6,4},{5,7},{7,5},{8,10},{10,8},{9,1... | collective-permute-start | bytes 196616 | tf_op jit(solution)/shard_map/ppermute | solution.py:482
  29.8 3.0 %collective-permute-done.9.other = f32[2,64,128]{2,1,0:T(8,128)S(1)} collective-permute-done((f32[2,64,128]{2,1,0:T(8,128)S(1)}, f32[2,64,128]{2,1,0:T(8,128)S(1)}, u32[]{:S(2)}, u32[]{:S(2)}) %collective-permute-start.9) | collective-permute-done | bytes 65568 | tf_op jit(solution)/shard_map/ppermute | solution.py:482
  32.8 0.0 copy-start
  32.8 0.1 collective-permute-start.10
  32.9 1.2 %collective-permute-done.10.got = f32[24,128]{1,0:T(8,128)S(1)} collective-permute-done((f32[24,128]{1,0:T(8,128)S(1)}, f32[24,128]{1,0:T(8,128)S(1)}, u32[]{:S(2)}, u32[]{:S(2)}) %collective-permute-start.10) | collective-permute-done | bytes 12320 | tf_op jit(solution)/shard_map/ppermute | solution.py:672
  34.1 0.7 %collective-permute-start.12 = (f32[160,128]{1,0:T(8,128)S(1)}, f32[160,128]{1,0:T(8,128)S(1)}, u32[]{:S(2)}, u32[]{:S(2)}) collective-permute-start(f32[160,128]{1,0:T(8,128)S(1)} %get-tuple-element.46.mine), channel_id=1, source_target_pairs={{4,8},{8,4},{5,9},{9,5},{6,10},{10,6},{7,11},{11,7},{20,24},{24,20... | collective-permute-start | bytes 245768 | tf_op jit(solution)/shard_map/ppermute | solution.py:32
  34.8 5.5 %collective-permute-start.11 = (f32[160,128]{1,0:T(8,128)S(1)}, f32[160,128]{1,0:T(8,128)S(1)}, u32[]{:S(2)}, u32[]{:S(2)}) collective-permute-start(f32[160,128]{1,0:T(8,128)S(1)} %get-tuple-element.46.mine), channel_id=1, source_target_pairs={{0,4},{4,0},{8,12},{12,8},{1,5},{5,1},{9,13},{13,9},{2,6},{6,2},{1... | collective-permute-start | bytes 245768 | tf_op jit(solution)/shard_map/ppermute | solution.py:32
  40.3 0.1 collective-permute-start.13
  40.4 3.5 %collective-permute-done.13 = f32[8,128]{1,0:T(8,128)S(1)} collective-permute-done((f32[8,128]{1,0:T(8,128)S(1)}, f32[8,128]{1,0:T(8,128)S(1)}, u32[]{:S(2)}, u32[]{:S(2)}) %collective-permute-start.13) | collective-permute-done | bytes 4128 | tf_op jit(solution)/shard_map/ppermute | solution.py:32
  43.9 1.7 %collective-permute-start.14 = (f32[8,128]{1,0:T(8,128)S(1)}, f32[8,128]{1,0:T(8,128)S(1)}, u32[]{:S(2)}, u32[]{:S(2)}) collective-permute-start(f32[8,128]{1,0:T(8,128)S(1)} %max.18), channel_id=1, source_target_pairs={{0,8},{4,12},{8,0},{12,4},{1,9},{5,13},{9,1},{13,5},{2,10},{6,14},... | collective-permute-start | bytes 12296 | tf_op jit(solution)/shard_map/ppermute | solution.py:32
  45.6 2.8 %collective-permute-done.14 = f32[8,128]{1,0:T(8,128)S(1)} collective-permute-done((f32[8,128]{1,0:T(8,128)S(1)}, f32[8,128]{1,0:T(8,128)S(1)}, u32[]{:S(2)}, u32[]{:S(2)}) %collective-permute-start.14) | collective-permute-done | bytes 4128 | tf_op jit(solution)/shard_map/ppermute | solution.py:32
  48.4 0.0 collective-permute-done.12.by_odd
  48.4 0.0 collective-permute-done.11.by_even
  48.4 0.0 copy-done
  48.4 0.2 shard_map.122
  48.6 0.8 %shard_map.123.mine = f32[2,64,128]{2,1,0:T(8,128)S(1)} custom-call(f32[6,80,128]{2,1,0:T(8,128)S(1)} %get-tuple-element.48.refs_0_, f32[2,6,80,128]{3,2,1,0:T(8,128)S(1)} %get-tuple-element.34.refs_1_, f32[2,6,80,128]{3,2,1,0:T(8,128)S(1)} %get-tuple-element.35.refs_2_, f32[2,4,80,128]{3,2,1,0:T(8,128)S(1)} %get-tuple-element.36.refs_3_, ...), custom_call_target="tpu_custom_call" | custom-call | bytes 4341760 | tf_op jit(solution)/shard_map/pallas_call | solution.py:40
  49.5 0.9 %collective-permute-start.15 = (f32[2,64,128]{2,1,0:T(8,128)S(1)}, f32[2,64,128]{2,1,0:T(8,128)S(1)}, u32[]{:S(2)}, u32[]{:S(2)}) collective-permute-start(f32[2,64,128]{2,1,0:T(8,128)S(1)} %shard_map.123.mine), channel_id=1, source_target_pairs={{0,2},{2,0},{1,3},{3,1},{4,6},{6,4},{5,7},{7,5},{8,10},{10,8},{9,1... | collective-permute-start | bytes 196616 | tf_op jit(solution)/shard_map/ppermute | solution.py:482
  50.4 3.4 %collective-permute-done.15.other = f32[2,64,128]{2,1,0:T(8,128)S(1)} collective-permute-done((f32[2,64,128]{2,1,0:T(8,128)S(1)}, f32[2,64,128]{2,1,0:T(8,128)S(1)}, u32[]{:S(2)}, u32[]{:S(2)}) %collective-permute-start.15) | collective-permute-done | bytes 65568 | tf_op jit(solution)/shard_map/ppermute | solution.py:482
  53.8 0.1 collective-permute-start.16
  53.9 1.2 %collective-permute-done.16 = f32[8,128]{1,0:T(8,128)S(1)} collective-permute-done((f32[8,128]{1,0:T(8,128)S(1)}, f32[8,128]{1,0:T(8,128)S(1)}, u32[]{:S(2)}, u32[]{:S(2)}) %collective-permute-start.16) | collective-permute-done | bytes 4128 | tf_op jit(solution)/shard_map/ppermute | solution.py:660
  55.0 2.3 %collective-permute-start.19 = (f32[8,128]{1,0:T(8,128)S(1)}, f32[8,128]{1,0:T(8,128)S(1)}, u32[]{:S(2)}, u32[]{:S(2)}) collective-permute-start(f32[8,128]{1,0:T(8,128)S(1)} %max.20), channel_id=1, source_target_pairs={{0,12},{4,8},{8,4},{12,0},{1,13},{5,9},{9,5},{13,1},{2,14},{6,10},... | collective-permute-start | bytes 12296 | tf_op jit(solution)/shard_map/ppermute | solution.py:491
  57.3 0.1 collective-permute-start.18
  57.4 2.0 %collective-permute-start.17 = (f32[8,128]{1,0:T(8,128)S(1)}, f32[8,128]{1,0:T(8,128)S(1)}, u32[]{:S(2)}, u32[]{:S(2)}) collective-permute-start(f32[8,128]{1,0:T(8,128)S(1)} %max.20), channel_id=1, source_target_pairs={{0,4},{4,0},{8,12},{12,8},{1,5},{5,1},{9,13},{13,9},{2,6},{6,2},{1... | collective-permute-start | bytes 12296 | tf_op jit(solution)/shard_map/ppermute | solution.py:491
  59.4 1.0 %collective-permute-done.19 = f32[8,128]{1,0:T(8,128)S(1)} collective-permute-done((f32[8,128]{1,0:T(8,128)S(1)}, f32[8,128]{1,0:T(8,128)S(1)}, u32[]{:S(2)}, u32[]{:S(2)}) %collective-permute-start.19) | collective-permute-done | bytes 4128 | tf_op jit(solution)/shard_map/ppermute | solution.py:491
  60.4 1.4 %collective-permute-done.18 = f32[8,128]{1,0:T(8,128)S(1)} collective-permute-done((f32[8,128]{1,0:T(8,128)S(1)}, f32[8,128]{1,0:T(8,128)S(1)}, u32[]{:S(2)}, u32[]{:S(2)}) %collective-permute-start.18) | collective-permute-done | bytes 4128 | tf_op jit(solution)/shard_map/ppermute | solution.py:491
  61.8 0.0 collective-permute-done.17
  61.8 0.8 %shard_map.125 = (f32[2,64,64]{2,1,0:T(8,128)}, f32[2,64,64]{2,1,0:T(8,128)}) custom-call(f32[2,64,128]{2,1,0:T(8,128)S(1)} %get-tuple-element.49.total, f32[8,128]{1,0:T(8,128)S(1)} %maximum_maximum_fusion.largest, f32[2,64,64]{2,1,0:T(8,128)S(1)} %get-tuple-element.51.velocity), custom_call_target="tpu_custom_call" | custom-call | bytes 102400 | tf_op jit(solution)/shard_map/pallas_call | solution.py:40
  (15 shorter events, 0.1 us)
Async XLA Ops:
  1.7 11.8 %collective-permute-start.1 = (f32[7,64,128]{2,1,0:T(8,128)S(1)}, f32[7,64,128]{2,1,0:T(8,128)S(1)}, u32[]{:S(2)}, u32[]{:S(2)}) collective-permute-start(f32[7,64,128]{2,1,0:T(8,128)S(1)} %get-tuple-element.27.first.refs_0_), channel_id=1, source_target_pairs={{4,8},{8,4},{5,9},{9,5},{6,10},{10,6},{7,11},{11,7},{20,24},{24,20... | collective-permute-start | bytes 688136 | tf_op jit(solution)/shard_map/ppermute | solution.py:32
  2.4 12.4 %collective-permute-start = (f32[7,64,128]{2,1,0:T(8,128)S(1)}, f32[7,64,128]{2,1,0:T(8,128)S(1)}, u32[]{:S(2)}, u32[]{:S(2)}) collective-permute-start(f32[7,64,128]{2,1,0:T(8,128)S(1)} %get-tuple-element.27.first.refs_0_), channel_id=1, source_target_pairs={{0,4},{4,0},{8,12},{12,8},{1,5},{5,1},{9,13},{13,9},{2,6},{6,2},{1... | collective-permute-start | bytes 688136 | tf_op jit(solution)/shard_map/ppermute | solution.py:32
  9.4 10.1 %collective-permute-start.3 = (f32[8,64,128]{2,1,0:T(8,128)S(1)}, f32[8,64,128]{2,1,0:T(8,128)S(1)}, u32[]{:S(2)}, u32[]{:S(2)}) collective-permute-start(f32[8,64,128]{2,1,0:T(8,128)S(1)} %get-tuple-element.28.refs_1_), channel_id=1, source_target_pairs={{4,8},{8,4},{5,9},{9,5},{6,10},{10,6},{7,11},{11,7},{20,24},{24,20... | collective-permute-start | bytes 786440 | tf_op jit(solution)/shard_map/ppermute | solution.py:32
  10.1 10.2 %collective-permute-start.2 = (f32[8,64,128]{2,1,0:T(8,128)S(1)}, f32[8,64,128]{2,1,0:T(8,128)S(1)}, u32[]{:S(2)}, u32[]{:S(2)}) collective-permute-start(f32[8,64,128]{2,1,0:T(8,128)S(1)} %get-tuple-element.28.refs_1_), channel_id=1, source_target_pairs={{0,4},{4,0},{8,12},{12,8},{1,5},{5,1},{9,13},{13,9},{2,6},{6,2},{1... | collective-permute-start | bytes 786440 | tf_op jit(solution)/shard_map/ppermute | solution.py:32
  11.8 4.5 %collective-permute-start.4 = (f32[48,128]{1,0:T(8,128)S(1)}, f32[48,128]{1,0:T(8,128)S(1)}, u32[]{:S(2)}, u32[]{:S(2)}) collective-permute-start(f32[48,128]{1,0:T(8,128)S(1)} %get-tuple-element.30), channel_id=1, source_target_pairs={{0,1},{1,0},{2,3},{3,2},{4,5},{5,4},{6,7},{7,6},{8,9},{9,8},{10,11... | collective-permute-start | bytes 73736 | tf_op jit(solution)/shard_map/ppermute | solution.py:32
  11.8 0.7 %copy-start.3 = (s32[2,2048]{1,0:T(2,128)S(1)}, s32[2,2048]{1,0:T(2,128)}, u32[]{:S(2)}) copy-start(s32[2,2048]{1,0:T(2,128)} %param.18) | copy-start | bytes 49156
  12.7 0.8 %copy-start.2 = (f32[2,2,2048]{2,1,0:T(2,128)S(1)}, f32[2,2,2048]{2,1,0:T(2,128)}, u32[]{:S(2)}) copy-start(f32[2,2,2048]{2,1,0:T(2,128)} %param.19) | copy-start | bytes 98308
  14.8 1.6 %copy-start.4 = (s32[2]{0:T(128)S(1)}, s32[2]{0:T(128)}, u32[]{:S(2)}) copy-start(s32[2]{0:T(128)} %param.17) | copy-start | bytes 28
  14.8 4.7 %collective-permute-start.7 = (f32[3,64,128]{2,1,0:T(8,128)S(1)}, f32[3,64,128]{2,1,0:T(8,128)S(1)}, u32[]{:S(2)}, u32[]{:S(2)}) collective-permute-start(f32[3,64,128]{2,1,0:T(8,128)S(1)} %pad_maximum_fusion), channel_id=1, source_target_pairs={{0,2},{2,0},{1,3},{3,1},{4,6},{6,4},{5,7},{7,5},{8,10},{10,8},{9,1... | collective-permute-start | bytes 294920 | tf_op jit(solution)/shard_map/ppermute | solution.py:32
  16.6 5.4 %collective-permute-start.5 = (f32[4,64,128]{2,1,0:T(8,128)S(1)}, f32[4,64,128]{2,1,0:T(8,128)S(1)}, u32[]{:S(2)}, u32[]{:S(2)}) collective-permute-start(f32[4,64,128]{2,1,0:T(8,128)S(1)} %get-tuple-element.31), channel_id=1, source_target_pairs={{0,4},{4,0},{8,12},{12,8},{1,5},{5,1},{9,13},{13,9},{2,6},{6,2},{1... | collective-permute-start | bytes 393224 | tf_op jit(solution)/shard_map/ppermute | solution.py:32
  18.7 3.4 %collective-permute-start.6 = (f32[4,64,128]{2,1,0:T(8,128)S(1)}, f32[4,64,128]{2,1,0:T(8,128)S(1)}, u32[]{:S(2)}, u32[]{:S(2)}) collective-permute-start(f32[4,64,128]{2,1,0:T(8,128)S(1)} %get-tuple-element.32), channel_id=1, source_target_pairs={{4,8},{8,4},{5,9},{9,5},{6,10},{10,6},{7,11},{11,7},{20,24},{24,20... | collective-permute-start | bytes 393224 | tf_op jit(solution)/shard_map/ppermute | solution.py:32
  22.1 3.5 %collective-permute-start.8 = (f32[480,128]{1,0:T(8,128)S(1)}, f32[480,128]{1,0:T(8,128)S(1)}, u32[]{:S(2)}, u32[]{:S(2)}) collective-permute-start(f32[480,128]{1,0:T(8,128)S(1)} %shard_map.116), channel_id=1, source_target_pairs={{0,1},{1,0},{2,3},{3,2},{4,5},{5,4},{6,7},{7,6},{8,9},{9,8},{10,11... | collective-permute-start | bytes 737288 | tf_op jit(solution)/shard_map/ppermute | solution.py:32
  25.5 0.7 %copy-start.1 = (f32[2,2]{1,0:T(2,128)S(1)}, f32[2,2]{1,0:T(2,128)}, u32[]{:S(2)}) copy-start(f32[2,2]{1,0:T(2,128)} %refs_15_.1) | copy-start | bytes 52
  28.3 4.6 %collective-permute-start.9 = (f32[2,64,128]{2,1,0:T(8,128)S(1)}, f32[2,64,128]{2,1,0:T(8,128)S(1)}, u32[]{:S(2)}, u32[]{:S(2)}) collective-permute-start(f32[2,64,128]{2,1,0:T(8,128)S(1)} %shard_map.119.mine), channel_id=1, source_target_pairs={{0,2},{2,0},{1,3},{3,1},{4,6},{6,4},{5,7},{7,5},{8,10},{10,8},{9,1... | collective-permute-start | bytes 196616 | tf_op jit(solution)/shard_map/ppermute | solution.py:482
  32.8 15.6 %copy-start = (f32[2,64,64]{2,1,0:T(8,128)S(1)}, f32[2,64,64]{2,1,0:T(8,128)}, u32[]{:S(2)}) copy-start(f32[2,64,64]{2,1,0:T(8,128)} %velocity.1) | copy-start | bytes 98308
  32.8 1.2 %collective-permute-start.10 = (f32[24,128]{1,0:T(8,128)S(1)}, f32[24,128]{1,0:T(8,128)S(1)}, u32[]{:S(2)}, u32[]{:S(2)}) collective-permute-start(f32[24,128]{1,0:T(8,128)S(1)} %get-tuple-element.45.mine), channel_id=1, source_target_pairs={{0,1},{1,0},{2,3},{3,2},{4,5},{5,4},{6,7},{7,6},{8,9},{9,8},{10,11... | collective-permute-start | bytes 36872 | tf_op jit(solution)/shard_map/ppermute | solution.py:672
  34.1 14.3 %collective-permute-start.12 = (f32[160,128]{1,0:T(8,128)S(1)}, f32[160,128]{1,0:T(8,128)S(1)}, u32[]{:S(2)}, u32[]{:S(2)}) collective-permute-start(f32[160,128]{1,0:T(8,128)S(1)} %get-tuple-element.46.mine), channel_id=1, source_target_pairs={{4,8},{8,4},{5,9},{9,5},{6,10},{10,6},{7,11},{11,7},{20,24},{24,20... | collective-permute-start | bytes 245768 | tf_op jit(solution)/shard_map/ppermute | solution.py:32
  34.8 13.6 %collective-permute-start.11 = (f32[160,128]{1,0:T(8,128)S(1)}, f32[160,128]{1,0:T(8,128)S(1)}, u32[]{:S(2)}, u32[]{:S(2)}) collective-permute-start(f32[160,128]{1,0:T(8,128)S(1)} %get-tuple-element.46.mine), channel_id=1, source_target_pairs={{0,4},{4,0},{8,12},{12,8},{1,5},{5,1},{9,13},{13,9},{2,6},{6,2},{1... | collective-permute-start | bytes 245768 | tf_op jit(solution)/shard_map/ppermute | solution.py:32
  40.3 3.6 %collective-permute-start.13 = (f32[8,128]{1,0:T(8,128)S(1)}, f32[8,128]{1,0:T(8,128)S(1)}, u32[]{:S(2)}, u32[]{:S(2)}) collective-permute-start(f32[8,128]{1,0:T(8,128)S(1)} %get-tuple-element.47), channel_id=1, source_target_pairs={{0,4},{4,0},{8,12},{12,8},{1,5},{5,1},{9,13},{13,9},{2,6},{6,2},{1... | collective-permute-start | bytes 12296 | tf_op jit(solution)/shard_map/ppermute | solution.py:32
  43.9 4.5 %collective-permute-start.14 = (f32[8,128]{1,0:T(8,128)S(1)}, f32[8,128]{1,0:T(8,128)S(1)}, u32[]{:S(2)}, u32[]{:S(2)}) collective-permute-start(f32[8,128]{1,0:T(8,128)S(1)} %max.18), channel_id=1, source_target_pairs={{0,8},{4,12},{8,0},{12,4},{1,9},{5,13},{9,1},{13,5},{2,10},{6,14},... | collective-permute-start | bytes 12296 | tf_op jit(solution)/shard_map/ppermute | solution.py:32
  49.5 4.3 %collective-permute-start.15 = (f32[2,64,128]{2,1,0:T(8,128)S(1)}, f32[2,64,128]{2,1,0:T(8,128)S(1)}, u32[]{:S(2)}, u32[]{:S(2)}) collective-permute-start(f32[2,64,128]{2,1,0:T(8,128)S(1)} %shard_map.123.mine), channel_id=1, source_target_pairs={{0,2},{2,0},{1,3},{3,1},{4,6},{6,4},{5,7},{7,5},{8,10},{10,8},{9,1... | collective-permute-start | bytes 196616 | tf_op jit(solution)/shard_map/ppermute | solution.py:482
  53.8 1.2 %collective-permute-start.16 = (f32[8,128]{1,0:T(8,128)S(1)}, f32[8,128]{1,0:T(8,128)S(1)}, u32[]{:S(2)}, u32[]{:S(2)}) collective-permute-start(f32[8,128]{1,0:T(8,128)S(1)} %get-tuple-element.50), channel_id=1, source_target_pairs={{0,1},{1,0},{2,3},{3,2},{4,5},{5,4},{6,7},{7,6},{8,9},{9,8},{10,11... | collective-permute-start | bytes 12296 | tf_op jit(solution)/shard_map/ppermute | solution.py:660
  55.0 5.4 %collective-permute-start.19 = (f32[8,128]{1,0:T(8,128)S(1)}, f32[8,128]{1,0:T(8,128)S(1)}, u32[]{:S(2)}, u32[]{:S(2)}) collective-permute-start(f32[8,128]{1,0:T(8,128)S(1)} %max.20), channel_id=1, source_target_pairs={{0,12},{4,8},{8,4},{12,0},{1,13},{5,9},{9,5},{13,1},{2,14},{6,10},... | collective-permute-start | bytes 12296 | tf_op jit(solution)/shard_map/ppermute | solution.py:491
  57.3 4.5 %collective-permute-start.18 = (f32[8,128]{1,0:T(8,128)S(1)}, f32[8,128]{1,0:T(8,128)S(1)}, u32[]{:S(2)}, u32[]{:S(2)}) collective-permute-start(f32[8,128]{1,0:T(8,128)S(1)} %max.20), channel_id=1, source_target_pairs={{0,8},{4,12},{8,0},{12,4},{1,9},{5,13},{9,1},{13,5},{2,10},{6,14},... | collective-permute-start | bytes 12296 | tf_op jit(solution)/shard_map/ppermute | solution.py:491
  57.4 4.4 %collective-permute-start.17 = (f32[8,128]{1,0:T(8,128)S(1)}, f32[8,128]{1,0:T(8,128)S(1)}, u32[]{:S(2)}, u32[]{:S(2)}) collective-permute-start(f32[8,128]{1,0:T(8,128)S(1)} %max.20), channel_id=1, source_target_pairs={{0,4},{4,0},{8,12},{12,8},{1,5},{5,1},{9,13},{13,9},{2,6},{6,2},{1... | collective-permute-start | bytes 12296 | tf_op jit(solution)/shard_map/ppermute | solution.py:491

commit v6 on v5

--- a/solution.py
+++ b/solution.py
@@ -79,7 +79,7 @@
         )
 
 
-def second_kernel(prev, last, late, out, late_out, sems):
+def second_kernel(prev, last, late, cells, observed, out, late_out, cells_out, observed_out, sems):
     shots, planes, _, _ = prev.shape
     copies = []
     start = 0
@@ -87,7 +87,8 @@
         for shot in range(shots):
             copies.append((field.at[shot], out.at[start : start + planes]))
             start += planes
-    copy_all(copies + [(late, late_out)], sems)
+    copies += [(late, late_out), (cells, cells_out), (observed, observed_out)]
+    copy_all(copies, sems)
 
 
 def spread_kernel(row_ref, col_ref, obs_ref, out_ref):
@@ -402,37 +403,35 @@
     largest[...] = tile_max(value)
 
 
-def widen_kernel(total, mine, got, out, largest):
-    planes, rows, _ = total.shape
-    wide = rows + 2 * PAD
-    lat_at = lax.axis_index("lat")
-    for at in range(planes):
-        part = got[at * PAD : (at + 1) * PAD]
-        start = at * wide
-        out[start : start + PAD] = jnp.where(lat_at == 1, part, 0.0)
-        out[start + PAD : start + PAD + rows] = total[at]
-        out[start + PAD + rows : start + wide] = jnp.where(lat_at == 0, part, 0.0)
-    largest[...] = jnp.maximum(mine[planes * PAD :], got[planes * PAD :])
-
-
-def restiff_kernel(stiff, mine, by_even, by_odd, largest, velocity, stiff_out, vel_out):
+def halo_edge_kernel(by_even, by_odd, out):
+    even = lax.axis_index("depth") % 2 == 0
+    first = lax.axis_index("lat") == 0
+    planes, rows, _ = by_even.shape
+    for side, (a, b) in enumerate(((by_odd, by_even), (by_even, by_odd))):
+        for at in range(planes):
+            value = jnp.where(even, a[at], b[at])
+            start = (side * planes + at) * PAD
+            out[start : start + PAD] = jnp.where(first, value[rows - PAD :], value[:PAD])
+
+
+def restiff_kernel(stiff, total, got, by_even, by_odd, got_halo, largest, velocity, stiff_out, vel_out):
     planes, rows, own = velocity.shape
-    wide = rows + 2 * PAD
     even = lax.axis_index("depth") % 2 == 0
     shot_at = lax.axis_index("shot")
-    cols = mine.shape[1]
+    lat_at = lax.axis_index("lat")
+    cols = total.shape[2]
     scale = jnp.max(jnp.max(largest[...], axis=1, keepdims=True), axis=0, keepdims=True) + EPSILON
     for at in range(-2, planes + 2):
         if 0 <= at < planes:
-            value = mine[at * wide : (at + 1) * wide]
+            value, part = total[at], got[at * PAD : (at + 1) * PAD]
         else:
             upper = at >= planes
             step = at - planes if upper else planes + at
-            first, second = (by_even, by_odd) if upper else (by_odd, by_even)
-            value = jnp.where(
-                even, first[step * wide : (step + 1) * wide], second[step * wide : (step + 1) * wide]
-            )
-        value = value / scale
+            a, b = (by_even, by_odd) if upper else (by_odd, by_even)
+            value = jnp.where(even, a[step], b[step])
+            start = (upper * planes + step) * PAD
+            part = got_halo[start : start + PAD]
+        value = with_rows(part, value, lat_at) / scale
         stiff_out[at + 2] = stiff[at + 2] * jnp.exp(-2.0 * STEP_SIZE * value)
         if 0 <= at < planes:
             shifted = pltpu.roll(value[PAD : PAD + rows], (cols - shot_at * own) % cols, 1)
@@ -467,7 +466,7 @@
     depth_count = lax.axis_size("depth")
     shot_count = lax.axis_size("shot")
     lat_count = lax.axis_size("lat")
-    if planes != 2 or wavelet.shape[1] != 2 or lat_count != 2:
+    if depth_count < 2 or planes != 2 or wavelet.shape[1] != 2 or lat_count != 2:
         raise ValueError("unsupported split")
     depth_at = lax.axis_index("depth")
     lat_at = lax.axis_index("lat")
@@ -482,21 +481,18 @@
             return block, lax.ppermute(block, "shot", swap)
         return lax.psum(block, "shot"), jnp.zeros_like(block)
 
-    def depth_max(value, from_pair=None):
+    def depth_max(value):
         if depth_count & (depth_count - 1):
             return lax.pmax(value, "depth")
-        first = 1 if from_pair is None else 2
-        if depth_count <= 4 and from_pair is None:
+        if depth_count <= 4:
             parts = [
-                lax.ppermute(value, "depth", [(i, i ^ k) for i in range(depth_count)])
+                send(value, "depth", [(i, i ^ k) for i in range(depth_count)])
                 for k in range(1, depth_count)
             ]
             for part in parts:
                 value = jnp.maximum(value, part)
             return value
-        if from_pair is not None:
-            value = jnp.maximum(value, from_pair)
-        step = first
+        step = 1
         while step < depth_count:
             pairs = [(i, i ^ step) for i in range(depth_count)]
             value = jnp.maximum(value, send(value, "depth", pairs))
@@ -509,7 +505,7 @@
     def load(kernel, shapes, args, scratch, count):
         return pl.pallas_call(
             kernel,
-            out_shape=tuple(pltpu.VMEM(shape, jnp.float32) for shape in shapes),
+            out_shape=tuple(pltpu.VMEM(*shape) for shape in shapes),
             in_specs=[hbm] * len(args),
             out_specs=tuple(spec for _ in shapes),
             scratch_shapes=scratch + [pltpu.SemaphoreType.DMA((count,))],
@@ -519,7 +515,7 @@
     own_planes = (shots + 1) * planes
     first, first_edges = load(
         first_kernel,
-        [(own_planes + 1, rows, cols), (own_planes * PAD, cols)],
+        [((own_planes + 1, rows, cols), jnp.float32), ((own_planes * PAD, cols), jnp.float32)],
         (fwd_now, density, velocity),
         [pltpu.VMEM(velocity.shape, jnp.float32)],
         shots + 2,
@@ -527,12 +523,17 @@
     first_odd = send(first, "depth", odds)
     first_even = send(first, "depth", evens)
     first_edges = send(first_edges, "lat", swap)
-    second, late = load(
+    second, late, cells, recorded = load(
         second_kernel,
-        [(2 * shots * planes, rows, cols), adj_late.shape],
-        (fwd_prev, adj_last, adj_late),
+        [
+            ((2 * shots * planes, rows, cols), jnp.float32),
+            (adj_late.shape, jnp.float32),
+            (receiver_cell.shape, receiver_cell.dtype),
+            (observed.shape, jnp.float32),
+        ],
+        (fwd_prev, adj_last, adj_late, receiver_cell, observed),
         [],
-        2 * shots + 1,
+        2 * shots + 3,
     )
     second_odd = send(second, "depth", odds)
     second_even = send(second, "depth", evens)
@@ -576,14 +577,14 @@
         )
         return jnp.where(inside, plane_at * wide + row_at, -1), cells % cols
 
-    row_id, col_id = place(receiver_cell, 1)
+    row_id, col_id = place(cells, 1)
     spread_shape = (3, (planes + 2) * wide, cols)
 
     def receivers(shot):
         (out,) = on_chip(
             spread_kernel,
             [spread_shape],
-            (row_id[shot : shot + 1], col_id[shot : shot + 1], observed[shot]),
+            (row_id[shot : shot + 1], col_id[shot : shot + 1], recorded[shot]),
             flops=14 * spread_shape[1] * cols * row_id.shape[1],
             limit=24,
         )
@@ -669,22 +670,16 @@
             )
         edge_rows = planes * PAD + 8
         summed, tail = on_chip(sum_kernel, [(planes, rows, cols), (edge_rows, cols)], (mine, other))
-        got = lax.ppermute(tail, "lat", swap)
-        widened, largest = on_chip(
-            widen_kernel, [(planes * wide, cols), (8, cols)], (summed, tail, got)
-        )
-        if depth_count & (depth_count - 1):
-            largest = lax.pmax(largest, "depth")
-        else:
-            from_pair = send(largest, "depth", evens)
-        by_even = send(widened, "depth", evens)
-        by_odd = send(widened, "depth", odds)
-        if not depth_count & (depth_count - 1):
-            largest = depth_max(largest, from_pair)
+        got = send(tail, "lat", swap)
+        by_even = send(summed, "depth", evens)
+        by_odd = send(summed, "depth", odds)
+        largest = depth_max(jnp.maximum(tail[planes * PAD :], got[planes * PAD :]))
+        (halo_tail,) = on_chip(halo_edge_kernel, [(2 * planes * PAD, cols)], (by_even, by_odd))
+        got_halo = send(halo_tail, "lat", swap)
         stiff, own_velocity = on_chip(
             restiff_kernel,
             [stiff.shape, velocity.shape],
-            (stiff, widened, by_even, by_odd, largest, own_velocity),
+            (stiff, summed, got, by_even, by_odd, got_halo, largest, own_velocity),
         )
 
 

time: 63 us -> 59.7 us (0.948)
  waiting for transfers between devices: 21.4 us -> 17.8 us
  starting transfers between devices: 28.3 us -> 30.2 us
  local copies, waits for them, and re-layouts: 2.24 us -> 0.83 us
    ppermute x13 -> x19, starting transfers between devices: 21.3 us -> 27.9 us  [send(): return lax.ppermute(block, axis, pairs)]
    ppermute x4 -> x0, starting transfers between devices: 4.46 us -> none  [the longest x3 4.39 us: depth_max(): lax.ppermute(value, 'depth', [(i, i ^ k) for i in range(depth_count)])]
    ppermute x4 -> x0, waiting for transfers between devices: 3.54 us -> none  [the longest x3 2.37 us: depth_max(): lax.ppermute(value, 'depth', [(i, i ^ k) for i in range(depth_count)])]
    unnamed x10 -> x6, local copies, waits for them, and re-layouts: 2.02 us -> 0.61 us
    ppermute x13 -> x19, waiting for transfers between devices: 10.3 us -> 9.9 us  [send(): return lax.ppermute(block, axis, pairs)]
  transfers between devices with their start and end apart: 20 -> 22, of which waited for: 12 -> 11; matrix products, arithmetic and copies ran while one was open for 1% -> 1% of each run, Pallas kernels for 7% -> 8%
where the time goes in v6:
time: 59.7 us; the launch traced here: 59.4 us
  starting transfers between devices  30.2 us (51%)
  waiting for transfers between devices  17.8 us (30%)
  Pallas kernels  9.49 us (16%)
  between operations  0.88 us (1%)
  local copies, waits for them, and re-layouts  0.83 us (1%)
    ppermute x19, starting transfers between devices, send(): return lax.ppermute(block, axis, pairs)  27.9 us
    ppermute x19, waiting for transfers between devices, send(): return lax.ppermute(block, axis, pairs)  9.9 us
    ppermute x2, waiting for transfers between devices, shot_terms(): return (block, lax.ppermute(block, 'shot', swap))  6.7 us
    pallas_call x11, Pallas kernels, on_chip(): pl.pallas_call(kernel, out_shape=outs, in_specs=[spec] * len(args), out_s...  6.12 us
    ppermute x2, starting transfers between devices, shot_terms(): return (block, lax.ppermute(block, 'shot', swap))  2.18 us
    pallas_call x2, Pallas kernels, load(): pl.pallas_call(kernel, out_shape=tuple((pltpu.VMEM(*shape) for shape in s...  2.15 us
    pallas_call x1, Pallas kernels, shards(): pl.pallas_call(functools.partial(prepare_kernel, len(halos), shots), out_...  1.22 us
  transfers between devices with their start and end apart: 22, of which 11 were waited for; matrix products, arithmetic and copies ran while one was open for 1% of the time, Pallas kernels for 8%

profile of v6, /device:TPU:0, one launch (start us, length us, event | category | flops | bytes accessed | tf_op | source)
XLA Modules:
  0.0 59.4 jit_solution(5360591320630020005)
XLA Ops:
  0.6 1.0 %shard_map.113 = (f32[7,64,128]{2,1,0:T(8,128)S(1)}, f32[48,128]{1,0:T(8,128)S(1)}) custom-call(f32[2,2,64,128]{3,2,1,0:T(8,128)} %now.1, f32[2,64,128]{2,1,0:T(8,128)} %dens.1, f32[2,64,64]{2,1,0:T(8,128)} %velocity.1), custom_call_target="tpu_custom_call" | custom-call | tf_op jit(solution)/shard_map/pallas_call | solution.py:506
  1.7 0.7 %collective-permute-start.1 = (f32[7,64,128]{2,1,0:T(8,128)S(1)}, f32[7,64,128]{2,1,0:T(8,128)S(1)}, u32[]{:S(2)}, u32[]{:S(2)}) collective-permute-start(f32[7,64,128]{2,1,0:T(8,128)S(1)} %get-tuple-element.27.first.refs_0_), channel_id=1, source_target_pairs={{4,8},{8,4},{5,9},{9,5},{6,10},{10,6},{7,11},{11,7},{20,24},{24,20... | collective-permute-start | bytes 688136 | tf_op jit(solution)/shard_map/ppermute | solution.py:32
  2.4 5.9 %collective-permute-start = (f32[7,64,128]{2,1,0:T(8,128)S(1)}, f32[7,64,128]{2,1,0:T(8,128)S(1)}, u32[]{:S(2)}, u32[]{:S(2)}) collective-permute-start(f32[7,64,128]{2,1,0:T(8,128)S(1)} %get-tuple-element.27.first.refs_0_), channel_id=1, source_target_pairs={{0,4},{4,0},{8,12},{12,8},{1,5},{5,1},{9,13},{13,9},{2,6},{6,2},{1... | collective-permute-start | bytes 688136 | tf_op jit(solution)/shard_map/ppermute | solution.py:32
  8.3 1.1 %shard_map.114 = (f32[8,64,128]{2,1,0:T(8,128)S(1)}, f32[2,2,64,128]{3,2,1,0:T(8,128)S(1)}, s32[2,2048]{1,0:T(2,128)S(1)}, f32[2,2,2048]{2,1,0:T(2,128)S(1)}) custom-call(f32[2,2,64,128]{3,2,1,0:T(8,128)} %prev.1, f32[2,2,64,128]{3,2,1,0:T(8,128)} %last.1, f32[2,2,64,128]{3,2,1,0:T(8,128)} %late.1, s32[2,2048]{1,0:T(2,128)} %cells.1, f32[2,2,2048]{2,1,0:T(2,128)} %observed.1), custom_call_target="tpu_custom_call" | custom-call | tf_op jit(solution)/shard_map/pallas_call | solution.py:506
  9.4 0.7 %collective-permute-start.3 = (f32[8,64,128]{2,1,0:T(8,128)S(1)}, f32[8,64,128]{2,1,0:T(8,128)S(1)}, u32[]{:S(2)}, u32[]{:S(2)}) collective-permute-start(f32[8,64,128]{2,1,0:T(8,128)S(1)} %get-tuple-element.28.refs_1_), channel_id=1, source_target_pairs={{4,8},{8,4},{5,9},{9,5},{6,10},{10,6},{7,11},{11,7},{20,24},{24,20... | collective-permute-start | bytes 786440 | tf_op jit(solution)/shard_map/ppermute | solution.py:32
  10.1 1.8 %collective-permute-start.2 = (f32[8,64,128]{2,1,0:T(8,128)S(1)}, f32[8,64,128]{2,1,0:T(8,128)S(1)}, u32[]{:S(2)}, u32[]{:S(2)}) collective-permute-start(f32[8,64,128]{2,1,0:T(8,128)S(1)} %get-tuple-element.28.refs_1_), channel_id=1, source_target_pairs={{0,4},{4,0},{8,12},{12,8},{1,5},{5,1},{9,13},{13,9},{2,6},{6,2},{1... | collective-permute-start | bytes 786440 | tf_op jit(solution)/shard_map/ppermute | solution.py:32
  11.9 0.0 collective-permute-start.4
  11.9 0.1 and_select_fusion
  12.1 0.0 collective-permute-done.1.by_odd.refs_4_
  12.1 2.7 %collective-permute-done.by_even.refs_3_ = f32[7,64,128]{2,1,0:T(8,128)S(1)} collective-permute-done((f32[7,64,128]{2,1,0:T(8,128)S(1)}, f32[7,64,128]{2,1,0:T(8,128)S(1)}, u32[]{:S(2)}, u32[]{:S(2)}) %collective-permute-start) | collective-permute-done | bytes 229408 | tf_op jit(solution)/shard_map/ppermute | solution.py:32
  14.8 0.0 copy-start.2
  14.8 1.6 %collective-permute-start.7 = (f32[3,64,128]{2,1,0:T(8,128)S(1)}, f32[3,64,128]{2,1,0:T(8,128)S(1)}, u32[]{:S(2)}, u32[]{:S(2)}) collective-permute-start(f32[3,64,128]{2,1,0:T(8,128)S(1)} %pad_maximum_fusion), channel_id=1, source_target_pairs={{0,2},{2,0},{1,3},{3,1},{4,6},{6,4},{5,7},{7,5},{8,10},{10,8},{9,1... | collective-permute-start | bytes 294920 | tf_op jit(solution)/shard_map/ppermute | solution.py:32
  16.3 0.0 copy-done.2
  16.4 0.0 collective-permute-done.4.edges
  16.4 0.2 shard_map.115
  16.6 2.1 %collective-permute-start.5 = (f32[4,64,128]{2,1,0:T(8,128)S(1)}, f32[4,64,128]{2,1,0:T(8,128)S(1)}, u32[]{:S(2)}, u32[]{:S(2)}) collective-permute-start(f32[4,64,128]{2,1,0:T(8,128)S(1)} %get-tuple-element.31), channel_id=1, source_target_pairs={{0,4},{4,0},{8,12},{12,8},{1,5},{5,1},{9,13},{13,9},{2,6},{6,2},{1... | collective-permute-start | bytes 393224 | tf_op jit(solution)/shard_map/ppermute | solution.py:32
  18.7 0.7 %collective-permute-start.6 = (f32[4,64,128]{2,1,0:T(8,128)S(1)}, f32[4,64,128]{2,1,0:T(8,128)S(1)}, u32[]{:S(2)}, u32[]{:S(2)}) collective-permute-start(f32[4,64,128]{2,1,0:T(8,128)S(1)} %get-tuple-element.32), channel_id=1, source_target_pairs={{4,8},{8,4},{5,9},{9,5},{6,10},{10,6},{7,11},{11,7},{20,24},{24,20... | collective-permute-start | bytes 393224 | tf_op jit(solution)/shard_map/ppermute | solution.py:32
  19.4 0.1 collective-permute-done.7
  19.5 0.0 collective-permute-done.3.refs_6_
  19.5 0.9 %collective-permute-done.2.refs_5_ = f32[8,64,128]{2,1,0:T(8,128)S(1)} collective-permute-done((f32[8,64,128]{2,1,0:T(8,128)S(1)}, f32[8,64,128]{2,1,0:T(8,128)S(1)}, u32[]{:S(2)}, u32[]{:S(2)}) %collective-permute-start.2) | collective-permute-done | bytes 262176 | tf_op jit(solution)/shard_map/ppermute | solution.py:32
  20.4 1.7 %collective-permute-done.5.refs_7_ = f32[4,64,128]{2,1,0:T(8,128)S(1)} collective-permute-done((f32[4,64,128]{2,1,0:T(8,128)S(1)}, f32[4,64,128]{2,1,0:T(8,128)S(1)}, u32[]{:S(2)}, u32[]{:S(2)}) %collective-permute-start.5) | collective-permute-done | bytes 131104 | tf_op jit(solution)/shard_map/ppermute | solution.py:32
  22.0 0.0 collective-permute-done.6.refs_8_
  22.0 0.1 shard_map.116
  22.1 0.1 collective-permute-start.8
  22.2 1.6 %shard_map.118.refs_13_.refs_12_ = f32[3,320,128]{2,1,0:T(8,128)S(1)} custom-call(s32[1,2048]{1,0:T(1,128)S(1)} %get-tuple-element.67.row_ref, s32[1,2048]{1,0:T(1,128)S(1)} %get-tuple-element.58.col_ref, f32[2,2048]{1,0:T(2,128)S(1)} %get-tuple-element.56.obs_ref), custom_call_target="tpu_custom_call" | custom-call | flops 1174405120 | bytes 32768 | tf_op jit(solution)/shard_map/pallas_call | solution.py:40
  23.8 0.1 copy.12
  23.9 0.1 copy.13
  24.0 1.6 %shard_map.117.refs_12_.refs_11_ = f32[3,320,128]{2,1,0:T(8,128)S(1)} custom-call(s32[1,2048]{1,0:T(1,128)S(1)} %get-tuple-element.66.row_ref, s32[1,2048]{1,0:T(1,128)S(1)} %get-tuple-element.59.col_ref, f32[2,2048]{1,0:T(2,128)S(1)} %get-tuple-element.57.obs_ref), custom_call_target="tpu_custom_call" | custom-call | flops 1174405120 | bytes 32768 | tf_op jit(solution)/shard_map/pallas_call | solution.py:40
  25.5 0.0 copy-start.1
  25.6 0.1 pad_add_fusion.refs_14_
  25.6 0.0 collective-permute-done.8.refs_11_
  25.6 0.6 copy-done.1
  26.2 1.2 %prepare.1 = (f32[2,6,80,128]{3,2,1,0:T(8,128)S(1)}, f32[2,6,80,128]{3,2,1,0:T(8,128)S(1)}, f32[2,4,80,128]{3,2,1,0:T(8,128)S(1)}, f32[2,4,80,128]{3,2,1,0:T(8,1...) custom-call(f32[7,64,128]{2,1,0:T(8,128)S(1)} %get-tuple-element.27., ...), custom_call_target="tpu_custom_call" | custom-call | tf_op jit(solution)/shard_map/prepare/pallas_call | solution.py:622
  27.4 0.8 %shard_map.119.mine = f32[2,64,128]{2,1,0:T(8,128)S(1)} custom-call(f32[6,80,128]{2,1,0:T(8,128)S(1)} %get-tuple-element.35.refs_0_.stiff, f32[2,6,80,128]{3,2,1,0:T(8,128)S(1)} %get-tuple-element.36.refs_1_, f32[2,6,80,128]{3,2,1,0:T(8,128)S(1)} %get-tuple-element.37.refs_2_, f32[2,4,80,128]{3,2,1,0:T(8,128)S(1)} %get-tuple-element.38.refs_3_, ...), custom_call_target="tpu_custom_call" | custom-call | bytes 4341760 | tf_op jit(solution)/shard_map/pallas_call | solution.py:40
  28.3 1.6 %collective-permute-start.9 = (f32[2,64,128]{2,1,0:T(8,128)S(1)}, f32[2,64,128]{2,1,0:T(8,128)S(1)}, u32[]{:S(2)}, u32[]{:S(2)}) collective-permute-start(f32[2,64,128]{2,1,0:T(8,128)S(1)} %shard_map.119.mine), channel_id=1, source_target_pairs={{0,2},{2,0},{1,3},{3,1},{4,6},{6,4},{5,7},{7,5},{8,10},{10,8},{9,1... | collective-permute-start | bytes 196616 | tf_op jit(solution)/shard_map/ppermute | solution.py:481
  29.8 3.0 %collective-permute-done.9.other = f32[2,64,128]{2,1,0:T(8,128)S(1)} collective-permute-done((f32[2,64,128]{2,1,0:T(8,128)S(1)}, f32[2,64,128]{2,1,0:T(8,128)S(1)}, u32[]{:S(2)}, u32[]{:S(2)}) %collective-permute-start.9) | collective-permute-done | bytes 65568 | tf_op jit(solution)/shard_map/ppermute | solution.py:481
  32.8 0.1 collective-permute-start.10
  32.9 0.7 %collective-permute-start.12 = (f32[2,64,128]{2,1,0:T(8,128)S(1)}, f32[2,64,128]{2,1,0:T(8,128)S(1)}, u32[]{:S(2)}, u32[]{:S(2)}) collective-permute-start(f32[2,64,128]{2,1,0:T(8,128)S(1)} %get-tuple-element.46.total), channel_id=1, source_target_pairs={{4,8},{8,4},{5,9},{9,5},{6,10},{10,6},{7,11},{11,7},{20,24},{24,20... | collective-permute-start | bytes 196616 | tf_op jit(solution)/shard_map/ppermute | solution.py:32
  33.6 4.8 %collective-permute-start.11 = (f32[2,64,128]{2,1,0:T(8,128)S(1)}, f32[2,64,128]{2,1,0:T(8,128)S(1)}, u32[]{:S(2)}, u32[]{:S(2)}) collective-permute-start(f32[2,64,128]{2,1,0:T(8,128)S(1)} %get-tuple-element.46.total), channel_id=1, source_target_pairs={{0,4},{4,0},{8,12},{12,8},{1,5},{5,1},{9,13},{13,9},{2,6},{6,2},{1... | collective-permute-start | bytes 196616 | tf_op jit(solution)/shard_map/ppermute | solution.py:32
  38.4 0.0 collective-permute-done.10.got
  38.4 3.0 %collective-permute-start.16 = (f32[8,128]{1,0:T(8,128)S(1)}, f32[8,128]{1,0:T(8,128)S(1)}, u32[]{:S(2)}, u32[]{:S(2)}) collective-permute-start(f32[8,128]{1,0:T(8,128)S(1)} %slice_maximum_fusion), channel_id=1, source_target_pairs={{0,12},{4,8},{8,4},{12,0},{1,13},{5,9},{9,5},{13,1},{2,14},{6,10},... | collective-permute-start | bytes 12296 | tf_op jit(solution)/shard_map/ppermute | solution.py:32
  41.4 0.0 collective-permute-start.15
  41.4 1.5 %collective-permute-start.14 = (f32[8,128]{1,0:T(8,128)S(1)}, f32[8,128]{1,0:T(8,128)S(1)}, u32[]{:S(2)}, u32[]{:S(2)}) collective-permute-start(f32[8,128]{1,0:T(8,128)S(1)} %slice_maximum_fusion), channel_id=1, source_target_pairs={{0,4},{4,0},{8,12},{12,8},{1,5},{5,1},{9,13},{13,9},{2,6},{6,2},{1... | collective-permute-start | bytes 12296 | tf_op jit(solution)/shard_map/ppermute | solution.py:32
  42.9 0.0 collective-permute-done.12.by_odd
  42.9 0.0 collective-permute-done.11.by_even
  42.9 0.1 collective-permute-start.13
  43.0 0.9 %collective-permute-done.16 = f32[8,128]{1,0:T(8,128)S(1)} collective-permute-done((f32[8,128]{1,0:T(8,128)S(1)}, f32[8,128]{1,0:T(8,128)S(1)}, u32[]{:S(2)}, u32[]{:S(2)}) %collective-permute-start.16) | collective-permute-done | bytes 4128 | tf_op jit(solution)/shard_map/ppermute | solution.py:32
  43.9 2.0 %collective-permute-done.15 = f32[8,128]{1,0:T(8,128)S(1)} collective-permute-done((f32[8,128]{1,0:T(8,128)S(1)}, f32[8,128]{1,0:T(8,128)S(1)}, u32[]{:S(2)}, u32[]{:S(2)}) %collective-permute-start.15) | collective-permute-done | bytes 4128 | tf_op jit(solution)/shard_map/ppermute | solution.py:32
  45.9 0.0 collective-permute-done.14
  45.9 0.0 collective-permute-done.13.got_halo
  45.9 0.0 copy-done
  45.9 0.2 shard_map.122
  46.2 0.8 %shard_map.123.mine = f32[2,64,128]{2,1,0:T(8,128)S(1)} custom-call(f32[6,80,128]{2,1,0:T(8,128)S(1)} %get-tuple-element.48.refs_0_, f32[2,6,80,128]{3,2,1,0:T(8,128)S(1)} %get-tuple-element.36.refs_1_, f32[2,6,80,128]{3,2,1,0:T(8,128)S(1)} %get-tuple-element.37.refs_2_, f32[2,4,80,128]{3,2,1,0:T(8,128)S(1)} %get-tuple-element.38.refs_3_, ...), custom_call_target="tpu_custom_call" | custom-call | bytes 4341760 | tf_op jit(solution)/shard_map/pallas_call | solution.py:40
  47.0 0.6 %collective-permute-start.17 = (f32[2,64,128]{2,1,0:T(8,128)S(1)}, f32[2,64,128]{2,1,0:T(8,128)S(1)}, u32[]{:S(2)}, u32[]{:S(2)}) collective-permute-start(f32[2,64,128]{2,1,0:T(8,128)S(1)} %shard_map.123.mine), channel_id=1, source_target_pairs={{0,2},{2,0},{1,3},{3,1},{4,6},{6,4},{5,7},{7,5},{8,10},{10,8},{9,1... | collective-permute-start | bytes 196616 | tf_op jit(solution)/shard_map/ppermute | solution.py:481
  47.6 3.7 %collective-permute-done.17.other = f32[2,64,128]{2,1,0:T(8,128)S(1)} collective-permute-done((f32[2,64,128]{2,1,0:T(8,128)S(1)}, f32[2,64,128]{2,1,0:T(8,128)S(1)}, u32[]{:S(2)}, u32[]{:S(2)}) %collective-permute-start.17) | collective-permute-done | bytes 65568 | tf_op jit(solution)/shard_map/ppermute | solution.py:481
  51.3 0.1 collective-permute-start.18
  51.4 1.2 %collective-permute-done.18 = f32[8,128]{1,0:T(8,128)S(1)} collective-permute-done((f32[8,128]{1,0:T(8,128)S(1)}, f32[8,128]{1,0:T(8,128)S(1)}, u32[]{:S(2)}, u32[]{:S(2)}) %collective-permute-start.18) | collective-permute-done | bytes 4128 | tf_op jit(solution)/shard_map/ppermute | solution.py:661
  52.6 1.5 %collective-permute-start.21 = (f32[8,128]{1,0:T(8,128)S(1)}, f32[8,128]{1,0:T(8,128)S(1)}, u32[]{:S(2)}, u32[]{:S(2)}) collective-permute-start(f32[8,128]{1,0:T(8,128)S(1)} %max.28), channel_id=1, source_target_pairs={{0,12},{4,8},{8,4},{12,0},{1,13},{5,9},{9,5},{13,1},{2,14},{6,10},... | collective-permute-start | bytes 12296 | tf_op jit(solution)/shard_map/ppermute | solution.py:32
  54.0 0.6 collective-permute-start.20
  54.6 2.4 %collective-permute-start.19 = (f32[8,128]{1,0:T(8,128)S(1)}, f32[8,128]{1,0:T(8,128)S(1)}, u32[]{:S(2)}, u32[]{:S(2)}) collective-permute-start(f32[8,128]{1,0:T(8,128)S(1)} %max.28), channel_id=1, source_target_pairs={{0,4},{4,0},{8,12},{12,8},{1,5},{5,1},{9,13},{13,9},{2,6},{6,2},{1... | collective-permute-start | bytes 12296 | tf_op jit(solution)/shard_map/ppermute | solution.py:32
  56.9 1.0 %collective-permute-done.21 = f32[8,128]{1,0:T(8,128)S(1)} collective-permute-done((f32[8,128]{1,0:T(8,128)S(1)}, f32[8,128]{1,0:T(8,128)S(1)}, u32[]{:S(2)}, u32[]{:S(2)}) %collective-permute-start.21) | collective-permute-done | bytes 4128 | tf_op jit(solution)/shard_map/ppermute | solution.py:32
  58.0 0.6 collective-permute-done.20
  58.5 0.0 collective-permute-done.19
  58.6 0.8 %shard_map.125 = (f32[2,64,64]{2,1,0:T(8,128)}, f32[2,64,64]{2,1,0:T(8,128)}) custom-call(f32[2,64,128]{2,1,0:T(8,128)S(1)} %get-tuple-element.49.total, f32[8,128]{1,0:T(8,128)S(1)} %maximum_maximum_fusion.largest, f32[2,64,64]{2,1,0:T(8,128)S(1)} %get-tuple-element.51.velocity), custom_call_target="tpu_custom_call" | custom-call | bytes 102400 | tf_op jit(solution)/shard_map/pallas_call | solution.py:40
  (15 shorter events, 0.1 us)
Async XLA Ops:
  1.7 10.4 %collective-permute-start.1 = (f32[7,64,128]{2,1,0:T(8,128)S(1)}, f32[7,64,128]{2,1,0:T(8,128)S(1)}, u32[]{:S(2)}, u32[]{:S(2)}) collective-permute-start(f32[7,64,128]{2,1,0:T(8,128)S(1)} %get-tuple-element.27.first.refs_0_), channel_id=1, source_target_pairs={{4,8},{8,4},{5,9},{9,5},{6,10},{10,6},{7,11},{11,7},{20,24},{24,20... | collective-permute-start | bytes 688136 | tf_op jit(solution)/shard_map/ppermute | solution.py:32
  2.4 12.4 %collective-permute-start = (f32[7,64,128]{2,1,0:T(8,128)S(1)}, f32[7,64,128]{2,1,0:T(8,128)S(1)}, u32[]{:S(2)}, u32[]{:S(2)}) collective-permute-start(f32[7,64,128]{2,1,0:T(8,128)S(1)} %get-tuple-element.27.first.refs_0_), channel_id=1, source_target_pairs={{0,4},{4,0},{8,12},{12,8},{1,5},{5,1},{9,13},{13,9},{2,6},{6,2},{1... | collective-permute-start | bytes 688136 | tf_op jit(solution)/shard_map/ppermute | solution.py:32
  9.4 10.1 %collective-permute-start.3 = (f32[8,64,128]{2,1,0:T(8,128)S(1)}, f32[8,64,128]{2,1,0:T(8,128)S(1)}, u32[]{:S(2)}, u32[]{:S(2)}) collective-permute-start(f32[8,64,128]{2,1,0:T(8,128)S(1)} %get-tuple-element.28.refs_1_), channel_id=1, source_target_pairs={{4,8},{8,4},{5,9},{9,5},{6,10},{10,6},{7,11},{11,7},{20,24},{24,20... | collective-permute-start | bytes 786440 | tf_op jit(solution)/shard_map/ppermute | solution.py:32
  10.1 10.3 %collective-permute-start.2 = (f32[8,64,128]{2,1,0:T(8,128)S(1)}, f32[8,64,128]{2,1,0:T(8,128)S(1)}, u32[]{:S(2)}, u32[]{:S(2)}) collective-permute-start(f32[8,64,128]{2,1,0:T(8,128)S(1)} %get-tuple-element.28.refs_1_), channel_id=1, source_target_pairs={{0,4},{4,0},{8,12},{12,8},{1,5},{5,1},{9,13},{13,9},{2,6},{6,2},{1... | collective-permute-start | bytes 786440 | tf_op jit(solution)/shard_map/ppermute | solution.py:32
  11.9 4.5 %collective-permute-start.4 = (f32[48,128]{1,0:T(8,128)S(1)}, f32[48,128]{1,0:T(8,128)S(1)}, u32[]{:S(2)}, u32[]{:S(2)}) collective-permute-start(f32[48,128]{1,0:T(8,128)S(1)} %get-tuple-element.30), channel_id=1, source_target_pairs={{0,1},{1,0},{2,3},{3,2},{4,5},{5,4},{6,7},{7,6},{8,9},{9,8},{10,11... | collective-permute-start | bytes 73736 | tf_op jit(solution)/shard_map/ppermute | solution.py:32
  14.8 1.6 %copy-start.2 = (s32[2]{0:T(128)S(1)}, s32[2]{0:T(128)}, u32[]{:S(2)}) copy-start(s32[2]{0:T(128)} %param.17) | copy-start | bytes 28
  14.8 4.7 %collective-permute-start.7 = (f32[3,64,128]{2,1,0:T(8,128)S(1)}, f32[3,64,128]{2,1,0:T(8,128)S(1)}, u32[]{:S(2)}, u32[]{:S(2)}) collective-permute-start(f32[3,64,128]{2,1,0:T(8,128)S(1)} %pad_maximum_fusion), channel_id=1, source_target_pairs={{0,2},{2,0},{1,3},{3,1},{4,6},{6,4},{5,7},{7,5},{8,10},{10,8},{9,1... | collective-permute-start | bytes 294920 | tf_op jit(solution)/shard_map/ppermute | solution.py:32
  16.6 5.4 %collective-permute-start.5 = (f32[4,64,128]{2,1,0:T(8,128)S(1)}, f32[4,64,128]{2,1,0:T(8,128)S(1)}, u32[]{:S(2)}, u32[]{:S(2)}) collective-permute-start(f32[4,64,128]{2,1,0:T(8,128)S(1)} %get-tuple-element.31), channel_id=1, source_target_pairs={{0,4},{4,0},{8,12},{12,8},{1,5},{5,1},{9,13},{13,9},{2,6},{6,2},{1... | collective-permute-start | bytes 393224 | tf_op jit(solution)/shard_map/ppermute | solution.py:32
  18.7 3.4 %collective-permute-start.6 = (f32[4,64,128]{2,1,0:T(8,128)S(1)}, f32[4,64,128]{2,1,0:T(8,128)S(1)}, u32[]{:S(2)}, u32[]{:S(2)}) collective-permute-start(f32[4,64,128]{2,1,0:T(8,128)S(1)} %get-tuple-element.32), channel_id=1, source_target_pairs={{4,8},{8,4},{5,9},{9,5},{6,10},{10,6},{7,11},{11,7},{20,24},{24,20... | collective-permute-start | bytes 393224 | tf_op jit(solution)/shard_map/ppermute | solution.py:32
  22.1 3.5 %collective-permute-start.8 = (f32[480,128]{1,0:T(8,128)S(1)}, f32[480,128]{1,0:T(8,128)S(1)}, u32[]{:S(2)}, u32[]{:S(2)}) collective-permute-start(f32[480,128]{1,0:T(8,128)S(1)} %shard_map.116), channel_id=1, source_target_pairs={{0,1},{1,0},{2,3},{3,2},{4,5},{5,4},{6,7},{7,6},{8,9},{9,8},{10,11... | collective-permute-start | bytes 737288 | tf_op jit(solution)/shard_map/ppermute | solution.py:32
  25.5 0.7 %copy-start.1 = (f32[2,2]{1,0:T(2,128)S(1)}, f32[2,2]{1,0:T(2,128)}, u32[]{:S(2)}) copy-start(f32[2,2]{1,0:T(2,128)} %refs_15_.1) | copy-start | bytes 52
  28.3 4.6 %collective-permute-start.9 = (f32[2,64,128]{2,1,0:T(8,128)S(1)}, f32[2,64,128]{2,1,0:T(8,128)S(1)}, u32[]{:S(2)}, u32[]{:S(2)}) collective-permute-start(f32[2,64,128]{2,1,0:T(8,128)S(1)} %shard_map.119.mine), channel_id=1, source_target_pairs={{0,2},{2,0},{1,3},{3,1},{4,6},{6,4},{5,7},{7,5},{8,10},{10,8},{9,1... | collective-permute-start | bytes 196616 | tf_op jit(solution)/shard_map/ppermute | solution.py:481
  32.8 5.6 %collective-permute-start.10 = (f32[24,128]{1,0:T(8,128)S(1)}, f32[24,128]{1,0:T(8,128)S(1)}, u32[]{:S(2)}, u32[]{:S(2)}) collective-permute-start(f32[24,128]{1,0:T(8,128)S(1)} %get-tuple-element.47), channel_id=1, source_target_pairs={{0,1},{1,0},{2,3},{3,2},{4,5},{5,4},{6,7},{7,6},{8,9},{9,8},{10,11... | collective-permute-start | bytes 36872 | tf_op jit(solution)/shard_map/ppermute | solution.py:32
  32.9 10.0 %collective-permute-start.12 = (f32[2,64,128]{2,1,0:T(8,128)S(1)}, f32[2,64,128]{2,1,0:T(8,128)S(1)}, u32[]{:S(2)}, u32[]{:S(2)}) collective-permute-start(f32[2,64,128]{2,1,0:T(8,128)S(1)} %get-tuple-element.46.total), channel_id=1, source_target_pairs={{4,8},{8,4},{5,9},{9,5},{6,10},{10,6},{7,11},{11,7},{20,24},{24,20... | collective-permute-start | bytes 196616 | tf_op jit(solution)/shard_map/ppermute | solution.py:32
  33.6 9.3 %collective-permute-start.11 = (f32[2,64,128]{2,1,0:T(8,128)S(1)}, f32[2,64,128]{2,1,0:T(8,128)S(1)}, u32[]{:S(2)}, u32[]{:S(2)}) collective-permute-start(f32[2,64,128]{2,1,0:T(8,128)S(1)} %get-tuple-element.46.total), channel_id=1, source_target_pairs={{0,4},{4,0},{8,12},{12,8},{1,5},{5,1},{9,13},{13,9},{2,6},{6,2},{1... | collective-permute-start | bytes 196616 | tf_op jit(solution)/shard_map/ppermute | solution.py:32
  38.4 7.5 %copy-start = (f32[2,64,64]{2,1,0:T(8,128)S(1)}, f32[2,64,64]{2,1,0:T(8,128)}, u32[]{:S(2)}) copy-start(f32[2,64,64]{2,1,0:T(8,128)} %velocity.1) | copy-start | bytes 98308
  38.4 5.5 %collective-permute-start.16 = (f32[8,128]{1,0:T(8,128)S(1)}, f32[8,128]{1,0:T(8,128)S(1)}, u32[]{:S(2)}, u32[]{:S(2)}) collective-permute-start(f32[8,128]{1,0:T(8,128)S(1)} %slice_maximum_fusion), channel_id=1, source_target_pairs={{0,12},{4,8},{8,4},{12,0},{1,13},{5,9},{9,5},{13,1},{2,14},{6,10},... | collective-permute-start | bytes 12296 | tf_op jit(solution)/shard_map/ppermute | solution.py:32
  41.4 4.5 %collective-permute-start.15 = (f32[8,128]{1,0:T(8,128)S(1)}, f32[8,128]{1,0:T(8,128)S(1)}, u32[]{:S(2)}, u32[]{:S(2)}) collective-permute-start(f32[8,128]{1,0:T(8,128)S(1)} %slice_maximum_fusion), channel_id=1, source_target_pairs={{0,8},{4,12},{8,0},{12,4},{1,9},{5,13},{9,1},{13,5},{2,10},{6,14},... | collective-permute-start | bytes 12296 | tf_op jit(solution)/shard_map/ppermute | solution.py:32
  41.4 4.5 %collective-permute-start.14 = (f32[8,128]{1,0:T(8,128)S(1)}, f32[8,128]{1,0:T(8,128)S(1)}, u32[]{:S(2)}, u32[]{:S(2)}) collective-permute-start(f32[8,128]{1,0:T(8,128)S(1)} %slice_maximum_fusion), channel_id=1, source_target_pairs={{0,4},{4,0},{8,12},{12,8},{1,5},{5,1},{9,13},{13,9},{2,6},{6,2},{1... | collective-permute-start | bytes 12296 | tf_op jit(solution)/shard_map/ppermute | solution.py:32
  42.9 3.0 %collective-permute-start.13 = (f32[32,128]{1,0:T(8,128)S(1)}, f32[32,128]{1,0:T(8,128)S(1)}, u32[]{:S(2)}, u32[]{:S(2)}) collective-permute-start(f32[32,128]{1,0:T(8,128)S(1)} %shard_map.121), channel_id=1, source_target_pairs={{0,1},{1,0},{2,3},{3,2},{4,5},{5,4},{6,7},{7,6},{8,9},{9,8},{10,11... | collective-permute-start | bytes 49160 | tf_op jit(solution)/shard_map/ppermute | solution.py:32
  47.0 4.3 %collective-permute-start.17 = (f32[2,64,128]{2,1,0:T(8,128)S(1)}, f32[2,64,128]{2,1,0:T(8,128)S(1)}, u32[]{:S(2)}, u32[]{:S(2)}) collective-permute-start(f32[2,64,128]{2,1,0:T(8,128)S(1)} %shard_map.123.mine), channel_id=1, source_target_pairs={{0,2},{2,0},{1,3},{3,1},{4,6},{6,4},{5,7},{7,5},{8,10},{10,8},{9,1... | collective-permute-start | bytes 196616 | tf_op jit(solution)/shard_map/ppermute | solution.py:481
  51.3 1.2 %collective-permute-start.18 = (f32[8,128]{1,0:T(8,128)S(1)}, f32[8,128]{1,0:T(8,128)S(1)}, u32[]{:S(2)}, u32[]{:S(2)}) collective-permute-start(f32[8,128]{1,0:T(8,128)S(1)} %get-tuple-element.50), channel_id=1, source_target_pairs={{0,1},{1,0},{2,3},{3,2},{4,5},{5,4},{6,7},{7,6},{8,9},{9,8},{10,11... | collective-permute-start | bytes 12296 | tf_op jit(solution)/shard_map/ppermute | solution.py:661
  52.6 5.4 %collective-permute-start.21 = (f32[8,128]{1,0:T(8,128)S(1)}, f32[8,128]{1,0:T(8,128)S(1)}, u32[]{:S(2)}, u32[]{:S(2)}) collective-permute-start(f32[8,128]{1,0:T(8,128)S(1)} %max.28), channel_id=1, source_target_pairs={{0,12},{4,8},{8,4},{12,0},{1,13},{5,9},{9,5},{13,1},{2,14},{6,10},... | collective-permute-start | bytes 12296 | tf_op jit(solution)/shard_map/ppermute | solution.py:32
  54.0 4.5 %collective-permute-start.20 = (f32[8,128]{1,0:T(8,128)S(1)}, f32[8,128]{1,0:T(8,128)S(1)}, u32[]{:S(2)}, u32[]{:S(2)}) collective-permute-start(f32[8,128]{1,0:T(8,128)S(1)} %max.28), channel_id=1, source_target_pairs={{0,8},{4,12},{8,0},{12,4},{1,9},{5,13},{9,1},{13,5},{2,10},{6,14},... | collective-permute-start | bytes 12296 | tf_op jit(solution)/shard_map/ppermute | solution.py:32
  54.6 4.0 %collective-permute-start.19 = (f32[8,128]{1,0:T(8,128)S(1)}, f32[8,128]{1,0:T(8,128)S(1)}, u32[]{:S(2)}, u32[]{:S(2)}) collective-permute-start(f32[8,128]{1,0:T(8,128)S(1)} %max.28), channel_id=1, source_target_pairs={{0,4},{4,0},{8,12},{12,8},{1,5},{5,1},{9,13},{13,9},{2,6},{6,2},{1... | collective-permute-start | bytes 12296 | tf_op jit(solution)/shard_map/ppermute | solution.py:32

commit v7 on v6

--- a/solution.py
+++ b/solution.py
@@ -124,14 +124,15 @@
 
 
 class Halo:
-    def __init__(self, first, second, late, first_by, second_by, third_by, vel):
+    def __init__(self, shape, first=None, second=None, late=None, by=(), vel=()):
         self.even = lax.axis_index("depth") % 2 == 0
         self.first, self.second, self.late, self.vel = first, second, late, vel
-        self.first_by, self.second_by, self.third_by = first_by, second_by, third_by
-        self.shots, self.planes, self.rows, self.cols = late.shape
-
-    def pick(self, pair, upper, index):
-        a, b = pair if upper else pair[::-1]
+        self.by = by
+        self.shots, self.planes, self.rows, self.cols = shape
+
+    def pick(self, batch, upper, index):
+        even, odd = self.by[batch]
+        a, b = (even, odd) if upper else (odd, even)
         return jnp.where(self.even, a[index], b[index])
 
     def plane(self, item):
@@ -150,43 +151,68 @@
                 value = shifted if value is None else jnp.where(column >= index * own, shifted, value)
             return value
         if which == LAP:
-            return self.pick(self.third_by, upper, shots + shot)
+            return self.pick("third", upper, shots + shot)
         if which == LATE:
-            return self.late[shot, at] if inside else self.pick(self.third_by, upper, shot)
+            return self.late[shot, at] if inside else self.pick("third", upper, shot)
         if which in (NOW, DENS):
             index = (shot if which == NOW else shots) * planes + step
-            return self.first[index] if inside else self.pick(self.first_by, upper, index)
+            return self.first[index] if inside else self.pick("first", upper, index)
         index = ((0 if which == PREV else shots) + shot) * planes + step
-        return self.second[index] if inside else self.pick(self.second_by, upper, index)
-
-    def plane_list(self):
+        return self.second[index] if inside else self.pick("second", upper, index)
+
+    def early_list(self):
         planes = self.planes
         out = []
-        for which, margin in ((NOW, 2), (PREV, 2), (LAST, 2), (LATE, 1)):
+        for which, margin in ((NOW, 2), (PREV, 2), (LAST, 2), (LATE, 0)):
             for shot in range(self.shots):
                 for at in range(-margin, planes + margin):
                     out.append((which, shot, at))
+        return out + [(DENS, 0, at) for at in range(-2, planes + 2)]
+
+    def final_list(self):
+        planes = self.planes
+        out = []
         for shot in range(self.shots):
-            out += [(LAP, shot, -2), (LAP, shot, planes + 1)]
-        for which in (DENS, VEL):
-            for at in range(-2, planes + 2):
-                out.append((which, 0, at))
-        return out
-
-
-def halo_of(refs):
-    first, second, late, fe, fo, se, so, te, to, *vel = refs
-    return Halo(first, second, late, (fe, fo), (se, so), (te, to), vel)
-
-
-def edge_kernel(*refs):
-    halo = halo_of(refs[:-1])
-    out = refs[-1]
+            out += [(LATE, shot, -1), (LATE, shot, planes), (LAP, shot, -2), (LAP, shot, planes + 1)]
+        return out + [(VEL, 0, at) for at in range(-2, planes + 2)]
+
+
+def write_edges(halo, items, out):
     first = lax.axis_index("lat") == 0
     rows = halo.rows
-    for index, item in enumerate(halo.plane_list()):
+    for index, item in enumerate(items):
         value = halo.plane(item)
         out[index * PAD : (index + 1) * PAD] = jnp.where(first, value[rows - PAD :], value[:PAD])
+
+
+def reader(halo, items, edges):
+    lat_at = lax.axis_index("lat")
+    where_is = {item: index for index, item in enumerate(items)}
+
+    def whole(which, shot, at):
+        item = (which, shot, at)
+        index = where_is[item]
+        return with_rows(edges[index * PAD : (index + 1) * PAD], halo.plane(item), lat_at)
+
+    return whole
+
+
+def early_halo(first, second, late, fe, fo, se, so):
+    return Halo(late.shape, first, second, late, {"first": (fe, fo), "second": (se, so)})
+
+
+def final_halo(shape, te, to, *vel):
+    return Halo(shape, by={"third": (te, to)}, vel=vel)
+
+
+def early_edge_kernel(*refs):
+    halo = early_halo(*refs[:7])
+    write_edges(halo, halo.early_list(), refs[7])
+
+
+def final_edge_kernel(shape, *refs):
+    halo = final_halo(shape, *refs[:-1])
+    write_edges(halo, halo.final_list(), refs[-1])
 
 
 def near_cols(value):
@@ -274,28 +300,20 @@
         to_odd[shots + shot] = jnp.where(even, ends[1], ends[0])
 
 
-def prepare_kernel(halos, shots, *refs):
-    halo = halo_of(refs[:halos])
-    edges, *dense = refs[halos : halos + 1 + shots]
-    source_at, wavelet = refs[halos + 1 + shots : halos + 3 + shots]
-    outs = refs[halos + 3 + shots :]
-    lap_out, base_out, turn_out, late_out, last_out, low_out, stiff_out = outs[:7]
-    cz, cx, cp, cm, now_buf, buoy_buf = outs[7:]
-    lat_at = lax.axis_index("lat")
+def early_kernel(full_rows, shots, *refs):
+    halo = early_halo(*refs[:7])
+    edges, *dense = refs[7 : 8 + shots]
+    source, wavelet = refs[8 + shots : 10 + shots]
+    lap_out, base_out, turn_out, late_own, late_near, last_out, low_out = refs[10 + shots : 17 + shots]
+    dens_out, cz, cx, cp, cm, now_buf, buoy_buf = refs[17 + shots :]
     rows, cols, planes = halo.rows, halo.cols, halo.planes
     wide = rows + 2 * PAD
-    where_is = {item: index for index, item in enumerate(halo.plane_list())}
-
-    def whole(which, shot, at):
-        item = (which, shot, at)
-        index = where_is[item]
-        return with_rows(edges[index * PAD : (index + 1) * PAD], halo.plane(item), lat_at)
+    whole = reader(halo, halo.early_list(), edges)
 
     for at in range(-2, planes + 2):
         density = whole(DENS, 0, at)
+        dens_out[at + 2] = density
         buoy_buf[at + 2] = inverse(density)
-        speed = whole(VEL, 0, at) * COURANT
-        stiff_out[at + 2] = speed * speed * density
         for shot in range(shots):
             now_buf[shot, at + 2] = whole(NOW, shot, at)
 
@@ -309,12 +327,19 @@
         couple(lambda k: buoy_buf[k + 2], at, put(cz), put(cx), put(cp), put(cm))
     line = lax.broadcasted_iota(jnp.int32, (wide, cols), 0)
     column = lax.broadcasted_iota(jnp.int32, (wide, cols), 1)
+    depth_start = lax.axis_index("depth") * planes
+    row_start = lax.axis_index("lat") * rows
     for shot in range(shots):
+        cell = source[shot]
+        source_line = lax.div(cell, cols)
+        source_plane = lax.div(source_line, full_rows) - depth_start
+        source_row = lax.rem(source_line, full_rows) - row_start + PAD
+        spot = (line == source_row) & (column == lax.rem(cell, cols))
         for at in range(-2, planes + 2):
-            here = (line + (at + 2) * wide == source_at[shot, 0]) & (column == source_at[shot, 1])
+            here = spot & (source_plane == at)
             middle = now_buf[shot, at + 2]
             if -1 <= at < planes + 1:
-                lap_out[shot, at + 2] = laplace(
+                lap_out[shot, at + 1] = laplace(
                     lambda k: now_buf[shot, k + 2],
                     at,
                     lambda k: cz[k + 2],
@@ -322,8 +347,6 @@
                     lambda k: cp[k + 2],
                     lambda k: cm[k + 2],
                 )
-            else:
-                lap_out[shot, at + 2] = whole(LAP, shot, at)
             base_out[shot, at + 2] = (
                 2.0 * middle - whole(PREV, shot, at) + jnp.where(here, wavelet[shot, 0], 0.0)
             )
@@ -331,21 +354,48 @@
             last_out[shot, at + 2] = newest
             if -1 <= at < planes + 1:
                 turn_out[shot, at + 1] = jnp.where(here, wavelet[shot, 1], 0.0) - middle
-                late_out[shot, at + 1] = (
-                    2.0 * newest
-                    - whole(LATE, shot, at)
-                    - dense[shot][2, (at + 1) * wide : (at + 2) * wide]
-                )
+                ahead = 2.0 * newest - dense[shot][2, (at + 1) * wide : (at + 2) * wide]
+                if 0 <= at < planes:
+                    late_own[shot, at] = ahead - whole(LATE, shot, at)
+                else:
+                    late_near[shot, int(at >= 0)] = ahead
             if 0 <= at < planes:
                 low_out[shot, at] = newest + dense[shot][1, (at + 1) * wide : (at + 2) * wide]
 
 
+def final_kernel(shape, vels, *refs):
+    te, to = refs[:2]
+    halo = final_halo(shape, te, to, *refs[2 : 2 + vels])
+    edges, dens, ahead, lap_far, late_near, stiff_out = refs[2 + vels :]
+    whole = reader(halo, halo.final_list(), edges)
+    planes = halo.planes
+    for at in range(-2, planes + 2):
+        speed = whole(VEL, 0, at) * COURANT
+        stiff_out[at + 2] = speed * speed * dens[at + 2]
+    for shot in range(halo.shots):
+        for side, (near, far) in enumerate(((-1, -2), (planes, planes + 1))):
+            lap_far[shot, side] = whole(LAP, shot, far)
+            late_near[shot, side] = ahead[shot, side] - whole(LATE, shot, near)
+
+
 def update_kernel(shots, *refs):
-    stiff, lap, base, turn, late, last, low, cz_ref, cx_ref, cp_ref, cm_ref = refs[:11]
-    dense = refs[11 : 11 + shots]
-    out, second, scaled, upper, lap_second = refs[11 + shots :]
+    stiff, lap_mid, lap_far, base, turn, late_own, late_near, last, low = refs[:9]
+    cz_ref, cx_ref, cp_ref, cm_ref = refs[9:13]
+    dense = refs[13 : 13 + shots]
+    out, second, scaled, upper, lap_second = refs[13 + shots :]
     planes = low.shape[1]
     wide, _ = low.shape[2:]
+
+    def lap(shot, at):
+        if 1 <= at < planes + 3:
+            return lap_mid[shot, at - 1]
+        return lap_far[shot, int(at > 0)]
+
+    def late(shot, at):
+        if 2 <= at < planes + 2:
+            return late_own[shot, at - 2]
+        return late_near[shot, int(at > 1)]
+
     cz = lambda k: cz_ref[k]
     cx = lambda k: cx_ref[k]
     cp = lambda k: cp_ref[k]
@@ -353,7 +403,7 @@
     for at in range(planes + 4):
         rigid = stiff[at]
         for shot in range(shots):
-            second[shot, at] = base[shot, at] + rigid * lap[shot, at]
+            second[shot, at] = base[shot, at] + rigid * lap(shot, at)
             scaled[shot, at] = rigid * last[shot, at]
     for at in range(1, planes + 3):
         rigid = stiff[at]
@@ -361,7 +411,7 @@
             hits = dense[shot][0, (at - 1) * wide : at * wide]
             lap_now = laplace(lambda k: second[shot, k], at, cz, cx, cp, cm)
             third = 2.0 * second[shot, at] + turn[shot, at - 1] + rigid * lap_now
-            adj = late[shot, at - 1] + hits * third
+            adj = late(shot, at) + hits * third
             adj = adj + laplace(lambda k: scaled[shot, k], at, cz, cx, cp, cm)
             upper[shot, at - 1] = adj
             if 2 <= at < planes + 2:
@@ -375,7 +425,7 @@
             hits = dense[shot][0, (at - 1) * wide : at * wide]
             lower = 2.0 * upper[shot, at - 1] - low[shot, at - 2] + hits * second[shot, at]
             lower = lower + laplace(lambda k: scaled[shot, k], at, cz, cx, cp, cm)
-            term = upper[shot, at - 1] * lap_second[shot, at - 2] + lower * lap[shot, at]
+            term = upper[shot, at - 1] * lap_second[shot, at - 2] + lower * lap(shot, at)
             total = term if total is None else total + term
         out[at - 2] = (stiff[at] * total)[PAD : wide - PAD]
 
@@ -403,35 +453,34 @@
     largest[...] = tile_max(value)
 
 
-def halo_edge_kernel(by_even, by_odd, out):
-    even = lax.axis_index("depth") % 2 == 0
-    first = lax.axis_index("lat") == 0
-    planes, rows, _ = by_even.shape
-    for side, (a, b) in enumerate(((by_odd, by_even), (by_even, by_odd))):
-        for at in range(planes):
-            value = jnp.where(even, a[at], b[at])
-            start = (side * planes + at) * PAD
-            out[start : start + PAD] = jnp.where(first, value[rows - PAD :], value[:PAD])
-
-
-def restiff_kernel(stiff, total, got, by_even, by_odd, got_halo, largest, velocity, stiff_out, vel_out):
+def widen_kernel(total, mine, got, out):
+    planes, rows, _ = total.shape
+    wide = rows + 2 * PAD
+    lat_at = lax.axis_index("lat")
+    for at in range(planes):
+        part = got[at * PAD : (at + 1) * PAD]
+        out[at * wide : (at + 1) * wide] = with_rows(part, total[at], lat_at)
+    out[planes * wide :] = jnp.maximum(mine[planes * PAD :], got[planes * PAD :])
+
+
+def restiff_kernel(stiff, mine, by_even, by_odd, largest, velocity, stiff_out, vel_out):
     planes, rows, own = velocity.shape
+    wide = rows + 2 * PAD
     even = lax.axis_index("depth") % 2 == 0
     shot_at = lax.axis_index("shot")
-    lat_at = lax.axis_index("lat")
-    cols = total.shape[2]
+    cols = mine.shape[1]
     scale = jnp.max(jnp.max(largest[...], axis=1, keepdims=True), axis=0, keepdims=True) + EPSILON
     for at in range(-2, planes + 2):
         if 0 <= at < planes:
-            value, part = total[at], got[at * PAD : (at + 1) * PAD]
+            value = mine[at * wide : (at + 1) * wide]
         else:
             upper = at >= planes
             step = at - planes if upper else planes + at
             a, b = (by_even, by_odd) if upper else (by_odd, by_even)
-            value = jnp.where(even, a[step], b[step])
-            start = (upper * planes + step) * PAD
-            part = got_halo[start : start + PAD]
-        value = with_rows(part, value, lat_at) / scale
+            value = jnp.where(
+                even, a[step * wide : (step + 1) * wide], b[step * wide : (step + 1) * wide]
+            )
+        value = value / scale
         stiff_out[at + 2] = stiff[at + 2] * jnp.exp(-2.0 * STEP_SIZE * value)
         if 0 <= at < planes:
             shifted = pltpu.roll(value[PAD : PAD + rows], (cols - shot_at * own) % cols, 1)
@@ -594,22 +643,19 @@
     for shot in range(shots):
         dense.append(receivers(shot))
     dense = tuple(dense)
-    source_at = jnp.stack(place(source_cell, 2), axis=1)
-
-    halos = (first, second, late, first_even, first_odd, second_even, second_odd)
-    halos += (third_even, third_odd) + tuple(parts)
-    strips = shots * (4 * planes + 16) + 2 * (planes + 4)
-    (edges,) = on_chip(edge_kernel, [(strips * PAD, cols)], halos)
+    early = (first, second, late, first_even, first_odd, second_even, second_odd)
+    strips = shots * (4 * planes + 12) + planes + 4
+    (edges,) = on_chip(early_edge_kernel, [(strips * PAD, cols)], early)
     edges = send(edges, "lat", swap)
-
     deep = planes + 4
     model = (wide, cols)
     scalars = pl.BlockSpec(memory_space=pltpu.SMEM)
-    prepared_shapes = [
-        (shots, deep) + model,
+    shapes = [
+        (shots, planes + 2) + model,
         (shots, deep) + model,
         (shots, planes + 2) + model,
-        (shots, planes + 2) + model,
+        (shots, planes) + model,
+        (shots, 2) + model,
         (shots, deep) + model,
         (shots, planes) + model,
         (deep,) + model,
@@ -618,30 +664,37 @@
         (planes + 3,) + model,
         (planes + 3,) + model,
     ]
-    vectors = halos + (edges,) + dense
-    prepared = pl.pallas_call(
-        functools.partial(prepare_kernel, len(halos), shots),
-        out_shape=tuple(pltpu.VMEM(shape, jnp.float32) for shape in prepared_shapes),
+    vectors = early + (edges,) + dense
+    outs = pl.pallas_call(
+        functools.partial(early_kernel, full_rows, shots),
+        out_shape=tuple(pltpu.VMEM(shape, jnp.float32) for shape in shapes),
         in_specs=[spec] * len(vectors) + [scalars, scalars],
-        out_specs=tuple(spec for _ in prepared_shapes),
+        out_specs=tuple(spec for _ in shapes),
         scratch_shapes=[
             pltpu.VMEM((shots, deep) + model, jnp.float32),
             pltpu.VMEM((deep,) + model, jnp.float32),
         ],
         compiler_params=pltpu.CompilerParams(vmem_limit_bytes=8 << 20),
-        name="prepare",
-    )(
-        *[pltpu.with_memory_space_constraint(a, pltpu.VMEM) for a in vectors],
-        source_at,
-        wavelet,
+        name="early",
+    )(*[pltpu.with_memory_space_constraint(a, pltpu.VMEM) for a in vectors], source_cell, wavelet)
+    lap, base, turn, late_own, ahead, last, low, dens, cz, cx, cp, cm = outs
+
+    final = (third_even, third_odd) + tuple(parts)
+    shape = adj_late.shape
+    strips = 4 * shots + planes + 4
+    (edges,) = on_chip(functools.partial(final_edge_kernel, shape), [(strips * PAD, cols)], final)
+    edges = send(edges, "lat", swap)
+    lap_far, late_near, stiff = on_chip(
+        functools.partial(final_kernel, shape, len(parts)),
+        [(shots, 2) + model, (shots, 2) + model, (deep,) + model],
+        final + (edges, dens, ahead),
     )
-    lap, base, turn, late, last, low, stiff, cz, cx, cp, cm = prepared
 
     def gradient_of(stiff):
         (out,) = on_chip(
             functools.partial(update_kernel, shots),
             [(planes, rows, cols)],
-            (stiff, lap, base, turn, late, last, low, cz, cx, cp, cm) + dense,
+            (stiff, lap, lap_far, base, turn, late_own, late_near, last, low, cz, cx, cp, cm) + dense,
             scratch=[
                 (shots, deep) + model,
                 (shots, deep) + model,
@@ -671,15 +724,24 @@
         edge_rows = planes * PAD + 8
         summed, tail = on_chip(sum_kernel, [(planes, rows, cols), (edge_rows, cols)], (mine, other))
         got = send(tail, "lat", swap)
-        by_even = send(summed, "depth", evens)
-        by_odd = send(summed, "depth", odds)
-        largest = depth_max(jnp.maximum(tail[planes * PAD :], got[planes * PAD :]))
-        (halo_tail,) = on_chip(halo_edge_kernel, [(2 * planes * PAD, cols)], (by_even, by_odd))
-        got_halo = send(halo_tail, "lat", swap)
+        (widened,) = on_chip(widen_kernel, [(planes * wide + 8, cols)], (summed, tail, got))
+        end = planes * wide
+        if depth_count == 4:
+            by_odd, by_even = [
+                send(widened, "depth", [(i, i ^ k) for i in range(4)]) for k in (3, 1)
+            ]
+            further = send(widened[end:], "depth", [(i, i ^ 2) for i in range(4)])
+            largest = jnp.maximum(
+                jnp.maximum(widened[end:], further), jnp.maximum(by_odd[end:], by_even[end:])
+            )
+        else:
+            by_even = send(widened, "depth", evens)
+            by_odd = send(widened, "depth", odds)
+            largest = depth_max(widened[end:])
         stiff, own_velocity = on_chip(
             restiff_kernel,
             [stiff.shape, velocity.shape],
-            (stiff, summed, got, by_even, by_odd, got_halo, largest, own_velocity),
+            (stiff, widened, by_even, by_odd, largest, own_velocity),
         )
 
 

time: 59.7 us -> 59.2 us (level)
  waiting for transfers between devices: 17.8 us -> 20 us
  starting transfers between devices: 30.2 us -> 28.3 us
  local copies, waits for them, and re-layouts: 0.83 us -> 0.05 us
    ppermute x19 -> x17, waiting for transfers between devices: 9.9 us -> 11.2 us  [send(): return lax.ppermute(block, axis, pairs)]
    ppermute x2, starting transfers between devices: 2.18 us -> 1.2 us  [shot_terms(): return (block, lax.ppermute(block, 'shot', swap))]
    ppermute x2, waiting for transfers between devices: 6.7 us -> 7.67 us  [shot_terms(): return (block, lax.ppermute(block, 'shot', swap))]
    ppermute x19 -> x17, starting transfers between devices: 27.9 us -> 27 us  [send(): return lax.ppermute(block, axis, pairs)]
    pallas_call x11 -> x13, Pallas kernels: 6.12 us -> 6.15 us  [on_chip(): pl.pallas_call(kernel, out_shape=outs, in_specs=[spec] * len(args), out_s...]
  transfers between devices with their start and end apart: 22 -> 20, of which waited for: 11 -> 8; matrix products, arithmetic and copies ran while one was open for 1% -> 0% of each run, Pallas kernels for 8% -> 10%
where the time goes in v7:
time: 59.2 us; the launch traced here: 59 us
  starting transfers between devices  28.3 us (48%)
  waiting for transfers between devices  20 us (34%)
  Pallas kernels  9.46 us (16%)
  between operations  0.97 us (2%)
    ppermute x17, starting transfers between devices, send(): return lax.ppermute(block, axis, pairs)  27 us
    ppermute x17, waiting for transfers between devices, send(): return lax.ppermute(block, axis, pairs)  11.2 us
    ppermute x2, waiting for transfers between devices, shot_terms(): return (block, lax.ppermute(block, 'shot', swap))  7.67 us
    pallas_call x13, Pallas kernels, on_chip(): pl.pallas_call(kernel, out_shape=outs, in_specs=[spec] * len(args), out_s...  6.15 us
    pallas_call x2, Pallas kernels, load(): pl.pallas_call(kernel, out_shape=tuple((pltpu.VMEM(*shape) for shape in s...  2.16 us
    ppermute x2, starting transfers between devices, shot_terms(): return (block, lax.ppermute(block, 'shot', swap))  1.2 us
  transfers between devices with their start and end apart: 20, of which 8 were waited for; matrix products, arithmetic and copies ran while one was open for 0% of the time, Pallas kernels for 10%

profile of v7, /device:TPU:0, one launch (start us, length us, event | category | flops | bytes accessed | tf_op | source)
XLA Modules:
  0.0 59.0 jit_solution(5053677102934403610)
XLA Ops:
  0.6 1.0 %shard_map.113 = (f32[7,64,128]{2,1,0:T(8,128)S(1)}, f32[48,128]{1,0:T(8,128)S(1)}) custom-call(f32[2,2,64,128]{3,2,1,0:T(8,128)} %now.1, f32[2,64,128]{2,1,0:T(8,128)} %dens.1, f32[2,64,64]{2,1,0:T(8,128)} %velocity.1), custom_call_target="tpu_custom_call" | custom-call | tf_op jit(solution)/shard_map/pallas_call | solution.py:555
  1.7 3.1 %collective-permute-start = (f32[7,64,128]{2,1,0:T(8,128)S(1)}, f32[7,64,128]{2,1,0:T(8,128)S(1)}, u32[]{:S(2)}, u32[]{:S(2)}) collective-permute-start(f32[7,64,128]{2,1,0:T(8,128)S(1)} %get-tuple-element.31.first.refs_0_), channel_id=1, source_target_pairs={{0,4},{4,0},{8,12},{12,8},{1,5},{5,1},{9,13},{13,9},{2,6},{6,2},{1... | collective-permute-start | bytes 688136 | tf_op jit(solution)/shard_map/ppermute | solution.py:32
  4.8 0.7 %collective-permute-start.1 = (f32[7,64,128]{2,1,0:T(8,128)S(1)}, f32[7,64,128]{2,1,0:T(8,128)S(1)}, u32[]{:S(2)}, u32[]{:S(2)}) collective-permute-start(f32[7,64,128]{2,1,0:T(8,128)S(1)} %get-tuple-element.31.first.refs_0_), channel_id=1, source_target_pairs={{4,8},{8,4},{5,9},{9,5},{6,10},{10,6},{7,11},{11,7},{20,24},{24,20... | collective-permute-start | bytes 688136 | tf_op jit(solution)/shard_map/ppermute | solution.py:32
  5.5 1.1 %shard_map.114 = (f32[8,64,128]{2,1,0:T(8,128)S(1)}, f32[2,2,64,128]{3,2,1,0:T(8,128)S(1)}, s32[2,2048]{1,0:T(2,128)S(1)}, f32[2,2,2048]{2,1,0:T(2,128)S(1)}) custom-call(f32[2,2,64,128]{3,2,1,0:T(8,128)} %prev.1, f32[2,2,64,128]{3,2,1,0:T(8,128)} %last.1, f32[2,2,64,128]{3,2,1,0:T(8,128)} %late.1, s32[2,2048]{1,0:T(2,128)} %cells.1, f32[2,2,2048]{2,1,0:T(2,128)} %observed.1), custom_call_target="tpu_custom_call" | custom-call | tf_op jit(solution)/shard_map/pallas_call | solution.py:555
  6.6 4.5 %collective-permute-start.7 = (f32[8,64,128]{2,1,0:T(8,128)S(1)}, f32[8,64,128]{2,1,0:T(8,128)S(1)}, u32[]{:S(2)}, u32[]{:S(2)}) collective-permute-start(f32[8,64,128]{2,1,0:T(8,128)S(1)} %get-tuple-element.36.refs_1_), channel_id=1, source_target_pairs={{0,4},{4,0},{8,12},{12,8},{1,5},{5,1},{9,13},{13,9},{2,6},{6,2},{1... | collective-permute-start | bytes 786440 | tf_op jit(solution)/shard_map/ppermute | solution.py:32
  11.0 0.7 %collective-permute-start.8 = (f32[8,64,128]{2,1,0:T(8,128)S(1)}, f32[8,64,128]{2,1,0:T(8,128)S(1)}, u32[]{:S(2)}, u32[]{:S(2)}) collective-permute-start(f32[8,64,128]{2,1,0:T(8,128)S(1)} %get-tuple-element.36.refs_1_), channel_id=1, source_target_pairs={{4,8},{8,4},{5,9},{9,5},{6,10},{10,6},{7,11},{11,7},{20,24},{24,20... | collective-permute-start | bytes 786440 | tf_op jit(solution)/shard_map/ppermute | solution.py:32
  11.7 0.1 collective-permute-start.2
  11.8 0.1 and_select_fusion
  12.0 0.0 collective-permute-done.by_even.refs_3_
  12.0 0.0 collective-permute-done.1.by_odd.refs_4_
  12.1 1.6 %collective-permute-start.5 = (f32[3,64,128]{2,1,0:T(8,128)S(1)}, f32[3,64,128]{2,1,0:T(8,128)S(1)}, u32[]{:S(2)}, u32[]{:S(2)}) collective-permute-start(f32[3,64,128]{2,1,0:T(8,128)S(1)} %pad_maximum_fusion), channel_id=1, source_target_pairs={{0,2},{2,0},{1,3},{3,1},{4,6},{6,4},{5,7},{7,5},{8,10},{10,8},{9,1... | collective-permute-start | bytes 294920 | tf_op jit(solution)/shard_map/ppermute | solution.py:32
  13.6 1.6 %shard_map.118.refs_8_.refs_13_ = f32[3,320,128]{2,1,0:T(8,128)S(1)} custom-call(s32[1,2048]{1,0:T(1,128)S(1)} %get-tuple-element.72.row_ref, s32[1,2048]{1,0:T(1,128)S(1)} %get-tuple-element.67.col_ref, f32[2,2048]{1,0:T(2,128)S(1)} %get-tuple-element.65.obs_ref), custom_call_target="tpu_custom_call" | custom-call | flops 1174405120 | bytes 32768 | tf_op jit(solution)/shard_map/pallas_call | solution.py:40
  15.2 0.0 collective-permute-done.2.edges
  15.2 0.2 shard_map.115
  15.4 3.8 %collective-permute-start.3 = (f32[4,64,128]{2,1,0:T(8,128)S(1)}, f32[4,64,128]{2,1,0:T(8,128)S(1)}, u32[]{:S(2)}, u32[]{:S(2)}) collective-permute-start(f32[4,64,128]{2,1,0:T(8,128)S(1)} %get-tuple-element.34), channel_id=1, source_target_pairs={{0,4},{4,0},{8,12},{12,8},{1,5},{5,1},{9,13},{13,9},{2,6},{6,2},{1... | collective-permute-start | bytes 393224 | tf_op jit(solution)/shard_map/ppermute | solution.py:32
  19.3 0.7 %collective-permute-start.4 = (f32[4,64,128]{2,1,0:T(8,128)S(1)}, f32[4,64,128]{2,1,0:T(8,128)S(1)}, u32[]{:S(2)}, u32[]{:S(2)}) collective-permute-start(f32[4,64,128]{2,1,0:T(8,128)S(1)} %get-tuple-element.35), channel_id=1, source_target_pairs={{4,8},{8,4},{5,9},{9,5},{6,10},{10,6},{7,11},{11,7},{20,24},{24,20... | collective-permute-start | bytes 393224 | tf_op jit(solution)/shard_map/ppermute | solution.py:32
  19.9 0.0 collective-permute-done.7.refs_5_
  20.0 0.0 collective-permute-done.8.refs_6_
  20.0 0.1 collective-permute-start.9
  20.1 0.0 collective-permute-done.5
  20.1 2.1 %collective-permute-done.3.refs_0_ = f32[4,64,128]{2,1,0:T(8,128)S(1)} collective-permute-done((f32[4,64,128]{2,1,0:T(8,128)S(1)}, f32[4,64,128]{2,1,0:T(8,128)S(1)}, u32[]{:S(2)}, u32[]{:S(2)}) %collective-permute-start.3) | collective-permute-done | bytes 131104 | tf_op jit(solution)/shard_map/ppermute | solution.py:32
  22.2 0.0 collective-permute-done.4.refs_1_
  22.2 0.1 shard_map.116
  22.3 0.1 collective-permute-start.6
  22.4 0.0 copy-start.1
  22.4 0.0 copy-start.2
  22.4 1.6 %shard_map.119.refs_9_.refs_14_ = f32[3,320,128]{2,1,0:T(8,128)S(1)} custom-call(s32[1,2048]{1,0:T(1,128)S(1)} %get-tuple-element.73.row_ref, s32[1,2048]{1,0:T(1,128)S(1)} %get-tuple-element.66.col_ref, f32[2,2048]{1,0:T(2,128)S(1)} %get-tuple-element.64.obs_ref), custom_call_target="tpu_custom_call" | custom-call | flops 1174405120 | bytes 32768 | tf_op jit(solution)/shard_map/pallas_call | solution.py:40
  24.0 0.0 collective-permute-done.9.refs_7_
  24.0 0.0 copy-done.1
  24.0 0.0 copy-done.2
  24.0 1.2 %early.1 = (f32[2,4,80,128]{3,2,1,0:T(8,128)S(1)}, f32[2,6,80,128]{3,2,1,0:T(8,128)S(1)}, f32[2,4,80,128]{3,2,1,0:T(8,128)S(1)}, f32[2,2,80,128]{3,2,1,0:T(8,128...) custom-call(f32[7,64,128]{2,1,0:T(8,128)S(1)} %get-tuple-element.31., ...), custom_call_target="tpu_custom_call" | custom-call | tf_op jit(solution)/shard_map/early/pallas_call | solution.py:668
  25.2 0.0 collective-permute-done.6.refs_4_
  25.2 0.1 shard_map.120
  25.3 0.7 %shard_map.121.mine = f32[2,64,128]{2,1,0:T(8,128)S(1)} custom-call(f32[6,80,128]{2,1,0:T(8,128)S(1)} %get-tuple-element.41.refs_0_.stiff, f32[2,4,80,128]{3,2,1,0:T(8,128)S(1)} %get-tuple-element.42.refs_1_, f32[2,2,80,128]{3,2,1,0:T(8,128)S(1)} %get-tuple-element.43.refs_2_, f32[2,6,80,128]{3,2,1,0:T(8,128)S(1)} %get-tuple-element.44.refs_3_, ...), custom_call_target="tpu_custom_call" | custom-call | bytes 4341760 | tf_op jit(solution)/shard_map/pallas_call | solution.py:40
  26.1 0.6 %collective-permute-start.10 = (f32[2,64,128]{2,1,0:T(8,128)S(1)}, f32[2,64,128]{2,1,0:T(8,128)S(1)}, u32[]{:S(2)}, u32[]{:S(2)}) collective-permute-start(f32[2,64,128]{2,1,0:T(8,128)S(1)} %shard_map.121.mine), channel_id=1, source_target_pairs={{0,2},{2,0},{1,3},{3,1},{4,6},{6,4},{5,7},{7,5},{8,10},{10,8},{9,1... | collective-permute-start | bytes 196616 | tf_op jit(solution)/shard_map/ppermute | solution.py:530
  26.7 3.9 %collective-permute-done.10.other = f32[2,64,128]{2,1,0:T(8,128)S(1)} collective-permute-done((f32[2,64,128]{2,1,0:T(8,128)S(1)}, f32[2,64,128]{2,1,0:T(8,128)S(1)}, u32[]{:S(2)}, u32[]{:S(2)}) %collective-permute-start.10) | collective-permute-done | bytes 65568 | tf_op jit(solution)/shard_map/ppermute | solution.py:530
  30.6 0.1 collective-permute-start.11
  30.7 1.2 %collective-permute-done.11.got = f32[24,128]{1,0:T(8,128)S(1)} collective-permute-done((f32[24,128]{1,0:T(8,128)S(1)}, f32[24,128]{1,0:T(8,128)S(1)}, u32[]{:S(2)}, u32[]{:S(2)}) %collective-permute-start.11) | collective-permute-done | bytes 12320 | tf_op jit(solution)/shard_map/ppermute | solution.py:32
  31.9 0.0 copy-start
  31.9 4.5 %collective-permute-start.12 = (f32[168,128]{1,0:T(8,128)S(1)}, f32[168,128]{1,0:T(8,128)S(1)}, u32[]{:S(2)}, u32[]{:S(2)}) collective-permute-start(f32[168,128]{1,0:T(8,128)S(1)} %shard_map.123.mine), channel_id=1, source_target_pairs={{0,4},{4,0},{8,12},{12,8},{1,5},{5,1},{9,13},{13,9},{2,6},{6,2},{1... | collective-permute-start | bytes 258056 | tf_op jit(solution)/shard_map/ppermute | solution.py:32
  36.3 2.9 %collective-permute-start.13 = (f32[168,128]{1,0:T(8,128)S(1)}, f32[168,128]{1,0:T(8,128)S(1)}, u32[]{:S(2)}, u32[]{:S(2)}) collective-permute-start(f32[168,128]{1,0:T(8,128)S(1)} %shard_map.123.mine), channel_id=1, source_target_pairs={{0,12},{4,8},{8,4},{12,0},{1,13},{5,9},{9,5},{13,1},{2,14},{6,10},... | collective-permute-start | bytes 258056 | tf_op jit(solution)/shard_map/ppermute | solution.py:32
  39.3 0.0 collective-permute-start.14
  39.3 4.5 %collective-permute-done.14 = f32[8,128]{1,0:T(8,128)S(1)} collective-permute-done((f32[8,128]{1,0:T(8,128)S(1)}, f32[8,128]{1,0:T(8,128)S(1)}, u32[]{:S(2)}, u32[]{:S(2)}) %collective-permute-start.14) | collective-permute-done | bytes 4128 | tf_op jit(solution)/shard_map/ppermute | solution.py:32
  43.8 0.0 collective-permute-done.12.by_even
  43.8 0.0 collective-permute-done.13.by_odd
  43.8 0.0 copy-done
  43.8 0.2 shard_map.124
  44.1 0.7 %shard_map.125.mine = f32[2,64,128]{2,1,0:T(8,128)S(1)} custom-call(f32[6,80,128]{2,1,0:T(8,128)S(1)} %get-tuple-element.56.refs_0_, f32[2,4,80,128]{3,2,1,0:T(8,128)S(1)} %get-tuple-element.42.refs_1_, f32[2,2,80,128]{3,2,1,0:T(8,128)S(1)} %get-tuple-element.43.refs_2_, f32[2,6,80,128]{3,2,1,0:T(8,128)S(1)} %get-tuple-element.44.refs_3_, ...), custom_call_target="tpu_custom_call" | custom-call | bytes 4341760 | tf_op jit(solution)/shard_map/pallas_call | solution.py:40
  44.8 0.6 %collective-permute-start.15 = (f32[2,64,128]{2,1,0:T(8,128)S(1)}, f32[2,64,128]{2,1,0:T(8,128)S(1)}, u32[]{:S(2)}, u32[]{:S(2)}) collective-permute-start(f32[2,64,128]{2,1,0:T(8,128)S(1)} %shard_map.125.mine), channel_id=1, source_target_pairs={{0,2},{2,0},{1,3},{3,1},{4,6},{6,4},{5,7},{7,5},{8,10},{10,8},{9,1... | collective-permute-start | bytes 196616 | tf_op jit(solution)/shard_map/ppermute | solution.py:530
  45.4 3.7 %collective-permute-done.15.other = f32[2,64,128]{2,1,0:T(8,128)S(1)} collective-permute-done((f32[2,64,128]{2,1,0:T(8,128)S(1)}, f32[2,64,128]{2,1,0:T(8,128)S(1)}, u32[]{:S(2)}, u32[]{:S(2)}) %collective-permute-start.15) | collective-permute-done | bytes 65568 | tf_op jit(solution)/shard_map/ppermute | solution.py:530
  49.1 0.1 collective-permute-start.16
  49.2 1.2 %collective-permute-done.16 = f32[8,128]{1,0:T(8,128)S(1)} collective-permute-done((f32[8,128]{1,0:T(8,128)S(1)}, f32[8,128]{1,0:T(8,128)S(1)}, u32[]{:S(2)}, u32[]{:S(2)}) %collective-permute-start.16) | collective-permute-done | bytes 4128 | tf_op jit(solution)/shard_map/ppermute | solution.py:714
  50.4 0.5 collective-permute-start.17
  50.9 1.8 %collective-permute-start.18 = (f32[8,128]{1,0:T(8,128)S(1)}, f32[8,128]{1,0:T(8,128)S(1)}, u32[]{:S(2)}, u32[]{:S(2)}) collective-permute-start(f32[8,128]{1,0:T(8,128)S(1)} %max.24), channel_id=1, source_target_pairs={{0,8},{4,12},{8,0},{12,4},{1,9},{5,13},{9,1},{13,5},{2,10},{6,14},... | collective-permute-start | bytes 12296 | tf_op jit(solution)/shard_map/ppermute | solution.py:32
  52.7 2.1 %collective-permute-start.19 = (f32[8,128]{1,0:T(8,128)S(1)}, f32[8,128]{1,0:T(8,128)S(1)}, u32[]{:S(2)}, u32[]{:S(2)}) collective-permute-start(f32[8,128]{1,0:T(8,128)S(1)} %max.24), channel_id=1, source_target_pairs={{0,12},{4,8},{8,4},{12,0},{1,13},{5,9},{9,5},{13,1},{2,14},{6,10},... | collective-permute-start | bytes 12296 | tf_op jit(solution)/shard_map/ppermute | solution.py:32
  54.8 0.0 collective-permute-done.17
  54.8 0.6 %collective-permute-done.18 = f32[8,128]{1,0:T(8,128)S(1)} collective-permute-done((f32[8,128]{1,0:T(8,128)S(1)}, f32[8,128]{1,0:T(8,128)S(1)}, u32[]{:S(2)}, u32[]{:S(2)}) %collective-permute-start.18) | collective-permute-done | bytes 4128 | tf_op jit(solution)/shard_map/ppermute | solution.py:32
  55.4 2.7 %collective-permute-done.19 = f32[8,128]{1,0:T(8,128)S(1)} collective-permute-done((f32[8,128]{1,0:T(8,128)S(1)}, f32[8,128]{1,0:T(8,128)S(1)}, u32[]{:S(2)}, u32[]{:S(2)}) %collective-permute-start.19) | collective-permute-done | bytes 4128 | tf_op jit(solution)/shard_map/ppermute | solution.py:32
  58.1 0.8 %shard_map.127 = (f32[2,64,64]{2,1,0:T(8,128)}, f32[2,64,64]{2,1,0:T(8,128)}) custom-call(f32[2,64,128]{2,1,0:T(8,128)S(1)} %get-tuple-element.57.total, f32[8,128]{1,0:T(8,128)S(1)} %maximum_maximum_fusion.largest, f32[2,64,64]{2,1,0:T(8,128)S(1)} %get-tuple-element.59.velocity), custom_call_target="tpu_custom_call" | custom-call | bytes 102400 | tf_op jit(solution)/shard_map/pallas_call | solution.py:40
  (14 shorter events, 0.2 us)
Async XLA Ops:
  1.7 10.3 %collective-permute-start = (f32[7,64,128]{2,1,0:T(8,128)S(1)}, f32[7,64,128]{2,1,0:T(8,128)S(1)}, u32[]{:S(2)}, u32[]{:S(2)}) collective-permute-start(f32[7,64,128]{2,1,0:T(8,128)S(1)} %get-tuple-element.31.first.refs_0_), channel_id=1, source_target_pairs={{0,4},{4,0},{8,12},{12,8},{1,5},{5,1},{9,13},{13,9},{2,6},{6,2},{1... | collective-permute-start | bytes 688136 | tf_op jit(solution)/shard_map/ppermute | solution.py:32
  4.8 7.2 %collective-permute-start.1 = (f32[7,64,128]{2,1,0:T(8,128)S(1)}, f32[7,64,128]{2,1,0:T(8,128)S(1)}, u32[]{:S(2)}, u32[]{:S(2)}) collective-permute-start(f32[7,64,128]{2,1,0:T(8,128)S(1)} %get-tuple-element.31.first.refs_0_), channel_id=1, source_target_pairs={{4,8},{8,4},{5,9},{9,5},{6,10},{10,6},{7,11},{11,7},{20,24},{24,20... | collective-permute-start | bytes 688136 | tf_op jit(solution)/shard_map/ppermute | solution.py:32
  6.6 13.4 %collective-permute-start.7 = (f32[8,64,128]{2,1,0:T(8,128)S(1)}, f32[8,64,128]{2,1,0:T(8,128)S(1)}, u32[]{:S(2)}, u32[]{:S(2)}) collective-permute-start(f32[8,64,128]{2,1,0:T(8,128)S(1)} %get-tuple-element.36.refs_1_), channel_id=1, source_target_pairs={{0,4},{4,0},{8,12},{12,8},{1,5},{5,1},{9,13},{13,9},{2,6},{6,2},{1... | collective-permute-start | bytes 786440 | tf_op jit(solution)/shard_map/ppermute | solution.py:32
  11.0 8.9 %collective-permute-start.8 = (f32[8,64,128]{2,1,0:T(8,128)S(1)}, f32[8,64,128]{2,1,0:T(8,128)S(1)}, u32[]{:S(2)}, u32[]{:S(2)}) collective-permute-start(f32[8,64,128]{2,1,0:T(8,128)S(1)} %get-tuple-element.36.refs_1_), channel_id=1, source_target_pairs={{4,8},{8,4},{5,9},{9,5},{6,10},{10,6},{7,11},{11,7},{20,24},{24,20... | collective-permute-start | bytes 786440 | tf_op jit(solution)/shard_map/ppermute | solution.py:32
  11.7 3.5 %collective-permute-start.2 = (f32[48,128]{1,0:T(8,128)S(1)}, f32[48,128]{1,0:T(8,128)S(1)}, u32[]{:S(2)}, u32[]{:S(2)}) collective-permute-start(f32[48,128]{1,0:T(8,128)S(1)} %get-tuple-element.32), channel_id=1, source_target_pairs={{0,1},{1,0},{2,3},{3,2},{4,5},{5,4},{6,7},{7,6},{8,9},{9,8},{10,11... | collective-permute-start | bytes 73736 | tf_op jit(solution)/shard_map/ppermute | solution.py:32
  12.1 8.0 %collective-permute-start.5 = (f32[3,64,128]{2,1,0:T(8,128)S(1)}, f32[3,64,128]{2,1,0:T(8,128)S(1)}, u32[]{:S(2)}, u32[]{:S(2)}) collective-permute-start(f32[3,64,128]{2,1,0:T(8,128)S(1)} %pad_maximum_fusion), channel_id=1, source_target_pairs={{0,2},{2,0},{1,3},{3,1},{4,6},{6,4},{5,7},{7,5},{8,10},{10,8},{9,1... | collective-permute-start | bytes 294920 | tf_op jit(solution)/shard_map/ppermute | solution.py:32
  15.4 6.8 %collective-permute-start.3 = (f32[4,64,128]{2,1,0:T(8,128)S(1)}, f32[4,64,128]{2,1,0:T(8,128)S(1)}, u32[]{:S(2)}, u32[]{:S(2)}) collective-permute-start(f32[4,64,128]{2,1,0:T(8,128)S(1)} %get-tuple-element.34), channel_id=1, source_target_pairs={{0,4},{4,0},{8,12},{12,8},{1,5},{5,1},{9,13},{13,9},{2,6},{6,2},{1... | collective-permute-start | bytes 393224 | tf_op jit(solution)/shard_map/ppermute | solution.py:32
  19.3 3.0 %collective-permute-start.4 = (f32[4,64,128]{2,1,0:T(8,128)S(1)}, f32[4,64,128]{2,1,0:T(8,128)S(1)}, u32[]{:S(2)}, u32[]{:S(2)}) collective-permute-start(f32[4,64,128]{2,1,0:T(8,128)S(1)} %get-tuple-element.35), channel_id=1, source_target_pairs={{4,8},{8,4},{5,9},{9,5},{6,10},{10,6},{7,11},{11,7},{20,24},{24,20... | collective-permute-start | bytes 393224 | tf_op jit(solution)/shard_map/ppermute | solution.py:32
  20.0 4.0 %collective-permute-start.9 = (f32[368,128]{1,0:T(8,128)S(1)}, f32[368,128]{1,0:T(8,128)S(1)}, u32[]{:S(2)}, u32[]{:S(2)}) collective-permute-start(f32[368,128]{1,0:T(8,128)S(1)} %shard_map.117), channel_id=1, source_target_pairs={{0,1},{1,0},{2,3},{3,2},{4,5},{5,4},{6,7},{7,6},{8,9},{9,8},{10,11... | collective-permute-start | bytes 565256 | tf_op jit(solution)/shard_map/ppermute | solution.py:32
  22.3 2.9 %collective-permute-start.6 = (f32[112,128]{1,0:T(8,128)S(1)}, f32[112,128]{1,0:T(8,128)S(1)}, u32[]{:S(2)}, u32[]{:S(2)}) collective-permute-start(f32[112,128]{1,0:T(8,128)S(1)} %shard_map.116), channel_id=1, source_target_pairs={{0,1},{1,0},{2,3},{3,2},{4,5},{5,4},{6,7},{7,6},{8,9},{9,8},{10,11... | collective-permute-start | bytes 172040 | tf_op jit(solution)/shard_map/ppermute | solution.py:32
  22.4 1.6 %copy-start.1 = (f32[2,2]{1,0:T(2,128)S(1)}, f32[2,2]{1,0:T(2,128)}, u32[]{:S(2)}) copy-start(f32[2,2]{1,0:T(2,128)} %refs_11_.1) | copy-start | bytes 52
  22.4 1.6 %copy-start.2 = (s32[2]{0:T(128)S(1)}, s32[2]{0:T(128)}, u32[]{:S(2)}) copy-start(s32[2]{0:T(128)} %refs_10_.1) | copy-start | bytes 28
  26.1 4.5 %collective-permute-start.10 = (f32[2,64,128]{2,1,0:T(8,128)S(1)}, f32[2,64,128]{2,1,0:T(8,128)S(1)}, u32[]{:S(2)}, u32[]{:S(2)}) collective-permute-start(f32[2,64,128]{2,1,0:T(8,128)S(1)} %shard_map.121.mine), channel_id=1, source_target_pairs={{0,2},{2,0},{1,3},{3,1},{4,6},{6,4},{5,7},{7,5},{8,10},{10,8},{9,1... | collective-permute-start | bytes 196616 | tf_op jit(solution)/shard_map/ppermute | solution.py:530
  30.6 1.2 %collective-permute-start.11 = (f32[24,128]{1,0:T(8,128)S(1)}, f32[24,128]{1,0:T(8,128)S(1)}, u32[]{:S(2)}, u32[]{:S(2)}) collective-permute-start(f32[24,128]{1,0:T(8,128)S(1)} %get-tuple-element.55.mine), channel_id=1, source_target_pairs={{0,1},{1,0},{2,3},{3,2},{4,5},{5,4},{6,7},{7,6},{8,9},{9,8},{10,11... | collective-permute-start | bytes 36872 | tf_op jit(solution)/shard_map/ppermute | solution.py:32
  31.9 12.0 %copy-start = (f32[2,64,64]{2,1,0:T(8,128)S(1)}, f32[2,64,64]{2,1,0:T(8,128)}, u32[]{:S(2)}) copy-start(f32[2,64,64]{2,1,0:T(8,128)} %velocity.1) | copy-start | bytes 98308
  31.9 11.9 %collective-permute-start.12 = (f32[168,128]{1,0:T(8,128)S(1)}, f32[168,128]{1,0:T(8,128)S(1)}, u32[]{:S(2)}, u32[]{:S(2)}) collective-permute-start(f32[168,128]{1,0:T(8,128)S(1)} %shard_map.123.mine), channel_id=1, source_target_pairs={{0,4},{4,0},{8,12},{12,8},{1,5},{5,1},{9,13},{13,9},{2,6},{6,2},{1... | collective-permute-start | bytes 258056 | tf_op jit(solution)/shard_map/ppermute | solution.py:32
  36.3 7.5 %collective-permute-start.13 = (f32[168,128]{1,0:T(8,128)S(1)}, f32[168,128]{1,0:T(8,128)S(1)}, u32[]{:S(2)}, u32[]{:S(2)}) collective-permute-start(f32[168,128]{1,0:T(8,128)S(1)} %shard_map.123.mine), channel_id=1, source_target_pairs={{0,12},{4,8},{8,4},{12,0},{1,13},{5,9},{9,5},{13,1},{2,14},{6,10},... | collective-permute-start | bytes 258056 | tf_op jit(solution)/shard_map/ppermute | solution.py:32
  39.3 4.5 %collective-permute-start.14 = (f32[8,128]{1,0:T(8,128)S(1)}, f32[8,128]{1,0:T(8,128)S(1)}, u32[]{:S(2)}, u32[]{:S(2)}) collective-permute-start(f32[8,128]{1,0:T(8,128)S(1)} %slice.57), channel_id=1, source_target_pairs={{0,8},{4,12},{8,0},{12,4},{1,9},{5,13},{9,1},{13,5},{2,10},{6,14},... | collective-permute-start | bytes 12296 | tf_op jit(solution)/shard_map/ppermute | solution.py:32
  44.8 4.3 %collective-permute-start.15 = (f32[2,64,128]{2,1,0:T(8,128)S(1)}, f32[2,64,128]{2,1,0:T(8,128)S(1)}, u32[]{:S(2)}, u32[]{:S(2)}) collective-permute-start(f32[2,64,128]{2,1,0:T(8,128)S(1)} %shard_map.125.mine), channel_id=1, source_target_pairs={{0,2},{2,0},{1,3},{3,1},{4,6},{6,4},{5,7},{7,5},{8,10},{10,8},{9,1... | collective-permute-start | bytes 196616 | tf_op jit(solution)/shard_map/ppermute | solution.py:530
  49.1 1.2 %collective-permute-start.16 = (f32[8,128]{1,0:T(8,128)S(1)}, f32[8,128]{1,0:T(8,128)S(1)}, u32[]{:S(2)}, u32[]{:S(2)}) collective-permute-start(f32[8,128]{1,0:T(8,128)S(1)} %get-tuple-element.58), channel_id=1, source_target_pairs={{0,1},{1,0},{2,3},{3,2},{4,5},{5,4},{6,7},{7,6},{8,9},{9,8},{10,11... | collective-permute-start | bytes 12296 | tf_op jit(solution)/shard_map/ppermute | solution.py:714
  50.4 4.4 %collective-permute-start.17 = (f32[8,128]{1,0:T(8,128)S(1)}, f32[8,128]{1,0:T(8,128)S(1)}, u32[]{:S(2)}, u32[]{:S(2)}) collective-permute-start(f32[8,128]{1,0:T(8,128)S(1)} %max.24), channel_id=1, source_target_pairs={{0,4},{4,0},{8,12},{12,8},{1,5},{5,1},{9,13},{13,9},{2,6},{6,2},{1... | collective-permute-start | bytes 12296 | tf_op jit(solution)/shard_map/ppermute | solution.py:32
  50.9 4.5 %collective-permute-start.18 = (f32[8,128]{1,0:T(8,128)S(1)}, f32[8,128]{1,0:T(8,128)S(1)}, u32[]{:S(2)}, u32[]{:S(2)}) collective-permute-start(f32[8,128]{1,0:T(8,128)S(1)} %max.24), channel_id=1, source_target_pairs={{0,8},{4,12},{8,0},{12,4},{1,9},{5,13},{9,1},{13,5},{2,10},{6,14},... | collective-permute-start | bytes 12296 | tf_op jit(solution)/shard_map/ppermute | solution.py:32
  52.7 5.4 %collective-permute-start.19 = (f32[8,128]{1,0:T(8,128)S(1)}, f32[8,128]{1,0:T(8,128)S(1)}, u32[]{:S(2)}, u32[]{:S(2)}) collective-permute-start(f32[8,128]{1,0:T(8,128)S(1)} %max.24), channel_id=1, source_target_pairs={{0,12},{4,8},{8,4},{12,0},{1,13},{5,9},{9,5},{13,1},{2,14},{6,10},... | collective-permute-start | bytes 12296 | tf_op jit(solution)/shard_map/ppermute | solution.py:32

commit v8 on v7

--- a/solution.py
+++ b/solution.py
@@ -146,8 +146,13 @@
             own = self.cols // len(self.vel)
             column = lax.broadcasted_iota(jnp.int32, (self.rows, self.cols), 1)
             value = None
-            for index, part in enumerate(self.vel):
-                shifted = pltpu.roll(part[block], (index - lane) * own % self.cols, 1)
+            planes_of = [part[block] for part in self.vel]
+            if len(planes_of) == 2:
+                mine, other = planes_of
+                here = lax.axis_index("shot") == 0
+                planes_of = [jnp.where(here, mine, other), jnp.where(here, other, mine)]
+            for index, part in enumerate(planes_of):
+                shifted = pltpu.roll(part, (index - lane) * own % self.cols, 1)
                 value = shifted if value is None else jnp.where(column >= index * own, shifted, value)
             return value
         if which == LAP:
@@ -253,10 +258,14 @@
     cm(at, 0.5 * (plane + below))
 
 
-def third_kernel(first, by_even, by_odd, edges, late, to_even, to_odd, now_buf, buoy_buf, cz, cx, cp, cm):
+def third_kernel(first, by_even, by_odd, edges, late, to_even, to_odd, lines, now_buf, buoy_buf, cz, cx, cp, cm):
     even = lax.axis_index("depth") % 2 == 0
     lat_at = lax.axis_index("lat")
     shots, planes, rows, cols = late.shape
+    place = (shots + 1) * planes
+    lines[0] = jnp.where(even, by_odd[place], by_even[place])
+    lines[1] = first[place]
+    lines[2] = jnp.where(even, by_even[place], by_odd[place])
 
     def whole(index, at):
         if 0 <= at < planes:
@@ -519,7 +528,6 @@
         raise ValueError("unsupported split")
     depth_at = lax.axis_index("depth")
     lat_at = lax.axis_index("lat")
-    shot_at = lax.axis_index("shot")
     evens = even_pairs(depth_count)
     odds = odd_pairs(depth_count)
     swap = [(0, 1), (1, 0)]
@@ -587,29 +595,21 @@
     second_odd = send(second, "depth", odds)
     second_even = send(second, "depth", evens)
 
-    even = depth_at % 2 == 0
-    lines = jnp.stack(
-        [
-            jnp.where(even, first_odd[own_planes], first_even[own_planes]),
-            first[own_planes],
-            jnp.where(even, first_even[own_planes], first_odd[own_planes]),
-        ]
-    )
-    if shot_count == 2:
-        other = send(lines, "shot", swap)
-        parts = [jnp.where(shot_at == 0, lines, other), jnp.where(shot_at == 0, other, lines)]
-    else:
-        gathered = lax.all_gather(lines, "shot")
-        parts = [gathered[k] for k in range(shot_count)]
     small = (planes + 1, wide, cols)
-    to_even, to_odd = on_chip(
+    to_even, to_odd, lines = on_chip(
         third_kernel,
-        [(2 * shots, rows, cols)] * 2,
+        [(2 * shots, rows, cols)] * 2 + [(3, rows, cols)],
         (first, first_even, first_odd, first_edges, late),
         scratch=[(shots, planes + 2, wide, cols), (planes + 2, wide, cols)] + [small] * 4,
     )
     third_odd = send(to_odd, "depth", odds)
     third_even = send(to_even, "depth", evens)
+
+    if shot_count == 2:
+        parts = (lines, send(lines, "shot", swap))
+    else:
+        gathered = lax.all_gather(lines, "shot")
+        parts = tuple(gathered[k] for k in range(shot_count))
 
     full_rows = rows * lat_count
     depth_start = depth_at * planes
@@ -679,7 +679,7 @@
     )(*[pltpu.with_memory_space_constraint(a, pltpu.VMEM) for a in vectors], source_cell, wavelet)
     lap, base, turn, late_own, ahead, last, low, dens, cz, cx, cp, cm = outs
 
-    final = (third_even, third_odd) + tuple(parts)
+    final = (third_even, third_odd) + parts
     shape = adj_late.shape
     strips = 4 * shots + planes + 4
     (edges,) = on_chip(functools.partial(final_edge_kernel, shape), [(strips * PAD, cols)], final)

time: 59.2 us -> 61.3 us (1.035)
  waiting for transfers between devices: 20 us -> 22.1 us
    ppermute x17, waiting for transfers between devices: 11.2 us -> 15.1 us  [send(): return lax.ppermute(block, axis, pairs)]
    ppermute x2, waiting for transfers between devices: 7.67 us -> 5.76 us  [shot_terms(): return (block, lax.ppermute(block, 'shot', swap))]
    ppermute x2, starting transfers between devices: 1.2 us -> 3.11 us  [shot_terms(): return (block, lax.ppermute(block, 'shot', swap))]
    ppermute x17, starting transfers between devices: 27 us -> 25.2 us  [send(): return lax.ppermute(block, axis, pairs)]
  transfers between devices with their start and end apart: 20 -> 20, of which waited for: 8 -> 11; matrix products, arithmetic and copies ran while one was open for 0% -> 0% of each run, Pallas kernels for 10% -> 9%
where the time goes in v8:
time: 61.3 us; the launch traced here: 61 us
  starting transfers between devices  28.4 us (46%)
  waiting for transfers between devices  22.1 us (36%)
  Pallas kernels  9.52 us (16%)
  between operations  0.86 us (1%)
    ppermute x17, starting transfers between devices, send(): return lax.ppermute(block, axis, pairs)  25.2 us
    ppermute x17, waiting for transfers between devices, send(): return lax.ppermute(block, axis, pairs)  15.1 us
    pallas_call x13, Pallas kernels, on_chip(): pl.pallas_call(kernel, out_shape=outs, in_specs=[spec] * len(args), out_s...  6.21 us
    ppermute x2, waiting for transfers between devices, shot_terms(): return (block, lax.ppermute(block, 'shot', swap))  5.76 us
    ppermute x2, starting transfers between devices, shot_terms(): return (block, lax.ppermute(block, 'shot', swap))  3.11 us
    pallas_call x2, Pallas kernels, load(): pl.pallas_call(kernel, out_shape=tuple((pltpu.VMEM(*shape) for shape in s...  2.15 us
  transfers between devices with their start and end apart: 20, of which 11 were waited for; matrix products, arithmetic and copies ran while one was open for 0% of the time, Pallas kernels for 9%

profile of v8, /device:TPU:0, one launch (start us, length us, event | category | flops | bytes accessed | tf_op | source)
XLA Modules:
  0.0 61.0 jit_solution(5607242499106444116)
XLA Ops:
  0.6 1.1 %shard_map.114 = (f32[8,64,128]{2,1,0:T(8,128)S(1)}, f32[2,2,64,128]{3,2,1,0:T(8,128)S(1)}, s32[2,2048]{1,0:T(2,128)S(1)}, f32[2,2,2048]{2,1,0:T(2,128)S(1)}) custom-call(f32[2,2,64,128]{3,2,1,0:T(8,128)} %prev.1, f32[2,2,64,128]{3,2,1,0:T(8,128)} %last.1, f32[2,2,64,128]{3,2,1,0:T(8,128)} %late.1, s32[2,2048]{1,0:T(2,128)} %cells.1, f32[2,2,2048]{2,1,0:T(2,128)} %observed.1), custom_call_target="tpu_custom_call" | custom-call | tf_op jit(solution)/shard_map/pallas_call | solution.py:563
  1.7 3.1 %collective-permute-start.7 = (f32[8,64,128]{2,1,0:T(8,128)S(1)}, f32[8,64,128]{2,1,0:T(8,128)S(1)}, u32[]{:S(2)}, u32[]{:S(2)}) collective-permute-start(f32[8,64,128]{2,1,0:T(8,128)S(1)} %get-tuple-element.38.refs_1_), channel_id=1, source_target_pairs={{0,4},{4,0},{8,12},{12,8},{1,5},{5,1},{9,13},{13,9},{2,6},{6,2},{1... | collective-permute-start | bytes 786440 | tf_op jit(solution)/shard_map/ppermute | solution.py:32
  4.9 0.7 %collective-permute-start.8 = (f32[8,64,128]{2,1,0:T(8,128)S(1)}, f32[8,64,128]{2,1,0:T(8,128)S(1)}, u32[]{:S(2)}, u32[]{:S(2)}) collective-permute-start(f32[8,64,128]{2,1,0:T(8,128)S(1)} %get-tuple-element.38.refs_1_), channel_id=1, source_target_pairs={{4,8},{8,4},{5,9},{9,5},{6,10},{10,6},{7,11},{11,7},{20,24},{24,20... | collective-permute-start | bytes 786440 | tf_op jit(solution)/shard_map/ppermute | solution.py:32
  5.5 1.0 %shard_map.113 = (f32[7,64,128]{2,1,0:T(8,128)S(1)}, f32[48,128]{1,0:T(8,128)S(1)}) custom-call(f32[2,2,64,128]{3,2,1,0:T(8,128)} %now.1, f32[2,64,128]{2,1,0:T(8,128)} %dens.1, f32[2,64,64]{2,1,0:T(8,128)} %velocity.1), custom_call_target="tpu_custom_call" | custom-call | tf_op jit(solution)/shard_map/pallas_call | solution.py:563
  6.6 4.4 %collective-permute-start = (f32[7,64,128]{2,1,0:T(8,128)S(1)}, f32[7,64,128]{2,1,0:T(8,128)S(1)}, u32[]{:S(2)}, u32[]{:S(2)}) collective-permute-start(f32[7,64,128]{2,1,0:T(8,128)S(1)} %get-tuple-element.32.first.refs_0_), channel_id=1, source_target_pairs={{0,4},{4,0},{8,12},{12,8},{1,5},{5,1},{9,13},{13,9},{2,6},{6,2},{1... | collective-permute-start | bytes 688136 | tf_op jit(solution)/shard_map/ppermute | solution.py:32
  11.0 0.7 %collective-permute-start.1 = (f32[7,64,128]{2,1,0:T(8,128)S(1)}, f32[7,64,128]{2,1,0:T(8,128)S(1)}, u32[]{:S(2)}, u32[]{:S(2)}) collective-permute-start(f32[7,64,128]{2,1,0:T(8,128)S(1)} %get-tuple-element.32.first.refs_0_), channel_id=1, source_target_pairs={{4,8},{8,4},{5,9},{9,5},{6,10},{10,6},{7,11},{11,7},{20,24},{24,20... | collective-permute-start | bytes 688136 | tf_op jit(solution)/shard_map/ppermute | solution.py:32
  11.7 0.1 collective-permute-start.2
  11.8 0.1 and_select_fusion
  12.0 1.0 %collective-permute-done.2.edges = f32[48,128]{1,0:T(8,128)S(1)} collective-permute-done((f32[48,128]{1,0:T(8,128)S(1)}, f32[48,128]{1,0:T(8,128)S(1)}, u32[]{:S(2)}, u32[]{:S(2)}) %collective-permute-start.2) | collective-permute-done | bytes 24608 | tf_op jit(solution)/shard_map/ppermute | solution.py:32
  13.0 3.1 %collective-permute-done.by_even.refs_3_ = f32[7,64,128]{2,1,0:T(8,128)S(1)} collective-permute-done((f32[7,64,128]{2,1,0:T(8,128)S(1)}, f32[7,64,128]{2,1,0:T(8,128)S(1)}, u32[]{:S(2)}, u32[]{:S(2)}) %collective-permute-start) | collective-permute-done | bytes 229408 | tf_op jit(solution)/shard_map/ppermute | solution.py:32
  16.1 0.0 collective-permute-done.1.by_odd.refs_4_
  16.1 0.2 shard_map.115
  16.3 4.8 %collective-permute-start.3 = (f32[4,64,128]{2,1,0:T(8,128)S(1)}, f32[4,64,128]{2,1,0:T(8,128)S(1)}, u32[]{:S(2)}, u32[]{:S(2)}) collective-permute-start(f32[4,64,128]{2,1,0:T(8,128)S(1)} %get-tuple-element.35), channel_id=1, source_target_pairs={{0,4},{4,0},{8,12},{12,8},{1,5},{5,1},{9,13},{13,9},{2,6},{6,2},{1... | collective-permute-start | bytes 393224 | tf_op jit(solution)/shard_map/ppermute | solution.py:32
  21.1 0.7 %collective-permute-start.4 = (f32[4,64,128]{2,1,0:T(8,128)S(1)}, f32[4,64,128]{2,1,0:T(8,128)S(1)}, u32[]{:S(2)}, u32[]{:S(2)}) collective-permute-start(f32[4,64,128]{2,1,0:T(8,128)S(1)} %get-tuple-element.36), channel_id=1, source_target_pairs={{4,8},{8,4},{5,9},{9,5},{6,10},{10,6},{7,11},{11,7},{20,24},{24,20... | collective-permute-start | bytes 393224 | tf_op jit(solution)/shard_map/ppermute | solution.py:32
  21.8 1.6 %collective-permute-start.5 = (f32[3,64,128]{2,1,0:T(8,128)S(1)}, f32[3,64,128]{2,1,0:T(8,128)S(1)}, u32[]{:S(2)}, u32[]{:S(2)}) collective-permute-start(f32[3,64,128]{2,1,0:T(8,128)S(1)} %get-tuple-element.37.refs_2_), channel_id=1, source_target_pairs={{0,2},{2,0},{1,3},{3,1},{4,6},{6,4},{5,7},{7,5},{8,10},{10,8},{9,1... | collective-permute-start | bytes 294920 | tf_op jit(solution)/shard_map/ppermute | solution.py:32
  23.4 0.0 collective-permute-done.7.refs_5_
  23.4 0.0 collective-permute-done.8.refs_6_
  23.4 0.1 collective-permute-start.9
  23.5 1.6 %shard_map.118.refs_8_.refs_13_ = f32[3,320,128]{2,1,0:T(8,128)S(1)} custom-call(s32[1,2048]{1,0:T(1,128)S(1)} %get-tuple-element.70.row_ref, s32[1,2048]{1,0:T(1,128)S(1)} %get-tuple-element.65.col_ref, f32[2,2048]{1,0:T(2,128)S(1)} %get-tuple-element.63.obs_ref), custom_call_target="tpu_custom_call" | custom-call | flops 1174405120 | bytes 32768 | tf_op jit(solution)/shard_map/pallas_call | solution.py:40
  25.1 1.4 %collective-permute-done.5.refs_3_ = f32[3,64,128]{2,1,0:T(8,128)S(1)} collective-permute-done((f32[3,64,128]{2,1,0:T(8,128)S(1)}, f32[3,64,128]{2,1,0:T(8,128)S(1)}, u32[]{:S(2)}, u32[]{:S(2)}) %collective-permute-start.5) | collective-permute-done | bytes 98336 | tf_op jit(solution)/shard_map/ppermute | solution.py:32
  26.5 0.0 collective-permute-done.3.refs_0_
  26.5 0.0 collective-permute-done.4.refs_1_
  26.5 0.1 shard_map.116
  26.6 0.1 collective-permute-start.6
  26.7 0.0 copy-start.1
  26.7 0.0 copy-start.2
  26.7 1.6 %shard_map.119.refs_9_.refs_14_ = f32[3,320,128]{2,1,0:T(8,128)S(1)} custom-call(s32[1,2048]{1,0:T(1,128)S(1)} %get-tuple-element.71.row_ref, s32[1,2048]{1,0:T(1,128)S(1)} %get-tuple-element.64.col_ref, f32[2,2048]{1,0:T(2,128)S(1)} %get-tuple-element.62.obs_ref), custom_call_target="tpu_custom_call" | custom-call | flops 1174405120 | bytes 32768 | tf_op jit(solution)/shard_map/pallas_call | solution.py:40
  28.3 0.0 collective-permute-done.9.refs_7_
  28.3 0.0 copy-done.1
  28.3 0.0 copy-done.2
  28.3 1.2 %early.1 = (f32[2,4,80,128]{3,2,1,0:T(8,128)S(1)}, f32[2,6,80,128]{3,2,1,0:T(8,128)S(1)}, f32[2,4,80,128]{3,2,1,0:T(8,128)S(1)}, f32[2,2,80,128]{3,2,1,0:T(8,128...) custom-call(f32[7,64,128]{2,1,0:T(8,128)S(1)} %get-tuple-element.32., ...), custom_call_target="tpu_custom_call" | custom-call | tf_op jit(solution)/shard_map/early/pallas_call | solution.py:668
  29.5 0.0 collective-permute-done.6.refs_4_
  29.5 0.2 shard_map.120
  29.6 0.7 %shard_map.121.mine = f32[2,64,128]{2,1,0:T(8,128)S(1)} custom-call(f32[6,80,128]{2,1,0:T(8,128)S(1)} %get-tuple-element.43.refs_0_.stiff, f32[2,4,80,128]{3,2,1,0:T(8,128)S(1)} %get-tuple-element.44.refs_1_, f32[2,2,80,128]{3,2,1,0:T(8,128)S(1)} %get-tuple-element.45.refs_2_, f32[2,6,80,128]{3,2,1,0:T(8,128)S(1)} %get-tuple-element.46.refs_3_, ...), custom_call_target="tpu_custom_call" | custom-call | bytes 4341760 | tf_op jit(solution)/shard_map/pallas_call | solution.py:40
  30.4 1.6 %collective-permute-start.10 = (f32[2,64,128]{2,1,0:T(8,128)S(1)}, f32[2,64,128]{2,1,0:T(8,128)S(1)}, u32[]{:S(2)}, u32[]{:S(2)}) collective-permute-start(f32[2,64,128]{2,1,0:T(8,128)S(1)} %shard_map.121.mine), channel_id=1, source_target_pairs={{0,2},{2,0},{1,3},{3,1},{4,6},{6,4},{5,7},{7,5},{8,10},{10,8},{9,1... | collective-permute-start | bytes 196616 | tf_op jit(solution)/shard_map/ppermute | solution.py:538
  31.9 3.0 %collective-permute-done.10.other = f32[2,64,128]{2,1,0:T(8,128)S(1)} collective-permute-done((f32[2,64,128]{2,1,0:T(8,128)S(1)}, f32[2,64,128]{2,1,0:T(8,128)S(1)}, u32[]{:S(2)}, u32[]{:S(2)}) %collective-permute-start.10) | collective-permute-done | bytes 65568 | tf_op jit(solution)/shard_map/ppermute | solution.py:538
  34.9 0.1 collective-permute-start.11
  35.0 1.2 %collective-permute-done.11.got = f32[24,128]{1,0:T(8,128)S(1)} collective-permute-done((f32[24,128]{1,0:T(8,128)S(1)}, f32[24,128]{1,0:T(8,128)S(1)}, u32[]{:S(2)}, u32[]{:S(2)}) %collective-permute-start.11) | collective-permute-done | bytes 12320 | tf_op jit(solution)/shard_map/ppermute | solution.py:32
  36.2 0.0 copy-start
  36.2 3.1 %collective-permute-start.12 = (f32[168,128]{1,0:T(8,128)S(1)}, f32[168,128]{1,0:T(8,128)S(1)}, u32[]{:S(2)}, u32[]{:S(2)}) collective-permute-start(f32[168,128]{1,0:T(8,128)S(1)} %shard_map.123.mine), channel_id=1, source_target_pairs={{0,4},{4,0},{8,12},{12,8},{1,5},{5,1},{9,13},{13,9},{2,6},{6,2},{1... | collective-permute-start | bytes 258056 | tf_op jit(solution)/shard_map/ppermute | solution.py:32
  39.3 1.2 %collective-permute-start.13 = (f32[168,128]{1,0:T(8,128)S(1)}, f32[168,128]{1,0:T(8,128)S(1)}, u32[]{:S(2)}, u32[]{:S(2)}) collective-permute-start(f32[168,128]{1,0:T(8,128)S(1)} %shard_map.123.mine), channel_id=1, source_target_pairs={{0,12},{4,8},{8,4},{12,0},{1,13},{5,9},{9,5},{13,1},{2,14},{6,10},... | collective-permute-start | bytes 258056 | tf_op jit(solution)/shard_map/ppermute | solution.py:32
  40.5 0.3 collective-permute-start.14
  40.8 4.5 %collective-permute-done.14 = f32[8,128]{1,0:T(8,128)S(1)} collective-permute-done((f32[8,128]{1,0:T(8,128)S(1)}, f32[8,128]{1,0:T(8,128)S(1)}, u32[]{:S(2)}, u32[]{:S(2)}) %collective-permute-start.14) | collective-permute-done | bytes 4128 | tf_op jit(solution)/shard_map/ppermute | solution.py:32
  45.3 0.0 collective-permute-done.12.by_even
  45.3 0.3 collective-permute-done.13.by_odd
  45.6 0.0 copy-done
  45.6 0.2 shard_map.124
  45.8 0.7 %shard_map.125.mine = f32[2,64,128]{2,1,0:T(8,128)S(1)} custom-call(f32[6,80,128]{2,1,0:T(8,128)S(1)} %get-tuple-element.58.refs_0_, f32[2,4,80,128]{3,2,1,0:T(8,128)S(1)} %get-tuple-element.44.refs_1_, f32[2,2,80,128]{3,2,1,0:T(8,128)S(1)} %get-tuple-element.45.refs_2_, f32[2,6,80,128]{3,2,1,0:T(8,128)S(1)} %get-tuple-element.46.refs_3_, ...), custom_call_target="tpu_custom_call" | custom-call | bytes 4341760 | tf_op jit(solution)/shard_map/pallas_call | solution.py:40
  46.6 1.6 %collective-permute-start.15 = (f32[2,64,128]{2,1,0:T(8,128)S(1)}, f32[2,64,128]{2,1,0:T(8,128)S(1)}, u32[]{:S(2)}, u32[]{:S(2)}) collective-permute-start(f32[2,64,128]{2,1,0:T(8,128)S(1)} %shard_map.125.mine), channel_id=1, source_target_pairs={{0,2},{2,0},{1,3},{3,1},{4,6},{6,4},{5,7},{7,5},{8,10},{10,8},{9,1... | collective-permute-start | bytes 196616 | tf_op jit(solution)/shard_map/ppermute | solution.py:538
  48.1 2.8 %collective-permute-done.15.other = f32[2,64,128]{2,1,0:T(8,128)S(1)} collective-permute-done((f32[2,64,128]{2,1,0:T(8,128)S(1)}, f32[2,64,128]{2,1,0:T(8,128)S(1)}, u32[]{:S(2)}, u32[]{:S(2)}) %collective-permute-start.15) | collective-permute-done | bytes 65568 | tf_op jit(solution)/shard_map/ppermute | solution.py:538
  50.9 0.1 collective-permute-start.16
  51.0 1.2 %collective-permute-done.16 = f32[8,128]{1,0:T(8,128)S(1)} collective-permute-done((f32[8,128]{1,0:T(8,128)S(1)}, f32[8,128]{1,0:T(8,128)S(1)}, u32[]{:S(2)}, u32[]{:S(2)}) %collective-permute-start.16) | collective-permute-done | bytes 4128 | tf_op jit(solution)/shard_map/ppermute | solution.py:714
  52.2 0.6 %collective-permute-start.17 = (f32[8,128]{1,0:T(8,128)S(1)}, f32[8,128]{1,0:T(8,128)S(1)}, u32[]{:S(2)}, u32[]{:S(2)}) collective-permute-start(f32[8,128]{1,0:T(8,128)S(1)} %max.24), channel_id=1, source_target_pairs={{0,4},{4,0},{8,12},{12,8},{1,5},{5,1},{9,13},{13,9},{2,6},{6,2},{1... | collective-permute-start | bytes 12296 | tf_op jit(solution)/shard_map/ppermute | solution.py:32
  52.8 2.0 %collective-permute-start.18 = (f32[8,128]{1,0:T(8,128)S(1)}, f32[8,128]{1,0:T(8,128)S(1)}, u32[]{:S(2)}, u32[]{:S(2)}) collective-permute-start(f32[8,128]{1,0:T(8,128)S(1)} %max.24), channel_id=1, source_target_pairs={{0,8},{4,12},{8,0},{12,4},{1,9},{5,13},{9,1},{13,5},{2,10},{6,14},... | collective-permute-start | bytes 12296 | tf_op jit(solution)/shard_map/ppermute | solution.py:32
  54.8 1.8 %collective-permute-start.19 = (f32[8,128]{1,0:T(8,128)S(1)}, f32[8,128]{1,0:T(8,128)S(1)}, u32[]{:S(2)}, u32[]{:S(2)}) collective-permute-start(f32[8,128]{1,0:T(8,128)S(1)} %max.24), channel_id=1, source_target_pairs={{0,12},{4,8},{8,4},{12,0},{1,13},{5,9},{9,5},{13,1},{2,14},{6,10},... | collective-permute-start | bytes 12296 | tf_op jit(solution)/shard_map/ppermute | solution.py:32
  56.5 0.0 collective-permute-done.17
  56.5 0.7 %collective-permute-done.18 = f32[8,128]{1,0:T(8,128)S(1)} collective-permute-done((f32[8,128]{1,0:T(8,128)S(1)}, f32[8,128]{1,0:T(8,128)S(1)}, u32[]{:S(2)}, u32[]{:S(2)}) %collective-permute-start.18) | collective-permute-done | bytes 4128 | tf_op jit(solution)/shard_map/ppermute | solution.py:32
  57.3 2.9 %collective-permute-done.19 = f32[8,128]{1,0:T(8,128)S(1)} collective-permute-done((f32[8,128]{1,0:T(8,128)S(1)}, f32[8,128]{1,0:T(8,128)S(1)}, u32[]{:S(2)}, u32[]{:S(2)}) %collective-permute-start.19) | collective-permute-done | bytes 4128 | tf_op jit(solution)/shard_map/ppermute | solution.py:32
  60.2 0.8 %shard_map.127 = (f32[2,64,64]{2,1,0:T(8,128)}, f32[2,64,64]{2,1,0:T(8,128)}) custom-call(f32[2,64,128]{2,1,0:T(8,128)S(1)} %get-tuple-element.59.total, f32[8,128]{1,0:T(8,128)S(1)} %maximum_maximum_fusion.largest, f32[2,64,64]{2,1,0:T(8,128)S(1)} %get-tuple-element.61.velocity), custom_call_target="tpu_custom_call" | custom-call | bytes 102400 | tf_op jit(solution)/shard_map/pallas_call | solution.py:40
  (10 shorter events, 0.1 us)
Async XLA Ops:
  1.7 21.6 %collective-permute-start.7 = (f32[8,64,128]{2,1,0:T(8,128)S(1)}, f32[8,64,128]{2,1,0:T(8,128)S(1)}, u32[]{:S(2)}, u32[]{:S(2)}) collective-permute-start(f32[8,64,128]{2,1,0:T(8,128)S(1)} %get-tuple-element.38.refs_1_), channel_id=1, source_target_pairs={{0,4},{4,0},{8,12},{12,8},{1,5},{5,1},{9,13},{13,9},{2,6},{6,2},{1... | collective-permute-start | bytes 786440 | tf_op jit(solution)/shard_map/ppermute | solution.py:32
  4.9 18.5 %collective-permute-start.8 = (f32[8,64,128]{2,1,0:T(8,128)S(1)}, f32[8,64,128]{2,1,0:T(8,128)S(1)}, u32[]{:S(2)}, u32[]{:S(2)}) collective-permute-start(f32[8,64,128]{2,1,0:T(8,128)S(1)} %get-tuple-element.38.refs_1_), channel_id=1, source_target_pairs={{4,8},{8,4},{5,9},{9,5},{6,10},{10,6},{7,11},{11,7},{20,24},{24,20... | collective-permute-start | bytes 786440 | tf_op jit(solution)/shard_map/ppermute | solution.py:32
  6.6 9.5 %collective-permute-start = (f32[7,64,128]{2,1,0:T(8,128)S(1)}, f32[7,64,128]{2,1,0:T(8,128)S(1)}, u32[]{:S(2)}, u32[]{:S(2)}) collective-permute-start(f32[7,64,128]{2,1,0:T(8,128)S(1)} %get-tuple-element.32.first.refs_0_), channel_id=1, source_target_pairs={{0,4},{4,0},{8,12},{12,8},{1,5},{5,1},{9,13},{13,9},{2,6},{6,2},{1... | collective-permute-start | bytes 688136 | tf_op jit(solution)/shard_map/ppermute | solution.py:32
  11.0 5.0 %collective-permute-start.1 = (f32[7,64,128]{2,1,0:T(8,128)S(1)}, f32[7,64,128]{2,1,0:T(8,128)S(1)}, u32[]{:S(2)}, u32[]{:S(2)}) collective-permute-start(f32[7,64,128]{2,1,0:T(8,128)S(1)} %get-tuple-element.32.first.refs_0_), channel_id=1, source_target_pairs={{4,8},{8,4},{5,9},{9,5},{6,10},{10,6},{7,11},{11,7},{20,24},{24,20... | collective-permute-start | bytes 688136 | tf_op jit(solution)/shard_map/ppermute | solution.py:32
  11.7 1.3 %collective-permute-start.2 = (f32[48,128]{1,0:T(8,128)S(1)}, f32[48,128]{1,0:T(8,128)S(1)}, u32[]{:S(2)}, u32[]{:S(2)}) collective-permute-start(f32[48,128]{1,0:T(8,128)S(1)} %get-tuple-element.33), channel_id=1, source_target_pairs={{0,1},{1,0},{2,3},{3,2},{4,5},{5,4},{6,7},{7,6},{8,9},{9,8},{10,11... | collective-permute-start | bytes 73736 | tf_op jit(solution)/shard_map/ppermute | solution.py:32
  16.3 10.2 %collective-permute-start.3 = (f32[4,64,128]{2,1,0:T(8,128)S(1)}, f32[4,64,128]{2,1,0:T(8,128)S(1)}, u32[]{:S(2)}, u32[]{:S(2)}) collective-permute-start(f32[4,64,128]{2,1,0:T(8,128)S(1)} %get-tuple-element.35), channel_id=1, source_target_pairs={{0,4},{4,0},{8,12},{12,8},{1,5},{5,1},{9,13},{13,9},{2,6},{6,2},{1... | collective-permute-start | bytes 393224 | tf_op jit(solution)/shard_map/ppermute | solution.py:32
  21.1 5.4 %collective-permute-start.4 = (f32[4,64,128]{2,1,0:T(8,128)S(1)}, f32[4,64,128]{2,1,0:T(8,128)S(1)}, u32[]{:S(2)}, u32[]{:S(2)}) collective-permute-start(f32[4,64,128]{2,1,0:T(8,128)S(1)} %get-tuple-element.36), channel_id=1, source_target_pairs={{4,8},{8,4},{5,9},{9,5},{6,10},{10,6},{7,11},{11,7},{20,24},{24,20... | collective-permute-start | bytes 393224 | tf_op jit(solution)/shard_map/ppermute | solution.py:32
  21.8 4.7 %collective-permute-start.5 = (f32[3,64,128]{2,1,0:T(8,128)S(1)}, f32[3,64,128]{2,1,0:T(8,128)S(1)}, u32[]{:S(2)}, u32[]{:S(2)}) collective-permute-start(f32[3,64,128]{2,1,0:T(8,128)S(1)} %get-tuple-element.37.refs_2_), channel_id=1, source_target_pairs={{0,2},{2,0},{1,3},{3,1},{4,6},{6,4},{5,7},{7,5},{8,10},{10,8},{9,1... | collective-permute-start | bytes 294920 | tf_op jit(solution)/shard_map/ppermute | solution.py:32
  23.4 4.9 %collective-permute-start.9 = (f32[368,128]{1,0:T(8,128)S(1)}, f32[368,128]{1,0:T(8,128)S(1)}, u32[]{:S(2)}, u32[]{:S(2)}) collective-permute-start(f32[368,128]{1,0:T(8,128)S(1)} %shard_map.117), channel_id=1, source_target_pairs={{0,1},{1,0},{2,3},{3,2},{4,5},{5,4},{6,7},{7,6},{8,9},{9,8},{10,11... | collective-permute-start | bytes 565256 | tf_op jit(solution)/shard_map/ppermute | solution.py:32
  26.6 2.9 %collective-permute-start.6 = (f32[112,128]{1,0:T(8,128)S(1)}, f32[112,128]{1,0:T(8,128)S(1)}, u32[]{:S(2)}, u32[]{:S(2)}) collective-permute-start(f32[112,128]{1,0:T(8,128)S(1)} %shard_map.116), channel_id=1, source_target_pairs={{0,1},{1,0},{2,3},{3,2},{4,5},{5,4},{6,7},{7,6},{8,9},{9,8},{10,11... | collective-permute-start | bytes 172040 | tf_op jit(solution)/shard_map/ppermute | solution.py:32
  26.7 1.6 %copy-start.1 = (f32[2,2]{1,0:T(2,128)S(1)}, f32[2,2]{1,0:T(2,128)}, u32[]{:S(2)}) copy-start(f32[2,2]{1,0:T(2,128)} %refs_11_.1) | copy-start | bytes 52
  26.7 1.6 %copy-start.2 = (s32[2]{0:T(128)S(1)}, s32[2]{0:T(128)}, u32[]{:S(2)}) copy-start(s32[2]{0:T(128)} %refs_10_.1) | copy-start | bytes 28
  30.4 4.5 %collective-permute-start.10 = (f32[2,64,128]{2,1,0:T(8,128)S(1)}, f32[2,64,128]{2,1,0:T(8,128)S(1)}, u32[]{:S(2)}, u32[]{:S(2)}) collective-permute-start(f32[2,64,128]{2,1,0:T(8,128)S(1)} %shard_map.121.mine), channel_id=1, source_target_pairs={{0,2},{2,0},{1,3},{3,1},{4,6},{6,4},{5,7},{7,5},{8,10},{10,8},{9,1... | collective-permute-start | bytes 196616 | tf_op jit(solution)/shard_map/ppermute | solution.py:538
  34.9 1.2 %collective-permute-start.11 = (f32[24,128]{1,0:T(8,128)S(1)}, f32[24,128]{1,0:T(8,128)S(1)}, u32[]{:S(2)}, u32[]{:S(2)}) collective-permute-start(f32[24,128]{1,0:T(8,128)S(1)} %get-tuple-element.57.mine), channel_id=1, source_target_pairs={{0,1},{1,0},{2,3},{3,2},{4,5},{5,4},{6,7},{7,6},{8,9},{9,8},{10,11... | collective-permute-start | bytes 36872 | tf_op jit(solution)/shard_map/ppermute | solution.py:32
  36.2 9.4 %copy-start = (f32[2,64,64]{2,1,0:T(8,128)S(1)}, f32[2,64,64]{2,1,0:T(8,128)}, u32[]{:S(2)}) copy-start(f32[2,64,64]{2,1,0:T(8,128)} %velocity.1) | copy-start | bytes 98308
  36.2 9.1 %collective-permute-start.12 = (f32[168,128]{1,0:T(8,128)S(1)}, f32[168,128]{1,0:T(8,128)S(1)}, u32[]{:S(2)}, u32[]{:S(2)}) collective-permute-start(f32[168,128]{1,0:T(8,128)S(1)} %shard_map.123.mine), channel_id=1, source_target_pairs={{0,4},{4,0},{8,12},{12,8},{1,5},{5,1},{9,13},{13,9},{2,6},{6,2},{1... | collective-permute-start | bytes 258056 | tf_op jit(solution)/shard_map/ppermute | solution.py:32
  39.3 6.3 %collective-permute-start.13 = (f32[168,128]{1,0:T(8,128)S(1)}, f32[168,128]{1,0:T(8,128)S(1)}, u32[]{:S(2)}, u32[]{:S(2)}) collective-permute-start(f32[168,128]{1,0:T(8,128)S(1)} %shard_map.123.mine), channel_id=1, source_target_pairs={{0,12},{4,8},{8,4},{12,0},{1,13},{5,9},{9,5},{13,1},{2,14},{6,10},... | collective-permute-start | bytes 258056 | tf_op jit(solution)/shard_map/ppermute | solution.py:32
  40.5 4.8 %collective-permute-start.14 = (f32[8,128]{1,0:T(8,128)S(1)}, f32[8,128]{1,0:T(8,128)S(1)}, u32[]{:S(2)}, u32[]{:S(2)}) collective-permute-start(f32[8,128]{1,0:T(8,128)S(1)} %slice.41), channel_id=1, source_target_pairs={{0,8},{4,12},{8,0},{12,4},{1,9},{5,13},{9,1},{13,5},{2,10},{6,14},... | collective-permute-start | bytes 12296 | tf_op jit(solution)/shard_map/ppermute | solution.py:32
  46.6 4.3 %collective-permute-start.15 = (f32[2,64,128]{2,1,0:T(8,128)S(1)}, f32[2,64,128]{2,1,0:T(8,128)S(1)}, u32[]{:S(2)}, u32[]{:S(2)}) collective-permute-start(f32[2,64,128]{2,1,0:T(8,128)S(1)} %shard_map.125.mine), channel_id=1, source_target_pairs={{0,2},{2,0},{1,3},{3,1},{4,6},{6,4},{5,7},{7,5},{8,10},{10,8},{9,1... | collective-permute-start | bytes 196616 | tf_op jit(solution)/shard_map/ppermute | solution.py:538
  50.9 1.2 %collective-permute-start.16 = (f32[8,128]{1,0:T(8,128)S(1)}, f32[8,128]{1,0:T(8,128)S(1)}, u32[]{:S(2)}, u32[]{:S(2)}) collective-permute-start(f32[8,128]{1,0:T(8,128)S(1)} %get-tuple-element.60), channel_id=1, source_target_pairs={{0,1},{1,0},{2,3},{3,2},{4,5},{5,4},{6,7},{7,6},{8,9},{9,8},{10,11... | collective-permute-start | bytes 12296 | tf_op jit(solution)/shard_map/ppermute | solution.py:714
  52.2 4.4 %collective-permute-start.17 = (f32[8,128]{1,0:T(8,128)S(1)}, f32[8,128]{1,0:T(8,128)S(1)}, u32[]{:S(2)}, u32[]{:S(2)}) collective-permute-start(f32[8,128]{1,0:T(8,128)S(1)} %max.24), channel_id=1, source_target_pairs={{0,4},{4,0},{8,12},{12,8},{1,5},{5,1},{9,13},{13,9},{2,6},{6,2},{1... | collective-permute-start | bytes 12296 | tf_op jit(solution)/shard_map/ppermute | solution.py:32
  52.8 4.5 %collective-permute-start.18 = (f32[8,128]{1,0:T(8,128)S(1)}, f32[8,128]{1,0:T(8,128)S(1)}, u32[]{:S(2)}, u32[]{:S(2)}) collective-permute-start(f32[8,128]{1,0:T(8,128)S(1)} %max.24), channel_id=1, source_target_pairs={{0,8},{4,12},{8,0},{12,4},{1,9},{5,13},{9,1},{13,5},{2,10},{6,14},... | collective-permute-start | bytes 12296 | tf_op jit(solution)/shard_map/ppermute | solution.py:32
  54.8 5.4 %collective-permute-start.19 = (f32[8,128]{1,0:T(8,128)S(1)}, f32[8,128]{1,0:T(8,128)S(1)}, u32[]{:S(2)}, u32[]{:S(2)}) collective-permute-start(f32[8,128]{1,0:T(8,128)S(1)} %max.24), channel_id=1, source_target_pairs={{0,12},{4,8},{8,4},{12,0},{1,13},{5,9},{9,5},{13,1},{2,14},{6,10},... | collective-permute-start | bytes 12296 | tf_op jit(solution)/shard_map/ppermute | solution.py:32

commit v9 on v8

--- a/solution.py
+++ b/solution.py
@@ -144,7 +144,7 @@
         if which == VEL:
             block, lane = (0, 1, 2)[(at + planes) // planes], (at + planes) % planes
             own = self.cols // len(self.vel)
-            column = lax.broadcasted_iota(jnp.int32, (self.rows, self.cols), 1)
+            column = lax.broadcasted_iota(jnp.int32, self.vel[0].shape[1:], 1)
             value = None
             planes_of = [part[block] for part in self.vel]
             if len(planes_of) == 2:
@@ -174,13 +174,6 @@
                     out.append((which, shot, at))
         return out + [(DENS, 0, at) for at in range(-2, planes + 2)]
 
-    def final_list(self):
-        planes = self.planes
-        out = []
-        for shot in range(self.shots):
-            out += [(LATE, shot, -1), (LATE, shot, planes), (LAP, shot, -2), (LAP, shot, planes + 1)]
-        return out + [(VEL, 0, at) for at in range(-2, planes + 2)]
-
 
 def write_edges(halo, items, out):
     first = lax.axis_index("lat") == 0
@@ -215,9 +208,10 @@
     write_edges(halo, halo.early_list(), refs[7])
 
 
-def final_edge_kernel(shape, *refs):
-    halo = final_halo(shape, *refs[:-1])
-    write_edges(halo, halo.final_list(), refs[-1])
+def stretch_kernel(lines, got, out):
+    lat_at = lax.axis_index("lat")
+    for block in range(3):
+        out[block] = with_rows(got[block * PAD : (block + 1) * PAD], lines[block], lat_at)
 
 
 def near_cols(value):
@@ -258,7 +252,9 @@
     cm(at, 0.5 * (plane + below))
 
 
-def third_kernel(first, by_even, by_odd, edges, late, to_even, to_odd, lines, now_buf, buoy_buf, cz, cx, cp, cm):
+def third_kernel(
+    first, by_even, by_odd, edges, late, to_even, to_odd, lines, line_edges, now_buf, buoy_buf, cz, cx, cp, cm
+):
     even = lax.axis_index("depth") % 2 == 0
     lat_at = lax.axis_index("lat")
     shots, planes, rows, cols = late.shape
@@ -266,6 +262,10 @@
     lines[0] = jnp.where(even, by_odd[place], by_even[place])
     lines[1] = first[place]
     lines[2] = jnp.where(even, by_even[place], by_odd[place])
+    for block in range(3):
+        line_edges[block * PAD : (block + 1) * PAD] = jnp.where(
+            lat_at == 0, lines[block, rows - PAD :], lines[block, :PAD]
+        )
 
     def whole(index, at):
         if 0 <= at < planes:
@@ -373,13 +373,16 @@
 
 
 def final_kernel(shape, vels, *refs):
-    te, to = refs[:2]
-    halo = final_halo(shape, te, to, *refs[2 : 2 + vels])
-    edges, dens, ahead, lap_far, late_near, stiff_out = refs[2 + vels :]
-    whole = reader(halo, halo.final_list(), edges)
+    halo = final_halo(shape, *refs[: 2 + vels])
+    dens, ahead, lap_far, late_near, stiff_out = refs[2 + vels :]
     planes = halo.planes
+    empty = jnp.zeros((PAD, halo.cols), jnp.float32)
+
+    def whole(which, shot, at):
+        return jnp.concatenate([empty, halo.plane((which, shot, at)), empty], axis=0)
+
     for at in range(-2, planes + 2):
-        speed = whole(VEL, 0, at) * COURANT
+        speed = halo.plane((VEL, 0, at)) * COURANT
         stiff_out[at + 2] = speed * speed * dens[at + 2]
     for shot in range(halo.shots):
         for side, (near, far) in enumerate(((-1, -2), (planes, planes + 1))):
@@ -462,14 +465,23 @@
     largest[...] = tile_max(value)
 
 
-def widen_kernel(total, mine, got, out):
+def widen_kernel(total, mine, got, out, to_even, to_odd):
     planes, rows, _ = total.shape
     wide = rows + 2 * PAD
     lat_at = lax.axis_index("lat")
+    even = lax.axis_index("depth") % 2 == 0
     for at in range(planes):
         part = got[at * PAD : (at + 1) * PAD]
         out[at * wide : (at + 1) * wide] = with_rows(part, total[at], lat_at)
-    out[planes * wide :] = jnp.maximum(mine[planes * PAD :], got[planes * PAD :])
+    low, top = out[:wide], out[(planes - 1) * wide :]
+    to_even[:wide] = jnp.where(even, top, low)
+    to_odd[:wide] = jnp.where(even, low, top)
+    low, top = total[0], total[planes - 1]
+    to_even[wide : wide + rows] = jnp.where(even, low, top)
+    to_odd[wide : wide + rows] = jnp.where(even, top, low)
+    largest = jnp.maximum(mine[planes * PAD :], got[planes * PAD :])
+    to_even[wide + rows :] = largest
+    to_odd[wide + rows :] = largest
 
 
 def restiff_kernel(stiff, mine, by_even, by_odd, largest, velocity, stiff_out, vel_out):
@@ -483,12 +495,13 @@
         if 0 <= at < planes:
             value = mine[at * wide : (at + 1) * wide]
         else:
-            upper = at >= planes
-            step = at - planes if upper else planes + at
-            a, b = (by_even, by_odd) if upper else (by_odd, by_even)
-            value = jnp.where(
-                even, a[step * wide : (step + 1) * wide], b[step * wide : (step + 1) * wide]
-            )
+            a, b = (by_even, by_odd) if at >= planes else (by_odd, by_even)
+            if at in (-1, planes):
+                value = jnp.where(even, a[:wide], b[:wide])
+            else:
+                value = jnp.where(even, a[wide : wide + rows], b[wide : wide + rows])
+                empty = jnp.zeros((PAD, cols), jnp.float32)
+                value = jnp.concatenate([empty, value, empty], axis=0)
         value = value / scale
         stiff_out[at + 2] = stiff[at + 2] * jnp.exp(-2.0 * STEP_SIZE * value)
         if 0 <= at < planes:
@@ -596,15 +609,17 @@
     second_even = send(second, "depth", evens)
 
     small = (planes + 1, wide, cols)
-    to_even, to_odd, lines = on_chip(
+    to_even, to_odd, lines, line_edges = on_chip(
         third_kernel,
-        [(2 * shots, rows, cols)] * 2 + [(3, rows, cols)],
+        [(2 * shots, rows, cols)] * 2 + [(3, rows, cols), (3 * PAD, cols)],
         (first, first_even, first_odd, first_edges, late),
         scratch=[(shots, planes + 2, wide, cols), (planes + 2, wide, cols)] + [small] * 4,
     )
+    line_edges = send(line_edges, "lat", swap)
     third_odd = send(to_odd, "depth", odds)
     third_even = send(to_even, "depth", evens)
 
+    (lines,) = on_chip(stretch_kernel, [(3, wide, cols)], (lines, line_edges))
     if shot_count == 2:
         parts = (lines, send(lines, "shot", swap))
     else:
@@ -681,13 +696,10 @@
 
     final = (third_even, third_odd) + parts
     shape = adj_late.shape
-    strips = 4 * shots + planes + 4
-    (edges,) = on_chip(functools.partial(final_edge_kernel, shape), [(strips * PAD, cols)], final)
-    edges = send(edges, "lat", swap)
     lap_far, late_near, stiff = on_chip(
         functools.partial(final_kernel, shape, len(parts)),
         [(shots, 2) + model, (shots, 2) + model, (deep,) + model],
-        final + (edges, dens, ahead),
+        final + (dens, ahead),
     )
 
     def gradient_of(stiff):
@@ -724,20 +736,23 @@
         edge_rows = planes * PAD + 8
         summed, tail = on_chip(sum_kernel, [(planes, rows, cols), (edge_rows, cols)], (mine, other))
         got = send(tail, "lat", swap)
-        (widened,) = on_chip(widen_kernel, [(planes * wide + 8, cols)], (summed, tail, got))
-        end = planes * wide
+        widened, to_even, to_odd = on_chip(
+            widen_kernel,
+            [(planes * wide, cols)] + [(wide + rows + 8, cols)] * 2,
+            (summed, tail, got),
+        )
+        end = wide + rows
         if depth_count == 4:
-            by_odd, by_even = [
-                send(widened, "depth", [(i, i ^ k) for i in range(4)]) for k in (3, 1)
-            ]
-            further = send(widened[end:], "depth", [(i, i ^ 2) for i in range(4)])
+            by_odd = send(to_odd, "depth", [(i, i ^ 3) for i in range(4)])
+            by_even = send(to_even, "depth", evens)
+            further = send(to_even[end:], "depth", [(i, i ^ 2) for i in range(4)])
             largest = jnp.maximum(
-                jnp.maximum(widened[end:], further), jnp.maximum(by_odd[end:], by_even[end:])
+                jnp.maximum(to_even[end:], further), jnp.maximum(by_odd[end:], by_even[end:])
             )
         else:
-            by_even = send(widened, "depth", evens)
-            by_odd = send(widened, "depth", odds)
-            largest = depth_max(widened[end:])
+            by_even = send(to_even, "depth", evens)
+            by_odd = send(to_odd, "depth", odds)
+            largest = depth_max(to_even[end:])
         stiff, own_velocity = on_chip(
             restiff_kernel,
             [stiff.shape, velocity.shape],

time: 61.3 us -> 59.8 us (0.976)
  starting transfers between devices: 28.4 us -> 26.8 us
    ppermute x2, waiting for transfers between devices: 5.76 us -> 7.32 us  [shot_terms(): return (block, lax.ppermute(block, 'shot', swap))]
    ppermute x2, starting transfers between devices: 3.11 us -> 1.57 us  [shot_terms(): return (block, lax.ppermute(block, 'shot', swap))]
    ppermute x17, waiting for transfers between devices: 15.1 us -> 13.7 us  [send(): return lax.ppermute(block, axis, pairs)]
  transfers between devices with their start and end apart: 20 -> 20, of which waited for: 11 -> 10; matrix products, arithmetic and copies ran while one was open for 0% -> 0% of each run, Pallas kernels for 9% -> 9%
where the time goes in v9:
time: 59.8 us; the launch traced here: 59.6 us
  starting transfers between devices  26.8 us (45%)
  waiting for transfers between devices  22.1 us (37%)
  Pallas kernels  9.5 us (16%)
  between operations  0.89 us (1%)
    ppermute x17, starting transfers between devices, send(): return lax.ppermute(block, axis, pairs)  25.2 us
    ppermute x17, waiting for transfers between devices, send(): return lax.ppermute(block, axis, pairs)  13.7 us
    ppermute x2, waiting for transfers between devices, shot_terms(): return (block, lax.ppermute(block, 'shot', swap))  7.32 us
    pallas_call x13, Pallas kernels, on_chip(): pl.pallas_call(kernel, out_shape=outs, in_specs=[spec] * len(args), out_s...  6.18 us
    pallas_call x2, Pallas kernels, load(): pl.pallas_call(kernel, out_shape=tuple((pltpu.VMEM(*shape) for shape in s...  2.15 us
    ppermute x2, starting transfers between devices, shot_terms(): return (block, lax.ppermute(block, 'shot', swap))  1.57 us
  transfers between devices with their start and end apart: 20, of which 10 were waited for; matrix products, arithmetic and copies ran while one was open for 0% of the time, Pallas kernels for 9%

profile of v9, /device:TPU:0, one launch (start us, length us, event | category | flops | bytes accessed | tf_op | source)
XLA Modules:
  0.0 59.6 jit_solution(17128443278660628112)
XLA Ops:
  0.6 1.1 %shard_map.114 = (f32[8,64,128]{2,1,0:T(8,128)S(1)}, f32[2,2,64,128]{3,2,1,0:T(8,128)S(1)}, s32[2,2048]{1,0:T(2,128)S(1)}, f32[2,2,2048]{2,1,0:T(2,128)S(1)}) custom-call(f32[2,2,64,128]{3,2,1,0:T(8,128)} %prev.1, f32[2,2,64,128]{3,2,1,0:T(8,128)} %last.1, f32[2,2,64,128]{3,2,1,0:T(8,128)} %late.1, s32[2,2048]{1,0:T(2,128)} %cells.1, f32[2,2,2048]{2,1,0:T(2,128)} %observed.1), custom_call_target="tpu_custom_call" | custom-call | tf_op jit(solution)/shard_map/pallas_call | solution.py:576
  1.7 3.1 %collective-permute-start.7 = (f32[8,64,128]{2,1,0:T(8,128)S(1)}, f32[8,64,128]{2,1,0:T(8,128)S(1)}, u32[]{:S(2)}, u32[]{:S(2)}) collective-permute-start(f32[8,64,128]{2,1,0:T(8,128)S(1)} %get-tuple-element.43.refs_1_), channel_id=1, source_target_pairs={{0,4},{4,0},{8,12},{12,8},{1,5},{5,1},{9,13},{13,9},{2,6},{6,2},{1... | collective-permute-start | bytes 786440 | tf_op jit(solution)/shard_map/ppermute | solution.py:32
  4.9 0.7 %collective-permute-start.8 = (f32[8,64,128]{2,1,0:T(8,128)S(1)}, f32[8,64,128]{2,1,0:T(8,128)S(1)}, u32[]{:S(2)}, u32[]{:S(2)}) collective-permute-start(f32[8,64,128]{2,1,0:T(8,128)S(1)} %get-tuple-element.43.refs_1_), channel_id=1, source_target_pairs={{4,8},{8,4},{5,9},{9,5},{6,10},{10,6},{7,11},{11,7},{20,24},{24,20... | collective-permute-start | bytes 786440 | tf_op jit(solution)/shard_map/ppermute | solution.py:32
  5.5 1.0 %shard_map.113 = (f32[7,64,128]{2,1,0:T(8,128)S(1)}, f32[48,128]{1,0:T(8,128)S(1)}) custom-call(f32[2,2,64,128]{3,2,1,0:T(8,128)} %now.1, f32[2,64,128]{2,1,0:T(8,128)} %dens.1, f32[2,64,64]{2,1,0:T(8,128)} %velocity.1), custom_call_target="tpu_custom_call" | custom-call | tf_op jit(solution)/shard_map/pallas_call | solution.py:576
  6.6 4.4 %collective-permute-start = (f32[7,64,128]{2,1,0:T(8,128)S(1)}, f32[7,64,128]{2,1,0:T(8,128)S(1)}, u32[]{:S(2)}, u32[]{:S(2)}) collective-permute-start(f32[7,64,128]{2,1,0:T(8,128)S(1)} %get-tuple-element.36.first.refs_0_), channel_id=1, source_target_pairs={{0,4},{4,0},{8,12},{12,8},{1,5},{5,1},{9,13},{13,9},{2,6},{6,2},{1... | collective-permute-start | bytes 688136 | tf_op jit(solution)/shard_map/ppermute | solution.py:32
  11.0 0.7 %collective-permute-start.1 = (f32[7,64,128]{2,1,0:T(8,128)S(1)}, f32[7,64,128]{2,1,0:T(8,128)S(1)}, u32[]{:S(2)}, u32[]{:S(2)}) collective-permute-start(f32[7,64,128]{2,1,0:T(8,128)S(1)} %get-tuple-element.36.first.refs_0_), channel_id=1, source_target_pairs={{4,8},{8,4},{5,9},{9,5},{6,10},{10,6},{7,11},{11,7},{20,24},{24,20... | collective-permute-start | bytes 688136 | tf_op jit(solution)/shard_map/ppermute | solution.py:32
  11.7 0.1 collective-permute-start.2
  11.8 0.1 and_select_fusion
  12.0 1.0 %collective-permute-done.2.edges = f32[48,128]{1,0:T(8,128)S(1)} collective-permute-done((f32[48,128]{1,0:T(8,128)S(1)}, f32[48,128]{1,0:T(8,128)S(1)}, u32[]{:S(2)}, u32[]{:S(2)}) %collective-permute-start.2) | collective-permute-done | bytes 24608 | tf_op jit(solution)/shard_map/ppermute | solution.py:32
  13.0 3.1 %collective-permute-done.by_even.refs_3_ = f32[7,64,128]{2,1,0:T(8,128)S(1)} collective-permute-done((f32[7,64,128]{2,1,0:T(8,128)S(1)}, f32[7,64,128]{2,1,0:T(8,128)S(1)}, u32[]{:S(2)}, u32[]{:S(2)}) %collective-permute-start) | collective-permute-done | bytes 229408 | tf_op jit(solution)/shard_map/ppermute | solution.py:32
  16.1 0.0 collective-permute-done.1.by_odd.refs_4_
  16.1 0.2 shard_map.115
  16.3 0.1 collective-permute-start.5
  16.4 4.8 %collective-permute-start.3 = (f32[4,64,128]{2,1,0:T(8,128)S(1)}, f32[4,64,128]{2,1,0:T(8,128)S(1)}, u32[]{:S(2)}, u32[]{:S(2)}) collective-permute-start(f32[4,64,128]{2,1,0:T(8,128)S(1)} %get-tuple-element.39), channel_id=1, source_target_pairs={{0,4},{4,0},{8,12},{12,8},{1,5},{5,1},{9,13},{13,9},{2,6},{6,2},{1... | collective-permute-start | bytes 393224 | tf_op jit(solution)/shard_map/ppermute | solution.py:32
  21.2 0.7 %collective-permute-start.4 = (f32[4,64,128]{2,1,0:T(8,128)S(1)}, f32[4,64,128]{2,1,0:T(8,128)S(1)}, u32[]{:S(2)}, u32[]{:S(2)}) collective-permute-start(f32[4,64,128]{2,1,0:T(8,128)S(1)} %get-tuple-element.40), channel_id=1, source_target_pairs={{4,8},{8,4},{5,9},{9,5},{6,10},{10,6},{7,11},{11,7},{20,24},{24,20... | collective-permute-start | bytes 393224 | tf_op jit(solution)/shard_map/ppermute | solution.py:32
  21.9 0.0 collective-permute-done.5.got
  21.9 1.6 %collective-permute-start.6 = (f32[3,80,128]{2,1,0:T(8,128)S(1)}, f32[3,80,128]{2,1,0:T(8,128)S(1)}, u32[]{:S(2)}, u32[]{:S(2)}) collective-permute-start(f32[3,80,128]{2,1,0:T(8,128)S(1)} %shard_map.116.refs_2_), channel_id=1, source_target_pairs={{0,2},{2,0},{1,3},{3,1},{4,6},{6,4},{5,7},{7,5},{8,10},{10,8},{9,1... | collective-permute-start | bytes 368648 | tf_op jit(solution)/shard_map/ppermute | solution.py:32
  23.5 0.0 collective-permute-done.7.refs_5_
  23.5 0.0 collective-permute-done.8.refs_6_
  23.5 0.1 collective-permute-start.9
  23.6 1.6 %shard_map.118.refs_8_.refs_13_ = f32[3,320,128]{2,1,0:T(8,128)S(1)} custom-call(s32[1,2048]{1,0:T(1,128)S(1)} %get-tuple-element.78.row_ref, s32[1,2048]{1,0:T(1,128)S(1)} %get-tuple-element.73.col_ref, f32[2,2048]{1,0:T(2,128)S(1)} %get-tuple-element.71.obs_ref), custom_call_target="tpu_custom_call" | custom-call | flops 1174405120 | bytes 32768 | tf_op jit(solution)/shard_map/pallas_call | solution.py:40
  25.2 0.0 copy-start.1
  25.2 0.0 copy-start.2
  25.2 1.6 %shard_map.119.refs_9_.refs_14_ = f32[3,320,128]{2,1,0:T(8,128)S(1)} custom-call(s32[1,2048]{1,0:T(1,128)S(1)} %get-tuple-element.79.row_ref, s32[1,2048]{1,0:T(1,128)S(1)} %get-tuple-element.72.col_ref, f32[2,2048]{1,0:T(2,128)S(1)} %get-tuple-element.70.obs_ref), custom_call_target="tpu_custom_call" | custom-call | flops 1174405120 | bytes 32768 | tf_op jit(solution)/shard_map/pallas_call | solution.py:40
  26.8 0.0 collective-permute-done.9.refs_7_
  26.8 0.0 copy-done.1
  26.8 0.0 copy-done.2
  26.8 1.2 %early.1 = (f32[2,4,80,128]{3,2,1,0:T(8,128)S(1)}, f32[2,6,80,128]{3,2,1,0:T(8,128)S(1)}, f32[2,4,80,128]{3,2,1,0:T(8,128)S(1)}, f32[2,2,80,128]{3,2,1,0:T(8,128...) custom-call(f32[7,64,128]{2,1,0:T(8,128)S(1)} %get-tuple-element.36., ...), custom_call_target="tpu_custom_call" | custom-call | tf_op jit(solution)/shard_map/early/pallas_call | solution.py:683
  28.0 0.0 collective-permute-done.3.refs_0_
  28.0 0.0 collective-permute-done.4.refs_1_
  28.0 0.0 collective-permute-done.6.refs_3_
  28.0 0.2 shard_map.120
  28.2 0.7 %shard_map.121.mine = f32[2,64,128]{2,1,0:T(8,128)S(1)} custom-call(f32[6,80,128]{2,1,0:T(8,128)S(1)} %get-tuple-element.48.refs_0_.stiff, f32[2,4,80,128]{3,2,1,0:T(8,128)S(1)} %get-tuple-element.49.refs_1_, f32[2,2,80,128]{3,2,1,0:T(8,128)S(1)} %get-tuple-element.50.refs_2_, f32[2,6,80,128]{3,2,1,0:T(8,128)S(1)} %get-tuple-element.51.refs_3_, ...), custom_call_target="tpu_custom_call" | custom-call | bytes 4341760 | tf_op jit(solution)/shard_map/pallas_call | solution.py:40
  28.9 0.9 %collective-permute-start.10 = (f32[2,64,128]{2,1,0:T(8,128)S(1)}, f32[2,64,128]{2,1,0:T(8,128)S(1)}, u32[]{:S(2)}, u32[]{:S(2)}) collective-permute-start(f32[2,64,128]{2,1,0:T(8,128)S(1)} %shard_map.121.mine), channel_id=1, source_target_pairs={{0,2},{2,0},{1,3},{3,1},{4,6},{6,4},{5,7},{7,5},{8,10},{10,8},{9,1... | collective-permute-start | bytes 196616 | tf_op jit(solution)/shard_map/ppermute | solution.py:551
  29.8 3.6 %collective-permute-done.10.other = f32[2,64,128]{2,1,0:T(8,128)S(1)} collective-permute-done((f32[2,64,128]{2,1,0:T(8,128)S(1)}, f32[2,64,128]{2,1,0:T(8,128)S(1)}, u32[]{:S(2)}, u32[]{:S(2)}) %collective-permute-start.10) | collective-permute-done | bytes 65568 | tf_op jit(solution)/shard_map/ppermute | solution.py:551
  33.5 0.0 copy-start
  33.5 0.1 collective-permute-start.11
  33.6 1.2 %collective-permute-done.11.got = f32[24,128]{1,0:T(8,128)S(1)} collective-permute-done((f32[24,128]{1,0:T(8,128)S(1)}, f32[24,128]{1,0:T(8,128)S(1)}, u32[]{:S(2)}, u32[]{:S(2)}) %collective-permute-start.11) | collective-permute-done | bytes 12320 | tf_op jit(solution)/shard_map/ppermute | solution.py:32
  34.8 3.1 %collective-permute-start.12 = (f32[152,128]{1,0:T(8,128)S(1)}, f32[152,128]{1,0:T(8,128)S(1)}, u32[]{:S(2)}, u32[]{:S(2)}) collective-permute-start(f32[152,128]{1,0:T(8,128)S(1)} %get-tuple-element.64), channel_id=1, source_target_pairs={{0,4},{4,0},{8,12},{12,8},{1,5},{5,1},{9,13},{13,9},{2,6},{6,2},{1... | collective-permute-start | bytes 233480 | tf_op jit(solution)/shard_map/ppermute | solution.py:32
  37.8 1.2 %collective-permute-start.13 = (f32[152,128]{1,0:T(8,128)S(1)}, f32[152,128]{1,0:T(8,128)S(1)}, u32[]{:S(2)}, u32[]{:S(2)}) collective-permute-start(f32[152,128]{1,0:T(8,128)S(1)} %get-tuple-element.65), channel_id=1, source_target_pairs={{0,12},{4,8},{8,4},{12,0},{1,13},{5,9},{9,5},{13,1},{2,14},{6,10},... | collective-permute-start | bytes 233480 | tf_op jit(solution)/shard_map/ppermute | solution.py:32
  39.0 0.3 collective-permute-start.14
  39.4 4.5 %collective-permute-done.14 = f32[8,128]{1,0:T(8,128)S(1)} collective-permute-done((f32[8,128]{1,0:T(8,128)S(1)}, f32[8,128]{1,0:T(8,128)S(1)}, u32[]{:S(2)}, u32[]{:S(2)}) %collective-permute-start.14) | collective-permute-done | bytes 4128 | tf_op jit(solution)/shard_map/ppermute | solution.py:32
  43.9 0.0 collective-permute-done.12.by_even
  43.9 0.2 collective-permute-done.13.by_odd
  44.1 0.0 copy-done
  44.1 0.2 shard_map.124
  44.3 0.8 %shard_map.125.mine = f32[2,64,128]{2,1,0:T(8,128)S(1)} custom-call(f32[6,80,128]{2,1,0:T(8,128)S(1)} %get-tuple-element.66.refs_0_, f32[2,4,80,128]{3,2,1,0:T(8,128)S(1)} %get-tuple-element.49.refs_1_, f32[2,2,80,128]{3,2,1,0:T(8,128)S(1)} %get-tuple-element.50.refs_2_, f32[2,6,80,128]{3,2,1,0:T(8,128)S(1)} %get-tuple-element.51.refs_3_, ...), custom_call_target="tpu_custom_call" | custom-call | bytes 4341760 | tf_op jit(solution)/shard_map/pallas_call | solution.py:40
  45.1 0.7 %collective-permute-start.15 = (f32[2,64,128]{2,1,0:T(8,128)S(1)}, f32[2,64,128]{2,1,0:T(8,128)S(1)}, u32[]{:S(2)}, u32[]{:S(2)}) collective-permute-start(f32[2,64,128]{2,1,0:T(8,128)S(1)} %shard_map.125.mine), channel_id=1, source_target_pairs={{0,2},{2,0},{1,3},{3,1},{4,6},{6,4},{5,7},{7,5},{8,10},{10,8},{9,1... | collective-permute-start | bytes 196616 | tf_op jit(solution)/shard_map/ppermute | solution.py:551
  45.7 3.7 %collective-permute-done.15.other = f32[2,64,128]{2,1,0:T(8,128)S(1)} collective-permute-done((f32[2,64,128]{2,1,0:T(8,128)S(1)}, f32[2,64,128]{2,1,0:T(8,128)S(1)}, u32[]{:S(2)}, u32[]{:S(2)}) %collective-permute-start.15) | collective-permute-done | bytes 65568 | tf_op jit(solution)/shard_map/ppermute | solution.py:551
  49.4 0.1 collective-permute-start.16
  49.5 1.2 %collective-permute-done.16 = f32[8,128]{1,0:T(8,128)S(1)} collective-permute-done((f32[8,128]{1,0:T(8,128)S(1)}, f32[8,128]{1,0:T(8,128)S(1)}, u32[]{:S(2)}, u32[]{:S(2)}) %collective-permute-start.16) | collective-permute-done | bytes 4128 | tf_op jit(solution)/shard_map/ppermute | solution.py:726
  50.7 0.6 %collective-permute-start.17 = (f32[8,128]{1,0:T(8,128)S(1)}, f32[8,128]{1,0:T(8,128)S(1)}, u32[]{:S(2)}, u32[]{:S(2)}) collective-permute-start(f32[8,128]{1,0:T(8,128)S(1)} %max.24), channel_id=1, source_target_pairs={{0,4},{4,0},{8,12},{12,8},{1,5},{5,1},{9,13},{13,9},{2,6},{6,2},{1... | collective-permute-start | bytes 12296 | tf_op jit(solution)/shard_map/ppermute | solution.py:32
  51.3 2.0 %collective-permute-start.18 = (f32[8,128]{1,0:T(8,128)S(1)}, f32[8,128]{1,0:T(8,128)S(1)}, u32[]{:S(2)}, u32[]{:S(2)}) collective-permute-start(f32[8,128]{1,0:T(8,128)S(1)} %max.24), channel_id=1, source_target_pairs={{0,8},{4,12},{8,0},{12,4},{1,9},{5,13},{9,1},{13,5},{2,10},{6,14},... | collective-permute-start | bytes 12296 | tf_op jit(solution)/shard_map/ppermute | solution.py:32
  53.3 1.7 %collective-permute-start.19 = (f32[8,128]{1,0:T(8,128)S(1)}, f32[8,128]{1,0:T(8,128)S(1)}, u32[]{:S(2)}, u32[]{:S(2)}) collective-permute-start(f32[8,128]{1,0:T(8,128)S(1)} %max.24), channel_id=1, source_target_pairs={{0,12},{4,8},{8,4},{12,0},{1,13},{5,9},{9,5},{13,1},{2,14},{6,10},... | collective-permute-start | bytes 12296 | tf_op jit(solution)/shard_map/ppermute | solution.py:32
  55.1 0.0 collective-permute-done.17
  55.1 0.7 %collective-permute-done.18 = f32[8,128]{1,0:T(8,128)S(1)} collective-permute-done((f32[8,128]{1,0:T(8,128)S(1)}, f32[8,128]{1,0:T(8,128)S(1)}, u32[]{:S(2)}, u32[]{:S(2)}) %collective-permute-start.18) | collective-permute-done | bytes 4128 | tf_op jit(solution)/shard_map/ppermute | solution.py:32
  55.8 2.9 %collective-permute-done.19 = f32[8,128]{1,0:T(8,128)S(1)} collective-permute-done((f32[8,128]{1,0:T(8,128)S(1)}, f32[8,128]{1,0:T(8,128)S(1)}, u32[]{:S(2)}, u32[]{:S(2)}) %collective-permute-start.19) | collective-permute-done | bytes 4128 | tf_op jit(solution)/shard_map/ppermute | solution.py:32
  58.8 0.8 %shard_map.127 = (f32[2,64,64]{2,1,0:T(8,128)}, f32[2,64,64]{2,1,0:T(8,128)}) custom-call(f32[2,64,128]{2,1,0:T(8,128)S(1)} %get-tuple-element.67.total, f32[8,128]{1,0:T(8,128)S(1)} %maximum_maximum_fusion.largest, f32[2,64,64]{2,1,0:T(8,128)S(1)} %get-tuple-element.69.velocity), custom_call_target="tpu_custom_call" | custom-call | bytes 102400 | tf_op jit(solution)/shard_map/pallas_call | solution.py:40
  (11 shorter events, 0.1 us)
Async XLA Ops:
  1.7 21.7 %collective-permute-start.7 = (f32[8,64,128]{2,1,0:T(8,128)S(1)}, f32[8,64,128]{2,1,0:T(8,128)S(1)}, u32[]{:S(2)}, u32[]{:S(2)}) collective-permute-start(f32[8,64,128]{2,1,0:T(8,128)S(1)} %get-tuple-element.43.refs_1_), channel_id=1, source_target_pairs={{0,4},{4,0},{8,12},{12,8},{1,5},{5,1},{9,13},{13,9},{2,6},{6,2},{1... | collective-permute-start | bytes 786440 | tf_op jit(solution)/shard_map/ppermute | solution.py:32
  4.9 18.6 %collective-permute-start.8 = (f32[8,64,128]{2,1,0:T(8,128)S(1)}, f32[8,64,128]{2,1,0:T(8,128)S(1)}, u32[]{:S(2)}, u32[]{:S(2)}) collective-permute-start(f32[8,64,128]{2,1,0:T(8,128)S(1)} %get-tuple-element.43.refs_1_), channel_id=1, source_target_pairs={{4,8},{8,4},{5,9},{9,5},{6,10},{10,6},{7,11},{11,7},{20,24},{24,20... | collective-permute-start | bytes 786440 | tf_op jit(solution)/shard_map/ppermute | solution.py:32
  6.6 9.5 %collective-permute-start = (f32[7,64,128]{2,1,0:T(8,128)S(1)}, f32[7,64,128]{2,1,0:T(8,128)S(1)}, u32[]{:S(2)}, u32[]{:S(2)}) collective-permute-start(f32[7,64,128]{2,1,0:T(8,128)S(1)} %get-tuple-element.36.first.refs_0_), channel_id=1, source_target_pairs={{0,4},{4,0},{8,12},{12,8},{1,5},{5,1},{9,13},{13,9},{2,6},{6,2},{1... | collective-permute-start | bytes 688136 | tf_op jit(solution)/shard_map/ppermute | solution.py:32
  11.0 5.0 %collective-permute-start.1 = (f32[7,64,128]{2,1,0:T(8,128)S(1)}, f32[7,64,128]{2,1,0:T(8,128)S(1)}, u32[]{:S(2)}, u32[]{:S(2)}) collective-permute-start(f32[7,64,128]{2,1,0:T(8,128)S(1)} %get-tuple-element.36.first.refs_0_), channel_id=1, source_target_pairs={{4,8},{8,4},{5,9},{9,5},{6,10},{10,6},{7,11},{11,7},{20,24},{24,20... | collective-permute-start | bytes 688136 | tf_op jit(solution)/shard_map/ppermute | solution.py:32
  11.7 1.3 %collective-permute-start.2 = (f32[48,128]{1,0:T(8,128)S(1)}, f32[48,128]{1,0:T(8,128)S(1)}, u32[]{:S(2)}, u32[]{:S(2)}) collective-permute-start(f32[48,128]{1,0:T(8,128)S(1)} %get-tuple-element.37), channel_id=1, source_target_pairs={{0,1},{1,0},{2,3},{3,2},{4,5},{5,4},{6,7},{7,6},{8,9},{9,8},{10,11... | collective-permute-start | bytes 73736 | tf_op jit(solution)/shard_map/ppermute | solution.py:32
  16.3 5.6 %collective-permute-start.5 = (f32[24,128]{1,0:T(8,128)S(1)}, f32[24,128]{1,0:T(8,128)S(1)}, u32[]{:S(2)}, u32[]{:S(2)}) collective-permute-start(f32[24,128]{1,0:T(8,128)S(1)} %get-tuple-element.42), channel_id=1, source_target_pairs={{0,1},{1,0},{2,3},{3,2},{4,5},{5,4},{6,7},{7,6},{8,9},{9,8},{10,11... | collective-permute-start | bytes 36872 | tf_op jit(solution)/shard_map/ppermute | solution.py:32
  16.4 11.6 %collective-permute-start.3 = (f32[4,64,128]{2,1,0:T(8,128)S(1)}, f32[4,64,128]{2,1,0:T(8,128)S(1)}, u32[]{:S(2)}, u32[]{:S(2)}) collective-permute-start(f32[4,64,128]{2,1,0:T(8,128)S(1)} %get-tuple-element.39), channel_id=1, source_target_pairs={{0,4},{4,0},{8,12},{12,8},{1,5},{5,1},{9,13},{13,9},{2,6},{6,2},{1... | collective-permute-start | bytes 393224 | tf_op jit(solution)/shard_map/ppermute | solution.py:32
  21.2 6.8 %collective-permute-start.4 = (f32[4,64,128]{2,1,0:T(8,128)S(1)}, f32[4,64,128]{2,1,0:T(8,128)S(1)}, u32[]{:S(2)}, u32[]{:S(2)}) collective-permute-start(f32[4,64,128]{2,1,0:T(8,128)S(1)} %get-tuple-element.40), channel_id=1, source_target_pairs={{4,8},{8,4},{5,9},{9,5},{6,10},{10,6},{7,11},{11,7},{20,24},{24,20... | collective-permute-start | bytes 393224 | tf_op jit(solution)/shard_map/ppermute | solution.py:32
  21.9 6.1 %collective-permute-start.6 = (f32[3,80,128]{2,1,0:T(8,128)S(1)}, f32[3,80,128]{2,1,0:T(8,128)S(1)}, u32[]{:S(2)}, u32[]{:S(2)}) collective-permute-start(f32[3,80,128]{2,1,0:T(8,128)S(1)} %shard_map.116.refs_2_), channel_id=1, source_target_pairs={{0,2},{2,0},{1,3},{3,1},{4,6},{6,4},{5,7},{7,5},{8,10},{10,8},{9,1... | collective-permute-start | bytes 368648 | tf_op jit(solution)/shard_map/ppermute | solution.py:32
  23.5 3.2 %collective-permute-start.9 = (f32[368,128]{1,0:T(8,128)S(1)}, f32[368,128]{1,0:T(8,128)S(1)}, u32[]{:S(2)}, u32[]{:S(2)}) collective-permute-start(f32[368,128]{1,0:T(8,128)S(1)} %shard_map.117), channel_id=1, source_target_pairs={{0,1},{1,0},{2,3},{3,2},{4,5},{5,4},{6,7},{7,6},{8,9},{9,8},{10,11... | collective-permute-start | bytes 565256 | tf_op jit(solution)/shard_map/ppermute | solution.py:32
  25.2 1.6 %copy-start.1 = (f32[2,2]{1,0:T(2,128)S(1)}, f32[2,2]{1,0:T(2,128)}, u32[]{:S(2)}) copy-start(f32[2,2]{1,0:T(2,128)} %refs_11_.1) | copy-start | bytes 52
  25.2 1.6 %copy-start.2 = (s32[2]{0:T(128)S(1)}, s32[2]{0:T(128)}, u32[]{:S(2)}) copy-start(s32[2]{0:T(128)} %refs_10_.1) | copy-start | bytes 28
  28.9 4.6 %collective-permute-start.10 = (f32[2,64,128]{2,1,0:T(8,128)S(1)}, f32[2,64,128]{2,1,0:T(8,128)S(1)}, u32[]{:S(2)}, u32[]{:S(2)}) collective-permute-start(f32[2,64,128]{2,1,0:T(8,128)S(1)} %shard_map.121.mine), channel_id=1, source_target_pairs={{0,2},{2,0},{1,3},{3,1},{4,6},{6,4},{5,7},{7,5},{8,10},{10,8},{9,1... | collective-permute-start | bytes 196616 | tf_op jit(solution)/shard_map/ppermute | solution.py:551
  33.5 10.6 %copy-start = (f32[2,64,64]{2,1,0:T(8,128)S(1)}, f32[2,64,64]{2,1,0:T(8,128)}, u32[]{:S(2)}) copy-start(f32[2,64,64]{2,1,0:T(8,128)} %velocity.1) | copy-start | bytes 98308
  33.5 1.2 %collective-permute-start.11 = (f32[24,128]{1,0:T(8,128)S(1)}, f32[24,128]{1,0:T(8,128)S(1)}, u32[]{:S(2)}, u32[]{:S(2)}) collective-permute-start(f32[24,128]{1,0:T(8,128)S(1)} %get-tuple-element.62.mine), channel_id=1, source_target_pairs={{0,1},{1,0},{2,3},{3,2},{4,5},{5,4},{6,7},{7,6},{8,9},{9,8},{10,11... | collective-permute-start | bytes 36872 | tf_op jit(solution)/shard_map/ppermute | solution.py:32
  34.8 9.1 %collective-permute-start.12 = (f32[152,128]{1,0:T(8,128)S(1)}, f32[152,128]{1,0:T(8,128)S(1)}, u32[]{:S(2)}, u32[]{:S(2)}) collective-permute-start(f32[152,128]{1,0:T(8,128)S(1)} %get-tuple-element.64), channel_id=1, source_target_pairs={{0,4},{4,0},{8,12},{12,8},{1,5},{5,1},{9,13},{13,9},{2,6},{6,2},{1... | collective-permute-start | bytes 233480 | tf_op jit(solution)/shard_map/ppermute | solution.py:32
  37.8 6.2 %collective-permute-start.13 = (f32[152,128]{1,0:T(8,128)S(1)}, f32[152,128]{1,0:T(8,128)S(1)}, u32[]{:S(2)}, u32[]{:S(2)}) collective-permute-start(f32[152,128]{1,0:T(8,128)S(1)} %get-tuple-element.65), channel_id=1, source_target_pairs={{0,12},{4,8},{8,4},{12,0},{1,13},{5,9},{9,5},{13,1},{2,14},{6,10},... | collective-permute-start | bytes 233480 | tf_op jit(solution)/shard_map/ppermute | solution.py:32
  39.0 4.8 %collective-permute-start.14 = (f32[8,128]{1,0:T(8,128)S(1)}, f32[8,128]{1,0:T(8,128)S(1)}, u32[]{:S(2)}, u32[]{:S(2)}) collective-permute-start(f32[8,128]{1,0:T(8,128)S(1)} %slice.34), channel_id=1, source_target_pairs={{0,8},{4,12},{8,0},{12,4},{1,9},{5,13},{9,1},{13,5},{2,10},{6,14},... | collective-permute-start | bytes 12296 | tf_op jit(solution)/shard_map/ppermute | solution.py:32
  45.1 4.3 %collective-permute-start.15 = (f32[2,64,128]{2,1,0:T(8,128)S(1)}, f32[2,64,128]{2,1,0:T(8,128)S(1)}, u32[]{:S(2)}, u32[]{:S(2)}) collective-permute-start(f32[2,64,128]{2,1,0:T(8,128)S(1)} %shard_map.125.mine), channel_id=1, source_target_pairs={{0,2},{2,0},{1,3},{3,1},{4,6},{6,4},{5,7},{7,5},{8,10},{10,8},{9,1... | collective-permute-start | bytes 196616 | tf_op jit(solution)/shard_map/ppermute | solution.py:551
  49.4 1.2 %collective-permute-start.16 = (f32[8,128]{1,0:T(8,128)S(1)}, f32[8,128]{1,0:T(8,128)S(1)}, u32[]{:S(2)}, u32[]{:S(2)}) collective-permute-start(f32[8,128]{1,0:T(8,128)S(1)} %get-tuple-element.68), channel_id=1, source_target_pairs={{0,1},{1,0},{2,3},{3,2},{4,5},{5,4},{6,7},{7,6},{8,9},{9,8},{10,11... | collective-permute-start | bytes 12296 | tf_op jit(solution)/shard_map/ppermute | solution.py:726
  50.7 4.4 %collective-permute-start.17 = (f32[8,128]{1,0:T(8,128)S(1)}, f32[8,128]{1,0:T(8,128)S(1)}, u32[]{:S(2)}, u32[]{:S(2)}) collective-permute-start(f32[8,128]{1,0:T(8,128)S(1)} %max.24), channel_id=1, source_target_pairs={{0,4},{4,0},{8,12},{12,8},{1,5},{5,1},{9,13},{13,9},{2,6},{6,2},{1... | collective-permute-start | bytes 12296 | tf_op jit(solution)/shard_map/ppermute | solution.py:32
  51.3 4.5 %collective-permute-start.18 = (f32[8,128]{1,0:T(8,128)S(1)}, f32[8,128]{1,0:T(8,128)S(1)}, u32[]{:S(2)}, u32[]{:S(2)}) collective-permute-start(f32[8,128]{1,0:T(8,128)S(1)} %max.24), channel_id=1, source_target_pairs={{0,8},{4,12},{8,0},{12,4},{1,9},{5,13},{9,1},{13,5},{2,10},{6,14},... | collective-permute-start | bytes 12296 | tf_op jit(solution)/shard_map/ppermute | solution.py:32
  53.3 5.4 %collective-permute-start.19 = (f32[8,128]{1,0:T(8,128)S(1)}, f32[8,128]{1,0:T(8,128)S(1)}, u32[]{:S(2)}, u32[]{:S(2)}) collective-permute-start(f32[8,128]{1,0:T(8,128)S(1)} %max.24), channel_id=1, source_target_pairs={{0,12},{4,8},{8,4},{12,0},{1,13},{5,9},{9,5},{13,1},{2,14},{6,10},... | collective-permute-start | bytes 12296 | tf_op jit(solution)/shard_map/ppermute | solution.py:32

commit v10 on v9

--- a/solution.py
+++ b/solution.py
@@ -394,7 +394,7 @@
     stiff, lap_mid, lap_far, base, turn, late_own, late_near, last, low = refs[:9]
     cz_ref, cx_ref, cp_ref, cm_ref = refs[9:13]
     dense = refs[13 : 13 + shots]
-    out, second, scaled, upper, lap_second = refs[13 + shots :]
+    out, second, scaled, upper, lap_second, scaled_near = refs[13 + shots :]
     planes = low.shape[1]
     wide, _ = low.shape[2:]
 
@@ -425,12 +425,17 @@
             third = 2.0 * second[shot, at] + turn[shot, at - 1] + rigid * lap_now
             adj = late(shot, at) + hits * third
             adj = adj + laplace(lambda k: scaled[shot, k], at, cz, cx, cp, cm)
-            upper[shot, at - 1] = adj
+            if 2 <= at < planes + 2:
+                upper[shot, at - 1] = adj
+            else:
+                scaled_near[shot, int(at > 1), PAD : wide - PAD] = (rigid * adj)[PAD : wide - PAD]
             if 2 <= at < planes + 2:
                 lap_second[shot, at - 2] = lap_now
-    for at in range(1, planes + 3):
-        for shot in range(shots):
+    for shot in range(shots):
+        for at in range(2, planes + 2):
             scaled[shot, at] = stiff[at] * upper[shot, at - 1]
+        for side, at in enumerate((1, planes + 2)):
+            scaled[shot, at, PAD : wide - PAD] = scaled_near[shot, side, PAD : wide - PAD]
     for at in range(2, planes + 2):
         total = None
         for shot in range(shots):
@@ -712,6 +717,7 @@
                 (shots, deep) + model,
                 (shots, planes + 2) + model,
                 (shots, planes) + model,
+                (shots, 2) + model,
             ],
         )
         return out

time: 59.8 us -> 59.8 us (level)
  no operation moved by 1% of the time
where the time goes in v10:
time: 59.8 us; the launch traced here: 59.6 us
  starting transfers between devices  26.8 us (45%)
  waiting for transfers between devices  22.1 us (37%)
  Pallas kernels  9.48 us (16%)
  between operations  0.9 us (2%)
    ppermute x17, starting transfers between devices, send(): return lax.ppermute(block, axis, pairs)  25.2 us
    ppermute x17, waiting for transfers between devices, send(): return lax.ppermute(block, axis, pairs)  13.7 us
    ppermute x2, waiting for transfers between devices, shot_terms(): return (block, lax.ppermute(block, 'shot', swap))  7.32 us
    pallas_call x13, Pallas kernels, on_chip(): pl.pallas_call(kernel, out_shape=outs, in_specs=[spec] * len(args), out_s...  6.16 us
    pallas_call x2, Pallas kernels, load(): pl.pallas_call(kernel, out_shape=tuple((pltpu.VMEM(*shape) for shape in s...  2.15 us
    ppermute x2, starting transfers between devices, shot_terms(): return (block, lax.ppermute(block, 'shot', swap))  1.57 us
  transfers between devices with their start and end apart: 20, of which 10 were waited for; matrix products, arithmetic and copies ran while one was open for 0% of the time, Pallas kernels for 9%

profile of v10, /device:TPU:0, one launch (start us, length us, event | category | flops | bytes accessed | tf_op | source)
XLA Modules:
  0.0 59.6 jit_solution(13463679879665075275)
XLA Ops:
  0.6 1.1 %shard_map.114 = (f32[8,64,128]{2,1,0:T(8,128)S(1)}, f32[2,2,64,128]{3,2,1,0:T(8,128)S(1)}, s32[2,2048]{1,0:T(2,128)S(1)}, f32[2,2,2048]{2,1,0:T(2,128)S(1)}) custom-call(f32[2,2,64,128]{3,2,1,0:T(8,128)} %prev.1, f32[2,2,64,128]{3,2,1,0:T(8,128)} %last.1, f32[2,2,64,128]{3,2,1,0:T(8,128)} %late.1, s32[2,2048]{1,0:T(2,128)} %cells.1, f32[2,2,2048]{2,1,0:T(2,128)} %observed.1), custom_call_target="tpu_custom_call" | custom-call | tf_op jit(solution)/shard_map/pallas_call | solution.py:581
  1.7 3.1 %collective-permute-start.7 = (f32[8,64,128]{2,1,0:T(8,128)S(1)}, f32[8,64,128]{2,1,0:T(8,128)S(1)}, u32[]{:S(2)}, u32[]{:S(2)}) collective-permute-start(f32[8,64,128]{2,1,0:T(8,128)S(1)} %get-tuple-element.43.refs_1_), channel_id=1, source_target_pairs={{0,4},{4,0},{8,12},{12,8},{1,5},{5,1},{9,13},{13,9},{2,6},{6,2},{1... | collective-permute-start | bytes 786440 | tf_op jit(solution)/shard_map/ppermute | solution.py:32
  4.9 0.7 %collective-permute-start.8 = (f32[8,64,128]{2,1,0:T(8,128)S(1)}, f32[8,64,128]{2,1,0:T(8,128)S(1)}, u32[]{:S(2)}, u32[]{:S(2)}) collective-permute-start(f32[8,64,128]{2,1,0:T(8,128)S(1)} %get-tuple-element.43.refs_1_), channel_id=1, source_target_pairs={{4,8},{8,4},{5,9},{9,5},{6,10},{10,6},{7,11},{11,7},{20,24},{24,20... | collective-permute-start | bytes 786440 | tf_op jit(solution)/shard_map/ppermute | solution.py:32
  5.5 1.0 %shard_map.113 = (f32[7,64,128]{2,1,0:T(8,128)S(1)}, f32[48,128]{1,0:T(8,128)S(1)}) custom-call(f32[2,2,64,128]{3,2,1,0:T(8,128)} %now.1, f32[2,64,128]{2,1,0:T(8,128)} %dens.1, f32[2,64,64]{2,1,0:T(8,128)} %velocity.1), custom_call_target="tpu_custom_call" | custom-call | tf_op jit(solution)/shard_map/pallas_call | solution.py:581
  6.6 4.4 %collective-permute-start = (f32[7,64,128]{2,1,0:T(8,128)S(1)}, f32[7,64,128]{2,1,0:T(8,128)S(1)}, u32[]{:S(2)}, u32[]{:S(2)}) collective-permute-start(f32[7,64,128]{2,1,0:T(8,128)S(1)} %get-tuple-element.36.first.refs_0_), channel_id=1, source_target_pairs={{0,4},{4,0},{8,12},{12,8},{1,5},{5,1},{9,13},{13,9},{2,6},{6,2},{1... | collective-permute-start | bytes 688136 | tf_op jit(solution)/shard_map/ppermute | solution.py:32
  11.0 0.7 %collective-permute-start.1 = (f32[7,64,128]{2,1,0:T(8,128)S(1)}, f32[7,64,128]{2,1,0:T(8,128)S(1)}, u32[]{:S(2)}, u32[]{:S(2)}) collective-permute-start(f32[7,64,128]{2,1,0:T(8,128)S(1)} %get-tuple-element.36.first.refs_0_), channel_id=1, source_target_pairs={{4,8},{8,4},{5,9},{9,5},{6,10},{10,6},{7,11},{11,7},{20,24},{24,20... | collective-permute-start | bytes 688136 | tf_op jit(solution)/shard_map/ppermute | solution.py:32
  11.7 0.1 collective-permute-start.2
  11.8 0.1 and_select_fusion
  12.0 1.0 %collective-permute-done.2.edges = f32[48,128]{1,0:T(8,128)S(1)} collective-permute-done((f32[48,128]{1,0:T(8,128)S(1)}, f32[48,128]{1,0:T(8,128)S(1)}, u32[]{:S(2)}, u32[]{:S(2)}) %collective-permute-start.2) | collective-permute-done | bytes 24608 | tf_op jit(solution)/shard_map/ppermute | solution.py:32
  13.0 3.1 %collective-permute-done.by_even.refs_3_ = f32[7,64,128]{2,1,0:T(8,128)S(1)} collective-permute-done((f32[7,64,128]{2,1,0:T(8,128)S(1)}, f32[7,64,128]{2,1,0:T(8,128)S(1)}, u32[]{:S(2)}, u32[]{:S(2)}) %collective-permute-start) | collective-permute-done | bytes 229408 | tf_op jit(solution)/shard_map/ppermute | solution.py:32
  16.1 0.0 collective-permute-done.1.by_odd.refs_4_
  16.1 0.2 shard_map.115
  16.3 0.1 collective-permute-start.5
  16.4 4.8 %collective-permute-start.3 = (f32[4,64,128]{2,1,0:T(8,128)S(1)}, f32[4,64,128]{2,1,0:T(8,128)S(1)}, u32[]{:S(2)}, u32[]{:S(2)}) collective-permute-start(f32[4,64,128]{2,1,0:T(8,128)S(1)} %get-tuple-element.39), channel_id=1, source_target_pairs={{0,4},{4,0},{8,12},{12,8},{1,5},{5,1},{9,13},{13,9},{2,6},{6,2},{1... | collective-permute-start | bytes 393224 | tf_op jit(solution)/shard_map/ppermute | solution.py:32
  21.2 0.7 %collective-permute-start.4 = (f32[4,64,128]{2,1,0:T(8,128)S(1)}, f32[4,64,128]{2,1,0:T(8,128)S(1)}, u32[]{:S(2)}, u32[]{:S(2)}) collective-permute-start(f32[4,64,128]{2,1,0:T(8,128)S(1)} %get-tuple-element.40), channel_id=1, source_target_pairs={{4,8},{8,4},{5,9},{9,5},{6,10},{10,6},{7,11},{11,7},{20,24},{24,20... | collective-permute-start | bytes 393224 | tf_op jit(solution)/shard_map/ppermute | solution.py:32
  21.9 0.0 collective-permute-done.5.got
  21.9 1.6 %collective-permute-start.6 = (f32[3,80,128]{2,1,0:T(8,128)S(1)}, f32[3,80,128]{2,1,0:T(8,128)S(1)}, u32[]{:S(2)}, u32[]{:S(2)}) collective-permute-start(f32[3,80,128]{2,1,0:T(8,128)S(1)} %shard_map.116.refs_2_), channel_id=1, source_target_pairs={{0,2},{2,0},{1,3},{3,1},{4,6},{6,4},{5,7},{7,5},{8,10},{10,8},{9,1... | collective-permute-start | bytes 368648 | tf_op jit(solution)/shard_map/ppermute | solution.py:32
  23.5 0.0 collective-permute-done.7.refs_5_
  23.5 0.0 collective-permute-done.8.refs_6_
  23.5 0.1 collective-permute-start.9
  23.6 1.6 %shard_map.118.refs_8_.refs_13_ = f32[3,320,128]{2,1,0:T(8,128)S(1)} custom-call(s32[1,2048]{1,0:T(1,128)S(1)} %get-tuple-element.78.row_ref, s32[1,2048]{1,0:T(1,128)S(1)} %get-tuple-element.73.col_ref, f32[2,2048]{1,0:T(2,128)S(1)} %get-tuple-element.71.obs_ref), custom_call_target="tpu_custom_call" | custom-call | flops 1174405120 | bytes 32768 | tf_op jit(solution)/shard_map/pallas_call | solution.py:40
  25.2 0.0 copy-start.1
  25.2 0.0 copy-start.2
  25.2 1.6 %shard_map.119.refs_9_.refs_14_ = f32[3,320,128]{2,1,0:T(8,128)S(1)} custom-call(s32[1,2048]{1,0:T(1,128)S(1)} %get-tuple-element.79.row_ref, s32[1,2048]{1,0:T(1,128)S(1)} %get-tuple-element.72.col_ref, f32[2,2048]{1,0:T(2,128)S(1)} %get-tuple-element.70.obs_ref), custom_call_target="tpu_custom_call" | custom-call | flops 1174405120 | bytes 32768 | tf_op jit(solution)/shard_map/pallas_call | solution.py:40
  26.8 0.0 collective-permute-done.9.refs_7_
  26.8 0.0 copy-done.1
  26.8 0.0 copy-done.2
  26.8 1.2 %early.1 = (f32[2,4,80,128]{3,2,1,0:T(8,128)S(1)}, f32[2,6,80,128]{3,2,1,0:T(8,128)S(1)}, f32[2,4,80,128]{3,2,1,0:T(8,128)S(1)}, f32[2,2,80,128]{3,2,1,0:T(8,128...) custom-call(f32[7,64,128]{2,1,0:T(8,128)S(1)} %get-tuple-element.36., ...), custom_call_target="tpu_custom_call" | custom-call | tf_op jit(solution)/shard_map/early/pallas_call | solution.py:688
  28.0 0.0 collective-permute-done.3.refs_0_
  28.0 0.0 collective-permute-done.4.refs_1_
  28.0 0.0 collective-permute-done.6.refs_3_
  28.0 0.2 shard_map.120
  28.2 0.7 %shard_map.121.mine = f32[2,64,128]{2,1,0:T(8,128)S(1)} custom-call(f32[6,80,128]{2,1,0:T(8,128)S(1)} %get-tuple-element.48.refs_0_.stiff, f32[2,4,80,128]{3,2,1,0:T(8,128)S(1)} %get-tuple-element.49.refs_1_, f32[2,2,80,128]{3,2,1,0:T(8,128)S(1)} %get-tuple-element.50.refs_2_, f32[2,6,80,128]{3,2,1,0:T(8,128)S(1)} %get-tuple-element.51.refs_3_, ...), custom_call_target="tpu_custom_call" | custom-call | bytes 4341760 | tf_op jit(solution)/shard_map/pallas_call | solution.py:40
  28.9 0.9 %collective-permute-start.10 = (f32[2,64,128]{2,1,0:T(8,128)S(1)}, f32[2,64,128]{2,1,0:T(8,128)S(1)}, u32[]{:S(2)}, u32[]{:S(2)}) collective-permute-start(f32[2,64,128]{2,1,0:T(8,128)S(1)} %shard_map.121.mine), channel_id=1, source_target_pairs={{0,2},{2,0},{1,3},{3,1},{4,6},{6,4},{5,7},{7,5},{8,10},{10,8},{9,1... | collective-permute-start | bytes 196616 | tf_op jit(solution)/shard_map/ppermute | solution.py:556
  29.8 3.6 %collective-permute-done.10.other = f32[2,64,128]{2,1,0:T(8,128)S(1)} collective-permute-done((f32[2,64,128]{2,1,0:T(8,128)S(1)}, f32[2,64,128]{2,1,0:T(8,128)S(1)}, u32[]{:S(2)}, u32[]{:S(2)}) %collective-permute-start.10) | collective-permute-done | bytes 65568 | tf_op jit(solution)/shard_map/ppermute | solution.py:556
  33.5 0.0 copy-start
  33.5 0.1 collective-permute-start.11
  33.6 1.2 %collective-permute-done.11.got = f32[24,128]{1,0:T(8,128)S(1)} collective-permute-done((f32[24,128]{1,0:T(8,128)S(1)}, f32[24,128]{1,0:T(8,128)S(1)}, u32[]{:S(2)}, u32[]{:S(2)}) %collective-permute-start.11) | collective-permute-done | bytes 12320 | tf_op jit(solution)/shard_map/ppermute | solution.py:32
  34.8 3.1 %collective-permute-start.12 = (f32[152,128]{1,0:T(8,128)S(1)}, f32[152,128]{1,0:T(8,128)S(1)}, u32[]{:S(2)}, u32[]{:S(2)}) collective-permute-start(f32[152,128]{1,0:T(8,128)S(1)} %get-tuple-element.64), channel_id=1, source_target_pairs={{0,4},{4,0},{8,12},{12,8},{1,5},{5,1},{9,13},{13,9},{2,6},{6,2},{1... | collective-permute-start | bytes 233480 | tf_op jit(solution)/shard_map/ppermute | solution.py:32
  37.8 1.2 %collective-permute-start.13 = (f32[152,128]{1,0:T(8,128)S(1)}, f32[152,128]{1,0:T(8,128)S(1)}, u32[]{:S(2)}, u32[]{:S(2)}) collective-permute-start(f32[152,128]{1,0:T(8,128)S(1)} %get-tuple-element.65), channel_id=1, source_target_pairs={{0,12},{4,8},{8,4},{12,0},{1,13},{5,9},{9,5},{13,1},{2,14},{6,10},... | collective-permute-start | bytes 233480 | tf_op jit(solution)/shard_map/ppermute | solution.py:32
  39.0 0.3 collective-permute-start.14
  39.4 4.5 %collective-permute-done.14 = f32[8,128]{1,0:T(8,128)S(1)} collective-permute-done((f32[8,128]{1,0:T(8,128)S(1)}, f32[8,128]{1,0:T(8,128)S(1)}, u32[]{:S(2)}, u32[]{:S(2)}) %collective-permute-start.14) | collective-permute-done | bytes 4128 | tf_op jit(solution)/shard_map/ppermute | solution.py:32
  43.9 0.0 collective-permute-done.12.by_even
  43.9 0.2 collective-permute-done.13.by_odd
  44.1 0.0 copy-done
  44.1 0.2 shard_map.124
  44.3 0.8 %shard_map.125.mine = f32[2,64,128]{2,1,0:T(8,128)S(1)} custom-call(f32[6,80,128]{2,1,0:T(8,128)S(1)} %get-tuple-element.66.refs_0_, f32[2,4,80,128]{3,2,1,0:T(8,128)S(1)} %get-tuple-element.49.refs_1_, f32[2,2,80,128]{3,2,1,0:T(8,128)S(1)} %get-tuple-element.50.refs_2_, f32[2,6,80,128]{3,2,1,0:T(8,128)S(1)} %get-tuple-element.51.refs_3_, ...), custom_call_target="tpu_custom_call" | custom-call | bytes 4341760 | tf_op jit(solution)/shard_map/pallas_call | solution.py:40
  45.1 0.7 %collective-permute-start.15 = (f32[2,64,128]{2,1,0:T(8,128)S(1)}, f32[2,64,128]{2,1,0:T(8,128)S(1)}, u32[]{:S(2)}, u32[]{:S(2)}) collective-permute-start(f32[2,64,128]{2,1,0:T(8,128)S(1)} %shard_map.125.mine), channel_id=1, source_target_pairs={{0,2},{2,0},{1,3},{3,1},{4,6},{6,4},{5,7},{7,5},{8,10},{10,8},{9,1... | collective-permute-start | bytes 196616 | tf_op jit(solution)/shard_map/ppermute | solution.py:556
  45.7 3.7 %collective-permute-done.15.other = f32[2,64,128]{2,1,0:T(8,128)S(1)} collective-permute-done((f32[2,64,128]{2,1,0:T(8,128)S(1)}, f32[2,64,128]{2,1,0:T(8,128)S(1)}, u32[]{:S(2)}, u32[]{:S(2)}) %collective-permute-start.15) | collective-permute-done | bytes 65568 | tf_op jit(solution)/shard_map/ppermute | solution.py:556
  49.4 0.1 collective-permute-start.16
  49.5 1.2 %collective-permute-done.16 = f32[8,128]{1,0:T(8,128)S(1)} collective-permute-done((f32[8,128]{1,0:T(8,128)S(1)}, f32[8,128]{1,0:T(8,128)S(1)}, u32[]{:S(2)}, u32[]{:S(2)}) %collective-permute-start.16) | collective-permute-done | bytes 4128 | tf_op jit(solution)/shard_map/ppermute | solution.py:732
  50.7 0.6 %collective-permute-start.17 = (f32[8,128]{1,0:T(8,128)S(1)}, f32[8,128]{1,0:T(8,128)S(1)}, u32[]{:S(2)}, u32[]{:S(2)}) collective-permute-start(f32[8,128]{1,0:T(8,128)S(1)} %max.24), channel_id=1, source_target_pairs={{0,4},{4,0},{8,12},{12,8},{1,5},{5,1},{9,13},{13,9},{2,6},{6,2},{1... | collective-permute-start | bytes 12296 | tf_op jit(solution)/shard_map/ppermute | solution.py:32
  51.3 2.0 %collective-permute-start.18 = (f32[8,128]{1,0:T(8,128)S(1)}, f32[8,128]{1,0:T(8,128)S(1)}, u32[]{:S(2)}, u32[]{:S(2)}) collective-permute-start(f32[8,128]{1,0:T(8,128)S(1)} %max.24), channel_id=1, source_target_pairs={{0,8},{4,12},{8,0},{12,4},{1,9},{5,13},{9,1},{13,5},{2,10},{6,14},... | collective-permute-start | bytes 12296 | tf_op jit(solution)/shard_map/ppermute | solution.py:32
  53.3 1.7 %collective-permute-start.19 = (f32[8,128]{1,0:T(8,128)S(1)}, f32[8,128]{1,0:T(8,128)S(1)}, u32[]{:S(2)}, u32[]{:S(2)}) collective-permute-start(f32[8,128]{1,0:T(8,128)S(1)} %max.24), channel_id=1, source_target_pairs={{0,12},{4,8},{8,4},{12,0},{1,13},{5,9},{9,5},{13,1},{2,14},{6,10},... | collective-permute-start | bytes 12296 | tf_op jit(solution)/shard_map/ppermute | solution.py:32
  55.0 0.0 collective-permute-done.17
  55.1 0.7 %collective-permute-done.18 = f32[8,128]{1,0:T(8,128)S(1)} collective-permute-done((f32[8,128]{1,0:T(8,128)S(1)}, f32[8,128]{1,0:T(8,128)S(1)}, u32[]{:S(2)}, u32[]{:S(2)}) %collective-permute-start.18) | collective-permute-done | bytes 4128 | tf_op jit(solution)/shard_map/ppermute | solution.py:32
  55.8 2.9 %collective-permute-done.19 = f32[8,128]{1,0:T(8,128)S(1)} collective-permute-done((f32[8,128]{1,0:T(8,128)S(1)}, f32[8,128]{1,0:T(8,128)S(1)}, u32[]{:S(2)}, u32[]{:S(2)}) %collective-permute-start.19) | collective-permute-done | bytes 4128 | tf_op jit(solution)/shard_map/ppermute | solution.py:32
  58.7 0.8 %shard_map.127 = (f32[2,64,64]{2,1,0:T(8,128)}, f32[2,64,64]{2,1,0:T(8,128)}) custom-call(f32[2,64,128]{2,1,0:T(8,128)S(1)} %get-tuple-element.67.total, f32[8,128]{1,0:T(8,128)S(1)} %maximum_maximum_fusion.largest, f32[2,64,64]{2,1,0:T(8,128)S(1)} %get-tuple-element.69.velocity), custom_call_target="tpu_custom_call" | custom-call | bytes 102400 | tf_op jit(solution)/shard_map/pallas_call | solution.py:40
  (11 shorter events, 0.1 us)
Async XLA Ops:
  1.7 21.7 %collective-permute-start.7 = (f32[8,64,128]{2,1,0:T(8,128)S(1)}, f32[8,64,128]{2,1,0:T(8,128)S(1)}, u32[]{:S(2)}, u32[]{:S(2)}) collective-permute-start(f32[8,64,128]{2,1,0:T(8,128)S(1)} %get-tuple-element.43.refs_1_), channel_id=1, source_target_pairs={{0,4},{4,0},{8,12},{12,8},{1,5},{5,1},{9,13},{13,9},{2,6},{6,2},{1... | collective-permute-start | bytes 786440 | tf_op jit(solution)/shard_map/ppermute | solution.py:32
  4.9 18.6 %collective-permute-start.8 = (f32[8,64,128]{2,1,0:T(8,128)S(1)}, f32[8,64,128]{2,1,0:T(8,128)S(1)}, u32[]{:S(2)}, u32[]{:S(2)}) collective-permute-start(f32[8,64,128]{2,1,0:T(8,128)S(1)} %get-tuple-element.43.refs_1_), channel_id=1, source_target_pairs={{4,8},{8,4},{5,9},{9,5},{6,10},{10,6},{7,11},{11,7},{20,24},{24,20... | collective-permute-start | bytes 786440 | tf_op jit(solution)/shard_map/ppermute | solution.py:32
  6.6 9.5 %collective-permute-start = (f32[7,64,128]{2,1,0:T(8,128)S(1)}, f32[7,64,128]{2,1,0:T(8,128)S(1)}, u32[]{:S(2)}, u32[]{:S(2)}) collective-permute-start(f32[7,64,128]{2,1,0:T(8,128)S(1)} %get-tuple-element.36.first.refs_0_), channel_id=1, source_target_pairs={{0,4},{4,0},{8,12},{12,8},{1,5},{5,1},{9,13},{13,9},{2,6},{6,2},{1... | collective-permute-start | bytes 688136 | tf_op jit(solution)/shard_map/ppermute | solution.py:32
  11.0 5.0 %collective-permute-start.1 = (f32[7,64,128]{2,1,0:T(8,128)S(1)}, f32[7,64,128]{2,1,0:T(8,128)S(1)}, u32[]{:S(2)}, u32[]{:S(2)}) collective-permute-start(f32[7,64,128]{2,1,0:T(8,128)S(1)} %get-tuple-element.36.first.refs_0_), channel_id=1, source_target_pairs={{4,8},{8,4},{5,9},{9,5},{6,10},{10,6},{7,11},{11,7},{20,24},{24,20... | collective-permute-start | bytes 688136 | tf_op jit(solution)/shard_map/ppermute | solution.py:32
  11.7 1.3 %collective-permute-start.2 = (f32[48,128]{1,0:T(8,128)S(1)}, f32[48,128]{1,0:T(8,128)S(1)}, u32[]{:S(2)}, u32[]{:S(2)}) collective-permute-start(f32[48,128]{1,0:T(8,128)S(1)} %get-tuple-element.37), channel_id=1, source_target_pairs={{0,1},{1,0},{2,3},{3,2},{4,5},{5,4},{6,7},{7,6},{8,9},{9,8},{10,11... | collective-permute-start | bytes 73736 | tf_op jit(solution)/shard_map/ppermute | solution.py:32
  16.3 5.6 %collective-permute-start.5 = (f32[24,128]{1,0:T(8,128)S(1)}, f32[24,128]{1,0:T(8,128)S(1)}, u32[]{:S(2)}, u32[]{:S(2)}) collective-permute-start(f32[24,128]{1,0:T(8,128)S(1)} %get-tuple-element.42), channel_id=1, source_target_pairs={{0,1},{1,0},{2,3},{3,2},{4,5},{5,4},{6,7},{7,6},{8,9},{9,8},{10,11... | collective-permute-start | bytes 36872 | tf_op jit(solution)/shard_map/ppermute | solution.py:32
  16.4 11.6 %collective-permute-start.3 = (f32[4,64,128]{2,1,0:T(8,128)S(1)}, f32[4,64,128]{2,1,0:T(8,128)S(1)}, u32[]{:S(2)}, u32[]{:S(2)}) collective-permute-start(f32[4,64,128]{2,1,0:T(8,128)S(1)} %get-tuple-element.39), channel_id=1, source_target_pairs={{0,4},{4,0},{8,12},{12,8},{1,5},{5,1},{9,13},{13,9},{2,6},{6,2},{1... | collective-permute-start | bytes 393224 | tf_op jit(solution)/shard_map/ppermute | solution.py:32
  21.2 6.8 %collective-permute-start.4 = (f32[4,64,128]{2,1,0:T(8,128)S(1)}, f32[4,64,128]{2,1,0:T(8,128)S(1)}, u32[]{:S(2)}, u32[]{:S(2)}) collective-permute-start(f32[4,64,128]{2,1,0:T(8,128)S(1)} %get-tuple-element.40), channel_id=1, source_target_pairs={{4,8},{8,4},{5,9},{9,5},{6,10},{10,6},{7,11},{11,7},{20,24},{24,20... | collective-permute-start | bytes 393224 | tf_op jit(solution)/shard_map/ppermute | solution.py:32
  21.9 6.1 %collective-permute-start.6 = (f32[3,80,128]{2,1,0:T(8,128)S(1)}, f32[3,80,128]{2,1,0:T(8,128)S(1)}, u32[]{:S(2)}, u32[]{:S(2)}) collective-permute-start(f32[3,80,128]{2,1,0:T(8,128)S(1)} %shard_map.116.refs_2_), channel_id=1, source_target_pairs={{0,2},{2,0},{1,3},{3,1},{4,6},{6,4},{5,7},{7,5},{8,10},{10,8},{9,1... | collective-permute-start | bytes 368648 | tf_op jit(solution)/shard_map/ppermute | solution.py:32
  23.5 3.2 %collective-permute-start.9 = (f32[368,128]{1,0:T(8,128)S(1)}, f32[368,128]{1,0:T(8,128)S(1)}, u32[]{:S(2)}, u32[]{:S(2)}) collective-permute-start(f32[368,128]{1,0:T(8,128)S(1)} %shard_map.117), channel_id=1, source_target_pairs={{0,1},{1,0},{2,3},{3,2},{4,5},{5,4},{6,7},{7,6},{8,9},{9,8},{10,11... | collective-permute-start | bytes 565256 | tf_op jit(solution)/shard_map/ppermute | solution.py:32
  25.2 1.6 %copy-start.1 = (f32[2,2]{1,0:T(2,128)S(1)}, f32[2,2]{1,0:T(2,128)}, u32[]{:S(2)}) copy-start(f32[2,2]{1,0:T(2,128)} %refs_11_.1) | copy-start | bytes 52
  25.2 1.6 %copy-start.2 = (s32[2]{0:T(128)S(1)}, s32[2]{0:T(128)}, u32[]{:S(2)}) copy-start(s32[2]{0:T(128)} %refs_10_.1) | copy-start | bytes 28
  28.9 4.6 %collective-permute-start.10 = (f32[2,64,128]{2,1,0:T(8,128)S(1)}, f32[2,64,128]{2,1,0:T(8,128)S(1)}, u32[]{:S(2)}, u32[]{:S(2)}) collective-permute-start(f32[2,64,128]{2,1,0:T(8,128)S(1)} %shard_map.121.mine), channel_id=1, source_target_pairs={{0,2},{2,0},{1,3},{3,1},{4,6},{6,4},{5,7},{7,5},{8,10},{10,8},{9,1... | collective-permute-start | bytes 196616 | tf_op jit(solution)/shard_map/ppermute | solution.py:556
  33.5 10.6 %copy-start = (f32[2,64,64]{2,1,0:T(8,128)S(1)}, f32[2,64,64]{2,1,0:T(8,128)}, u32[]{:S(2)}) copy-start(f32[2,64,64]{2,1,0:T(8,128)} %velocity.1) | copy-start | bytes 98308
  33.5 1.2 %collective-permute-start.11 = (f32[24,128]{1,0:T(8,128)S(1)}, f32[24,128]{1,0:T(8,128)S(1)}, u32[]{:S(2)}, u32[]{:S(2)}) collective-permute-start(f32[24,128]{1,0:T(8,128)S(1)} %get-tuple-element.62.mine), channel_id=1, source_target_pairs={{0,1},{1,0},{2,3},{3,2},{4,5},{5,4},{6,7},{7,6},{8,9},{9,8},{10,11... | collective-permute-start | bytes 36872 | tf_op jit(solution)/shard_map/ppermute | solution.py:32
  34.8 9.1 %collective-permute-start.12 = (f32[152,128]{1,0:T(8,128)S(1)}, f32[152,128]{1,0:T(8,128)S(1)}, u32[]{:S(2)}, u32[]{:S(2)}) collective-permute-start(f32[152,128]{1,0:T(8,128)S(1)} %get-tuple-element.64), channel_id=1, source_target_pairs={{0,4},{4,0},{8,12},{12,8},{1,5},{5,1},{9,13},{13,9},{2,6},{6,2},{1... | collective-permute-start | bytes 233480 | tf_op jit(solution)/shard_map/ppermute | solution.py:32
  37.8 6.2 %collective-permute-start.13 = (f32[152,128]{1,0:T(8,128)S(1)}, f32[152,128]{1,0:T(8,128)S(1)}, u32[]{:S(2)}, u32[]{:S(2)}) collective-permute-start(f32[152,128]{1,0:T(8,128)S(1)} %get-tuple-element.65), channel_id=1, source_target_pairs={{0,12},{4,8},{8,4},{12,0},{1,13},{5,9},{9,5},{13,1},{2,14},{6,10},... | collective-permute-start | bytes 233480 | tf_op jit(solution)/shard_map/ppermute | solution.py:32
  39.0 4.8 %collective-permute-start.14 = (f32[8,128]{1,0:T(8,128)S(1)}, f32[8,128]{1,0:T(8,128)S(1)}, u32[]{:S(2)}, u32[]{:S(2)}) collective-permute-start(f32[8,128]{1,0:T(8,128)S(1)} %slice.34), channel_id=1, source_target_pairs={{0,8},{4,12},{8,0},{12,4},{1,9},{5,13},{9,1},{13,5},{2,10},{6,14},... | collective-permute-start | bytes 12296 | tf_op jit(solution)/shard_map/ppermute | solution.py:32
  45.1 4.3 %collective-permute-start.15 = (f32[2,64,128]{2,1,0:T(8,128)S(1)}, f32[2,64,128]{2,1,0:T(8,128)S(1)}, u32[]{:S(2)}, u32[]{:S(2)}) collective-permute-start(f32[2,64,128]{2,1,0:T(8,128)S(1)} %shard_map.125.mine), channel_id=1, source_target_pairs={{0,2},{2,0},{1,3},{3,1},{4,6},{6,4},{5,7},{7,5},{8,10},{10,8},{9,1... | collective-permute-start | bytes 196616 | tf_op jit(solution)/shard_map/ppermute | solution.py:556
  49.4 1.2 %collective-permute-start.16 = (f32[8,128]{1,0:T(8,128)S(1)}, f32[8,128]{1,0:T(8,128)S(1)}, u32[]{:S(2)}, u32[]{:S(2)}) collective-permute-start(f32[8,128]{1,0:T(8,128)S(1)} %get-tuple-element.68), channel_id=1, source_target_pairs={{0,1},{1,0},{2,3},{3,2},{4,5},{5,4},{6,7},{7,6},{8,9},{9,8},{10,11... | collective-permute-start | bytes 12296 | tf_op jit(solution)/shard_map/ppermute | solution.py:732
  50.7 4.4 %collective-permute-start.17 = (f32[8,128]{1,0:T(8,128)S(1)}, f32[8,128]{1,0:T(8,128)S(1)}, u32[]{:S(2)}, u32[]{:S(2)}) collective-permute-start(f32[8,128]{1,0:T(8,128)S(1)} %max.24), channel_id=1, source_target_pairs={{0,4},{4,0},{8,12},{12,8},{1,5},{5,1},{9,13},{13,9},{2,6},{6,2},{1... | collective-permute-start | bytes 12296 | tf_op jit(solution)/shard_map/ppermute | solution.py:32
  51.3 4.5 %collective-permute-start.18 = (f32[8,128]{1,0:T(8,128)S(1)}, f32[8,128]{1,0:T(8,128)S(1)}, u32[]{:S(2)}, u32[]{:S(2)}) collective-permute-start(f32[8,128]{1,0:T(8,128)S(1)} %max.24), channel_id=1, source_target_pairs={{0,8},{4,12},{8,0},{12,4},{1,9},{5,13},{9,1},{13,5},{2,10},{6,14},... | collective-permute-start | bytes 12296 | tf_op jit(solution)/shard_map/ppermute | solution.py:32
  53.3 5.4 %collective-permute-start.19 = (f32[8,128]{1,0:T(8,128)S(1)}, f32[8,128]{1,0:T(8,128)S(1)}, u32[]{:S(2)}, u32[]{:S(2)}) collective-permute-start(f32[8,128]{1,0:T(8,128)S(1)} %max.24), channel_id=1, source_target_pairs={{0,12},{4,8},{8,4},{12,0},{1,13},{5,9},{9,5},{13,1},{2,14},{6,10},... | collective-permute-start | bytes 12296 | tf_op jit(solution)/shard_map/ppermute | solution.py:32

commit v11 on v10

--- a/solution.py
+++ b/solution.py
@@ -514,16 +514,22 @@
             vel_out[at] = velocity[at] * jnp.exp(-STEP_SIZE * shifted[:, :own])
 
 
-def finish_kernel(total, largest, velocity, vel_out, dir_out):
+def finish_kernel(total, largest, velocity, vel_out, dir_out, vel_buf, dir_buf, sems):
     planes, _, own = velocity.shape
     shot_at = lax.axis_index("shot")
     cols = total.shape[2]
     scale = jnp.max(jnp.max(largest[...], axis=1, keepdims=True), axis=0, keepdims=True) + EPSILON
     for at in range(planes):
         value = total[at] / scale
-        shifted = pltpu.roll(value, (cols - shot_at * own) % cols, 1)[:, :own]
-        dir_out[at] = shifted
-        vel_out[at] = velocity[at] * jnp.exp(-STEP_SIZE * shifted)
+        dir_buf[at] = pltpu.roll(value, (cols - shot_at * own) % cols, 1)[:, :own]
+    to_dir = pltpu.make_async_copy(dir_buf, dir_out, sems.at[0])
+    to_dir.start()
+    for at in range(planes):
+        vel_buf[at] = velocity[at] * jnp.exp(-STEP_SIZE * dir_buf[at])
+    to_vel = pltpu.make_async_copy(vel_buf, vel_out, sems.at[1])
+    to_vel.start()
+    to_dir.wait()
+    to_vel.wait()
 
 
 def shards(
@@ -731,13 +737,24 @@
             )
             largest = jnp.maximum(largest, lax.ppermute(largest, "lat", swap))
             largest = depth_max(largest)
-            return tuple(
-                on_chip(
-                    finish_kernel,
-                    [velocity.shape, velocity.shape],
-                    (summed, largest, own_velocity),
-                    keep=False,
-                )
+            shape = velocity.shape
+            return pl.pallas_call(
+                finish_kernel,
+                out_shape=(jax.ShapeDtypeStruct(shape, jnp.float32),) * 2,
+                in_specs=[spec] * 3,
+                out_specs=(pl.BlockSpec(memory_space=pltpu.HBM),) * 2,
+                scratch_shapes=[
+                    pltpu.VMEM(shape, jnp.float32),
+                    pltpu.VMEM(shape, jnp.float32),
+                    pltpu.SemaphoreType.DMA((2,)),
+                ],
+                compiler_params=pltpu.CompilerParams(vmem_limit_bytes=8 << 20),
+                name="finish",
+            )(
+                *[
+                    pltpu.with_memory_space_constraint(a, pltpu.VMEM)
+                    for a in (summed, largest, own_velocity)
+                ]
             )
         edge_rows = planes * PAD + 8
         summed, tail = on_chip(sum_kernel, [(planes, rows, cols), (edge_rows, cols)], (mine, other))

time: 59.8 us -> 59.8 us (level)
    pallas_call x0 -> x1, Pallas kernels: none -> 0.86 us  [shards(): pl.pallas_call(finish_kernel, out_shape=(jax.ShapeDtypeStruct(shape, jnp....]
    pallas_call x13 -> x12, Pallas kernels: 6.16 us -> 5.33 us  [on_chip(): pl.pallas_call(kernel, out_shape=outs, in_specs=[spec] * len(args), out_s...]
where the time goes in v11:
time: 59.8 us; the launch traced here: 59.6 us
  starting transfers between devices  26.8 us (45%)
  waiting for transfers between devices  22.1 us (37%)
  Pallas kernels  9.5 us (16%)
  between operations  0.9 us (2%)
    ppermute x17, starting transfers between devices, send(): return lax.ppermute(block, axis, pairs)  25.2 us
    ppermute x17, waiting for transfers between devices, send(): return lax.ppermute(block, axis, pairs)  13.7 us
    ppermute x2, waiting for transfers between devices, shot_terms(): return (block, lax.ppermute(block, 'shot', swap))  7.32 us
    pallas_call x12, Pallas kernels, on_chip(): pl.pallas_call(kernel, out_shape=outs, in_specs=[spec] * len(args), out_s...  5.33 us
    pallas_call x2, Pallas kernels, load(): pl.pallas_call(kernel, out_shape=tuple((pltpu.VMEM(*shape) for shape in s...  2.15 us
    ppermute x2, starting transfers between devices, shot_terms(): return (block, lax.ppermute(block, 'shot', swap))  1.57 us
  transfers between devices with their start and end apart: 20, of which 10 were waited for; matrix products, arithmetic and copies ran while one was open for 0% of the time, Pallas kernels for 9%

profile of v11, /device:TPU:0, one launch (start us, length us, event | category | flops | bytes accessed | tf_op | source)
XLA Modules:
  0.0 59.6 jit_solution(6153628733645701608)
XLA Ops:
  0.6 1.1 %shard_map.114 = (f32[8,64,128]{2,1,0:T(8,128)S(1)}, f32[2,2,64,128]{3,2,1,0:T(8,128)S(1)}, s32[2,2048]{1,0:T(2,128)S(1)}, f32[2,2,2048]{2,1,0:T(2,128)S(1)}) custom-call(f32[2,2,64,128]{3,2,1,0:T(8,128)} %prev.1, f32[2,2,64,128]{3,2,1,0:T(8,128)} %last.1, f32[2,2,64,128]{3,2,1,0:T(8,128)} %late.1, s32[2,2048]{1,0:T(2,128)} %cells.1, f32[2,2,2048]{2,1,0:T(2,128)} %observed.1), custom_call_target="tpu_custom_call" | custom-call | tf_op jit(solution)/shard_map/pallas_call | solution.py:587
  1.7 3.1 %collective-permute-start.7 = (f32[8,64,128]{2,1,0:T(8,128)S(1)}, f32[8,64,128]{2,1,0:T(8,128)S(1)}, u32[]{:S(2)}, u32[]{:S(2)}) collective-permute-start(f32[8,64,128]{2,1,0:T(8,128)S(1)} %get-tuple-element.43.refs_1_), channel_id=1, source_target_pairs={{0,4},{4,0},{8,12},{12,8},{1,5},{5,1},{9,13},{13,9},{2,6},{6,2},{1... | collective-permute-start | bytes 786440 | tf_op jit(solution)/shard_map/ppermute | solution.py:32
  4.9 0.7 %collective-permute-start.8 = (f32[8,64,128]{2,1,0:T(8,128)S(1)}, f32[8,64,128]{2,1,0:T(8,128)S(1)}, u32[]{:S(2)}, u32[]{:S(2)}) collective-permute-start(f32[8,64,128]{2,1,0:T(8,128)S(1)} %get-tuple-element.43.refs_1_), channel_id=1, source_target_pairs={{4,8},{8,4},{5,9},{9,5},{6,10},{10,6},{7,11},{11,7},{20,24},{24,20... | collective-permute-start | bytes 786440 | tf_op jit(solution)/shard_map/ppermute | solution.py:32
  5.5 1.0 %shard_map.113 = (f32[7,64,128]{2,1,0:T(8,128)S(1)}, f32[48,128]{1,0:T(8,128)S(1)}) custom-call(f32[2,2,64,128]{3,2,1,0:T(8,128)} %now.1, f32[2,64,128]{2,1,0:T(8,128)} %dens.1, f32[2,64,64]{2,1,0:T(8,128)} %velocity.1), custom_call_target="tpu_custom_call" | custom-call | tf_op jit(solution)/shard_map/pallas_call | solution.py:587
  6.6 4.4 %collective-permute-start = (f32[7,64,128]{2,1,0:T(8,128)S(1)}, f32[7,64,128]{2,1,0:T(8,128)S(1)}, u32[]{:S(2)}, u32[]{:S(2)}) collective-permute-start(f32[7,64,128]{2,1,0:T(8,128)S(1)} %get-tuple-element.36.first.refs_0_), channel_id=1, source_target_pairs={{0,4},{4,0},{8,12},{12,8},{1,5},{5,1},{9,13},{13,9},{2,6},{6,2},{1... | collective-permute-start | bytes 688136 | tf_op jit(solution)/shard_map/ppermute | solution.py:32
  11.0 0.7 %collective-permute-start.1 = (f32[7,64,128]{2,1,0:T(8,128)S(1)}, f32[7,64,128]{2,1,0:T(8,128)S(1)}, u32[]{:S(2)}, u32[]{:S(2)}) collective-permute-start(f32[7,64,128]{2,1,0:T(8,128)S(1)} %get-tuple-element.36.first.refs_0_), channel_id=1, source_target_pairs={{4,8},{8,4},{5,9},{9,5},{6,10},{10,6},{7,11},{11,7},{20,24},{24,20... | collective-permute-start | bytes 688136 | tf_op jit(solution)/shard_map/ppermute | solution.py:32
  11.7 0.1 collective-permute-start.2
  11.8 0.1 and_select_fusion
  12.0 1.0 %collective-permute-done.2.edges = f32[48,128]{1,0:T(8,128)S(1)} collective-permute-done((f32[48,128]{1,0:T(8,128)S(1)}, f32[48,128]{1,0:T(8,128)S(1)}, u32[]{:S(2)}, u32[]{:S(2)}) %collective-permute-start.2) | collective-permute-done | bytes 24608 | tf_op jit(solution)/shard_map/ppermute | solution.py:32
  13.0 3.1 %collective-permute-done.by_even.refs_3_ = f32[7,64,128]{2,1,0:T(8,128)S(1)} collective-permute-done((f32[7,64,128]{2,1,0:T(8,128)S(1)}, f32[7,64,128]{2,1,0:T(8,128)S(1)}, u32[]{:S(2)}, u32[]{:S(2)}) %collective-permute-start) | collective-permute-done | bytes 229408 | tf_op jit(solution)/shard_map/ppermute | solution.py:32
  16.1 0.0 collective-permute-done.1.by_odd.refs_4_
  16.1 0.2 shard_map.115
  16.3 0.1 collective-permute-start.5
  16.4 4.8 %collective-permute-start.3 = (f32[4,64,128]{2,1,0:T(8,128)S(1)}, f32[4,64,128]{2,1,0:T(8,128)S(1)}, u32[]{:S(2)}, u32[]{:S(2)}) collective-permute-start(f32[4,64,128]{2,1,0:T(8,128)S(1)} %get-tuple-element.39), channel_id=1, source_target_pairs={{0,4},{4,0},{8,12},{12,8},{1,5},{5,1},{9,13},{13,9},{2,6},{6,2},{1... | collective-permute-start | bytes 393224 | tf_op jit(solution)/shard_map/ppermute | solution.py:32
  21.2 0.7 %collective-permute-start.4 = (f32[4,64,128]{2,1,0:T(8,128)S(1)}, f32[4,64,128]{2,1,0:T(8,128)S(1)}, u32[]{:S(2)}, u32[]{:S(2)}) collective-permute-start(f32[4,64,128]{2,1,0:T(8,128)S(1)} %get-tuple-element.40), channel_id=1, source_target_pairs={{4,8},{8,4},{5,9},{9,5},{6,10},{10,6},{7,11},{11,7},{20,24},{24,20... | collective-permute-start | bytes 393224 | tf_op jit(solution)/shard_map/ppermute | solution.py:32
  21.9 0.0 collective-permute-done.5.got
  21.9 1.6 %collective-permute-start.6 = (f32[3,80,128]{2,1,0:T(8,128)S(1)}, f32[3,80,128]{2,1,0:T(8,128)S(1)}, u32[]{:S(2)}, u32[]{:S(2)}) collective-permute-start(f32[3,80,128]{2,1,0:T(8,128)S(1)} %shard_map.116.refs_2_), channel_id=1, source_target_pairs={{0,2},{2,0},{1,3},{3,1},{4,6},{6,4},{5,7},{7,5},{8,10},{10,8},{9,1... | collective-permute-start | bytes 368648 | tf_op jit(solution)/shard_map/ppermute | solution.py:32
  23.5 0.0 collective-permute-done.7.refs_5_
  23.5 0.0 collective-permute-done.8.refs_6_
  23.5 0.1 collective-permute-start.9
  23.6 1.6 %shard_map.118.refs_8_.refs_13_ = f32[3,320,128]{2,1,0:T(8,128)S(1)} custom-call(s32[1,2048]{1,0:T(1,128)S(1)} %get-tuple-element.78.row_ref, s32[1,2048]{1,0:T(1,128)S(1)} %get-tuple-element.73.col_ref, f32[2,2048]{1,0:T(2,128)S(1)} %get-tuple-element.71.obs_ref), custom_call_target="tpu_custom_call" | custom-call | flops 1174405120 | bytes 32768 | tf_op jit(solution)/shard_map/pallas_call | solution.py:40
  25.2 0.0 copy-start.1
  25.2 0.0 copy-start.2
  25.2 1.6 %shard_map.119.refs_9_.refs_14_ = f32[3,320,128]{2,1,0:T(8,128)S(1)} custom-call(s32[1,2048]{1,0:T(1,128)S(1)} %get-tuple-element.79.row_ref, s32[1,2048]{1,0:T(1,128)S(1)} %get-tuple-element.72.col_ref, f32[2,2048]{1,0:T(2,128)S(1)} %get-tuple-element.70.obs_ref), custom_call_target="tpu_custom_call" | custom-call | flops 1174405120 | bytes 32768 | tf_op jit(solution)/shard_map/pallas_call | solution.py:40
  26.8 0.0 collective-permute-done.9.refs_7_
  26.8 0.0 copy-done.1
  26.8 0.0 copy-done.2
  26.8 1.2 %early.1 = (f32[2,4,80,128]{3,2,1,0:T(8,128)S(1)}, f32[2,6,80,128]{3,2,1,0:T(8,128)S(1)}, f32[2,4,80,128]{3,2,1,0:T(8,128)S(1)}, f32[2,2,80,128]{3,2,1,0:T(8,128...) custom-call(f32[7,64,128]{2,1,0:T(8,128)S(1)} %get-tuple-element.36., ...), custom_call_target="tpu_custom_call" | custom-call | tf_op jit(solution)/shard_map/early/pallas_call | solution.py:694
  28.0 0.0 collective-permute-done.3.refs_0_
  28.0 0.0 collective-permute-done.4.refs_1_
  28.0 0.0 collective-permute-done.6.refs_3_
  28.0 0.2 shard_map.120
  28.2 0.7 %shard_map.121.mine = f32[2,64,128]{2,1,0:T(8,128)S(1)} custom-call(f32[6,80,128]{2,1,0:T(8,128)S(1)} %get-tuple-element.48.refs_0_.stiff, f32[2,4,80,128]{3,2,1,0:T(8,128)S(1)} %get-tuple-element.49.refs_1_, f32[2,2,80,128]{3,2,1,0:T(8,128)S(1)} %get-tuple-element.50.refs_2_, f32[2,6,80,128]{3,2,1,0:T(8,128)S(1)} %get-tuple-element.51.refs_3_, ...), custom_call_target="tpu_custom_call" | custom-call | bytes 4341760 | tf_op jit(solution)/shard_map/pallas_call | solution.py:40
  28.9 0.9 %collective-permute-start.10 = (f32[2,64,128]{2,1,0:T(8,128)S(1)}, f32[2,64,128]{2,1,0:T(8,128)S(1)}, u32[]{:S(2)}, u32[]{:S(2)}) collective-permute-start(f32[2,64,128]{2,1,0:T(8,128)S(1)} %shard_map.121.mine), channel_id=1, source_target_pairs={{0,2},{2,0},{1,3},{3,1},{4,6},{6,4},{5,7},{7,5},{8,10},{10,8},{9,1... | collective-permute-start | bytes 196616 | tf_op jit(solution)/shard_map/ppermute | solution.py:562
  29.8 3.6 %collective-permute-done.10.other = f32[2,64,128]{2,1,0:T(8,128)S(1)} collective-permute-done((f32[2,64,128]{2,1,0:T(8,128)S(1)}, f32[2,64,128]{2,1,0:T(8,128)S(1)}, u32[]{:S(2)}, u32[]{:S(2)}) %collective-permute-start.10) | collective-permute-done | bytes 65568 | tf_op jit(solution)/shard_map/ppermute | solution.py:562
  33.5 0.0 copy-start
  33.5 0.1 collective-permute-start.11
  33.6 1.2 %collective-permute-done.11.got = f32[24,128]{1,0:T(8,128)S(1)} collective-permute-done((f32[24,128]{1,0:T(8,128)S(1)}, f32[24,128]{1,0:T(8,128)S(1)}, u32[]{:S(2)}, u32[]{:S(2)}) %collective-permute-start.11) | collective-permute-done | bytes 12320 | tf_op jit(solution)/shard_map/ppermute | solution.py:32
  34.8 3.1 %collective-permute-start.12 = (f32[152,128]{1,0:T(8,128)S(1)}, f32[152,128]{1,0:T(8,128)S(1)}, u32[]{:S(2)}, u32[]{:S(2)}) collective-permute-start(f32[152,128]{1,0:T(8,128)S(1)} %get-tuple-element.64), channel_id=1, source_target_pairs={{0,4},{4,0},{8,12},{12,8},{1,5},{5,1},{9,13},{13,9},{2,6},{6,2},{1... | collective-permute-start | bytes 233480 | tf_op jit(solution)/shard_map/ppermute | solution.py:32
  37.8 1.2 %collective-permute-start.13 = (f32[152,128]{1,0:T(8,128)S(1)}, f32[152,128]{1,0:T(8,128)S(1)}, u32[]{:S(2)}, u32[]{:S(2)}) collective-permute-start(f32[152,128]{1,0:T(8,128)S(1)} %get-tuple-element.65), channel_id=1, source_target_pairs={{0,12},{4,8},{8,4},{12,0},{1,13},{5,9},{9,5},{13,1},{2,14},{6,10},... | collective-permute-start | bytes 233480 | tf_op jit(solution)/shard_map/ppermute | solution.py:32
  39.0 0.3 collective-permute-start.14
  39.4 4.5 %collective-permute-done.14 = f32[8,128]{1,0:T(8,128)S(1)} collective-permute-done((f32[8,128]{1,0:T(8,128)S(1)}, f32[8,128]{1,0:T(8,128)S(1)}, u32[]{:S(2)}, u32[]{:S(2)}) %collective-permute-start.14) | collective-permute-done | bytes 4128 | tf_op jit(solution)/shard_map/ppermute | solution.py:32
  43.9 0.0 collective-permute-done.12.by_even
  43.9 0.2 collective-permute-done.13.by_odd
  44.1 0.0 copy-done
  44.1 0.2 shard_map.124
  44.3 0.8 %shard_map.125.mine = f32[2,64,128]{2,1,0:T(8,128)S(1)} custom-call(f32[6,80,128]{2,1,0:T(8,128)S(1)} %get-tuple-element.66.refs_0_, f32[2,4,80,128]{3,2,1,0:T(8,128)S(1)} %get-tuple-element.49.refs_1_, f32[2,2,80,128]{3,2,1,0:T(8,128)S(1)} %get-tuple-element.50.refs_2_, f32[2,6,80,128]{3,2,1,0:T(8,128)S(1)} %get-tuple-element.51.refs_3_, ...), custom_call_target="tpu_custom_call" | custom-call | bytes 4341760 | tf_op jit(solution)/shard_map/pallas_call | solution.py:40
  45.1 0.7 %collective-permute-start.15 = (f32[2,64,128]{2,1,0:T(8,128)S(1)}, f32[2,64,128]{2,1,0:T(8,128)S(1)}, u32[]{:S(2)}, u32[]{:S(2)}) collective-permute-start(f32[2,64,128]{2,1,0:T(8,128)S(1)} %shard_map.125.mine), channel_id=1, source_target_pairs={{0,2},{2,0},{1,3},{3,1},{4,6},{6,4},{5,7},{7,5},{8,10},{10,8},{9,1... | collective-permute-start | bytes 196616 | tf_op jit(solution)/shard_map/ppermute | solution.py:562
  45.7 3.7 %collective-permute-done.15.other = f32[2,64,128]{2,1,0:T(8,128)S(1)} collective-permute-done((f32[2,64,128]{2,1,0:T(8,128)S(1)}, f32[2,64,128]{2,1,0:T(8,128)S(1)}, u32[]{:S(2)}, u32[]{:S(2)}) %collective-permute-start.15) | collective-permute-done | bytes 65568 | tf_op jit(solution)/shard_map/ppermute | solution.py:562
  49.4 0.1 collective-permute-start.16
  49.5 1.2 %collective-permute-done.16 = f32[8,128]{1,0:T(8,128)S(1)} collective-permute-done((f32[8,128]{1,0:T(8,128)S(1)}, f32[8,128]{1,0:T(8,128)S(1)}, u32[]{:S(2)}, u32[]{:S(2)}) %collective-permute-start.16) | collective-permute-done | bytes 4128 | tf_op jit(solution)/shard_map/ppermute | solution.py:738
  50.7 0.6 %collective-permute-start.17 = (f32[8,128]{1,0:T(8,128)S(1)}, f32[8,128]{1,0:T(8,128)S(1)}, u32[]{:S(2)}, u32[]{:S(2)}) collective-permute-start(f32[8,128]{1,0:T(8,128)S(1)} %max.24), channel_id=1, source_target_pairs={{0,4},{4,0},{8,12},{12,8},{1,5},{5,1},{9,13},{13,9},{2,6},{6,2},{1... | collective-permute-start | bytes 12296 | tf_op jit(solution)/shard_map/ppermute | solution.py:32
  51.3 2.0 %collective-permute-start.18 = (f32[8,128]{1,0:T(8,128)S(1)}, f32[8,128]{1,0:T(8,128)S(1)}, u32[]{:S(2)}, u32[]{:S(2)}) collective-permute-start(f32[8,128]{1,0:T(8,128)S(1)} %max.24), channel_id=1, source_target_pairs={{0,8},{4,12},{8,0},{12,4},{1,9},{5,13},{9,1},{13,5},{2,10},{6,14},... | collective-permute-start | bytes 12296 | tf_op jit(solution)/shard_map/ppermute | solution.py:32
  53.3 1.7 %collective-permute-start.19 = (f32[8,128]{1,0:T(8,128)S(1)}, f32[8,128]{1,0:T(8,128)S(1)}, u32[]{:S(2)}, u32[]{:S(2)}) collective-permute-start(f32[8,128]{1,0:T(8,128)S(1)} %max.24), channel_id=1, source_target_pairs={{0,12},{4,8},{8,4},{12,0},{1,13},{5,9},{9,5},{13,1},{2,14},{6,10},... | collective-permute-start | bytes 12296 | tf_op jit(solution)/shard_map/ppermute | solution.py:32
  55.0 0.0 collective-permute-done.17
  55.1 0.7 %collective-permute-done.18 = f32[8,128]{1,0:T(8,128)S(1)} collective-permute-done((f32[8,128]{1,0:T(8,128)S(1)}, f32[8,128]{1,0:T(8,128)S(1)}, u32[]{:S(2)}, u32[]{:S(2)}) %collective-permute-start.18) | collective-permute-done | bytes 4128 | tf_op jit(solution)/shard_map/ppermute | solution.py:32
  55.8 2.9 %collective-permute-done.19 = f32[8,128]{1,0:T(8,128)S(1)} collective-permute-done((f32[8,128]{1,0:T(8,128)S(1)}, f32[8,128]{1,0:T(8,128)S(1)}, u32[]{:S(2)}, u32[]{:S(2)}) %collective-permute-start.19) | collective-permute-done | bytes 4128 | tf_op jit(solution)/shard_map/ppermute | solution.py:32
  58.7 0.9 %finish.1 = (f32[2,64,64]{2,1,0:T(8,128)}, f32[2,64,64]{2,1,0:T(8,128)}) custom-call(f32[2,64,128]{2,1,0:T(8,128)S(1)} %get-tuple-element.67.total, f32[8,128]{1,0:T(8,128)S(1)} %maximum_maximum_fusion.largest, f32[2,64,64]{2,1,0:T(8,128)S(1)} %get-tuple-element.69.velocity), custom_call_target="tpu_custom_call" | custom-call | tf_op jit(solution)/shard_map/finish/pallas_call | solution.py:741
  (11 shorter events, 0.1 us)
Async XLA Ops:
  1.7 21.7 %collective-permute-start.7 = (f32[8,64,128]{2,1,0:T(8,128)S(1)}, f32[8,64,128]{2,1,0:T(8,128)S(1)}, u32[]{:S(2)}, u32[]{:S(2)}) collective-permute-start(f32[8,64,128]{2,1,0:T(8,128)S(1)} %get-tuple-element.43.refs_1_), channel_id=1, source_target_pairs={{0,4},{4,0},{8,12},{12,8},{1,5},{5,1},{9,13},{13,9},{2,6},{6,2},{1... | collective-permute-start | bytes 786440 | tf_op jit(solution)/shard_map/ppermute | solution.py:32
  4.9 18.6 %collective-permute-start.8 = (f32[8,64,128]{2,1,0:T(8,128)S(1)}, f32[8,64,128]{2,1,0:T(8,128)S(1)}, u32[]{:S(2)}, u32[]{:S(2)}) collective-permute-start(f32[8,64,128]{2,1,0:T(8,128)S(1)} %get-tuple-element.43.refs_1_), channel_id=1, source_target_pairs={{4,8},{8,4},{5,9},{9,5},{6,10},{10,6},{7,11},{11,7},{20,24},{24,20... | collective-permute-start | bytes 786440 | tf_op jit(solution)/shard_map/ppermute | solution.py:32
  6.6 9.5 %collective-permute-start = (f32[7,64,128]{2,1,0:T(8,128)S(1)}, f32[7,64,128]{2,1,0:T(8,128)S(1)}, u32[]{:S(2)}, u32[]{:S(2)}) collective-permute-start(f32[7,64,128]{2,1,0:T(8,128)S(1)} %get-tuple-element.36.first.refs_0_), channel_id=1, source_target_pairs={{0,4},{4,0},{8,12},{12,8},{1,5},{5,1},{9,13},{13,9},{2,6},{6,2},{1... | collective-permute-start | bytes 688136 | tf_op jit(solution)/shard_map/ppermute | solution.py:32
  11.0 5.0 %collective-permute-start.1 = (f32[7,64,128]{2,1,0:T(8,128)S(1)}, f32[7,64,128]{2,1,0:T(8,128)S(1)}, u32[]{:S(2)}, u32[]{:S(2)}) collective-permute-start(f32[7,64,128]{2,1,0:T(8,128)S(1)} %get-tuple-element.36.first.refs_0_), channel_id=1, source_target_pairs={{4,8},{8,4},{5,9},{9,5},{6,10},{10,6},{7,11},{11,7},{20,24},{24,20... | collective-permute-start | bytes 688136 | tf_op jit(solution)/shard_map/ppermute | solution.py:32
  11.7 1.3 %collective-permute-start.2 = (f32[48,128]{1,0:T(8,128)S(1)}, f32[48,128]{1,0:T(8,128)S(1)}, u32[]{:S(2)}, u32[]{:S(2)}) collective-permute-start(f32[48,128]{1,0:T(8,128)S(1)} %get-tuple-element.37), channel_id=1, source_target_pairs={{0,1},{1,0},{2,3},{3,2},{4,5},{5,4},{6,7},{7,6},{8,9},{9,8},{10,11... | collective-permute-start | bytes 73736 | tf_op jit(solution)/shard_map/ppermute | solution.py:32
  16.3 5.6 %collective-permute-start.5 = (f32[24,128]{1,0:T(8,128)S(1)}, f32[24,128]{1,0:T(8,128)S(1)}, u32[]{:S(2)}, u32[]{:S(2)}) collective-permute-start(f32[24,128]{1,0:T(8,128)S(1)} %get-tuple-element.42), channel_id=1, source_target_pairs={{0,1},{1,0},{2,3},{3,2},{4,5},{5,4},{6,7},{7,6},{8,9},{9,8},{10,11... | collective-permute-start | bytes 36872 | tf_op jit(solution)/shard_map/ppermute | solution.py:32
  16.4 11.6 %collective-permute-start.3 = (f32[4,64,128]{2,1,0:T(8,128)S(1)}, f32[4,64,128]{2,1,0:T(8,128)S(1)}, u32[]{:S(2)}, u32[]{:S(2)}) collective-permute-start(f32[4,64,128]{2,1,0:T(8,128)S(1)} %get-tuple-element.39), channel_id=1, source_target_pairs={{0,4},{4,0},{8,12},{12,8},{1,5},{5,1},{9,13},{13,9},{2,6},{6,2},{1... | collective-permute-start | bytes 393224 | tf_op jit(solution)/shard_map/ppermute | solution.py:32
  21.2 6.8 %collective-permute-start.4 = (f32[4,64,128]{2,1,0:T(8,128)S(1)}, f32[4,64,128]{2,1,0:T(8,128)S(1)}, u32[]{:S(2)}, u32[]{:S(2)}) collective-permute-start(f32[4,64,128]{2,1,0:T(8,128)S(1)} %get-tuple-element.40), channel_id=1, source_target_pairs={{4,8},{8,4},{5,9},{9,5},{6,10},{10,6},{7,11},{11,7},{20,24},{24,20... | collective-permute-start | bytes 393224 | tf_op jit(solution)/shard_map/ppermute | solution.py:32
  21.9 6.1 %collective-permute-start.6 = (f32[3,80,128]{2,1,0:T(8,128)S(1)}, f32[3,80,128]{2,1,0:T(8,128)S(1)}, u32[]{:S(2)}, u32[]{:S(2)}) collective-permute-start(f32[3,80,128]{2,1,0:T(8,128)S(1)} %shard_map.116.refs_2_), channel_id=1, source_target_pairs={{0,2},{2,0},{1,3},{3,1},{4,6},{6,4},{5,7},{7,5},{8,10},{10,8},{9,1... | collective-permute-start | bytes 368648 | tf_op jit(solution)/shard_map/ppermute | solution.py:32
  23.5 3.2 %collective-permute-start.9 = (f32[368,128]{1,0:T(8,128)S(1)}, f32[368,128]{1,0:T(8,128)S(1)}, u32[]{:S(2)}, u32[]{:S(2)}) collective-permute-start(f32[368,128]{1,0:T(8,128)S(1)} %shard_map.117), channel_id=1, source_target_pairs={{0,1},{1,0},{2,3},{3,2},{4,5},{5,4},{6,7},{7,6},{8,9},{9,8},{10,11... | collective-permute-start | bytes 565256 | tf_op jit(solution)/shard_map/ppermute | solution.py:32
  25.2 1.6 %copy-start.1 = (f32[2,2]{1,0:T(2,128)S(1)}, f32[2,2]{1,0:T(2,128)}, u32[]{:S(2)}) copy-start(f32[2,2]{1,0:T(2,128)} %refs_11_.1) | copy-start | bytes 52
  25.2 1.6 %copy-start.2 = (s32[2]{0:T(128)S(1)}, s32[2]{0:T(128)}, u32[]{:S(2)}) copy-start(s32[2]{0:T(128)} %refs_10_.1) | copy-start | bytes 28
  28.9 4.6 %collective-permute-start.10 = (f32[2,64,128]{2,1,0:T(8,128)S(1)}, f32[2,64,128]{2,1,0:T(8,128)S(1)}, u32[]{:S(2)}, u32[]{:S(2)}) collective-permute-start(f32[2,64,128]{2,1,0:T(8,128)S(1)} %shard_map.121.mine), channel_id=1, source_target_pairs={{0,2},{2,0},{1,3},{3,1},{4,6},{6,4},{5,7},{7,5},{8,10},{10,8},{9,1... | collective-permute-start | bytes 196616 | tf_op jit(solution)/shard_map/ppermute | solution.py:562
  33.5 10.6 %copy-start = (f32[2,64,64]{2,1,0:T(8,128)S(1)}, f32[2,64,64]{2,1,0:T(8,128)}, u32[]{:S(2)}) copy-start(f32[2,64,64]{2,1,0:T(8,128)} %velocity.1) | copy-start | bytes 98308
  33.5 1.2 %collective-permute-start.11 = (f32[24,128]{1,0:T(8,128)S(1)}, f32[24,128]{1,0:T(8,128)S(1)}, u32[]{:S(2)}, u32[]{:S(2)}) collective-permute-start(f32[24,128]{1,0:T(8,128)S(1)} %get-tuple-element.62.mine), channel_id=1, source_target_pairs={{0,1},{1,0},{2,3},{3,2},{4,5},{5,4},{6,7},{7,6},{8,9},{9,8},{10,11... | collective-permute-start | bytes 36872 | tf_op jit(solution)/shard_map/ppermute | solution.py:32
  34.8 9.1 %collective-permute-start.12 = (f32[152,128]{1,0:T(8,128)S(1)}, f32[152,128]{1,0:T(8,128)S(1)}, u32[]{:S(2)}, u32[]{:S(2)}) collective-permute-start(f32[152,128]{1,0:T(8,128)S(1)} %get-tuple-element.64), channel_id=1, source_target_pairs={{0,4},{4,0},{8,12},{12,8},{1,5},{5,1},{9,13},{13,9},{2,6},{6,2},{1... | collective-permute-start | bytes 233480 | tf_op jit(solution)/shard_map/ppermute | solution.py:32
  37.8 6.2 %collective-permute-start.13 = (f32[152,128]{1,0:T(8,128)S(1)}, f32[152,128]{1,0:T(8,128)S(1)}, u32[]{:S(2)}, u32[]{:S(2)}) collective-permute-start(f32[152,128]{1,0:T(8,128)S(1)} %get-tuple-element.65), channel_id=1, source_target_pairs={{0,12},{4,8},{8,4},{12,0},{1,13},{5,9},{9,5},{13,1},{2,14},{6,10},... | collective-permute-start | bytes 233480 | tf_op jit(solution)/shard_map/ppermute | solution.py:32
  39.0 4.8 %collective-permute-start.14 = (f32[8,128]{1,0:T(8,128)S(1)}, f32[8,128]{1,0:T(8,128)S(1)}, u32[]{:S(2)}, u32[]{:S(2)}) collective-permute-start(f32[8,128]{1,0:T(8,128)S(1)} %slice.34), channel_id=1, source_target_pairs={{0,8},{4,12},{8,0},{12,4},{1,9},{5,13},{9,1},{13,5},{2,10},{6,14},... | collective-permute-start | bytes 12296 | tf_op jit(solution)/shard_map/ppermute | solution.py:32
  45.1 4.3 %collective-permute-start.15 = (f32[2,64,128]{2,1,0:T(8,128)S(1)}, f32[2,64,128]{2,1,0:T(8,128)S(1)}, u32[]{:S(2)}, u32[]{:S(2)}) collective-permute-start(f32[2,64,128]{2,1,0:T(8,128)S(1)} %shard_map.125.mine), channel_id=1, source_target_pairs={{0,2},{2,0},{1,3},{3,1},{4,6},{6,4},{5,7},{7,5},{8,10},{10,8},{9,1... | collective-permute-start | bytes 196616 | tf_op jit(solution)/shard_map/ppermute | solution.py:562
  49.4 1.2 %collective-permute-start.16 = (f32[8,128]{1,0:T(8,128)S(1)}, f32[8,128]{1,0:T(8,128)S(1)}, u32[]{:S(2)}, u32[]{:S(2)}) collective-permute-start(f32[8,128]{1,0:T(8,128)S(1)} %get-tuple-element.68), channel_id=1, source_target_pairs={{0,1},{1,0},{2,3},{3,2},{4,5},{5,4},{6,7},{7,6},{8,9},{9,8},{10,11... | collective-permute-start | bytes 12296 | tf_op jit(solution)/shard_map/ppermute | solution.py:738
  50.7 4.4 %collective-permute-start.17 = (f32[8,128]{1,0:T(8,128)S(1)}, f32[8,128]{1,0:T(8,128)S(1)}, u32[]{:S(2)}, u32[]{:S(2)}) collective-permute-start(f32[8,128]{1,0:T(8,128)S(1)} %max.24), channel_id=1, source_target_pairs={{0,4},{4,0},{8,12},{12,8},{1,5},{5,1},{9,13},{13,9},{2,6},{6,2},{1... | collective-permute-start | bytes 12296 | tf_op jit(solution)/shard_map/ppermute | solution.py:32
  51.3 4.5 %collective-permute-start.18 = (f32[8,128]{1,0:T(8,128)S(1)}, f32[8,128]{1,0:T(8,128)S(1)}, u32[]{:S(2)}, u32[]{:S(2)}) collective-permute-start(f32[8,128]{1,0:T(8,128)S(1)} %max.24), channel_id=1, source_target_pairs={{0,8},{4,12},{8,0},{12,4},{1,9},{5,13},{9,1},{13,5},{2,10},{6,14},... | collective-permute-start | bytes 12296 | tf_op jit(solution)/shard_map/ppermute | solution.py:32
  53.3 5.4 %collective-permute-start.19 = (f32[8,128]{1,0:T(8,128)S(1)}, f32[8,128]{1,0:T(8,128)S(1)}, u32[]{:S(2)}, u32[]{:S(2)}) collective-permute-start(f32[8,128]{1,0:T(8,128)S(1)} %max.24), channel_id=1, source_target_pairs={{0,12},{4,8},{8,4},{12,0},{1,13},{5,9},{9,5},{13,1},{2,14},{6,10},... | collective-permute-start | bytes 12296 | tf_op jit(solution)/shard_map/ppermute | solution.py:32
